TPU v7x, 32 devices: a whole 2x2x4 slice. The times are simulated.
32 devices in a mesh: cols: 32 (over z, y, x, core).
Axes of the slice: x: 2, y: 2, z: 4, core: 2. Of those that a mesh axis runs over, the one named last changes fastest.
Arguments:
- mortality: bfloat16 [1024, 16384], P('cols'), may hold values from -18 to 18
Outputs:
- projected: bfloat16 [1024, 16384], P('cols')
All inputs are finite; a program needn't handle non-finite values.
Results may differ from a plain program's by a relative error of at most 0.02.
Values may be sent and summed in bfloat16 or wider, within the bound.
No kernel may reach another device: no remote copies, remote signals or barrier semaphores. Data moves between devices by JAX's collectives and lax.ppermute only.
A program may use at most 64 MiB of HBM per device.

v0:
```python
import jax
import jax.numpy as jnp
from jax import lax
from jax.experimental import pallas as pl
from jax.experimental.pallas import tpu as pltpu
from jax.sharding import PartitionSpec as P

RANK = 128
LEVELS = 5
SWEEPS = 3
PLANE = 8
PLANES = 2**LEVELS // PLANE
TILE = 8
PANEL = 64
PIVOT_SHARE = 2e-5

precise = lax.Precision.HIGHEST
f32 = jnp.float32
bf16 = jnp.bfloat16


def iota2(shape, dim):
    return lax.broadcasted_iota(jnp.int32, shape, dim)


def dot(a, b, ca, cb, precision=precise):
    return lax.dot_general(a, b, (((ca,), (cb,)), ((), ())), precision=precision, preferred_element_type=f32)


def dot_low(a, b, ca, cb):
    return dot(a, b, ca, cb, None)


def lanes_of(x, k):
    return jnp.broadcast_to(x[:, k : k + 1], x.shape)


def rows_of(x, s):
    return jnp.broadcast_to(x[s : s + 1, :], x.shape)


def eliminate(sets, first, ahead):
    lane = iota2((TILE, RANK), 1)
    sub = iota2((TILE, RANK), 0)
    count = len(sets[0])
    early = [None] * len(sets)
    for t in range(count):
        g = TILE * (first + t)
        spread, coming = [], []
        for n, tiles in enumerate(sets):
            cols = {} if early[n] is None else {t: early[n]}
            for i in range(t + len(cols), count):
                cols[i] = [lanes_of(tiles[i], g + j) for j in range(TILE)]
            spread.append(cols)
            near = (t, t + 1) if ahead and t + 1 < count else ()
            coming.append({i: [lanes_of(tiles[i], g + TILE + j) for j in range(TILE)] for i in near})
        for k in range(TILE):
            here = lane == g + k
            for tiles, cols, look in zip(sets, spread, coming):
                pivot_row = [rows_of(cols[t][j], k) if j >= k else None for j in range(TILE)]
                inv = 1.0 / pivot_row[k]
                scaled = [pivot_row[j] * inv if j > k else None for j in range(TILE)]
                row = jnp.where(here, 1.0, rows_of(tiles[t], k)) * inv
                look_row = [rows_of(x, k) * inv for x in look[t]] if look else None
                for i in range(t, count):
                    col = cols[i][k]
                    if i == t:
                        col = jnp.where(sub > k, col, 0.0)
                        kept = jnp.where(here & (sub > k), 0.0, tiles[i])
                    else:
                        kept = jnp.where(here, 0.0, tiles[i])
                    for j in range(k + 1, TILE):
                        cols[i][j] = cols[i][j] - col * scaled[j]
                    tiles[i] = kept - col * row
                    if i in look:
                        look[i] = [x - col * y for x, y in zip(look[i], look_row)]
        early = [look.get(t + 1) for look in coming]
    return sets


def inverse_factors(matrices):
    alone = len(matrices) == 1
    size = PANEL if alone else PANEL // 2
    rests = list(matrices)
    done = [[] for _ in rests]
    for lo in range(0, RANK, size):
        hi = lo + size
        sets = [[rest[TILE * t : TILE * t + TILE, :] for t in range(size // TILE)] for rest in rests]
        for n, tiles in enumerate(eliminate(sets, lo // TILE, alone)):
            panel = jnp.concatenate(tiles, 0)
            done[n].append(panel)
            if hi == RANK:
                continue
            r = iota2((size, RANK), 0) + lo
            c = iota2((size, RANK), 1)
            pivots = jnp.sum(jnp.where(r == c, panel, 0.0), 1, keepdims=True)
            rows = jnp.where(r == c, 1.0, jnp.where((c > r) & (c < hi), 0.0, panel))
            tail = rests[n][size:, :]
            c = iota2(tail.shape, 1)
            tail = jnp.where((c >= lo) & (c < hi), 0.0, tail)
            rests[n] = tail - dot(panel * (1.0 / pivots), rows, 0, 0)[hi:, :]
    results = []
    for panels in done:
        x = jnp.concatenate(panels, 0)
        r = iota2((RANK, RANK), 0)
        c = iota2((RANK, RANK), 1)
        pivots = jnp.sum(jnp.where(r == c, x, 0.0), 1, keepdims=True)
        unit = jnp.where(r > c, x, jnp.where(r == c, 1.0, 0.0))
        results.append((unit * lax.rsqrt(pivots), pivots))
    return results


def diagonal_of(x):
    return jnp.sum(jnp.where(iota2(x.shape, 0) == iota2(x.shape, 1), x, 0.0), 1, keepdims=True)


def leading_spaces(grams, work):
    for gram, (gram_ref, imaged_ref, _) in zip(grams, work):
        largest = jnp.maximum(diagonal_of(gram[:RANK, :RANK]), diagonal_of(gram[RANK:, RANK:]))
        gram = gram * (1.0 / jnp.max(largest, keepdims=True))
        gram_ref[...] = gram
        imaged = gram[:, :RANK]
        for step in range(SWEEPS - 1):
            imaged = dot(gram, imaged, 1, 0)
        imaged_ref[...] = imaged

    def attempt(step):
        inners = [dot(imaged_ref[...], imaged_ref[...], 0, 0) for _, imaged_ref, _ in work]
        share = None
        for inner, (factor, pivots), (_, imaged_ref, frame_ref) in zip(inners, inverse_factors(inners), work):
            frame_ref[...] = dot(imaged_ref[...], factor, 1, 1)
            ratio = pivots / diagonal_of(inner)
            share = ratio if share is None else jnp.where(ratio < share, ratio, share)
        good = jnp.logical_and(step == 0, jnp.min(share) > PIVOT_SHARE)
        last = jnp.logical_or(good, step == SWEEPS)

        @pl.when(jnp.logical_not(last))
        def _():
            for gram_ref, imaged_ref, frame_ref in work:
                first = gram_ref[:, :RANK]
                imaged_ref[...] = jnp.where(step == 0, first, dot(gram_ref[...], frame_ref[...], 1, 0))

        return jnp.where(last, SWEEPS + 1, step + 1)

    lax.while_loop(lambda step: step <= SWEEPS, attempt, jnp.int32(0))
    return [frame_ref[...].astype(bf16) for _, _, frame_ref in work]


work_shapes = [pltpu.VMEM((2 * RANK, 2 * RANK), f32)] + [pltpu.VMEM((2 * RANK, RANK), f32)] * 2


def place(pos_ref):
    pos = pos_ref[0]
    return pos % 2, pos // PLANE % PLANES


def split(blocks, core, mine_ref, theirs_ref):
    half = mine_ref.shape[1]
    for b, block in enumerate(blocks):
        low, high = block[:half, :], block[half:, :]
        mine_ref[b] = jnp.where(core == 1, high, low)
        theirs_ref[b] = jnp.where(core == 1, low, high)


def joined(mine_ref, other_ref, core, b):
    mine, other = mine_ref[b], other_ref[b]
    low = jnp.where(core == 1, other, mine)
    high = jnp.where(core == 1, mine, other)
    return jnp.concatenate([low, high], 0)


def chunk(z, m, width):
    return pl.ds(pl.multiple_of((z ^ m) * width, width), width)


def member(pos_ref):
    return pos_ref[0] % PLANE


def parts_kernel(pos_ref, x_ref, *refs):
    width = refs[0].shape[1]
    for m in range(PLANE):
        refs[m][...] = x_ref[:, chunk(member(pos_ref), m, width)]


def gram_kernel(pos_ref, *refs):
    parts, (rows_ref, mine_ref, theirs_ref) = refs[:PLANE], refs[PLANE:]
    core, _ = place(pos_ref)
    height = parts[0].shape[0]
    for m in range(PLANE):
        rows_ref[chunk(member(pos_ref), m, height), :] = parts[m][...]
    rows = rows_ref[...]
    gram = dot_low(rows, rows, 1, 1)
    split([gram[:RANK, :RANK], gram[RANK:, :RANK], gram[RANK:, RANK:]], core, mine_ref, theirs_ref)


def square(a, b, d):
    return jnp.concatenate([jnp.concatenate([a, b.T], 1), jnp.concatenate([b, d], 1)], 0)


def plane_gram(mine_ref, other_ref, core):
    return square(*[joined(mine_ref, other_ref, core, b) for b in range(3)])


def node_kernel(pos_ref, mine_ref, other_ref, rows_ref, *refs):
    nodes, low_ref, work = refs[:PLANES], refs[PLANES], refs[PLANES + 1 :]
    core, z = place(pos_ref)
    (low,) = leading_spaces([plane_gram(mine_ref, other_ref, core)], [work])
    low_ref[...] = low
    width = nodes[0].shape[1]
    for m in range(PLANES):
        nodes[m][...] = dot_low(low, rows_ref[:, chunk(z, m, width)], 0, 0).astype(bf16)


def reduced(gram, low):
    wide = low.astype(f32)
    return dot(wide, dot(gram, wide, 1, 0), 0, 0)


def diag_kernel(pos_ref, mine_ref, other_ref, low_ref, diag_ref):
    core, _ = place(pos_ref)
    diag = reduced(plane_gram(mine_ref, other_ref, core), low_ref[...])
    half = diag_ref.shape[1]
    diag_ref[0] = jnp.where(core == 1, diag[half:, :], diag[:half, :]).astype(diag_ref.dtype)


PAIRS = [(i, j) for i in range(PLANES) for j in range(i + 1, PLANES)]


def cross_kernel(pos_ref, *refs):
    nodes, (mine_ref, theirs_ref, all_ref) = refs[:PLANES], refs[PLANES:]
    core, z = place(pos_ref)
    for m in range(PLANES):
        all_ref[z ^ m] = nodes[m][...]
    split([dot_low(all_ref[j], all_ref[i], 1, 1) for i, j in PAIRS], core, mine_ref, theirs_ref)


def top_kernel(pos_ref, mine_ref, other_ref, *refs):
    nodes, (top_ref, gram_ref, low_ref), refs = refs[:PLANES], refs[PLANES : PLANES + 3], refs[PLANES + 3 :]
    all_ref, diag_ref, work = refs[0], refs[1], [refs[2:5], refs[5:8]]
    core, z = place(pos_ref)
    for m in range(PLANES):
        all_ref[z ^ m] = nodes[m][...]
        diag_ref[z ^ m] = joined(mine_ref, other_ref, core, len(PAIRS) + m)
    cross = {pair: joined(mine_ref, other_ref, core, b) for b, pair in enumerate(PAIRS)}
    gram_a = square(diag_ref[0], cross[0, 1], diag_ref[1])
    gram_b = square(diag_ref[2], cross[2, 3], diag_ref[3])
    low_a, low_b = leading_spaces([gram_a, gram_b], work)
    between = jnp.concatenate(
        [
            jnp.concatenate([cross[0, 2], cross[1, 2]], 1),
            jnp.concatenate([cross[0, 3], cross[1, 3]], 1),
        ],
        0,
    )
    gram = square(
        reduced(gram_a, low_a),
        dot(low_b.astype(f32), dot(between, low_a.astype(f32), 1, 0), 0, 0),
        reduced(gram_b, low_b),
    )
    gram_ref[...] = gram
    (low,) = leading_spaces([gram], work[:1])
    low_ref[...] = low
    node_a = dot_low(low_a, jnp.concatenate([all_ref[0], all_ref[1]], 0), 0, 0).astype(bf16)
    node_b = dot_low(low_b, jnp.concatenate([all_ref[2], all_ref[3]], 0), 0, 0).astype(bf16)
    top_ref[...] = dot_low(low, jnp.concatenate([node_a, node_b], 0), 0, 0).astype(bf16)


def factor_kernel(gram_ref, low_ref, factor_ref):
    factor_ref[...] = inverse_factors([reduced(gram_ref[...], low_ref[...])])[0][0]


def coeffs_kernel(pos_ref, rows_ref, factor_ref, *refs):
    tops, (mine_ref, theirs_ref) = refs[:PLANES], refs[PLANES:]
    core, z = place(pos_ref)
    width = tops[0].shape[1]
    total = None
    for m in range(PLANES):
        part = dot_low(rows_ref[:, chunk(z, m, width)], tops[m][...], 1, 1)
        total = part if total is None else total + part
    split([dot(total, factor_ref[...], 1, 1)], core, mine_ref, theirs_ref)


def project_kernel(pos_ref, mine_ref, other_ref, factor_ref, *refs):
    tops, outs, solved_ref = refs[:PLANES], refs[PLANES:-1], refs[-1]
    core, z = place(pos_ref)
    height, width = outs[0].shape[0], tops[0].shape[1]
    solved_ref[...] = dot(joined(mine_ref, other_ref, core, 0), factor_ref[...], 1, 0)
    solved = [solved_ref[chunk(member(pos_ref), m, height), :] for m in range(PLANE)]
    solved = jnp.concatenate(solved, 0).astype(bf16)
    for c in range(PLANES):
        made = dot_low(solved, tops[c][...], 1, 0).astype(bf16)
        for m in range(PLANE):
            outs[m][:, chunk(z, c, width)] = made[m * height : (m + 1) * height, :]


def whole_kernel(pos_ref, *refs):
    parts, out_ref = refs[:PLANE], refs[PLANE]
    width = parts[0].shape[1]
    for m in range(PLANE):
        out_ref[:, chunk(member(pos_ref), m, width)] = parts[m][...]


smem = pl.BlockSpec(memory_space=pltpu.SMEM)
vmem = pl.BlockSpec(memory_space=pltpu.VMEM)


def kernel(fn, outs, *args, scratch=(), scalar=True):
    single = not isinstance(outs, (list, tuple))
    shapes = [outs] if single else list(outs)
    res = pl.pallas_call(
        fn,
        out_shape=[jax.ShapeDtypeStruct(s, d) for s, d in shapes] if not single else None,
        in_specs=[smem if scalar and i == 0 else vmem for i in range(len(args))],
        out_specs=[vmem for _ in shapes],
        scratch_shapes=list(scratch),
        compiler_params=pltpu.CompilerParams(vmem_limit_bytes=40 * 2**20),
        name=fn.__name__,
    )(*args)
    return res


def body(mortality):
    count = lax.axis_size("cols")
    pos = lax.axis_index("cols").astype(jnp.int32).reshape(1)

    def swap(x, apart):
        return lax.ppermute(x, "cols", [(i, i ^ apart) for i in range(count)])

    def swap_all(parts, unit):
        return [parts[0]] + [swap(parts[m], unit * m) for m in range(1, len(parts))]

    def sum4(parts):
        parts = [p.astype(f32) for p in parts]
        return (parts[0] + parts[1]) + (parts[2] + parts[3])

    def plane_sum(mine, theirs):
        return sum4(swap_all([(mine + swap(theirs, 1)).astype(bf16)] * 4, 2))

    block, total = mortality.shape
    height, width = block * PLANE, total // PLANE
    part = width // PLANES
    half = RANK // 2

    parts = kernel(parts_kernel, [((block, width), bf16)] * PLANE, pos, mortality)
    parts = swap_all(parts, 1)
    rows, mine, theirs = kernel(
        gram_kernel, [((height, width), bf16)] + [((3, half, RANK), f32)] * 2, pos, *parts
    )
    mine = plane_sum(mine, theirs)
    other = swap(mine, 1)
    *nodes, low = kernel(
        node_kernel,
        [((RANK, part), bf16)] * PLANES + [((2 * RANK, RANK), bf16)],
        pos, mine, other, rows,
        scratch=work_shapes,
    )
    nodes = swap_all(nodes, PLANE)
    (diag,) = kernel(diag_kernel, [((1, half, RANK), bf16)], pos, mine, other, low)

    mine, theirs = kernel(
        cross_kernel,
        [((len(PAIRS), half, RANK), f32)] * 2,
        pos, *nodes,
        scratch=[pltpu.VMEM((PLANES, RANK, part), bf16)],
    )
    mine = plane_sum(mine, theirs)
    both = swap_all([jnp.concatenate([mine.astype(bf16), diag], 0)] * PLANES, PLANE)
    mine = jnp.concatenate([sum4([x[: len(PAIRS)] for x in both])] + [x[len(PAIRS) :].astype(f32) for x in both], 0)
    top, gram, low = kernel(
        top_kernel,
        [((RANK, part), bf16), ((2 * RANK, 2 * RANK), f32), ((2 * RANK, RANK), bf16)],
        pos, mine, swap(mine, 1), *nodes,
        scratch=[pltpu.VMEM((PLANES, RANK, part), bf16), pltpu.VMEM((PLANES, RANK, RANK), f32)] + work_shapes * 2,
    )
    tops = swap_all([top] * PLANES, PLANE)
    (factor,) = kernel(factor_kernel, [((RANK, RANK), f32)], gram, low, scalar=False)

    mine, theirs = kernel(coeffs_kernel, [((1, height // 2, RANK), f32)] * 2, pos, rows, factor, *tops)
    mine = plane_sum(mine, theirs)
    outs = kernel(
        project_kernel,
        [((block, width), bf16)] * PLANE,
        pos, mine, swap(mine, 1), factor, *tops,
        scratch=[pltpu.VMEM((height, RANK), f32)],
    )
    (result,) = kernel(whole_kernel, [((block, total), bf16)], pos, *swap_all(outs, 1))
    return result


def solution(mesh):
    in_specs = (P("cols", None),)
    out_specs = P("cols", None)
    return jax.shard_map(body, mesh=mesh, in_specs=in_specs, out_specs=out_specs, check_vma=False)
```

profile of v0, /device:TPU:0, one launch (start us, length us, event | category | flops | bytes accessed | tf_op | source)
XLA Modules:
  0.0 129.8 jit_solution(12625681276121145087)
XLA Ops:
  0.0 1.2 copy-done
  1.3 0.5 collective-permute-start
  1.8 2.6 %collective-permute-start.1 = (bf16[32,2048]{1,0:T(8,128)(2,1)S(1)}, bf16[32,2048]{1,0:T(8,128)(2,1)S(1)}, u32[]{:S(2)}, u32[]{:S(2)}) collective-permute-start(bf16[32,2048]{1,0:T(8,128)(2,1)S(1)} %get-tuple-element.38), channel_id=1, source_target_pairs={{0,2},{1,3},{2,0},{3,1},{4,6},{5,7},{6,4},{7,5},{8,10},{9,11},{10,... | collective-permute-start | bytes 393224 | tf_op jit(solution)/shard_map/ppermute | solution.py:328
  4.5 1.8 %collective-permute-start.3 = (bf16[32,2048]{1,0:T(8,128)(2,1)S(1)}, bf16[32,2048]{1,0:T(8,128)(2,1)S(1)}, u32[]{:S(2)}, u32[]{:S(2)}) collective-permute-start(bf16[32,2048]{1,0:T(8,128)(2,1)S(1)} %get-tuple-element.40), channel_id=1, source_target_pairs={{0,4},{1,5},{2,6},{3,7},{4,0},{5,1},{6,2},{7,3},{8,12},{9,13},{10,... | collective-permute-start | bytes 393224 | tf_op jit(solution)/shard_map/ppermute | solution.py:328
  6.2 2.6 %collective-permute-start.5 = (bf16[32,2048]{1,0:T(8,128)(2,1)S(1)}, bf16[32,2048]{1,0:T(8,128)(2,1)S(1)}, u32[]{:S(2)}, u32[]{:S(2)}) collective-permute-start(bf16[32,2048]{1,0:T(8,128)(2,1)S(1)} %get-tuple-element.42), channel_id=1, source_target_pairs={{0,6},{1,7},{2,4},{3,5},{4,2},{5,3},{6,0},{7,1},{8,14},{9,15},{10,... | collective-permute-start | bytes 393224 | tf_op jit(solution)/shard_map/ppermute | solution.py:328
  8.8 1.6 %collective-permute-start.6 = (bf16[32,2048]{1,0:T(8,128)(2,1)S(1)}, bf16[32,2048]{1,0:T(8,128)(2,1)S(1)}, u32[]{:S(2)}, u32[]{:S(2)}) collective-permute-start(bf16[32,2048]{1,0:T(8,128)(2,1)S(1)} %get-tuple-element.43), channel_id=1, source_target_pairs={{0,7},{1,6},{2,5},{3,4},{4,3},{5,2},{6,1},{7,0},{8,15},{9,14},{10,... | collective-permute-start | bytes 393224 | tf_op jit(solution)/shard_map/ppermute | solution.py:328
  10.4 0.6 collective-permute-done.2.refs_3_
  11.0 6.9 %collective-permute-done.4.refs_5_ = bf16[32,2048]{1,0:T(8,128)(2,1)S(1)} collective-permute-done((bf16[32,2048]{1,0:T(8,128)(2,1)S(1)}, bf16[32,2048]{1,0:T(8,128)(2,1)S(1)}, u32[]{:S(2)}, u32[]{:S(2)}) %collective-permute-start.4) | collective-permute-done | bytes 131104 | tf_op jit(solution)/shard_map/ppermute | solution.py:328
  17.9 0.5 gram_kernel.1
  18.5 0.6 collective-permute-start.7
  19.1 0.9 collective-permute-done.7
  20.0 2.8 %collective-permute-start.10 = (bf16[3,64,128]{2,1,0:T(8,128)(2,1)S(1)}, bf16[3,64,128]{2,1,0:T(8,128)(2,1)S(1)}, u32[]{:S(2)}, u32[]{:S(2)}) collective-permute-start(bf16[3,64,128]{2,1,0:T(8,128)(2,1)S(1)} %add_convert_fusion.2), channel_id=1, source_target_pairs={{0,6},{1,7},{2,4},{3,5},{4,2},{5,3},{6,0},{7,1},{8,14},{9,15},{10,... | collective-permute-start | bytes 147464 | tf_op jit(solution)/shard_map/ppermute | solution.py:328
  22.8 0.5 collective-permute-start.9
  23.3 0.3 collective-permute-start.8
  23.6 1.5 %collective-permute-done.10 = bf16[3,64,128]{2,1,0:T(8,128)(2,1)S(1)} collective-permute-done((bf16[3,64,128]{2,1,0:T(8,128)(2,1)S(1)}, bf16[3,64,128]{2,1,0:T(8,128)(2,1)S(1)}, u32[]{:S(2)}, u32[]{:S(2)}) %collective-permute-start.10) | collective-permute-done | bytes 49184 | tf_op jit(solution)/shard_map/ppermute | solution.py:328
  25.1 1.8 %collective-permute-done.9 = bf16[3,64,128]{2,1,0:T(8,128)(2,1)S(1)} collective-permute-done((bf16[3,64,128]{2,1,0:T(8,128)(2,1)S(1)}, bf16[3,64,128]{2,1,0:T(8,128)(2,1)S(1)}, u32[]{:S(2)}, u32[]{:S(2)}) %collective-permute-start.9) | collective-permute-done | bytes 49184 | tf_op jit(solution)/shard_map/ppermute | solution.py:328
  26.9 0.5 collective-permute-done.8
  27.5 1.3 collective-permute-done.11.other_ref
  28.8 5.6 %node_kernel.1 = (bf16[128,512]{1,0:T(8,128)(2,1)S(1)}, bf16[128,512]{1,0:T(8,128)(2,1)S(1)}, bf16[128,512]{1,0:T(8,128)(2,1)S(1)}, bf16[128,512]{1,0:T(8,128)(2,1)S(1)}, bf16[256,128]{1,0:T(8,128)(2,1)S(1)}) custom-call(s32[1]{0:T(128)} %bitcast.pos_ref, f32[3,64,128]{2,1,0:T(8,128)S(1)} %add_add_fusion.mine_ref, ...), custom_call_target="tpu_custom_call" | custom-call | tf_op jit(solution)/shard_map/node_kernel/pallas_call | solution.py:311
  34.4 1.6 %collective-permute-start.12 = (bf16[128,512]{1,0:T(8,128)(2,1)S(1)}, bf16[128,512]{1,0:T(8,128)(2,1)S(1)}, u32[]{:S(2)}, u32[]{:S(2)}) collective-permute-start(bf16[128,512]{1,0:T(8,128)(2,1)S(1)} %get-tuple-element.48), channel_id=1, source_target_pairs={{0,8},{1,9},{2,10},{3,11},{4,12},{5,13},{6,14},{7,15},{8,0},{9,1},... | collective-permute-start | bytes 393224 | tf_op jit(solution)/shard_map/ppermute | solution.py:328
  36.0 2.6 %collective-permute-start.13 = (bf16[128,512]{1,0:T(8,128)(2,1)S(1)}, bf16[128,512]{1,0:T(8,128)(2,1)S(1)}, u32[]{:S(2)}, u32[]{:S(2)}) collective-permute-start(bf16[128,512]{1,0:T(8,128)(2,1)S(1)} %get-tuple-element.49), channel_id=1, source_target_pairs={{0,16},{1,17},{2,18},{3,19},{4,20},{5,21},{6,22},{7,23},{8,24},{9,... | collective-permute-start | bytes 393224 | tf_op jit(solution)/shard_map/ppermute | solution.py:328
  38.6 0.2 collective-permute-start.14
  38.8 3.1 %collective-permute-done.12.refs_1_ = bf16[128,512]{1,0:T(8,128)(2,1)S(1)} collective-permute-done((bf16[128,512]{1,0:T(8,128)(2,1)S(1)}, bf16[128,512]{1,0:T(8,128)(2,1)S(1)}, u32[]{:S(2)}, u32[]{:S(2)}) %collective-permute-start.12) | collective-permute-done | bytes 131104 | tf_op jit(solution)/shard_map/ppermute | solution.py:328
  42.0 7.0 %collective-permute-done.13.refs_2_ = bf16[128,512]{1,0:T(8,128)(2,1)S(1)} collective-permute-done((bf16[128,512]{1,0:T(8,128)(2,1)S(1)}, bf16[128,512]{1,0:T(8,128)(2,1)S(1)}, u32[]{:S(2)}, u32[]{:S(2)}) %collective-permute-start.13) | collective-permute-done | bytes 131104 | tf_op jit(solution)/shard_map/ppermute | solution.py:328
  48.9 0.4 cross_kernel.1
  49.4 1.4 %collective-permute-done.15 = f32[6,64,128]{2,1,0:T(8,128)S(1)} collective-permute-done((f32[6,64,128]{2,1,0:T(8,128)S(1)}, f32[6,64,128]{2,1,0:T(8,128)S(1)}, u32[]{:S(2)}, u32[]{:S(2)}) %collective-permute-start.15) | collective-permute-done | bytes 196640 | tf_op jit(solution)/shard_map/ppermute | solution.py:328
  50.9 1.6 %collective-permute-start.18 = (bf16[6,64,128]{2,1,0:T(8,128)(2,1)S(1)}, bf16[6,64,128]{2,1,0:T(8,128)(2,1)S(1)}, u32[]{:S(2)}, u32[]{:S(2)}) collective-permute-start(bf16[6,64,128]{2,1,0:T(8,128)(2,1)S(1)} %add_convert_fusion.1), channel_id=1, source_target_pairs={{0,6},{1,7},{2,4},{3,5},{4,2},{5,3},{6,0},{7,1},{8,14},{9,15},{10,... | collective-permute-start | bytes 294920 | tf_op jit(solution)/shard_map/ppermute | solution.py:328
  52.5 0.5 collective-permute-start.17
  53.0 1.5 %collective-permute-start.16 = (bf16[6,64,128]{2,1,0:T(8,128)(2,1)S(1)}, bf16[6,64,128]{2,1,0:T(8,128)(2,1)S(1)}, u32[]{:S(2)}, u32[]{:S(2)}) collective-permute-start(bf16[6,64,128]{2,1,0:T(8,128)(2,1)S(1)} %add_convert_fusion.1), channel_id=1, source_target_pairs={{0,2},{1,3},{2,0},{3,1},{4,6},{5,7},{6,4},{7,5},{8,10},{9,11},{10,... | collective-permute-start | bytes 294920 | tf_op jit(solution)/shard_map/ppermute | solution.py:328
  54.4 0.8 diag_kernel.1
  55.3 2.0 %collective-permute-done.18 = bf16[6,64,128]{2,1,0:T(8,128)(2,1)S(1)} collective-permute-done((bf16[6,64,128]{2,1,0:T(8,128)(2,1)S(1)}, bf16[6,64,128]{2,1,0:T(8,128)(2,1)S(1)}, u32[]{:S(2)}, u32[]{:S(2)}) %collective-permute-start.18) | collective-permute-done | bytes 98336 | tf_op jit(solution)/shard_map/ppermute | solution.py:328
  57.3 1.5 %collective-permute-done.17 = bf16[6,64,128]{2,1,0:T(8,128)(2,1)S(1)} collective-permute-done((bf16[6,64,128]{2,1,0:T(8,128)(2,1)S(1)}, bf16[6,64,128]{2,1,0:T(8,128)(2,1)S(1)}, u32[]{:S(2)}, u32[]{:S(2)}) %collective-permute-start.17) | collective-permute-done | bytes 98336 | tf_op jit(solution)/shard_map/ppermute | solution.py:328
  58.8 0.1 collective-permute-done.16
  59.0 2.5 %collective-permute-start.21 = (bf16[7,64,128]{2,1,0:T(8,128)(2,1)S(1)}, bf16[7,64,128]{2,1,0:T(8,128)(2,1)S(1)}, u32[]{:S(2)}, u32[]{:S(2)}) collective-permute-start(bf16[7,64,128]{2,1,0:T(8,128)(2,1)S(1)} %pad_maximum_fusion), channel_id=1, source_target_pairs={{0,24},{1,25},{2,26},{3,27},{4,28},{5,29},{6,30},{7,31},{8,16},{9,... | collective-permute-start | bytes 344072 | tf_op jit(solution)/shard_map/ppermute | solution.py:328
  61.5 1.3 %collective-permute-start.20 = (bf16[7,64,128]{2,1,0:T(8,128)(2,1)S(1)}, bf16[7,64,128]{2,1,0:T(8,128)(2,1)S(1)}, u32[]{:S(2)}, u32[]{:S(2)}) collective-permute-start(bf16[7,64,128]{2,1,0:T(8,128)(2,1)S(1)} %pad_maximum_fusion), channel_id=1, source_target_pairs={{0,16},{1,17},{2,18},{3,19},{4,20},{5,21},{6,22},{7,23},{8,24},{9,... | collective-permute-start | bytes 344072 | tf_op jit(solution)/shard_map/ppermute | solution.py:328
  62.8 0.6 collective-permute-start.19
  63.4 2.8 %collective-permute-done.21 = bf16[7,64,128]{2,1,0:T(8,128)(2,1)S(1)} collective-permute-done((bf16[7,64,128]{2,1,0:T(8,128)(2,1)S(1)}, bf16[7,64,128]{2,1,0:T(8,128)(2,1)S(1)}, u32[]{:S(2)}, u32[]{:S(2)}) %collective-permute-start.21) | collective-permute-done | bytes 114720 | tf_op jit(solution)/shard_map/ppermute | solution.py:328
  66.3 6.9 %collective-permute-done.20 = bf16[7,64,128]{2,1,0:T(8,128)(2,1)S(1)} collective-permute-done((bf16[7,64,128]{2,1,0:T(8,128)(2,1)S(1)}, bf16[7,64,128]{2,1,0:T(8,128)(2,1)S(1)}, u32[]{:S(2)}, u32[]{:S(2)}) %collective-permute-start.20) | collective-permute-done | bytes 114720 | tf_op jit(solution)/shard_map/ppermute | solution.py:328
  73.3 1.6 %collective-permute-done.22.other_ref = f32[10,64,128]{2,1,0:T(8,128)S(1)} collective-permute-done((f32[10,64,128]{2,1,0:T(8,128)S(1)}, f32[10,64,128]{2,1,0:T(8,128)S(1)}, u32[]{:S(2)}, u32[]{:S(2)}) %collective-permute-start.22) | collective-permute-done | bytes 327712 | tf_op jit(solution)/shard_map/ppermute | solution.py:328
  74.9 14.8 %top_kernel.1 = (bf16[128,512]{1,0:T(8,128)(2,1)S(1)}, f32[256,256]{1,0:T(8,128)S(1)}, bf16[256,128]{1,0:T(8,128)(2,1)S(1)}) custom-call(s32[1]{0:T(128)} %bitcast.pos_ref, f32[10,64,128]{2,1,0:T(8,128)S(1)} %convert_dynamic-update-slice_fusion.mine_ref, f32[10,64,128]{2,1,0:T(8,128)S(1)} %collective-permute-done.22.other_ref, ...), custom_call_target="tpu_custom_call" | custom-call | tf_op jit(solution)/shard_map/top_kernel/pallas_call | solution.py:311
  89.8 2.6 %collective-permute-start.25 = (bf16[128,512]{1,0:T(8,128)(2,1)S(1)}, bf16[128,512]{1,0:T(8,128)(2,1)S(1)}, u32[]{:S(2)}, u32[]{:S(2)}) collective-permute-start(bf16[128,512]{1,0:T(8,128)(2,1)S(1)} %get-tuple-element.56.refs_0_), channel_id=1, source_target_pairs={{0,24},{1,25},{2,26},{3,27},{4,28},{5,29},{6,30},{7,31},{8,16},{9,... | collective-permute-start | bytes 393224 | tf_op jit(solution)/shard_map/ppermute | solution.py:328
  92.3 1.9 %collective-permute-start.23 = (bf16[128,512]{1,0:T(8,128)(2,1)S(1)}, bf16[128,512]{1,0:T(8,128)(2,1)S(1)}, u32[]{:S(2)}, u32[]{:S(2)}) collective-permute-start(bf16[128,512]{1,0:T(8,128)(2,1)S(1)} %get-tuple-element.56.refs_0_), channel_id=1, source_target_pairs={{0,8},{1,9},{2,10},{3,11},{4,12},{5,13},{6,14},{7,15},{8,0},{9,1},... | collective-permute-start | bytes 393224 | tf_op jit(solution)/shard_map/ppermute | solution.py:328
  94.2 4.0 %factor_kernel.1.factor_ref = f32[128,128]{1,0:T(8,128)S(1)} custom-call(f32[256,256]{1,0:T(8,128)S(1)} %get-tuple-element.54.gram_ref, bf16[256,128]{1,0:T(8,128)(2,1)S(1)} %get-tuple-element.55.low_ref), custom_call_target="tpu_custom_call" | custom-call | tf_op jit(solution)/shard_map/factor_kernel/pallas_call | solution.py:311
  98.2 4.7 %collective-permute-done.24.refs_2_ = bf16[128,512]{1,0:T(8,128)(2,1)S(1)} collective-permute-done((bf16[128,512]{1,0:T(8,128)(2,1)S(1)}, bf16[128,512]{1,0:T(8,128)(2,1)S(1)}, u32[]{:S(2)}, u32[]{:S(2)}) %collective-permute-start.24) | collective-permute-done | bytes 131104 | tf_op jit(solution)/shard_map/ppermute | solution.py:328
  102.9 0.8 coeffs_kernel.1
  103.8 0.2 collective-permute-start.26
  103.9 1.1 collective-permute-done.26
  105.1 1.5 %collective-permute-start.29 = (bf16[1,128,128]{2,1,0:T(8,128)(2,1)S(1)}, bf16[1,128,128]{2,1,0:T(8,128)(2,1)S(1)}, u32[]{:S(2)}, u32[]{:S(2)}) collective-permute-start(bf16[1,128,128]{2,1,0:T(8,128)(2,1)S(1)} %add_convert_fusion.3), channel_id=1, source_target_pairs={{0,6},{1,7},{2,4},{3,5},{4,2},{5,3},{6,0},{7,1},{8,14},{9,15},{10,... | collective-permute-start | bytes 98312 | tf_op jit(solution)/shard_map/ppermute | solution.py:328
  106.6 0.3 collective-permute-start.28
  107.0 1.7 %collective-permute-start.27 = (bf16[1,128,128]{2,1,0:T(8,128)(2,1)S(1)}, bf16[1,128,128]{2,1,0:T(8,128)(2,1)S(1)}, u32[]{:S(2)}, u32[]{:S(2)}) collective-permute-start(bf16[1,128,128]{2,1,0:T(8,128)(2,1)S(1)} %add_convert_fusion.3), channel_id=1, source_target_pairs={{0,2},{1,3},{2,0},{3,1},{4,6},{5,7},{6,4},{7,5},{8,10},{9,11},{10,... | collective-permute-start | bytes 98312 | tf_op jit(solution)/shard_map/ppermute | solution.py:328
  108.6 1.3 %collective-permute-done.29 = bf16[1,128,128]{2,1,0:T(8,128)(2,1)S(1)} collective-permute-done((bf16[1,128,128]{2,1,0:T(8,128)(2,1)S(1)}, bf16[1,128,128]{2,1,0:T(8,128)(2,1)S(1)}, u32[]{:S(2)}, u32[]{:S(2)}) %collective-permute-start.29) | collective-permute-done | bytes 32800 | tf_op jit(solution)/shard_map/ppermute | solution.py:328
  110.0 0.6 collective-permute-done.28
  110.6 0.3 collective-permute-done.27
  111.0 1.2 collective-permute-done.30.other_ref
  112.2 0.8 project_kernel.1
  113.0 0.2 collective-permute-start.31
  113.2 1.7 %collective-permute-start.32 = (bf16[32,2048]{1,0:T(8,128)(2,1)S(1)}, bf16[32,2048]{1,0:T(8,128)(2,1)S(1)}, u32[]{:S(2)}, u32[]{:S(2)}) collective-permute-start(bf16[32,2048]{1,0:T(8,128)(2,1)S(1)} %get-tuple-element.61), channel_id=1, source_target_pairs={{0,2},{1,3},{2,0},{3,1},{4,6},{5,7},{6,4},{7,5},{8,10},{9,11},{10,... | collective-permute-start | bytes 393224 | tf_op jit(solution)/shard_map/ppermute | solution.py:328
  114.9 1.7 %collective-permute-start.34 = (bf16[32,2048]{1,0:T(8,128)(2,1)S(1)}, bf16[32,2048]{1,0:T(8,128)(2,1)S(1)}, u32[]{:S(2)}, u32[]{:S(2)}) collective-permute-start(bf16[32,2048]{1,0:T(8,128)(2,1)S(1)} %get-tuple-element.63), channel_id=1, source_target_pairs={{0,4},{1,5},{2,6},{3,7},{4,0},{5,1},{6,2},{7,3},{8,12},{9,13},{10,... | collective-permute-start | bytes 393224 | tf_op jit(solution)/shard_map/ppermute | solution.py:328
  116.7 1.4 %collective-permute-start.36 = (bf16[32,2048]{1,0:T(8,128)(2,1)S(1)}, bf16[32,2048]{1,0:T(8,128)(2,1)S(1)}, u32[]{:S(2)}, u32[]{:S(2)}) collective-permute-start(bf16[32,2048]{1,0:T(8,128)(2,1)S(1)} %get-tuple-element.65), channel_id=1, source_target_pairs={{0,6},{1,7},{2,4},{3,5},{4,2},{5,3},{6,0},{7,1},{8,14},{9,15},{10,... | collective-permute-start | bytes 393224 | tf_op jit(solution)/shard_map/ppermute | solution.py:328
  118.2 1.4 %collective-permute-done.32.refs_2_ = bf16[32,2048]{1,0:T(8,128)(2,1)S(1)} collective-permute-done((bf16[32,2048]{1,0:T(8,128)(2,1)S(1)}, bf16[32,2048]{1,0:T(8,128)(2,1)S(1)}, u32[]{:S(2)}, u32[]{:S(2)}) %collective-permute-start.32) | collective-permute-done | bytes 131104 | tf_op jit(solution)/shard_map/ppermute | solution.py:328
  119.5 0.2 collective-permute-start.37
  119.8 1.8 %collective-permute-done.33.refs_3_ = bf16[32,2048]{1,0:T(8,128)(2,1)S(1)} collective-permute-done((bf16[32,2048]{1,0:T(8,128)(2,1)S(1)}, bf16[32,2048]{1,0:T(8,128)(2,1)S(1)}, u32[]{:S(2)}, u32[]{:S(2)}) %collective-permute-start.33) | collective-permute-done | bytes 131104 | tf_op jit(solution)/shard_map/ppermute | solution.py:328
  121.6 7.2 %collective-permute-done.35.refs_5_ = bf16[32,2048]{1,0:T(8,128)(2,1)S(1)} collective-permute-done((bf16[32,2048]{1,0:T(8,128)(2,1)S(1)}, bf16[32,2048]{1,0:T(8,128)(2,1)S(1)}, u32[]{:S(2)}, u32[]{:S(2)}) %collective-permute-start.35) | collective-permute-done | bytes 131104 | tf_op jit(solution)/shard_map/ppermute | solution.py:328
  128.8 1.0 whole_kernel.1
  (36 shorter events, 0.8 us)
Async XLA Ops:
  0.0 1.2 copy-start
  1.3 4.9 %collective-permute-start = (bf16[32,2048]{1,0:T(8,128)(2,1)S(1)}, bf16[32,2048]{1,0:T(8,128)(2,1)S(1)}, u32[]{:S(2)}, u32[]{:S(2)}) collective-permute-start(bf16[32,2048]{1,0:T(8,128)(2,1)S(1)} %get-tuple-element.37), channel_id=1, source_target_pairs={{0,1},{1,0},{2,3},{3,2},{4,5},{5,4},{6,7},{7,6},{8,9},{9,8},{10,11... | collective-permute-start | bytes 393224 | tf_op jit(solution)/shard_map/ppermute | solution.py:328
  1.8 7.0 %collective-permute-start.1 = (bf16[32,2048]{1,0:T(8,128)(2,1)S(1)}, bf16[32,2048]{1,0:T(8,128)(2,1)S(1)}, u32[]{:S(2)}, u32[]{:S(2)}) collective-permute-start(bf16[32,2048]{1,0:T(8,128)(2,1)S(1)} %get-tuple-element.38), channel_id=1, source_target_pairs={{0,2},{1,3},{2,0},{3,1},{4,6},{5,7},{6,4},{7,5},{8,10},{9,11},{10,... | collective-permute-start | bytes 393224 | tf_op jit(solution)/shard_map/ppermute | solution.py:328
  4.4 6.6 %collective-permute-start.2 = (bf16[32,2048]{1,0:T(8,128)(2,1)S(1)}, bf16[32,2048]{1,0:T(8,128)(2,1)S(1)}, u32[]{:S(2)}, u32[]{:S(2)}) collective-permute-start(bf16[32,2048]{1,0:T(8,128)(2,1)S(1)} %get-tuple-element.39), channel_id=1, source_target_pairs={{0,3},{1,2},{2,1},{3,0},{4,7},{5,6},{6,5},{7,4},{8,11},{9,10},{10,... | collective-permute-start | bytes 393224 | tf_op jit(solution)/shard_map/ppermute | solution.py:328
  4.5 6.6 %collective-permute-start.3 = (bf16[32,2048]{1,0:T(8,128)(2,1)S(1)}, bf16[32,2048]{1,0:T(8,128)(2,1)S(1)}, u32[]{:S(2)}, u32[]{:S(2)}) collective-permute-start(bf16[32,2048]{1,0:T(8,128)(2,1)S(1)} %get-tuple-element.40), channel_id=1, source_target_pairs={{0,4},{1,5},{2,6},{3,7},{4,0},{5,1},{6,2},{7,3},{8,12},{9,13},{10,... | collective-permute-start | bytes 393224 | tf_op jit(solution)/shard_map/ppermute | solution.py:328
  6.2 11.7 %collective-permute-start.4 = (bf16[32,2048]{1,0:T(8,128)(2,1)S(1)}, bf16[32,2048]{1,0:T(8,128)(2,1)S(1)}, u32[]{:S(2)}, u32[]{:S(2)}) collective-permute-start(bf16[32,2048]{1,0:T(8,128)(2,1)S(1)} %get-tuple-element.41), channel_id=1, source_target_pairs={{0,5},{1,4},{2,7},{3,6},{4,1},{5,0},{6,3},{7,2},{8,13},{9,12},{10,... | collective-permute-start | bytes 393224 | tf_op jit(solution)/shard_map/ppermute | solution.py:328
  6.2 11.7 %collective-permute-start.5 = (bf16[32,2048]{1,0:T(8,128)(2,1)S(1)}, bf16[32,2048]{1,0:T(8,128)(2,1)S(1)}, u32[]{:S(2)}, u32[]{:S(2)}) collective-permute-start(bf16[32,2048]{1,0:T(8,128)(2,1)S(1)} %get-tuple-element.42), channel_id=1, source_target_pairs={{0,6},{1,7},{2,4},{3,5},{4,2},{5,3},{6,0},{7,1},{8,14},{9,15},{10,... | collective-permute-start | bytes 393224 | tf_op jit(solution)/shard_map/ppermute | solution.py:328
  8.8 9.1 %collective-permute-start.6 = (bf16[32,2048]{1,0:T(8,128)(2,1)S(1)}, bf16[32,2048]{1,0:T(8,128)(2,1)S(1)}, u32[]{:S(2)}, u32[]{:S(2)}) collective-permute-start(bf16[32,2048]{1,0:T(8,128)(2,1)S(1)} %get-tuple-element.43), channel_id=1, source_target_pairs={{0,7},{1,6},{2,5},{3,4},{4,3},{5,2},{6,1},{7,0},{8,15},{9,14},{10,... | collective-permute-start | bytes 393224 | tf_op jit(solution)/shard_map/ppermute | solution.py:328
  18.5 1.6 %collective-permute-start.7 = (f32[3,64,128]{2,1,0:T(8,128)S(1)}, f32[3,64,128]{2,1,0:T(8,128)S(1)}, u32[]{:S(2)}, u32[]{:S(2)}) collective-permute-start(f32[3,64,128]{2,1,0:T(8,128)S(1)} %get-tuple-element.46), channel_id=1, source_target_pairs={{0,1},{1,0},{2,3},{3,2},{4,5},{5,4},{6,7},{7,6},{8,9},{9,8},{10,11... | collective-permute-start | bytes 294920 | tf_op jit(solution)/shard_map/ppermute | solution.py:328
  20.0 5.1 %collective-permute-start.10 = (bf16[3,64,128]{2,1,0:T(8,128)(2,1)S(1)}, bf16[3,64,128]{2,1,0:T(8,128)(2,1)S(1)}, u32[]{:S(2)}, u32[]{:S(2)}) collective-permute-start(bf16[3,64,128]{2,1,0:T(8,128)(2,1)S(1)} %add_convert_fusion.2), channel_id=1, source_target_pairs={{0,6},{1,7},{2,4},{3,5},{4,2},{5,3},{6,0},{7,1},{8,14},{9,15},{10,... | collective-permute-start | bytes 147464 | tf_op jit(solution)/shard_map/ppermute | solution.py:328
  22.8 4.1 %collective-permute-start.9 = (bf16[3,64,128]{2,1,0:T(8,128)(2,1)S(1)}, bf16[3,64,128]{2,1,0:T(8,128)(2,1)S(1)}, u32[]{:S(2)}, u32[]{:S(2)}) collective-permute-start(bf16[3,64,128]{2,1,0:T(8,128)(2,1)S(1)} %add_convert_fusion.2), channel_id=1, source_target_pairs={{0,4},{1,5},{2,6},{3,7},{4,0},{5,1},{6,2},{7,3},{8,12},{9,13},{10,... | collective-permute-start | bytes 147464 | tf_op jit(solution)/shard_map/ppermute | solution.py:328
  23.3 4.1 %collective-permute-start.8 = (bf16[3,64,128]{2,1,0:T(8,128)(2,1)S(1)}, bf16[3,64,128]{2,1,0:T(8,128)(2,1)S(1)}, u32[]{:S(2)}, u32[]{:S(2)}) collective-permute-start(bf16[3,64,128]{2,1,0:T(8,128)(2,1)S(1)} %add_convert_fusion.2), channel_id=1, source_target_pairs={{0,2},{1,3},{2,0},{3,1},{4,6},{5,7},{6,4},{7,5},{8,10},{9,11},{10,... | collective-permute-start | bytes 147464 | tf_op jit(solution)/shard_map/ppermute | solution.py:328
  27.4 1.4 %collective-permute-start.11 = (f32[3,64,128]{2,1,0:T(8,128)S(1)}, f32[3,64,128]{2,1,0:T(8,128)S(1)}, u32[]{:S(2)}, u32[]{:S(2)}) collective-permute-start(f32[3,64,128]{2,1,0:T(8,128)S(1)} %add_add_fusion.mine_ref), channel_id=1, source_target_pairs={{0,1},{1,0},{2,3},{3,2},{4,5},{5,4},{6,7},{7,6},{8,9},{9,8},{10,11... | collective-permute-start | bytes 294920 | tf_op jit(solution)/shard_map/ppermute | solution.py:328
  34.4 7.6 %collective-permute-start.12 = (bf16[128,512]{1,0:T(8,128)(2,1)S(1)}, bf16[128,512]{1,0:T(8,128)(2,1)S(1)}, u32[]{:S(2)}, u32[]{:S(2)}) collective-permute-start(bf16[128,512]{1,0:T(8,128)(2,1)S(1)} %get-tuple-element.48), channel_id=1, source_target_pairs={{0,8},{1,9},{2,10},{3,11},{4,12},{5,13},{6,14},{7,15},{8,0},{9,1},... | collective-permute-start | bytes 393224 | tf_op jit(solution)/shard_map/ppermute | solution.py:328
  36.0 12.9 %collective-permute-start.13 = (bf16[128,512]{1,0:T(8,128)(2,1)S(1)}, bf16[128,512]{1,0:T(8,128)(2,1)S(1)}, u32[]{:S(2)}, u32[]{:S(2)}) collective-permute-start(bf16[128,512]{1,0:T(8,128)(2,1)S(1)} %get-tuple-element.49), channel_id=1, source_target_pairs={{0,16},{1,17},{2,18},{3,19},{4,20},{5,21},{6,22},{7,23},{8,24},{9,... | collective-permute-start | bytes 393224 | tf_op jit(solution)/shard_map/ppermute | solution.py:328
  38.6 10.3 %collective-permute-start.14 = (bf16[128,512]{1,0:T(8,128)(2,1)S(1)}, bf16[128,512]{1,0:T(8,128)(2,1)S(1)}, u32[]{:S(2)}, u32[]{:S(2)}) collective-permute-start(bf16[128,512]{1,0:T(8,128)(2,1)S(1)} %get-tuple-element.50), channel_id=1, source_target_pairs={{0,24},{1,25},{2,26},{3,27},{4,28},{5,29},{6,30},{7,31},{8,16},{9,... | collective-permute-start | bytes 393224 | tf_op jit(solution)/shard_map/ppermute | solution.py:328
  49.3 1.5 %collective-permute-start.15 = (f32[6,64,128]{2,1,0:T(8,128)S(1)}, f32[6,64,128]{2,1,0:T(8,128)S(1)}, u32[]{:S(2)}, u32[]{:S(2)}) collective-permute-start(f32[6,64,128]{2,1,0:T(8,128)S(1)} %get-tuple-element.52), channel_id=1, source_target_pairs={{0,1},{1,0},{2,3},{3,2},{4,5},{5,4},{6,7},{7,6},{8,9},{9,8},{10,11... | collective-permute-start | bytes 589832 | tf_op jit(solution)/shard_map/ppermute | solution.py:328
  50.9 6.4 %collective-permute-start.18 = (bf16[6,64,128]{2,1,0:T(8,128)(2,1)S(1)}, bf16[6,64,128]{2,1,0:T(8,128)(2,1)S(1)}, u32[]{:S(2)}, u32[]{:S(2)}) collective-permute-start(bf16[6,64,128]{2,1,0:T(8,128)(2,1)S(1)} %add_convert_fusion.1), channel_id=1, source_target_pairs={{0,6},{1,7},{2,4},{3,5},{4,2},{5,3},{6,0},{7,1},{8,14},{9,15},{10,... | collective-permute-start | bytes 294920 | tf_op jit(solution)/shard_map/ppermute | solution.py:328
  52.5 6.3 %collective-permute-start.17 = (bf16[6,64,128]{2,1,0:T(8,128)(2,1)S(1)}, bf16[6,64,128]{2,1,0:T(8,128)(2,1)S(1)}, u32[]{:S(2)}, u32[]{:S(2)}) collective-permute-start(bf16[6,64,128]{2,1,0:T(8,128)(2,1)S(1)} %add_convert_fusion.1), channel_id=1, source_target_pairs={{0,4},{1,5},{2,6},{3,7},{4,0},{5,1},{6,2},{7,3},{8,12},{9,13},{10,... | collective-permute-start | bytes 294920 | tf_op jit(solution)/shard_map/ppermute | solution.py:328
  53.0 5.9 %collective-permute-start.16 = (bf16[6,64,128]{2,1,0:T(8,128)(2,1)S(1)}, bf16[6,64,128]{2,1,0:T(8,128)(2,1)S(1)}, u32[]{:S(2)}, u32[]{:S(2)}) collective-permute-start(bf16[6,64,128]{2,1,0:T(8,128)(2,1)S(1)} %add_convert_fusion.1), channel_id=1, source_target_pairs={{0,2},{1,3},{2,0},{3,1},{4,6},{5,7},{6,4},{7,5},{8,10},{9,11},{10,... | collective-permute-start | bytes 294920 | tf_op jit(solution)/shard_map/ppermute | solution.py:328
  59.0 7.3 %collective-permute-start.21 = (bf16[7,64,128]{2,1,0:T(8,128)(2,1)S(1)}, bf16[7,64,128]{2,1,0:T(8,128)(2,1)S(1)}, u32[]{:S(2)}, u32[]{:S(2)}) collective-permute-start(bf16[7,64,128]{2,1,0:T(8,128)(2,1)S(1)} %pad_maximum_fusion), channel_id=1, source_target_pairs={{0,24},{1,25},{2,26},{3,27},{4,28},{5,29},{6,30},{7,31},{8,16},{9,... | collective-permute-start | bytes 344072 | tf_op jit(solution)/shard_map/ppermute | solution.py:328
  61.5 11.6 %collective-permute-start.20 = (bf16[7,64,128]{2,1,0:T(8,128)(2,1)S(1)}, bf16[7,64,128]{2,1,0:T(8,128)(2,1)S(1)}, u32[]{:S(2)}, u32[]{:S(2)}) collective-permute-start(bf16[7,64,128]{2,1,0:T(8,128)(2,1)S(1)} %pad_maximum_fusion), channel_id=1, source_target_pairs={{0,16},{1,17},{2,18},{3,19},{4,20},{5,21},{6,22},{7,23},{8,24},{9,... | collective-permute-start | bytes 344072 | tf_op jit(solution)/shard_map/ppermute | solution.py:328
  62.8 10.3 %collective-permute-start.19 = (bf16[7,64,128]{2,1,0:T(8,128)(2,1)S(1)}, bf16[7,64,128]{2,1,0:T(8,128)(2,1)S(1)}, u32[]{:S(2)}, u32[]{:S(2)}) collective-permute-start(bf16[7,64,128]{2,1,0:T(8,128)(2,1)S(1)} %pad_maximum_fusion), channel_id=1, source_target_pairs={{0,8},{1,9},{2,10},{3,11},{4,12},{5,13},{6,14},{7,15},{8,0},{9,1},... | collective-permute-start | bytes 344072 | tf_op jit(solution)/shard_map/ppermute | solution.py:328
  73.2 1.7 %collective-permute-start.22 = (f32[10,64,128]{2,1,0:T(8,128)S(1)}, f32[10,64,128]{2,1,0:T(8,128)S(1)}, u32[]{:S(2)}, u32[]{:S(2)}) collective-permute-start(f32[10,64,128]{2,1,0:T(8,128)S(1)} %convert_dynamic-update-slice_fusion.mine_ref), channel_id=1, source_target_pairs={{0,1},{1,0},{2,3},{3,2},{4,5},{5,4},{6,7},{7,6},{8,9},{9,8},{10,11... | collective-permute-start | bytes 983048 | tf_op jit(solution)/shard_map/ppermute | solution.py:328
  89.8 8.4 %collective-permute-start.25 = (bf16[128,512]{1,0:T(8,128)(2,1)S(1)}, bf16[128,512]{1,0:T(8,128)(2,1)S(1)}, u32[]{:S(2)}, u32[]{:S(2)}) collective-permute-start(bf16[128,512]{1,0:T(8,128)(2,1)S(1)} %get-tuple-element.56.refs_0_), channel_id=1, source_target_pairs={{0,24},{1,25},{2,26},{3,27},{4,28},{5,29},{6,30},{7,31},{8,16},{9,... | collective-permute-start | bytes 393224 | tf_op jit(solution)/shard_map/ppermute | solution.py:328
  92.3 10.6 %collective-permute-start.24 = (bf16[128,512]{1,0:T(8,128)(2,1)S(1)}, bf16[128,512]{1,0:T(8,128)(2,1)S(1)}, u32[]{:S(2)}, u32[]{:S(2)}) collective-permute-start(bf16[128,512]{1,0:T(8,128)(2,1)S(1)} %get-tuple-element.56.refs_0_), channel_id=1, source_target_pairs={{0,16},{1,17},{2,18},{3,19},{4,20},{5,21},{6,22},{7,23},{8,24},{9,... | collective-permute-start | bytes 393224 | tf_op jit(solution)/shard_map/ppermute | solution.py:328
  92.3 10.6 %collective-permute-start.23 = (bf16[128,512]{1,0:T(8,128)(2,1)S(1)}, bf16[128,512]{1,0:T(8,128)(2,1)S(1)}, u32[]{:S(2)}, u32[]{:S(2)}) collective-permute-start(bf16[128,512]{1,0:T(8,128)(2,1)S(1)} %get-tuple-element.56.refs_0_), channel_id=1, source_target_pairs={{0,8},{1,9},{2,10},{3,11},{4,12},{5,13},{6,14},{7,15},{8,0},{9,1},... | collective-permute-start | bytes 393224 | tf_op jit(solution)/shard_map/ppermute | solution.py:328
  103.8 1.3 %collective-permute-start.26 = (f32[1,128,128]{2,1,0:T(8,128)S(1)}, f32[1,128,128]{2,1,0:T(8,128)S(1)}, u32[]{:S(2)}, u32[]{:S(2)}) collective-permute-start(f32[1,128,128]{2,1,0:T(8,128)S(1)} %get-tuple-element.58), channel_id=1, source_target_pairs={{0,1},{1,0},{2,3},{3,2},{4,5},{5,4},{6,7},{7,6},{8,9},{9,8},{10,11... | collective-permute-start | bytes 196616 | tf_op jit(solution)/shard_map/ppermute | solution.py:328
  105.1 4.9 %collective-permute-start.29 = (bf16[1,128,128]{2,1,0:T(8,128)(2,1)S(1)}, bf16[1,128,128]{2,1,0:T(8,128)(2,1)S(1)}, u32[]{:S(2)}, u32[]{:S(2)}) collective-permute-start(bf16[1,128,128]{2,1,0:T(8,128)(2,1)S(1)} %add_convert_fusion.3), channel_id=1, source_target_pairs={{0,6},{1,7},{2,4},{3,5},{4,2},{5,3},{6,0},{7,1},{8,14},{9,15},{10,... | collective-permute-start | bytes 98312 | tf_op jit(solution)/shard_map/ppermute | solution.py:328
  106.6 3.9 %collective-permute-start.28 = (bf16[1,128,128]{2,1,0:T(8,128)(2,1)S(1)}, bf16[1,128,128]{2,1,0:T(8,128)(2,1)S(1)}, u32[]{:S(2)}, u32[]{:S(2)}) collective-permute-start(bf16[1,128,128]{2,1,0:T(8,128)(2,1)S(1)} %add_convert_fusion.3), channel_id=1, source_target_pairs={{0,4},{1,5},{2,6},{3,7},{4,0},{5,1},{6,2},{7,3},{8,12},{9,13},{10,... | collective-permute-start | bytes 98312 | tf_op jit(solution)/shard_map/ppermute | solution.py:328
  107.0 3.9 %collective-permute-start.27 = (bf16[1,128,128]{2,1,0:T(8,128)(2,1)S(1)}, bf16[1,128,128]{2,1,0:T(8,128)(2,1)S(1)}, u32[]{:S(2)}, u32[]{:S(2)}) collective-permute-start(bf16[1,128,128]{2,1,0:T(8,128)(2,1)S(1)} %add_convert_fusion.3), channel_id=1, source_target_pairs={{0,2},{1,3},{2,0},{3,1},{4,6},{5,7},{6,4},{7,5},{8,10},{9,11},{10,... | collective-permute-start | bytes 98312 | tf_op jit(solution)/shard_map/ppermute | solution.py:328
  110.9 1.3 %collective-permute-start.30 = (f32[1,128,128]{2,1,0:T(8,128)S(1)}, f32[1,128,128]{2,1,0:T(8,128)S(1)}, u32[]{:S(2)}, u32[]{:S(2)}) collective-permute-start(f32[1,128,128]{2,1,0:T(8,128)S(1)} %add_add_fusion.1.mine_ref), channel_id=1, source_target_pairs={{0,1},{1,0},{2,3},{3,2},{4,5},{5,4},{6,7},{7,6},{8,9},{9,8},{10,11... | collective-permute-start | bytes 196616 | tf_op jit(solution)/shard_map/ppermute | solution.py:328
  113.0 3.7 %collective-permute-start.31 = (bf16[32,2048]{1,0:T(8,128)(2,1)S(1)}, bf16[32,2048]{1,0:T(8,128)(2,1)S(1)}, u32[]{:S(2)}, u32[]{:S(2)}) collective-permute-start(bf16[32,2048]{1,0:T(8,128)(2,1)S(1)} %get-tuple-element.60), channel_id=1, source_target_pairs={{0,1},{1,0},{2,3},{3,2},{4,5},{5,4},{6,7},{7,6},{8,9},{9,8},{10,11... | collective-permute-start | bytes 393224 | tf_op jit(solution)/shard_map/ppermute | solution.py:328
  113.2 6.3 %collective-permute-start.32 = (bf16[32,2048]{1,0:T(8,128)(2,1)S(1)}, bf16[32,2048]{1,0:T(8,128)(2,1)S(1)}, u32[]{:S(2)}, u32[]{:S(2)}) collective-permute-start(bf16[32,2048]{1,0:T(8,128)(2,1)S(1)} %get-tuple-element.61), channel_id=1, source_target_pairs={{0,2},{1,3},{2,0},{3,1},{4,6},{5,7},{6,4},{7,5},{8,10},{9,11},{10,... | collective-permute-start | bytes 393224 | tf_op jit(solution)/shard_map/ppermute | solution.py:328
  114.9 6.6 %collective-permute-start.33 = (bf16[32,2048]{1,0:T(8,128)(2,1)S(1)}, bf16[32,2048]{1,0:T(8,128)(2,1)S(1)}, u32[]{:S(2)}, u32[]{:S(2)}) collective-permute-start(bf16[32,2048]{1,0:T(8,128)(2,1)S(1)} %get-tuple-element.62), channel_id=1, source_target_pairs={{0,3},{1,2},{2,1},{3,0},{4,7},{5,6},{6,5},{7,4},{8,11},{9,10},{10,... | collective-permute-start | bytes 393224 | tf_op jit(solution)/shard_map/ppermute | solution.py:328
  114.9 6.6 %collective-permute-start.34 = (bf16[32,2048]{1,0:T(8,128)(2,1)S(1)}, bf16[32,2048]{1,0:T(8,128)(2,1)S(1)}, u32[]{:S(2)}, u32[]{:S(2)}) collective-permute-start(bf16[32,2048]{1,0:T(8,128)(2,1)S(1)} %get-tuple-element.63), channel_id=1, source_target_pairs={{0,4},{1,5},{2,6},{3,7},{4,0},{5,1},{6,2},{7,3},{8,12},{9,13},{10,... | collective-permute-start | bytes 393224 | tf_op jit(solution)/shard_map/ppermute | solution.py:328
  116.6 12.1 %collective-permute-start.35 = (bf16[32,2048]{1,0:T(8,128)(2,1)S(1)}, bf16[32,2048]{1,0:T(8,128)(2,1)S(1)}, u32[]{:S(2)}, u32[]{:S(2)}) collective-permute-start(bf16[32,2048]{1,0:T(8,128)(2,1)S(1)} %get-tuple-element.64), channel_id=1, source_target_pairs={{0,5},{1,4},{2,7},{3,6},{4,1},{5,0},{6,3},{7,2},{8,13},{9,12},{10,... | collective-permute-start | bytes 393224 | tf_op jit(solution)/shard_map/ppermute | solution.py:328
  116.7 12.0 %collective-permute-start.36 = (bf16[32,2048]{1,0:T(8,128)(2,1)S(1)}, bf16[32,2048]{1,0:T(8,128)(2,1)S(1)}, u32[]{:S(2)}, u32[]{:S(2)}) collective-permute-start(bf16[32,2048]{1,0:T(8,128)(2,1)S(1)} %get-tuple-element.65), channel_id=1, source_target_pairs={{0,6},{1,7},{2,4},{3,5},{4,2},{5,3},{6,0},{7,1},{8,14},{9,15},{10,... | collective-permute-start | bytes 393224 | tf_op jit(solution)/shard_map/ppermute | solution.py:328
  119.5 9.2 %collective-permute-start.37 = (bf16[32,2048]{1,0:T(8,128)(2,1)S(1)}, bf16[32,2048]{1,0:T(8,128)(2,1)S(1)}, u32[]{:S(2)}, u32[]{:S(2)}) collective-permute-start(bf16[32,2048]{1,0:T(8,128)(2,1)S(1)} %get-tuple-element.66), channel_id=1, source_target_pairs={{0,7},{1,6},{2,5},{3,4},{4,3},{5,2},{6,1},{7,0},{8,15},{9,14},{10,... | collective-permute-start | bytes 393224 | tf_op jit(solution)/shard_map/ppermute | solution.py:328
where the time goes:
time: 130 us
  waiting for transfers between devices  59.6 us (46%)
  starting transfers between devices  39.6 us (30%)
  Pallas kernels  28.9 us (22%)
    ppermute x38, waiting for transfers between devices, swap(): return lax.ppermute(x, 'cols', [(i, i ^ apart) for i in range(count)])  59.6 us
    ppermute x38, starting transfers between devices, swap(): return lax.ppermute(x, 'cols', [(i, i ^ apart) for i in range(count)])  39.6 us
    pallas_call x10, Pallas kernels, kernel(): pl.pallas_call(fn, out_shape=[jax.ShapeDtypeStruct(s, d) for s, d in shap...  28.9 us
  transfers between devices with their start and end apart: 38, of which 25 were waited for; matrix products, arithmetic and copies ran while one was open for 0% of the time, Pallas kernels for 4%

commit v1 on v0

--- a/solution.py
+++ b/solution.py
@@ -177,10 +177,17 @@
     return pos_ref[0] % PLANE
 
 
+def copy_all(copies):
+    for c in copies:
+        c.start()
+    for c in copies:
+        c.wait()
+
+
 def parts_kernel(pos_ref, x_ref, *refs):
-    width = refs[0].shape[1]
-    for m in range(PLANE):
-        refs[m][...] = x_ref[:, chunk(member(pos_ref), m, width)]
+    parts, sems = refs[:PLANE], refs[PLANE]
+    where = [x_ref.at[:, chunk(member(pos_ref), m, parts[m].shape[1])] for m in range(PLANE)]
+    copy_all([pltpu.make_async_copy(where[m], parts[m], sems.at[m]) for m in range(PLANE)])
 
 
 def gram_kernel(pos_ref, *refs):
@@ -224,7 +231,9 @@
     diag_ref[0] = jnp.where(core == 1, diag[half:, :], diag[:half, :]).astype(diag_ref.dtype)
 
 
-PAIRS = [(i, j) for i in range(PLANES) for j in range(i + 1, PLANES)]
+NEAR = [(0, 1), (2, 3)]
+FAR = [(0, 2), (0, 3), (1, 2), (1, 3)]
+PAIRS = NEAR + FAR
 
 
 def cross_kernel(pos_ref, *refs):
@@ -235,17 +244,26 @@
     split([dot_low(all_ref[j], all_ref[i], 1, 1) for i, j in PAIRS], core, mine_ref, theirs_ref)
 
 
-def top_kernel(pos_ref, mine_ref, other_ref, *refs):
-    nodes, (top_ref, gram_ref, low_ref), refs = refs[:PLANES], refs[PLANES : PLANES + 3], refs[PLANES + 3 :]
+def pair_kernel(pos_ref, mine_ref, other_ref, *refs):
+    nodes, outs, refs = refs[:PLANES], refs[PLANES : PLANES + 6], refs[PLANES + 6 :]
     all_ref, diag_ref, work = refs[0], refs[1], [refs[2:5], refs[5:8]]
     core, z = place(pos_ref)
     for m in range(PLANES):
         all_ref[z ^ m] = nodes[m][...]
-        diag_ref[z ^ m] = joined(mine_ref, other_ref, core, len(PAIRS) + m)
-    cross = {pair: joined(mine_ref, other_ref, core, b) for b, pair in enumerate(PAIRS)}
-    gram_a = square(diag_ref[0], cross[0, 1], diag_ref[1])
-    gram_b = square(diag_ref[2], cross[2, 3], diag_ref[3])
-    low_a, low_b = leading_spaces([gram_a, gram_b], work)
+        diag_ref[z ^ m] = joined(mine_ref, other_ref, core, len(NEAR) + m)
+    grams = [square(diag_ref[i], joined(mine_ref, other_ref, core, b), diag_ref[j]) for b, (i, j) in enumerate(NEAR)]
+    lows = leading_spaces(grams, work)
+    for n, (gram, low, (i, j)) in enumerate(zip(grams, lows, NEAR)):
+        low_ref, diag_out, node_ref = outs[3 * n : 3 * n + 3]
+        low_ref[...] = low
+        diag_out[...] = reduced(gram, low)
+        node_ref[...] = dot_low(low, jnp.concatenate([all_ref[i], all_ref[j]], 0), 0, 0).astype(bf16)
+
+
+def top_kernel(pos_ref, mine_ref, other_ref, low_a, diag_a, node_a, low_b, diag_b, node_b, *refs):
+    (top_ref, gram_ref, low_ref), work = refs[:3], refs[3:]
+    core, _ = place(pos_ref)
+    cross = {pair: joined(mine_ref, other_ref, core, b) for b, pair in enumerate(FAR)}
     between = jnp.concatenate(
         [
             jnp.concatenate([cross[0, 2], cross[1, 2]], 1),
@@ -253,17 +271,12 @@
         ],
         0,
     )
-    gram = square(
-        reduced(gram_a, low_a),
-        dot(low_b.astype(f32), dot(between, low_a.astype(f32), 1, 0), 0, 0),
-        reduced(gram_b, low_b),
-    )
+    between = dot(low_b[...].astype(f32), dot(between, low_a[...].astype(f32), 1, 0), 0, 0)
+    gram = square(diag_a[...], between, diag_b[...])
     gram_ref[...] = gram
-    (low,) = leading_spaces([gram], work[:1])
+    (low,) = leading_spaces([gram], [work])
     low_ref[...] = low
-    node_a = dot_low(low_a, jnp.concatenate([all_ref[0], all_ref[1]], 0), 0, 0).astype(bf16)
-    node_b = dot_low(low_b, jnp.concatenate([all_ref[2], all_ref[3]], 0), 0, 0).astype(bf16)
-    top_ref[...] = dot_low(low, jnp.concatenate([node_a, node_b], 0), 0, 0).astype(bf16)
+    top_ref[...] = dot_low(low, jnp.concatenate([node_a[...], node_b[...]], 0), 0, 0).astype(bf16)
 
 
 def factor_kernel(gram_ref, low_ref, factor_ref):
@@ -295,24 +308,24 @@
 
 
 def whole_kernel(pos_ref, *refs):
-    parts, out_ref = refs[:PLANE], refs[PLANE]
-    width = parts[0].shape[1]
-    for m in range(PLANE):
-        out_ref[:, chunk(member(pos_ref), m, width)] = parts[m][...]
+    parts, out_ref, sems = refs[:PLANE], refs[PLANE], refs[PLANE + 1]
+    where = [out_ref.at[:, chunk(member(pos_ref), m, parts[m].shape[1])] for m in range(PLANE)]
+    copy_all([pltpu.make_async_copy(parts[m], where[m], sems.at[m]) for m in range(PLANE)])
 
 
 smem = pl.BlockSpec(memory_space=pltpu.SMEM)
 vmem = pl.BlockSpec(memory_space=pltpu.VMEM)
-
-
-def kernel(fn, outs, *args, scratch=(), scalar=True):
+hbm = pl.BlockSpec(memory_space=pltpu.HBM)
+
+
+def kernel(fn, outs, *args, scratch=(), scalar=True, far_in=False, far_out=False):
     single = not isinstance(outs, (list, tuple))
     shapes = [outs] if single else list(outs)
     res = pl.pallas_call(
         fn,
         out_shape=[jax.ShapeDtypeStruct(s, d) for s, d in shapes] if not single else None,
-        in_specs=[smem if scalar and i == 0 else vmem for i in range(len(args))],
-        out_specs=[vmem for _ in shapes],
+        in_specs=[smem if scalar and i == 0 else hbm if far_in else vmem for i in range(len(args))],
+        out_specs=[hbm if far_out else vmem for _ in shapes],
         scratch_shapes=list(scratch),
         compiler_params=pltpu.CompilerParams(vmem_limit_bytes=40 * 2**20),
         name=fn.__name__,
@@ -342,7 +355,13 @@
     part = width // PLANES
     half = RANK // 2
 
-    parts = kernel(parts_kernel, [((block, width), bf16)] * PLANE, pos, mortality)
+    sems = [pltpu.SemaphoreType.DMA((PLANE,))]
+    parts = kernel(
+        parts_kernel,
+        [((block, width), bf16)] * PLANE,
+        pos, pltpu.with_memory_space_constraint(mortality, pltpu.HBM),
+        scratch=sems, far_in=True,
+    )
     parts = swap_all(parts, 1)
     rows, mine, theirs = kernel(
         gram_kernel, [((height, width), bf16)] + [((3, half, RANK), f32)] * 2, pos, *parts
@@ -365,13 +384,24 @@
         scratch=[pltpu.VMEM((PLANES, RANK, part), bf16)],
     )
     mine = plane_sum(mine, theirs)
-    both = swap_all([jnp.concatenate([mine.astype(bf16), diag], 0)] * PLANES, PLANE)
-    mine = jnp.concatenate([sum4([x[: len(PAIRS)] for x in both])] + [x[len(PAIRS) :].astype(f32) for x in both], 0)
+    low_sum = mine.astype(bf16)
+    near = swap_all([jnp.concatenate([low_sum[: len(NEAR)], diag], 0)] * PLANES, PLANE)
+    far = swap_all([low_sum[len(NEAR) :]] * PLANES, PLANE)
+    mine = jnp.concatenate([sum4([x[: len(NEAR)] for x in near])] + [x[len(NEAR) :].astype(f32) for x in near], 0)
+    pair_shapes = [((2 * RANK, RANK), bf16), ((RANK, RANK), f32), ((RANK, part), bf16)]
+    pairs = kernel(
+        pair_kernel,
+        pair_shapes * 2,
+        pos, mine, swap(mine, 1), *nodes,
+        scratch=[pltpu.VMEM((PLANES, RANK, part), bf16), pltpu.VMEM((PLANES, RANK, RANK), f32)] + work_shapes * 2,
+    )
+    far, pairs = lax.optimization_barrier((far, pairs))
+    mine = sum4(far)
     top, gram, low = kernel(
         top_kernel,
         [((RANK, part), bf16), ((2 * RANK, 2 * RANK), f32), ((2 * RANK, RANK), bf16)],
-        pos, mine, swap(mine, 1), *nodes,
-        scratch=[pltpu.VMEM((PLANES, RANK, part), bf16), pltpu.VMEM((PLANES, RANK, RANK), f32)] + work_shapes * 2,
+        pos, mine, swap(mine, 1), *pairs,
+        scratch=work_shapes,
     )
     tops = swap_all([top] * PLANES, PLANE)
     (factor,) = kernel(factor_kernel, [((RANK, RANK), f32)], gram, low, scalar=False)
@@ -384,7 +414,9 @@
         pos, mine, swap(mine, 1), factor, *tops,
         scratch=[pltpu.VMEM((height, RANK), f32)],
     )
-    (result,) = kernel(whole_kernel, [((block, total), bf16)], pos, *swap_all(outs, 1))
+    (result,) = kernel(
+        whole_kernel, [((block, total), bf16)], pos, *swap_all(outs, 1), scratch=sems, far_out=True
+    )
     return result
 
 

time: 130 us -> 131 us (level)
  starting transfers between devices: 39.6 us -> 45 us
  waiting for transfers between devices: 59.6 us -> 54.7 us
  Pallas kernels: 28.9 us -> 30.3 us
    ppermute x38 -> x42, starting transfers between devices: 39.6 us -> 45 us  [swap(): return lax.ppermute(x, 'cols', [(i, i ^ apart) for i in range(count)])]
    ppermute x38 -> x42, waiting for transfers between devices: 59.6 us -> 54.7 us  [swap(): return lax.ppermute(x, 'cols', [(i, i ^ apart) for i in range(count)])]
    pallas_call x10 -> x11, Pallas kernels: 28.9 us -> 30.3 us  [kernel(): pl.pallas_call(fn, out_shape=[jax.ShapeDtypeStruct(s, d) for s, d in shap...]
  transfers between devices with their start and end apart: 38 -> 42, of which waited for: 25 -> 24; matrix products, arithmetic and copies ran while one was open for 0% -> 0% of each run, Pallas kernels for 4% -> 11%
where the time goes in v1:
time: 131 us
  waiting for transfers between devices  54.7 us (42%)
  starting transfers between devices  45 us (34%)
  Pallas kernels  30.3 us (23%)
    ppermute x42, waiting for transfers between devices, swap(): return lax.ppermute(x, 'cols', [(i, i ^ apart) for i in range(count)])  54.7 us
    ppermute x42, starting transfers between devices, swap(): return lax.ppermute(x, 'cols', [(i, i ^ apart) for i in range(count)])  45 us
    pallas_call x11, Pallas kernels, kernel(): pl.pallas_call(fn, out_shape=[jax.ShapeDtypeStruct(s, d) for s, d in shap...  30.3 us
  transfers between devices with their start and end apart: 42, of which 24 were waited for; matrix products, arithmetic and copies ran while one was open for 0% of the time, Pallas kernels for 11%

profile of v1, /device:TPU:0, one launch (start us, length us, event | category | flops | bytes accessed | tf_op | source)
XLA Modules:
  0.0 130.7 jit_solution(17187625600867763384)
XLA Ops:
  0.0 1.4 %parts_kernel.1 = (bf16[32,2048]{1,0:T(8,128)(2,1)S(1)}, bf16[32,2048]{1,0:T(8,128)(2,1)S(1)}, bf16[32,2048]{1,0:T(8,128)(2,1)S(1)}, bf16[32,2048]{1,0:T(8,128)(...) custom-call(s32[1]{0:T(128)} %bitcast.pos_ref, ...), custom_call_target="tpu_custom_call" | custom-call | tf_op jit(solution)/shard_map/parts_kernel/pallas_call | solution.py:324
  1.4 0.5 collective-permute-start
  1.9 2.6 %collective-permute-start.1 = (bf16[32,2048]{1,0:T(8,128)(2,1)S(1)}, bf16[32,2048]{1,0:T(8,128)(2,1)S(1)}, u32[]{:S(2)}, u32[]{:S(2)}) collective-permute-start(bf16[32,2048]{1,0:T(8,128)(2,1)S(1)} %get-tuple-element.54), channel_id=1, source_target_pairs={{0,2},{1,3},{2,0},{3,1},{4,6},{5,7},{6,4},{7,5},{8,10},{9,11},{10,... | collective-permute-start | bytes 393224 | tf_op jit(solution)/shard_map/ppermute | solution.py:341
  4.5 1.8 %collective-permute-start.3 = (bf16[32,2048]{1,0:T(8,128)(2,1)S(1)}, bf16[32,2048]{1,0:T(8,128)(2,1)S(1)}, u32[]{:S(2)}, u32[]{:S(2)}) collective-permute-start(bf16[32,2048]{1,0:T(8,128)(2,1)S(1)} %get-tuple-element.56), channel_id=1, source_target_pairs={{0,4},{1,5},{2,6},{3,7},{4,0},{5,1},{6,2},{7,3},{8,12},{9,13},{10,... | collective-permute-start | bytes 393224 | tf_op jit(solution)/shard_map/ppermute | solution.py:341
  6.3 2.6 %collective-permute-start.5 = (bf16[32,2048]{1,0:T(8,128)(2,1)S(1)}, bf16[32,2048]{1,0:T(8,128)(2,1)S(1)}, u32[]{:S(2)}, u32[]{:S(2)}) collective-permute-start(bf16[32,2048]{1,0:T(8,128)(2,1)S(1)} %get-tuple-element.58), channel_id=1, source_target_pairs={{0,6},{1,7},{2,4},{3,5},{4,2},{5,3},{6,0},{7,1},{8,14},{9,15},{10,... | collective-permute-start | bytes 393224 | tf_op jit(solution)/shard_map/ppermute | solution.py:341
  8.9 1.6 %collective-permute-start.6 = (bf16[32,2048]{1,0:T(8,128)(2,1)S(1)}, bf16[32,2048]{1,0:T(8,128)(2,1)S(1)}, u32[]{:S(2)}, u32[]{:S(2)}) collective-permute-start(bf16[32,2048]{1,0:T(8,128)(2,1)S(1)} %get-tuple-element.59), channel_id=1, source_target_pairs={{0,7},{1,6},{2,5},{3,4},{4,3},{5,2},{6,1},{7,0},{8,15},{9,14},{10,... | collective-permute-start | bytes 393224 | tf_op jit(solution)/shard_map/ppermute | solution.py:341
  10.5 0.6 collective-permute-done.2.refs_3_
  11.1 6.9 %collective-permute-done.4.refs_5_ = bf16[32,2048]{1,0:T(8,128)(2,1)S(1)} collective-permute-done((bf16[32,2048]{1,0:T(8,128)(2,1)S(1)}, bf16[32,2048]{1,0:T(8,128)(2,1)S(1)}, u32[]{:S(2)}, u32[]{:S(2)}) %collective-permute-start.4) | collective-permute-done | bytes 131104 | tf_op jit(solution)/shard_map/ppermute | solution.py:341
  18.0 0.5 gram_kernel.1
  18.5 0.6 collective-permute-start.7
  19.1 0.9 collective-permute-done.7
  20.1 2.8 %collective-permute-start.10 = (bf16[3,64,128]{2,1,0:T(8,128)(2,1)S(1)}, bf16[3,64,128]{2,1,0:T(8,128)(2,1)S(1)}, u32[]{:S(2)}, u32[]{:S(2)}) collective-permute-start(bf16[3,64,128]{2,1,0:T(8,128)(2,1)S(1)} %add_convert_fusion.2), channel_id=1, source_target_pairs={{0,6},{1,7},{2,4},{3,5},{4,2},{5,3},{6,0},{7,1},{8,14},{9,15},{10,... | collective-permute-start | bytes 147464 | tf_op jit(solution)/shard_map/ppermute | solution.py:341
  22.9 0.5 collective-permute-start.8
  23.7 1.5 %collective-permute-done.10 = bf16[3,64,128]{2,1,0:T(8,128)(2,1)S(1)} collective-permute-done((bf16[3,64,128]{2,1,0:T(8,128)(2,1)S(1)}, bf16[3,64,128]{2,1,0:T(8,128)(2,1)S(1)}, u32[]{:S(2)}, u32[]{:S(2)}) %collective-permute-start.10) | collective-permute-done | bytes 49184 | tf_op jit(solution)/shard_map/ppermute | solution.py:341
  25.2 1.8 %collective-permute-done.8 = bf16[3,64,128]{2,1,0:T(8,128)(2,1)S(1)} collective-permute-done((bf16[3,64,128]{2,1,0:T(8,128)(2,1)S(1)}, bf16[3,64,128]{2,1,0:T(8,128)(2,1)S(1)}, u32[]{:S(2)}, u32[]{:S(2)}) %collective-permute-start.8) | collective-permute-done | bytes 49184 | tf_op jit(solution)/shard_map/ppermute | solution.py:341
  26.9 0.5 collective-permute-done.9
  27.6 1.3 collective-permute-done.11.other_ref
  28.9 5.4 %node_kernel.1 = (bf16[128,512]{1,0:T(8,128)(2,1)S(1)}, bf16[128,512]{1,0:T(8,128)(2,1)S(1)}, bf16[128,512]{1,0:T(8,128)(2,1)S(1)}, bf16[128,512]{1,0:T(8,128)(2,1)S(1)}, bf16[256,128]{1,0:T(8,128)(2,1)S(1)}) custom-call(s32[1]{0:T(128)} %bitcast.pos_ref, f32[3,64,128]{2,1,0:T(8,128)S(1)} %add_add_fusion.1.mine_ref, ...), custom_call_target="tpu_custom_call" | custom-call | tf_op jit(solution)/shard_map/node_kernel/pallas_call | solution.py:324
  34.3 1.6 %collective-permute-start.12 = (bf16[128,512]{1,0:T(8,128)(2,1)S(1)}, bf16[128,512]{1,0:T(8,128)(2,1)S(1)}, u32[]{:S(2)}, u32[]{:S(2)}) collective-permute-start(bf16[128,512]{1,0:T(8,128)(2,1)S(1)} %get-tuple-element.64), channel_id=1, source_target_pairs={{0,8},{1,9},{2,10},{3,11},{4,12},{5,13},{6,14},{7,15},{8,0},{9,1},... | collective-permute-start | bytes 393224 | tf_op jit(solution)/shard_map/ppermute | solution.py:341
  36.0 2.6 %collective-permute-start.13 = (bf16[128,512]{1,0:T(8,128)(2,1)S(1)}, bf16[128,512]{1,0:T(8,128)(2,1)S(1)}, u32[]{:S(2)}, u32[]{:S(2)}) collective-permute-start(bf16[128,512]{1,0:T(8,128)(2,1)S(1)} %get-tuple-element.65), channel_id=1, source_target_pairs={{0,16},{1,17},{2,18},{3,19},{4,20},{5,21},{6,22},{7,23},{8,24},{9,... | collective-permute-start | bytes 393224 | tf_op jit(solution)/shard_map/ppermute | solution.py:341
  38.8 3.1 %collective-permute-done.12.refs_1_ = bf16[128,512]{1,0:T(8,128)(2,1)S(1)} collective-permute-done((bf16[128,512]{1,0:T(8,128)(2,1)S(1)}, bf16[128,512]{1,0:T(8,128)(2,1)S(1)}, u32[]{:S(2)}, u32[]{:S(2)}) %collective-permute-start.12) | collective-permute-done | bytes 131104 | tf_op jit(solution)/shard_map/ppermute | solution.py:341
  41.9 7.0 %collective-permute-done.13.refs_2_ = bf16[128,512]{1,0:T(8,128)(2,1)S(1)} collective-permute-done((bf16[128,512]{1,0:T(8,128)(2,1)S(1)}, bf16[128,512]{1,0:T(8,128)(2,1)S(1)}, u32[]{:S(2)}, u32[]{:S(2)}) %collective-permute-start.13) | collective-permute-done | bytes 131104 | tf_op jit(solution)/shard_map/ppermute | solution.py:341
  48.9 0.4 cross_kernel.1
  49.4 1.4 %collective-permute-done.15 = f32[6,64,128]{2,1,0:T(8,128)S(1)} collective-permute-done((f32[6,64,128]{2,1,0:T(8,128)S(1)}, f32[6,64,128]{2,1,0:T(8,128)S(1)}, u32[]{:S(2)}, u32[]{:S(2)}) %collective-permute-start.15) | collective-permute-done | bytes 196640 | tf_op jit(solution)/shard_map/ppermute | solution.py:341
  50.8 1.6 %collective-permute-start.16 = (bf16[6,64,128]{2,1,0:T(8,128)(2,1)S(1)}, bf16[6,64,128]{2,1,0:T(8,128)(2,1)S(1)}, u32[]{:S(2)}, u32[]{:S(2)}) collective-permute-start(bf16[6,64,128]{2,1,0:T(8,128)(2,1)S(1)} %add_convert_fusion.1), channel_id=1, source_target_pairs={{0,2},{1,3},{2,0},{3,1},{4,6},{5,7},{6,4},{7,5},{8,10},{9,11},{10,... | collective-permute-start | bytes 294920 | tf_op jit(solution)/shard_map/ppermute | solution.py:341
  52.4 0.5 collective-permute-start.17
  52.9 1.5 %collective-permute-start.18 = (bf16[6,64,128]{2,1,0:T(8,128)(2,1)S(1)}, bf16[6,64,128]{2,1,0:T(8,128)(2,1)S(1)}, u32[]{:S(2)}, u32[]{:S(2)}) collective-permute-start(bf16[6,64,128]{2,1,0:T(8,128)(2,1)S(1)} %add_convert_fusion.1), channel_id=1, source_target_pairs={{0,6},{1,7},{2,4},{3,5},{4,2},{5,3},{6,0},{7,1},{8,14},{9,15},{10,... | collective-permute-start | bytes 294920 | tf_op jit(solution)/shard_map/ppermute | solution.py:341
  54.4 0.8 diag_kernel.1
  55.2 0.5 collective-permute-done.16
  55.7 3.4 %collective-permute-done.17 = bf16[6,64,128]{2,1,0:T(8,128)(2,1)S(1)} collective-permute-done((bf16[6,64,128]{2,1,0:T(8,128)(2,1)S(1)}, bf16[6,64,128]{2,1,0:T(8,128)(2,1)S(1)}, u32[]{:S(2)}, u32[]{:S(2)}) %collective-permute-start.17) | collective-permute-done | bytes 98336 | tf_op jit(solution)/shard_map/ppermute | solution.py:341
  59.2 2.4 %collective-permute-start.22 = (bf16[3,64,128]{2,1,0:T(8,128)(2,1)S(1)}, bf16[3,64,128]{2,1,0:T(8,128)(2,1)S(1)}, u32[]{:S(2)}, u32[]{:S(2)}) collective-permute-start(bf16[3,64,128]{2,1,0:T(8,128)(2,1)S(1)} %pad_maximum_fusion), channel_id=1, source_target_pairs={{0,8},{1,9},{2,10},{3,11},{4,12},{5,13},{6,14},{7,15},{8,0},{9,1},... | collective-permute-start | bytes 147464 | tf_op jit(solution)/shard_map/ppermute | solution.py:341
  61.6 1.1 collective-permute-start.23
  62.7 1.4 %collective-permute-start.24 = (bf16[3,64,128]{2,1,0:T(8,128)(2,1)S(1)}, bf16[3,64,128]{2,1,0:T(8,128)(2,1)S(1)}, u32[]{:S(2)}, u32[]{:S(2)}) collective-permute-start(bf16[3,64,128]{2,1,0:T(8,128)(2,1)S(1)} %pad_maximum_fusion), channel_id=1, source_target_pairs={{0,24},{1,25},{2,26},{3,27},{4,28},{5,29},{6,30},{7,31},{8,16},{9,... | collective-permute-start | bytes 147464 | tf_op jit(solution)/shard_map/ppermute | solution.py:341
  64.0 3.0 %collective-permute-done.23 = bf16[3,64,128]{2,1,0:T(8,128)(2,1)S(1)} collective-permute-done((bf16[3,64,128]{2,1,0:T(8,128)(2,1)S(1)}, bf16[3,64,128]{2,1,0:T(8,128)(2,1)S(1)}, u32[]{:S(2)}, u32[]{:S(2)}) %collective-permute-start.23) | collective-permute-done | bytes 49184 | tf_op jit(solution)/shard_map/ppermute | solution.py:341
  67.1 1.6 %collective-permute-done.24 = bf16[3,64,128]{2,1,0:T(8,128)(2,1)S(1)} collective-permute-done((bf16[3,64,128]{2,1,0:T(8,128)(2,1)S(1)}, bf16[3,64,128]{2,1,0:T(8,128)(2,1)S(1)}, u32[]{:S(2)}, u32[]{:S(2)}) %collective-permute-start.24) | collective-permute-done | bytes 49184 | tf_op jit(solution)/shard_map/ppermute | solution.py:341
  68.8 0.6 collective-permute-start.19
  69.5 1.4 %collective-permute-start.20 = (bf16[4,64,128]{2,1,0:T(8,128)(2,1)S(1)}, bf16[4,64,128]{2,1,0:T(8,128)(2,1)S(1)}, u32[]{:S(2)}, u32[]{:S(2)}) collective-permute-start(bf16[4,64,128]{2,1,0:T(8,128)(2,1)S(1)} %slice.32), channel_id=1, source_target_pairs={{0,16},{1,17},{2,18},{3,19},{4,20},{5,21},{6,22},{7,23},{8,24},{9,... | collective-permute-start | bytes 196616 | tf_op jit(solution)/shard_map/ppermute | solution.py:341
  70.8 2.4 %collective-permute-start.21 = (bf16[4,64,128]{2,1,0:T(8,128)(2,1)S(1)}, bf16[4,64,128]{2,1,0:T(8,128)(2,1)S(1)}, u32[]{:S(2)}, u32[]{:S(2)}) collective-permute-start(bf16[4,64,128]{2,1,0:T(8,128)(2,1)S(1)} %slice.32), channel_id=1, source_target_pairs={{0,24},{1,25},{2,26},{3,27},{4,28},{5,29},{6,30},{7,31},{8,16},{9,... | collective-permute-start | bytes 196616 | tf_op jit(solution)/shard_map/ppermute | solution.py:341
  73.3 9.2 %pair_kernel.1 = (bf16[256,128]{1,0:T(8,128)(2,1)S(1)}, f32[128,128]{1,0:T(8,128)S(1)}, bf16[128,512]{1,0:T(8,128)(2,1)S(1)}, bf16[256,128]{1,0:T(8,128)(2,1)S(1...) custom-call(s32[1]{0:T(128)} %bitcast.pos_ref, f32[6,64,128]{2,1,0:T(8,128)S(1)} %convert_dynamic-update-slice_fusion.mine_ref, ...), custom_call_target="tpu_custom_call" | custom-call | tf_op jit(solution)/shard_map/pair_kernel/pallas_call | solution.py:324
  82.6 1.3 %collective-permute-done.26.other_ref = f32[4,64,128]{2,1,0:T(8,128)S(1)} collective-permute-done((f32[4,64,128]{2,1,0:T(8,128)S(1)}, f32[4,64,128]{2,1,0:T(8,128)S(1)}, u32[]{:S(2)}, u32[]{:S(2)}) %collective-permute-start.26) | collective-permute-done | bytes 131104 | tf_op jit(solution)/shard_map/ppermute | solution.py:341
  83.9 5.9 %top_kernel.1 = (bf16[128,512]{1,0:T(8,128)(2,1)S(1)}, f32[256,256]{1,0:T(8,128)S(1)}, bf16[256,128]{1,0:T(8,128)(2,1)S(1)}) custom-call(s32[1]{0:T(128)} %bitcast.pos_ref, f32[4,64,128]{2,1,0:T(8,128)S(1)} %add_add_fusion.mine_ref, f32[4,64,128]{2,1,0:T(8,128)S(1)} %collective-permute-done.26.other_ref, bf16[256,128]{1,0:T(8,128)(2,1)S(1)} %get-tuple-element.80.low_a, ...), custom_call_target="tpu_custom_call" | custom-call | tf_op jit(solution)/shard_map/top_kernel/pallas_call | solution.py:324
  89.9 1.9 %collective-permute-start.28 = (bf16[128,512]{1,0:T(8,128)(2,1)S(1)}, bf16[128,512]{1,0:T(8,128)(2,1)S(1)}, u32[]{:S(2)}, u32[]{:S(2)}) collective-permute-start(bf16[128,512]{1,0:T(8,128)(2,1)S(1)} %get-tuple-element.88.refs_0_), channel_id=1, source_target_pairs={{0,16},{1,17},{2,18},{3,19},{4,20},{5,21},{6,22},{7,23},{8,24},{9,... | collective-permute-start | bytes 393224 | tf_op jit(solution)/shard_map/ppermute | solution.py:341
  91.9 2.4 %collective-permute-start.29 = (bf16[128,512]{1,0:T(8,128)(2,1)S(1)}, bf16[128,512]{1,0:T(8,128)(2,1)S(1)}, u32[]{:S(2)}, u32[]{:S(2)}) collective-permute-start(bf16[128,512]{1,0:T(8,128)(2,1)S(1)} %get-tuple-element.88.refs_0_), channel_id=1, source_target_pairs={{0,24},{1,25},{2,26},{3,27},{4,28},{5,29},{6,30},{7,31},{8,16},{9,... | collective-permute-start | bytes 393224 | tf_op jit(solution)/shard_map/ppermute | solution.py:341
  94.3 4.0 %factor_kernel.1.factor_ref = f32[128,128]{1,0:T(8,128)S(1)} custom-call(f32[256,256]{1,0:T(8,128)S(1)} %get-tuple-element.86.gram_ref, bf16[256,128]{1,0:T(8,128)(2,1)S(1)} %get-tuple-element.87.low_ref), custom_call_target="tpu_custom_call" | custom-call | tf_op jit(solution)/shard_map/factor_kernel/pallas_call | solution.py:324
  98.3 4.6 %collective-permute-done.28.refs_2_ = bf16[128,512]{1,0:T(8,128)(2,1)S(1)} collective-permute-done((bf16[128,512]{1,0:T(8,128)(2,1)S(1)}, bf16[128,512]{1,0:T(8,128)(2,1)S(1)}, u32[]{:S(2)}, u32[]{:S(2)}) %collective-permute-start.28) | collective-permute-done | bytes 131104 | tf_op jit(solution)/shard_map/ppermute | solution.py:341
  102.9 0.8 coeffs_kernel.1
  103.8 1.2 collective-permute-done.30
  105.1 0.6 collective-permute-start.31
  105.7 1.2 collective-permute-start.32
  106.8 1.8 %collective-permute-start.33 = (bf16[1,128,128]{2,1,0:T(8,128)(2,1)S(1)}, bf16[1,128,128]{2,1,0:T(8,128)(2,1)S(1)}, u32[]{:S(2)}, u32[]{:S(2)}) collective-permute-start(bf16[1,128,128]{2,1,0:T(8,128)(2,1)S(1)} %add_convert_fusion.3), channel_id=1, source_target_pairs={{0,6},{1,7},{2,4},{3,5},{4,2},{5,3},{6,0},{7,1},{8,14},{9,15},{10,... | collective-permute-start | bytes 98312 | tf_op jit(solution)/shard_map/ppermute | solution.py:341
  108.6 0.4 collective-permute-done.31
  109.1 0.5 collective-permute-done.32
  109.6 2.1 %collective-permute-done.33 = bf16[1,128,128]{2,1,0:T(8,128)(2,1)S(1)} collective-permute-done((bf16[1,128,128]{2,1,0:T(8,128)(2,1)S(1)}, bf16[1,128,128]{2,1,0:T(8,128)(2,1)S(1)}, u32[]{:S(2)}, u32[]{:S(2)}) %collective-permute-start.33) | collective-permute-done | bytes 32800 | tf_op jit(solution)/shard_map/ppermute | solution.py:341
  111.7 1.2 collective-permute-done.34.other_ref
  113.0 0.8 project_kernel.1
  114.0 1.2 collective-permute-start.36
  115.1 0.5 collective-permute-start.37
  115.7 0.9 collective-permute-start.38
  116.6 0.9 collective-permute-start.39
  117.5 1.8 %collective-permute-start.40 = (bf16[32,2048]{1,0:T(8,128)(2,1)S(1)}, bf16[32,2048]{1,0:T(8,128)(2,1)S(1)}, u32[]{:S(2)}, u32[]{:S(2)}) collective-permute-start(bf16[32,2048]{1,0:T(8,128)(2,1)S(1)} %get-tuple-element.97), channel_id=1, source_target_pairs={{0,6},{1,7},{2,4},{3,5},{4,2},{5,3},{6,0},{7,1},{8,14},{9,15},{10,... | collective-permute-start | bytes 393224 | tf_op jit(solution)/shard_map/ppermute | solution.py:341
  119.3 1.0 collective-permute-done.36.refs_2_
  120.7 1.3 collective-permute-done.37.refs_3_
  122.0 7.5 %collective-permute-done.39.refs_5_ = bf16[32,2048]{1,0:T(8,128)(2,1)S(1)} collective-permute-done((bf16[32,2048]{1,0:T(8,128)(2,1)S(1)}, bf16[32,2048]{1,0:T(8,128)(2,1)S(1)}, u32[]{:S(2)}, u32[]{:S(2)}) %collective-permute-start.39) | collective-permute-done | bytes 131104 | tf_op jit(solution)/shard_map/ppermute | solution.py:341
  129.5 1.0 whole_kernel.1
  (46 shorter events, 2.0 us)
Async XLA Ops:
  1.4 4.9 %collective-permute-start = (bf16[32,2048]{1,0:T(8,128)(2,1)S(1)}, bf16[32,2048]{1,0:T(8,128)(2,1)S(1)}, u32[]{:S(2)}, u32[]{:S(2)}) collective-permute-start(bf16[32,2048]{1,0:T(8,128)(2,1)S(1)} %get-tuple-element.53), channel_id=1, source_target_pairs={{0,1},{1,0},{2,3},{3,2},{4,5},{5,4},{6,7},{7,6},{8,9},{9,8},{10,11... | collective-permute-start | bytes 393224 | tf_op jit(solution)/shard_map/ppermute | solution.py:341
  1.9 7.0 %collective-permute-start.1 = (bf16[32,2048]{1,0:T(8,128)(2,1)S(1)}, bf16[32,2048]{1,0:T(8,128)(2,1)S(1)}, u32[]{:S(2)}, u32[]{:S(2)}) collective-permute-start(bf16[32,2048]{1,0:T(8,128)(2,1)S(1)} %get-tuple-element.54), channel_id=1, source_target_pairs={{0,2},{1,3},{2,0},{3,1},{4,6},{5,7},{6,4},{7,5},{8,10},{9,11},{10,... | collective-permute-start | bytes 393224 | tf_op jit(solution)/shard_map/ppermute | solution.py:341
  4.4 6.6 %collective-permute-start.2 = (bf16[32,2048]{1,0:T(8,128)(2,1)S(1)}, bf16[32,2048]{1,0:T(8,128)(2,1)S(1)}, u32[]{:S(2)}, u32[]{:S(2)}) collective-permute-start(bf16[32,2048]{1,0:T(8,128)(2,1)S(1)} %get-tuple-element.55), channel_id=1, source_target_pairs={{0,3},{1,2},{2,1},{3,0},{4,7},{5,6},{6,5},{7,4},{8,11},{9,10},{10,... | collective-permute-start | bytes 393224 | tf_op jit(solution)/shard_map/ppermute | solution.py:341
  4.5 6.6 %collective-permute-start.3 = (bf16[32,2048]{1,0:T(8,128)(2,1)S(1)}, bf16[32,2048]{1,0:T(8,128)(2,1)S(1)}, u32[]{:S(2)}, u32[]{:S(2)}) collective-permute-start(bf16[32,2048]{1,0:T(8,128)(2,1)S(1)} %get-tuple-element.56), channel_id=1, source_target_pairs={{0,4},{1,5},{2,6},{3,7},{4,0},{5,1},{6,2},{7,3},{8,12},{9,13},{10,... | collective-permute-start | bytes 393224 | tf_op jit(solution)/shard_map/ppermute | solution.py:341
  6.3 11.7 %collective-permute-start.4 = (bf16[32,2048]{1,0:T(8,128)(2,1)S(1)}, bf16[32,2048]{1,0:T(8,128)(2,1)S(1)}, u32[]{:S(2)}, u32[]{:S(2)}) collective-permute-start(bf16[32,2048]{1,0:T(8,128)(2,1)S(1)} %get-tuple-element.57), channel_id=1, source_target_pairs={{0,5},{1,4},{2,7},{3,6},{4,1},{5,0},{6,3},{7,2},{8,13},{9,12},{10,... | collective-permute-start | bytes 393224 | tf_op jit(solution)/shard_map/ppermute | solution.py:341
  6.3 11.7 %collective-permute-start.5 = (bf16[32,2048]{1,0:T(8,128)(2,1)S(1)}, bf16[32,2048]{1,0:T(8,128)(2,1)S(1)}, u32[]{:S(2)}, u32[]{:S(2)}) collective-permute-start(bf16[32,2048]{1,0:T(8,128)(2,1)S(1)} %get-tuple-element.58), channel_id=1, source_target_pairs={{0,6},{1,7},{2,4},{3,5},{4,2},{5,3},{6,0},{7,1},{8,14},{9,15},{10,... | collective-permute-start | bytes 393224 | tf_op jit(solution)/shard_map/ppermute | solution.py:341
  8.9 9.1 %collective-permute-start.6 = (bf16[32,2048]{1,0:T(8,128)(2,1)S(1)}, bf16[32,2048]{1,0:T(8,128)(2,1)S(1)}, u32[]{:S(2)}, u32[]{:S(2)}) collective-permute-start(bf16[32,2048]{1,0:T(8,128)(2,1)S(1)} %get-tuple-element.59), channel_id=1, source_target_pairs={{0,7},{1,6},{2,5},{3,4},{4,3},{5,2},{6,1},{7,0},{8,15},{9,14},{10,... | collective-permute-start | bytes 393224 | tf_op jit(solution)/shard_map/ppermute | solution.py:341
  18.5 1.6 %collective-permute-start.7 = (f32[3,64,128]{2,1,0:T(8,128)S(1)}, f32[3,64,128]{2,1,0:T(8,128)S(1)}, u32[]{:S(2)}, u32[]{:S(2)}) collective-permute-start(f32[3,64,128]{2,1,0:T(8,128)S(1)} %get-tuple-element.62), channel_id=1, source_target_pairs={{0,1},{1,0},{2,3},{3,2},{4,5},{5,4},{6,7},{7,6},{8,9},{9,8},{10,11... | collective-permute-start | bytes 294920 | tf_op jit(solution)/shard_map/ppermute | solution.py:341
  20.1 5.1 %collective-permute-start.10 = (bf16[3,64,128]{2,1,0:T(8,128)(2,1)S(1)}, bf16[3,64,128]{2,1,0:T(8,128)(2,1)S(1)}, u32[]{:S(2)}, u32[]{:S(2)}) collective-permute-start(bf16[3,64,128]{2,1,0:T(8,128)(2,1)S(1)} %add_convert_fusion.2), channel_id=1, source_target_pairs={{0,6},{1,7},{2,4},{3,5},{4,2},{5,3},{6,0},{7,1},{8,14},{9,15},{10,... | collective-permute-start | bytes 147464 | tf_op jit(solution)/shard_map/ppermute | solution.py:341
  22.9 4.1 %collective-permute-start.8 = (bf16[3,64,128]{2,1,0:T(8,128)(2,1)S(1)}, bf16[3,64,128]{2,1,0:T(8,128)(2,1)S(1)}, u32[]{:S(2)}, u32[]{:S(2)}) collective-permute-start(bf16[3,64,128]{2,1,0:T(8,128)(2,1)S(1)} %add_convert_fusion.2), channel_id=1, source_target_pairs={{0,2},{1,3},{2,0},{3,1},{4,6},{5,7},{6,4},{7,5},{8,10},{9,11},{10,... | collective-permute-start | bytes 147464 | tf_op jit(solution)/shard_map/ppermute | solution.py:341
  23.4 4.1 %collective-permute-start.9 = (bf16[3,64,128]{2,1,0:T(8,128)(2,1)S(1)}, bf16[3,64,128]{2,1,0:T(8,128)(2,1)S(1)}, u32[]{:S(2)}, u32[]{:S(2)}) collective-permute-start(bf16[3,64,128]{2,1,0:T(8,128)(2,1)S(1)} %add_convert_fusion.2), channel_id=1, source_target_pairs={{0,4},{1,5},{2,6},{3,7},{4,0},{5,1},{6,2},{7,3},{8,12},{9,13},{10,... | collective-permute-start | bytes 147464 | tf_op jit(solution)/shard_map/ppermute | solution.py:341
  27.5 1.4 %collective-permute-start.11 = (f32[3,64,128]{2,1,0:T(8,128)S(1)}, f32[3,64,128]{2,1,0:T(8,128)S(1)}, u32[]{:S(2)}, u32[]{:S(2)}) collective-permute-start(f32[3,64,128]{2,1,0:T(8,128)S(1)} %add_add_fusion.1.mine_ref), channel_id=1, source_target_pairs={{0,1},{1,0},{2,3},{3,2},{4,5},{5,4},{6,7},{7,6},{8,9},{9,8},{10,11... | collective-permute-start | bytes 294920 | tf_op jit(solution)/shard_map/ppermute | solution.py:341
  34.3 7.6 %collective-permute-start.12 = (bf16[128,512]{1,0:T(8,128)(2,1)S(1)}, bf16[128,512]{1,0:T(8,128)(2,1)S(1)}, u32[]{:S(2)}, u32[]{:S(2)}) collective-permute-start(bf16[128,512]{1,0:T(8,128)(2,1)S(1)} %get-tuple-element.64), channel_id=1, source_target_pairs={{0,8},{1,9},{2,10},{3,11},{4,12},{5,13},{6,14},{7,15},{8,0},{9,1},... | collective-permute-start | bytes 393224 | tf_op jit(solution)/shard_map/ppermute | solution.py:341
  36.0 12.9 %collective-permute-start.13 = (bf16[128,512]{1,0:T(8,128)(2,1)S(1)}, bf16[128,512]{1,0:T(8,128)(2,1)S(1)}, u32[]{:S(2)}, u32[]{:S(2)}) collective-permute-start(bf16[128,512]{1,0:T(8,128)(2,1)S(1)} %get-tuple-element.65), channel_id=1, source_target_pairs={{0,16},{1,17},{2,18},{3,19},{4,20},{5,21},{6,22},{7,23},{8,24},{9,... | collective-permute-start | bytes 393224 | tf_op jit(solution)/shard_map/ppermute | solution.py:341
  38.5 10.3 %collective-permute-start.14 = (bf16[128,512]{1,0:T(8,128)(2,1)S(1)}, bf16[128,512]{1,0:T(8,128)(2,1)S(1)}, u32[]{:S(2)}, u32[]{:S(2)}) collective-permute-start(bf16[128,512]{1,0:T(8,128)(2,1)S(1)} %get-tuple-element.66), channel_id=1, source_target_pairs={{0,24},{1,25},{2,26},{3,27},{4,28},{5,29},{6,30},{7,31},{8,16},{9,... | collective-permute-start | bytes 393224 | tf_op jit(solution)/shard_map/ppermute | solution.py:341
  49.3 1.5 %collective-permute-start.15 = (f32[6,64,128]{2,1,0:T(8,128)S(1)}, f32[6,64,128]{2,1,0:T(8,128)S(1)}, u32[]{:S(2)}, u32[]{:S(2)}) collective-permute-start(f32[6,64,128]{2,1,0:T(8,128)S(1)} %get-tuple-element.68), channel_id=1, source_target_pairs={{0,1},{1,0},{2,3},{3,2},{4,5},{5,4},{6,7},{7,6},{8,9},{9,8},{10,11... | collective-permute-start | bytes 589832 | tf_op jit(solution)/shard_map/ppermute | solution.py:341
  50.8 4.9 %collective-permute-start.16 = (bf16[6,64,128]{2,1,0:T(8,128)(2,1)S(1)}, bf16[6,64,128]{2,1,0:T(8,128)(2,1)S(1)}, u32[]{:S(2)}, u32[]{:S(2)}) collective-permute-start(bf16[6,64,128]{2,1,0:T(8,128)(2,1)S(1)} %add_convert_fusion.1), channel_id=1, source_target_pairs={{0,2},{1,3},{2,0},{3,1},{4,6},{5,7},{6,4},{7,5},{8,10},{9,11},{10,... | collective-permute-start | bytes 294920 | tf_op jit(solution)/shard_map/ppermute | solution.py:341
  52.4 6.7 %collective-permute-start.17 = (bf16[6,64,128]{2,1,0:T(8,128)(2,1)S(1)}, bf16[6,64,128]{2,1,0:T(8,128)(2,1)S(1)}, u32[]{:S(2)}, u32[]{:S(2)}) collective-permute-start(bf16[6,64,128]{2,1,0:T(8,128)(2,1)S(1)} %add_convert_fusion.1), channel_id=1, source_target_pairs={{0,4},{1,5},{2,6},{3,7},{4,0},{5,1},{6,2},{7,3},{8,12},{9,13},{10,... | collective-permute-start | bytes 294920 | tf_op jit(solution)/shard_map/ppermute | solution.py:341
  52.9 6.2 %collective-permute-start.18 = (bf16[6,64,128]{2,1,0:T(8,128)(2,1)S(1)}, bf16[6,64,128]{2,1,0:T(8,128)(2,1)S(1)}, u32[]{:S(2)}, u32[]{:S(2)}) collective-permute-start(bf16[6,64,128]{2,1,0:T(8,128)(2,1)S(1)} %add_convert_fusion.1), channel_id=1, source_target_pairs={{0,6},{1,7},{2,4},{3,5},{4,2},{5,3},{6,0},{7,1},{8,14},{9,15},{10,... | collective-permute-start | bytes 294920 | tf_op jit(solution)/shard_map/ppermute | solution.py:341
  59.2 4.9 %collective-permute-start.22 = (bf16[3,64,128]{2,1,0:T(8,128)(2,1)S(1)}, bf16[3,64,128]{2,1,0:T(8,128)(2,1)S(1)}, u32[]{:S(2)}, u32[]{:S(2)}) collective-permute-start(bf16[3,64,128]{2,1,0:T(8,128)(2,1)S(1)} %pad_maximum_fusion), channel_id=1, source_target_pairs={{0,8},{1,9},{2,10},{3,11},{4,12},{5,13},{6,14},{7,15},{8,0},{9,1},... | collective-permute-start | bytes 147464 | tf_op jit(solution)/shard_map/ppermute | solution.py:341
  61.6 5.5 %collective-permute-start.23 = (bf16[3,64,128]{2,1,0:T(8,128)(2,1)S(1)}, bf16[3,64,128]{2,1,0:T(8,128)(2,1)S(1)}, u32[]{:S(2)}, u32[]{:S(2)}) collective-permute-start(bf16[3,64,128]{2,1,0:T(8,128)(2,1)S(1)} %pad_maximum_fusion), channel_id=1, source_target_pairs={{0,16},{1,17},{2,18},{3,19},{4,20},{5,21},{6,22},{7,23},{8,24},{9,... | collective-permute-start | bytes 147464 | tf_op jit(solution)/shard_map/ppermute | solution.py:341
  62.7 6.0 %collective-permute-start.24 = (bf16[3,64,128]{2,1,0:T(8,128)(2,1)S(1)}, bf16[3,64,128]{2,1,0:T(8,128)(2,1)S(1)}, u32[]{:S(2)}, u32[]{:S(2)}) collective-permute-start(bf16[3,64,128]{2,1,0:T(8,128)(2,1)S(1)} %pad_maximum_fusion), channel_id=1, source_target_pairs={{0,24},{1,25},{2,26},{3,27},{4,28},{5,29},{6,30},{7,31},{8,16},{9,... | collective-permute-start | bytes 147464 | tf_op jit(solution)/shard_map/ppermute | solution.py:341
  68.7 4.5 %collective-permute-start.25 = (f32[6,64,128]{2,1,0:T(8,128)S(1)}, f32[6,64,128]{2,1,0:T(8,128)S(1)}, u32[]{:S(2)}, u32[]{:S(2)}) collective-permute-start(f32[6,64,128]{2,1,0:T(8,128)S(1)} %convert_dynamic-update-slice_fusion.mine_ref), channel_id=1, source_target_pairs={{0,1},{1,0},{2,3},{3,2},{4,5},{5,4},{6,7},{7,6},{8,9},{9,8},{10,11... | collective-permute-start | bytes 589832 | tf_op jit(solution)/shard_map/ppermute | solution.py:341
  68.8 13.6 %collective-permute-start.19 = (bf16[4,64,128]{2,1,0:T(8,128)(2,1)S(1)}, bf16[4,64,128]{2,1,0:T(8,128)(2,1)S(1)}, u32[]{:S(2)}, u32[]{:S(2)}) collective-permute-start(bf16[4,64,128]{2,1,0:T(8,128)(2,1)S(1)} %slice.32), channel_id=1, source_target_pairs={{0,8},{1,9},{2,10},{3,11},{4,12},{5,13},{6,14},{7,15},{8,0},{9,1},... | collective-permute-start | bytes 196616 | tf_op jit(solution)/shard_map/ppermute | solution.py:341
  69.5 13.0 %collective-permute-start.20 = (bf16[4,64,128]{2,1,0:T(8,128)(2,1)S(1)}, bf16[4,64,128]{2,1,0:T(8,128)(2,1)S(1)}, u32[]{:S(2)}, u32[]{:S(2)}) collective-permute-start(bf16[4,64,128]{2,1,0:T(8,128)(2,1)S(1)} %slice.32), channel_id=1, source_target_pairs={{0,16},{1,17},{2,18},{3,19},{4,20},{5,21},{6,22},{7,23},{8,24},{9,... | collective-permute-start | bytes 196616 | tf_op jit(solution)/shard_map/ppermute | solution.py:341
  70.8 11.6 %collective-permute-start.21 = (bf16[4,64,128]{2,1,0:T(8,128)(2,1)S(1)}, bf16[4,64,128]{2,1,0:T(8,128)(2,1)S(1)}, u32[]{:S(2)}, u32[]{:S(2)}) collective-permute-start(bf16[4,64,128]{2,1,0:T(8,128)(2,1)S(1)} %slice.32), channel_id=1, source_target_pairs={{0,24},{1,25},{2,26},{3,27},{4,28},{5,29},{6,30},{7,31},{8,16},{9,... | collective-permute-start | bytes 196616 | tf_op jit(solution)/shard_map/ppermute | solution.py:341
  82.5 1.4 %collective-permute-start.26 = (f32[4,64,128]{2,1,0:T(8,128)S(1)}, f32[4,64,128]{2,1,0:T(8,128)S(1)}, u32[]{:S(2)}, u32[]{:S(2)}) collective-permute-start(f32[4,64,128]{2,1,0:T(8,128)S(1)} %add_add_fusion.mine_ref), channel_id=1, source_target_pairs={{0,1},{1,0},{2,3},{3,2},{4,5},{5,4},{6,7},{7,6},{8,9},{9,8},{10,11... | collective-permute-start | bytes 393224 | tf_op jit(solution)/shard_map/ppermute | solution.py:341
  89.9 8.4 %collective-permute-start.27 = (bf16[128,512]{1,0:T(8,128)(2,1)S(1)}, bf16[128,512]{1,0:T(8,128)(2,1)S(1)}, u32[]{:S(2)}, u32[]{:S(2)}) collective-permute-start(bf16[128,512]{1,0:T(8,128)(2,1)S(1)} %get-tuple-element.88.refs_0_), channel_id=1, source_target_pairs={{0,8},{1,9},{2,10},{3,11},{4,12},{5,13},{6,14},{7,15},{8,0},{9,1},... | collective-permute-start | bytes 393224 | tf_op jit(solution)/shard_map/ppermute | solution.py:341
  89.9 13.0 %collective-permute-start.28 = (bf16[128,512]{1,0:T(8,128)(2,1)S(1)}, bf16[128,512]{1,0:T(8,128)(2,1)S(1)}, u32[]{:S(2)}, u32[]{:S(2)}) collective-permute-start(bf16[128,512]{1,0:T(8,128)(2,1)S(1)} %get-tuple-element.88.refs_0_), channel_id=1, source_target_pairs={{0,16},{1,17},{2,18},{3,19},{4,20},{5,21},{6,22},{7,23},{8,24},{9,... | collective-permute-start | bytes 393224 | tf_op jit(solution)/shard_map/ppermute | solution.py:341
  91.9 11.0 %collective-permute-start.29 = (bf16[128,512]{1,0:T(8,128)(2,1)S(1)}, bf16[128,512]{1,0:T(8,128)(2,1)S(1)}, u32[]{:S(2)}, u32[]{:S(2)}) collective-permute-start(bf16[128,512]{1,0:T(8,128)(2,1)S(1)} %get-tuple-element.88.refs_0_), channel_id=1, source_target_pairs={{0,24},{1,25},{2,26},{3,27},{4,28},{5,29},{6,30},{7,31},{8,16},{9,... | collective-permute-start | bytes 393224 | tf_op jit(solution)/shard_map/ppermute | solution.py:341
  103.7 1.3 %collective-permute-start.30 = (f32[1,128,128]{2,1,0:T(8,128)S(1)}, f32[1,128,128]{2,1,0:T(8,128)S(1)}, u32[]{:S(2)}, u32[]{:S(2)}) collective-permute-start(f32[1,128,128]{2,1,0:T(8,128)S(1)} %get-tuple-element.90), channel_id=1, source_target_pairs={{0,1},{1,0},{2,3},{3,2},{4,5},{5,4},{6,7},{7,6},{8,9},{9,8},{10,11... | collective-permute-start | bytes 196616 | tf_op jit(solution)/shard_map/ppermute | solution.py:341
  105.1 4.0 %collective-permute-start.31 = (bf16[1,128,128]{2,1,0:T(8,128)(2,1)S(1)}, bf16[1,128,128]{2,1,0:T(8,128)(2,1)S(1)}, u32[]{:S(2)}, u32[]{:S(2)}) collective-permute-start(bf16[1,128,128]{2,1,0:T(8,128)(2,1)S(1)} %add_convert_fusion.3), channel_id=1, source_target_pairs={{0,2},{1,3},{2,0},{3,1},{4,6},{5,7},{6,4},{7,5},{8,10},{9,11},{10,... | collective-permute-start | bytes 98312 | tf_op jit(solution)/shard_map/ppermute | solution.py:341
  105.7 3.9 %collective-permute-start.32 = (bf16[1,128,128]{2,1,0:T(8,128)(2,1)S(1)}, bf16[1,128,128]{2,1,0:T(8,128)(2,1)S(1)}, u32[]{:S(2)}, u32[]{:S(2)}) collective-permute-start(bf16[1,128,128]{2,1,0:T(8,128)(2,1)S(1)} %add_convert_fusion.3), channel_id=1, source_target_pairs={{0,4},{1,5},{2,6},{3,7},{4,0},{5,1},{6,2},{7,3},{8,12},{9,13},{10,... | collective-permute-start | bytes 98312 | tf_op jit(solution)/shard_map/ppermute | solution.py:341
  106.8 4.8 %collective-permute-start.33 = (bf16[1,128,128]{2,1,0:T(8,128)(2,1)S(1)}, bf16[1,128,128]{2,1,0:T(8,128)(2,1)S(1)}, u32[]{:S(2)}, u32[]{:S(2)}) collective-permute-start(bf16[1,128,128]{2,1,0:T(8,128)(2,1)S(1)} %add_convert_fusion.3), channel_id=1, source_target_pairs={{0,6},{1,7},{2,4},{3,5},{4,2},{5,3},{6,0},{7,1},{8,14},{9,15},{10,... | collective-permute-start | bytes 98312 | tf_op jit(solution)/shard_map/ppermute | solution.py:341
  111.7 1.3 %collective-permute-start.34 = (f32[1,128,128]{2,1,0:T(8,128)S(1)}, f32[1,128,128]{2,1,0:T(8,128)S(1)}, u32[]{:S(2)}, u32[]{:S(2)}) collective-permute-start(f32[1,128,128]{2,1,0:T(8,128)S(1)} %add_add_fusion.2.mine_ref), channel_id=1, source_target_pairs={{0,1},{1,0},{2,3},{3,2},{4,5},{5,4},{6,7},{7,6},{8,9},{9,8},{10,11... | collective-permute-start | bytes 196616 | tf_op jit(solution)/shard_map/ppermute | solution.py:341
  113.8 3.7 %collective-permute-start.35 = (bf16[32,2048]{1,0:T(8,128)(2,1)S(1)}, bf16[32,2048]{1,0:T(8,128)(2,1)S(1)}, u32[]{:S(2)}, u32[]{:S(2)}) collective-permute-start(bf16[32,2048]{1,0:T(8,128)(2,1)S(1)} %get-tuple-element.92), channel_id=1, source_target_pairs={{0,1},{1,0},{2,3},{3,2},{4,5},{5,4},{6,7},{7,6},{8,9},{9,8},{10,11... | collective-permute-start | bytes 393224 | tf_op jit(solution)/shard_map/ppermute | solution.py:341
  114.0 6.3 %collective-permute-start.36 = (bf16[32,2048]{1,0:T(8,128)(2,1)S(1)}, bf16[32,2048]{1,0:T(8,128)(2,1)S(1)}, u32[]{:S(2)}, u32[]{:S(2)}) collective-permute-start(bf16[32,2048]{1,0:T(8,128)(2,1)S(1)} %get-tuple-element.93), channel_id=1, source_target_pairs={{0,2},{1,3},{2,0},{3,1},{4,6},{5,7},{6,4},{7,5},{8,10},{9,11},{10,... | collective-permute-start | bytes 393224 | tf_op jit(solution)/shard_map/ppermute | solution.py:341
  115.1 6.8 %collective-permute-start.37 = (bf16[32,2048]{1,0:T(8,128)(2,1)S(1)}, bf16[32,2048]{1,0:T(8,128)(2,1)S(1)}, u32[]{:S(2)}, u32[]{:S(2)}) collective-permute-start(bf16[32,2048]{1,0:T(8,128)(2,1)S(1)} %get-tuple-element.94), channel_id=1, source_target_pairs={{0,3},{1,2},{2,1},{3,0},{4,7},{5,6},{6,5},{7,4},{8,11},{9,10},{10,... | collective-permute-start | bytes 393224 | tf_op jit(solution)/shard_map/ppermute | solution.py:341
  115.7 6.3 %collective-permute-start.38 = (bf16[32,2048]{1,0:T(8,128)(2,1)S(1)}, bf16[32,2048]{1,0:T(8,128)(2,1)S(1)}, u32[]{:S(2)}, u32[]{:S(2)}) collective-permute-start(bf16[32,2048]{1,0:T(8,128)(2,1)S(1)} %get-tuple-element.95), channel_id=1, source_target_pairs={{0,4},{1,5},{2,6},{3,7},{4,0},{5,1},{6,2},{7,3},{8,12},{9,13},{10,... | collective-permute-start | bytes 393224 | tf_op jit(solution)/shard_map/ppermute | solution.py:341
  116.6 12.9 %collective-permute-start.39 = (bf16[32,2048]{1,0:T(8,128)(2,1)S(1)}, bf16[32,2048]{1,0:T(8,128)(2,1)S(1)}, u32[]{:S(2)}, u32[]{:S(2)}) collective-permute-start(bf16[32,2048]{1,0:T(8,128)(2,1)S(1)} %get-tuple-element.96), channel_id=1, source_target_pairs={{0,5},{1,4},{2,7},{3,6},{4,1},{5,0},{6,3},{7,2},{8,13},{9,12},{10,... | collective-permute-start | bytes 393224 | tf_op jit(solution)/shard_map/ppermute | solution.py:341
  117.5 12.0 %collective-permute-start.40 = (bf16[32,2048]{1,0:T(8,128)(2,1)S(1)}, bf16[32,2048]{1,0:T(8,128)(2,1)S(1)}, u32[]{:S(2)}, u32[]{:S(2)}) collective-permute-start(bf16[32,2048]{1,0:T(8,128)(2,1)S(1)} %get-tuple-element.97), channel_id=1, source_target_pairs={{0,6},{1,7},{2,4},{3,5},{4,2},{5,3},{6,0},{7,1},{8,14},{9,15},{10,... | collective-permute-start | bytes 393224 | tf_op jit(solution)/shard_map/ppermute | solution.py:341
  120.3 9.2 %collective-permute-start.41 = (bf16[32,2048]{1,0:T(8,128)(2,1)S(1)}, bf16[32,2048]{1,0:T(8,128)(2,1)S(1)}, u32[]{:S(2)}, u32[]{:S(2)}) collective-permute-start(bf16[32,2048]{1,0:T(8,128)(2,1)S(1)} %get-tuple-element.98), channel_id=1, source_target_pairs={{0,7},{1,6},{2,5},{3,4},{4,3},{5,2},{6,1},{7,0},{8,15},{9,14},{10,... | collective-permute-start | bytes 393224 | tf_op jit(solution)/shard_map/ppermute | solution.py:341

commit v2 on v0

--- a/solution.py
+++ b/solution.py
@@ -12,7 +12,9 @@
 PLANES = 2**LEVELS // PLANE
 TILE = 8
 PANEL = 64
-PIVOT_SHARE = 2e-5
+PLANE_ORDER = (0, 6, 7, 2, 4, 3, 5, 1)
+TREE_ORDER = (0, 3, 2, 1)
+PIVOT_SHARE = 2e-4
 
 precise = lax.Precision.HIGHEST
 f32 = jnp.float32
@@ -29,6 +31,20 @@
 
 def dot_low(a, b, ca, cb):
     return dot(a, b, ca, cb, None)
+
+
+def halves(x):
+    high = x.astype(bf16)
+    return high, (x - high.astype(f32)).astype(bf16)
+
+
+def dot_split(a, b, ca, cb):
+    ah, al = (a, None) if a.dtype == bf16 else halves(a)
+    bh, bl = (b, None) if b.dtype == bf16 else halves(b)
+    total = dot_low(ah, bh, ca, cb)
+    if bl is not None:
+        total = total + dot_low(ah, bl, ca, cb)
+    return total if al is None else total + dot_low(al, bh, ca, cb)
 
 
 def lanes_of(x, k):
@@ -121,7 +137,7 @@
         gram_ref[...] = gram
         imaged = gram[:, :RANK]
         for step in range(SWEEPS - 1):
-            imaged = dot(gram, imaged, 1, 0)
+            imaged = dot_split(gram, imaged, 1, 0)
         imaged_ref[...] = imaged
 
     def attempt(step):
@@ -179,16 +195,16 @@
 
 def parts_kernel(pos_ref, x_ref, *refs):
     width = refs[0].shape[1]
-    for m in range(PLANE):
-        refs[m][...] = x_ref[:, chunk(member(pos_ref), m, width)]
+    for ref, m in zip(refs, PLANE_ORDER):
+        ref[...] = x_ref[:, chunk(member(pos_ref), m, width)]
 
 
 def gram_kernel(pos_ref, *refs):
     parts, (rows_ref, mine_ref, theirs_ref) = refs[:PLANE], refs[PLANE:]
     core, _ = place(pos_ref)
     height = parts[0].shape[0]
-    for m in range(PLANE):
-        rows_ref[chunk(member(pos_ref), m, height), :] = parts[m][...]
+    for ref, m in zip(parts, PLANE_ORDER):
+        rows_ref[chunk(member(pos_ref), m, height), :] = ref[...]
     rows = rows_ref[...]
     gram = dot_low(rows, rows, 1, 1)
     split([gram[:RANK, :RANK], gram[RANK:, :RANK], gram[RANK:, RANK:]], core, mine_ref, theirs_ref)
@@ -208,13 +224,12 @@
     (low,) = leading_spaces([plane_gram(mine_ref, other_ref, core)], [work])
     low_ref[...] = low
     width = nodes[0].shape[1]
-    for m in range(PLANES):
-        nodes[m][...] = dot_low(low, rows_ref[:, chunk(z, m, width)], 0, 0).astype(bf16)
+    for ref, m in zip(nodes, TREE_ORDER):
+        ref[...] = dot_low(low, rows_ref[:, chunk(z, m, width)], 0, 0).astype(bf16)
 
 
 def reduced(gram, low):
-    wide = low.astype(f32)
-    return dot(wide, dot(gram, wide, 1, 0), 0, 0)
+    return dot_split(low, dot_split(gram, low, 1, 0), 0, 0)
 
 
 def diag_kernel(pos_ref, mine_ref, other_ref, low_ref, diag_ref):
@@ -230,8 +245,8 @@
 def cross_kernel(pos_ref, *refs):
     nodes, (mine_ref, theirs_ref, all_ref) = refs[:PLANES], refs[PLANES:]
     core, z = place(pos_ref)
-    for m in range(PLANES):
-        all_ref[z ^ m] = nodes[m][...]
+    for ref, m in zip(nodes, TREE_ORDER):
+        all_ref[z ^ m] = ref[...]
     split([dot_low(all_ref[j], all_ref[i], 1, 1) for i, j in PAIRS], core, mine_ref, theirs_ref)
 
 
@@ -239,8 +254,8 @@
     nodes, (top_ref, gram_ref, low_ref), refs = refs[:PLANES], refs[PLANES : PLANES + 3], refs[PLANES + 3 :]
     all_ref, diag_ref, work = refs[0], refs[1], [refs[2:5], refs[5:8]]
     core, z = place(pos_ref)
-    for m in range(PLANES):
-        all_ref[z ^ m] = nodes[m][...]
+    for ref, m in zip(nodes, TREE_ORDER):
+        all_ref[z ^ m] = ref[...]
         diag_ref[z ^ m] = joined(mine_ref, other_ref, core, len(PAIRS) + m)
     cross = {pair: joined(mine_ref, other_ref, core, b) for b, pair in enumerate(PAIRS)}
     gram_a = square(diag_ref[0], cross[0, 1], diag_ref[1])
@@ -255,7 +270,7 @@
     )
     gram = square(
         reduced(gram_a, low_a),
-        dot(low_b.astype(f32), dot(between, low_a.astype(f32), 1, 0), 0, 0),
+        dot_split(low_b, dot_split(between, low_a, 1, 0), 0, 0),
         reduced(gram_b, low_b),
     )
     gram_ref[...] = gram
@@ -275,8 +290,8 @@
     core, z = place(pos_ref)
     width = tops[0].shape[1]
     total = None
-    for m in range(PLANES):
-        part = dot_low(rows_ref[:, chunk(z, m, width)], tops[m][...], 1, 1)
+    for m, ref in enumerate(tops):
+        part = dot_low(rows_ref[:, chunk(z, m, width)], ref[...], 1, 1)
         total = part if total is None else total + part
     split([dot(total, factor_ref[...], 1, 1)], core, mine_ref, theirs_ref)
 
@@ -286,19 +301,19 @@
     core, z = place(pos_ref)
     height, width = outs[0].shape[0], tops[0].shape[1]
     solved_ref[...] = dot(joined(mine_ref, other_ref, core, 0), factor_ref[...], 1, 0)
-    solved = [solved_ref[chunk(member(pos_ref), m, height), :] for m in range(PLANE)]
+    solved = [solved_ref[chunk(member(pos_ref), m, height), :] for m in PLANE_ORDER]
     solved = jnp.concatenate(solved, 0).astype(bf16)
-    for c in range(PLANES):
-        made = dot_low(solved, tops[c][...], 1, 0).astype(bf16)
-        for m in range(PLANE):
-            outs[m][:, chunk(z, c, width)] = made[m * height : (m + 1) * height, :]
+    for m, ref in enumerate(tops):
+        made = dot_low(solved, ref[...], 1, 0).astype(bf16)
+        for k in range(PLANE):
+            outs[k][:, chunk(z, m, width)] = made[k * height : (k + 1) * height, :]
 
 
 def whole_kernel(pos_ref, *refs):
     parts, out_ref = refs[:PLANE], refs[PLANE]
     width = parts[0].shape[1]
-    for m in range(PLANE):
-        out_ref[:, chunk(member(pos_ref), m, width)] = parts[m][...]
+    for ref, m in zip(parts, PLANE_ORDER):
+        out_ref[:, chunk(member(pos_ref), m, width)] = ref[...]
 
 
 smem = pl.BlockSpec(memory_space=pltpu.SMEM)
@@ -327,15 +342,15 @@
     def swap(x, apart):
         return lax.ppermute(x, "cols", [(i, i ^ apart) for i in range(count)])
 
-    def swap_all(parts, unit):
-        return [parts[0]] + [swap(parts[m], unit * m) for m in range(1, len(parts))]
+    def swap_all(parts, order, unit=1):
+        return [x if m == 0 else swap(x, unit * m) for x, m in zip(parts, order)]
 
     def sum4(parts):
         parts = [p.astype(f32) for p in parts]
         return (parts[0] + parts[1]) + (parts[2] + parts[3])
 
     def plane_sum(mine, theirs):
-        return sum4(swap_all([(mine + swap(theirs, 1)).astype(bf16)] * 4, 2))
+        return sum4(swap_all([(mine + swap(theirs, 1)).astype(bf16)] * 4, range(4), 2))
 
     block, total = mortality.shape
     height, width = block * PLANE, total // PLANE
@@ -343,7 +358,7 @@
     half = RANK // 2
 
     parts = kernel(parts_kernel, [((block, width), bf16)] * PLANE, pos, mortality)
-    parts = swap_all(parts, 1)
+    parts = swap_all(parts, PLANE_ORDER)
     rows, mine, theirs = kernel(
         gram_kernel, [((height, width), bf16)] + [((3, half, RANK), f32)] * 2, pos, *parts
     )
@@ -355,7 +370,7 @@
         pos, mine, other, rows,
         scratch=work_shapes,
     )
-    nodes = swap_all(nodes, PLANE)
+    nodes = swap_all(nodes, TREE_ORDER, PLANE)
     (diag,) = kernel(diag_kernel, [((1, half, RANK), bf16)], pos, mine, other, low)
 
     mine, theirs = kernel(
@@ -365,7 +380,7 @@
         scratch=[pltpu.VMEM((PLANES, RANK, part), bf16)],
     )
     mine = plane_sum(mine, theirs)
-    both = swap_all([jnp.concatenate([mine.astype(bf16), diag], 0)] * PLANES, PLANE)
+    both = swap_all([jnp.concatenate([mine.astype(bf16), diag], 0)] * PLANES, range(PLANES), PLANE)
     mine = jnp.concatenate([sum4([x[: len(PAIRS)] for x in both])] + [x[len(PAIRS) :].astype(f32) for x in both], 0)
     top, gram, low = kernel(
         top_kernel,
@@ -373,7 +388,7 @@
         pos, mine, swap(mine, 1), *nodes,
         scratch=[pltpu.VMEM((PLANES, RANK, part), bf16), pltpu.VMEM((PLANES, RANK, RANK), f32)] + work_shapes * 2,
     )
-    tops = swap_all([top] * PLANES, PLANE)
+    tops = swap_all([top] * PLANES, range(PLANES), PLANE)
     (factor,) = kernel(factor_kernel, [((RANK, RANK), f32)], gram, low, scalar=False)
 
     mine, theirs = kernel(coeffs_kernel, [((1, height // 2, RANK), f32)] * 2, pos, rows, factor, *tops)
@@ -384,7 +399,7 @@
         pos, mine, swap(mine, 1), factor, *tops,
         scratch=[pltpu.VMEM((height, RANK), f32)],
     )
-    (result,) = kernel(whole_kernel, [((block, total), bf16)], pos, *swap_all(outs, 1))
+    (result,) = kernel(whole_kernel, [((block, total), bf16)], pos, *swap_all(outs, PLANE_ORDER))
     return result
 
 

time: 130 us -> 124 us (0.954)
  Pallas kernels: 28.9 us -> 25.2 us
    pallas_call x10, Pallas kernels: 28.9 us -> 25.2 us  [kernel(): pl.pallas_call(fn, out_shape=[jax.ShapeDtypeStruct(s, d) for s, d in shap...]
  transfers between devices with their start and end apart: 38 -> 38, of which waited for: 25 -> 31; matrix products, arithmetic and copies ran while one was open for 0% -> 0% of each run, Pallas kernels for 4% -> 3%
where the time goes in v2:
time: 124 us
  waiting for transfers between devices  58.5 us (47%)
  starting transfers between devices  38.9 us (31%)
  Pallas kernels  25.2 us (20%)
    ppermute x38, waiting for transfers between devices, swap(): return lax.ppermute(x, 'cols', [(i, i ^ apart) for i in range(count)])  58.5 us
    ppermute x38, starting transfers between devices, swap(): return lax.ppermute(x, 'cols', [(i, i ^ apart) for i in range(count)])  38.9 us
    pallas_call x10, Pallas kernels, kernel(): pl.pallas_call(fn, out_shape=[jax.ShapeDtypeStruct(s, d) for s, d in shap...  25.2 us
  transfers between devices with their start and end apart: 38, of which 31 were waited for; matrix products, arithmetic and copies ran while one was open for 0% of the time, Pallas kernels for 3%

profile of v2, /device:TPU:0, one launch (start us, length us, event | category | flops | bytes accessed | tf_op | source)
XLA Modules:
  0.0 124.3 jit_solution(13311844454787749571)
XLA Ops:
  0.0 1.2 copy-done
  1.3 4.0 %collective-permute-start = (bf16[32,2048]{1,0:T(8,128)(2,1)S(1)}, bf16[32,2048]{1,0:T(8,128)(2,1)S(1)}, u32[]{:S(2)}, u32[]{:S(2)}) collective-permute-start(bf16[32,2048]{1,0:T(8,128)(2,1)S(1)} %get-tuple-element.37), channel_id=1, source_target_pairs={{0,6},{1,7},{2,4},{3,5},{4,2},{5,3},{6,0},{7,1},{8,14},{9,15},{10,... | collective-permute-start | bytes 393224 | tf_op jit(solution)/shard_map/ppermute | solution.py:343
  5.3 1.1 collective-permute-start.2
  6.4 1.5 %collective-permute-start.3 = (bf16[32,2048]{1,0:T(8,128)(2,1)S(1)}, bf16[32,2048]{1,0:T(8,128)(2,1)S(1)}, u32[]{:S(2)}, u32[]{:S(2)}) collective-permute-start(bf16[32,2048]{1,0:T(8,128)(2,1)S(1)} %get-tuple-element.40), channel_id=1, source_target_pairs={{0,4},{1,5},{2,6},{3,7},{4,0},{5,1},{6,2},{7,3},{8,12},{9,13},{10,... | collective-permute-start | bytes 393224 | tf_op jit(solution)/shard_map/ppermute | solution.py:343
  7.9 0.6 collective-permute-start.4
  8.5 0.7 collective-permute-done.refs_1_
  9.2 2.8 %collective-permute-done.1.refs_2_ = bf16[32,2048]{1,0:T(8,128)(2,1)S(1)} collective-permute-done((bf16[32,2048]{1,0:T(8,128)(2,1)S(1)}, bf16[32,2048]{1,0:T(8,128)(2,1)S(1)}, u32[]{:S(2)}, u32[]{:S(2)}) %collective-permute-start.1) | collective-permute-done | bytes 131104 | tf_op jit(solution)/shard_map/ppermute | solution.py:343
  12.0 3.4 %collective-permute-done.2.refs_3_ = bf16[32,2048]{1,0:T(8,128)(2,1)S(1)} collective-permute-done((bf16[32,2048]{1,0:T(8,128)(2,1)S(1)}, bf16[32,2048]{1,0:T(8,128)(2,1)S(1)}, u32[]{:S(2)}, u32[]{:S(2)}) %collective-permute-start.2) | collective-permute-done | bytes 131104 | tf_op jit(solution)/shard_map/ppermute | solution.py:343
  15.5 1.1 collective-permute-done.4.refs_5_
  16.6 0.7 collective-permute-done.5.refs_6_
  17.3 0.5 gram_kernel.1
  18.0 1.2 collective-permute-done.7
  19.2 2.6 %collective-permute-start.10 = (bf16[3,64,128]{2,1,0:T(8,128)(2,1)S(1)}, bf16[3,64,128]{2,1,0:T(8,128)(2,1)S(1)}, u32[]{:S(2)}, u32[]{:S(2)}) collective-permute-start(bf16[3,64,128]{2,1,0:T(8,128)(2,1)S(1)} %add_convert_fusion.2), channel_id=1, source_target_pairs={{0,6},{1,7},{2,4},{3,5},{4,2},{5,3},{6,0},{7,1},{8,14},{9,15},{10,... | collective-permute-start | bytes 147464 | tf_op jit(solution)/shard_map/ppermute | solution.py:343
  21.8 0.5 collective-permute-start.9
  22.2 0.5 collective-permute-start.8
  22.8 1.5 %collective-permute-done.10 = bf16[3,64,128]{2,1,0:T(8,128)(2,1)S(1)} collective-permute-done((bf16[3,64,128]{2,1,0:T(8,128)(2,1)S(1)}, bf16[3,64,128]{2,1,0:T(8,128)(2,1)S(1)}, u32[]{:S(2)}, u32[]{:S(2)}) %collective-permute-start.10) | collective-permute-done | bytes 49184 | tf_op jit(solution)/shard_map/ppermute | solution.py:343
  24.3 1.6 %collective-permute-done.9 = bf16[3,64,128]{2,1,0:T(8,128)(2,1)S(1)} collective-permute-done((bf16[3,64,128]{2,1,0:T(8,128)(2,1)S(1)}, bf16[3,64,128]{2,1,0:T(8,128)(2,1)S(1)}, u32[]{:S(2)}, u32[]{:S(2)}) %collective-permute-start.9) | collective-permute-done | bytes 49184 | tf_op jit(solution)/shard_map/ppermute | solution.py:343
  25.9 0.5 collective-permute-done.8
  26.4 1.3 %collective-permute-done.11.other_ref = f32[3,64,128]{2,1,0:T(8,128)S(1)} collective-permute-done((f32[3,64,128]{2,1,0:T(8,128)S(1)}, f32[3,64,128]{2,1,0:T(8,128)S(1)}, u32[]{:S(2)}, u32[]{:S(2)}) %collective-permute-start.11) | collective-permute-done | bytes 98336 | tf_op jit(solution)/shard_map/ppermute | solution.py:343
  27.7 4.9 %node_kernel.1 = (bf16[128,512]{1,0:T(8,128)(2,1)S(1)}, bf16[128,512]{1,0:T(8,128)(2,1)S(1)}, bf16[128,512]{1,0:T(8,128)(2,1)S(1)}, bf16[128,512]{1,0:T(8,128)(2,1)S(1)}, bf16[256,128]{1,0:T(8,128)(2,1)S(1)}) custom-call(s32[1]{0:T(128)} %bitcast.pos_ref, f32[3,64,128]{2,1,0:T(8,128)S(1)} %add_add_fusion.mine_ref, ...), custom_call_target="tpu_custom_call" | custom-call | tf_op jit(solution)/shard_map/node_kernel/pallas_call | solution.py:326
  32.7 3.7 %collective-permute-start.12 = (bf16[128,512]{1,0:T(8,128)(2,1)S(1)}, bf16[128,512]{1,0:T(8,128)(2,1)S(1)}, u32[]{:S(2)}, u32[]{:S(2)}) collective-permute-start(bf16[128,512]{1,0:T(8,128)(2,1)S(1)} %get-tuple-element.48), channel_id=1, source_target_pairs={{0,24},{1,25},{2,26},{3,27},{4,28},{5,29},{6,30},{7,31},{8,16},{9,... | collective-permute-start | bytes 393224 | tf_op jit(solution)/shard_map/ppermute | solution.py:343
  36.4 0.8 collective-permute-start.14
  37.1 3.8 %collective-permute-done.12.refs_1_ = bf16[128,512]{1,0:T(8,128)(2,1)S(1)} collective-permute-done((bf16[128,512]{1,0:T(8,128)(2,1)S(1)}, bf16[128,512]{1,0:T(8,128)(2,1)S(1)}, u32[]{:S(2)}, u32[]{:S(2)}) %collective-permute-start.12) | collective-permute-done | bytes 131104 | tf_op jit(solution)/shard_map/ppermute | solution.py:343
  40.9 6.8 %collective-permute-done.13.refs_2_ = bf16[128,512]{1,0:T(8,128)(2,1)S(1)} collective-permute-done((bf16[128,512]{1,0:T(8,128)(2,1)S(1)}, bf16[128,512]{1,0:T(8,128)(2,1)S(1)}, u32[]{:S(2)}, u32[]{:S(2)}) %collective-permute-start.13) | collective-permute-done | bytes 131104 | tf_op jit(solution)/shard_map/ppermute | solution.py:343
  47.8 0.4 cross_kernel.1
  48.3 1.4 %collective-permute-done.15 = f32[6,64,128]{2,1,0:T(8,128)S(1)} collective-permute-done((f32[6,64,128]{2,1,0:T(8,128)S(1)}, f32[6,64,128]{2,1,0:T(8,128)S(1)}, u32[]{:S(2)}, u32[]{:S(2)}) %collective-permute-start.15) | collective-permute-done | bytes 196640 | tf_op jit(solution)/shard_map/ppermute | solution.py:343
  49.7 1.6 %collective-permute-start.18 = (bf16[6,64,128]{2,1,0:T(8,128)(2,1)S(1)}, bf16[6,64,128]{2,1,0:T(8,128)(2,1)S(1)}, u32[]{:S(2)}, u32[]{:S(2)}) collective-permute-start(bf16[6,64,128]{2,1,0:T(8,128)(2,1)S(1)} %add_convert_fusion.1), channel_id=1, source_target_pairs={{0,6},{1,7},{2,4},{3,5},{4,2},{5,3},{6,0},{7,1},{8,14},{9,15},{10,... | collective-permute-start | bytes 294920 | tf_op jit(solution)/shard_map/ppermute | solution.py:343
  51.3 0.5 collective-permute-start.17
  51.8 1.5 %collective-permute-start.16 = (bf16[6,64,128]{2,1,0:T(8,128)(2,1)S(1)}, bf16[6,64,128]{2,1,0:T(8,128)(2,1)S(1)}, u32[]{:S(2)}, u32[]{:S(2)}) collective-permute-start(bf16[6,64,128]{2,1,0:T(8,128)(2,1)S(1)} %add_convert_fusion.1), channel_id=1, source_target_pairs={{0,2},{1,3},{2,0},{3,1},{4,6},{5,7},{6,4},{7,5},{8,10},{9,11},{10,... | collective-permute-start | bytes 294920 | tf_op jit(solution)/shard_map/ppermute | solution.py:343
  53.3 0.4 diag_kernel.1
  53.7 2.4 %collective-permute-done.18 = bf16[6,64,128]{2,1,0:T(8,128)(2,1)S(1)} collective-permute-done((bf16[6,64,128]{2,1,0:T(8,128)(2,1)S(1)}, bf16[6,64,128]{2,1,0:T(8,128)(2,1)S(1)}, u32[]{:S(2)}, u32[]{:S(2)}) %collective-permute-start.18) | collective-permute-done | bytes 98336 | tf_op jit(solution)/shard_map/ppermute | solution.py:343
  56.2 1.5 %collective-permute-done.17 = bf16[6,64,128]{2,1,0:T(8,128)(2,1)S(1)} collective-permute-done((bf16[6,64,128]{2,1,0:T(8,128)(2,1)S(1)}, bf16[6,64,128]{2,1,0:T(8,128)(2,1)S(1)}, u32[]{:S(2)}, u32[]{:S(2)}) %collective-permute-start.17) | collective-permute-done | bytes 98336 | tf_op jit(solution)/shard_map/ppermute | solution.py:343
  57.8 2.5 %collective-permute-start.21 = (bf16[7,64,128]{2,1,0:T(8,128)(2,1)S(1)}, bf16[7,64,128]{2,1,0:T(8,128)(2,1)S(1)}, u32[]{:S(2)}, u32[]{:S(2)}) collective-permute-start(bf16[7,64,128]{2,1,0:T(8,128)(2,1)S(1)} %pad_maximum_fusion), channel_id=1, source_target_pairs={{0,24},{1,25},{2,26},{3,27},{4,28},{5,29},{6,30},{7,31},{8,16},{9,... | collective-permute-start | bytes 344072 | tf_op jit(solution)/shard_map/ppermute | solution.py:343
  60.4 1.9 %collective-permute-start.19 = (bf16[7,64,128]{2,1,0:T(8,128)(2,1)S(1)}, bf16[7,64,128]{2,1,0:T(8,128)(2,1)S(1)}, u32[]{:S(2)}, u32[]{:S(2)}) collective-permute-start(bf16[7,64,128]{2,1,0:T(8,128)(2,1)S(1)} %pad_maximum_fusion), channel_id=1, source_target_pairs={{0,8},{1,9},{2,10},{3,11},{4,12},{5,13},{6,14},{7,15},{8,0},{9,1},... | collective-permute-start | bytes 344072 | tf_op jit(solution)/shard_map/ppermute | solution.py:343
  62.3 3.5 %collective-permute-done.21 = bf16[7,64,128]{2,1,0:T(8,128)(2,1)S(1)} collective-permute-done((bf16[7,64,128]{2,1,0:T(8,128)(2,1)S(1)}, bf16[7,64,128]{2,1,0:T(8,128)(2,1)S(1)}, u32[]{:S(2)}, u32[]{:S(2)}) %collective-permute-start.21) | collective-permute-done | bytes 114720 | tf_op jit(solution)/shard_map/ppermute | solution.py:343
  65.8 3.7 %collective-permute-done.20 = bf16[7,64,128]{2,1,0:T(8,128)(2,1)S(1)} collective-permute-done((bf16[7,64,128]{2,1,0:T(8,128)(2,1)S(1)}, bf16[7,64,128]{2,1,0:T(8,128)(2,1)S(1)}, u32[]{:S(2)}, u32[]{:S(2)}) %collective-permute-start.20) | collective-permute-done | bytes 114720 | tf_op jit(solution)/shard_map/ppermute | solution.py:343
  69.8 1.6 %collective-permute-done.22.other_ref = f32[10,64,128]{2,1,0:T(8,128)S(1)} collective-permute-done((f32[10,64,128]{2,1,0:T(8,128)S(1)}, f32[10,64,128]{2,1,0:T(8,128)S(1)}, u32[]{:S(2)}, u32[]{:S(2)}) %collective-permute-start.22) | collective-permute-done | bytes 327712 | tf_op jit(solution)/shard_map/ppermute | solution.py:343
  71.4 12.7 %top_kernel.1 = (bf16[128,512]{1,0:T(8,128)(2,1)S(1)}, f32[256,256]{1,0:T(8,128)S(1)}, bf16[256,128]{1,0:T(8,128)(2,1)S(1)}) custom-call(s32[1]{0:T(128)} %bitcast.pos_ref, f32[10,64,128]{2,1,0:T(8,128)S(1)} %convert_dynamic-update-slice_fusion.mine_ref, f32[10,64,128]{2,1,0:T(8,128)S(1)} %collective-permute-done.22.other_ref, ...), custom_call_target="tpu_custom_call" | custom-call | tf_op jit(solution)/shard_map/top_kernel/pallas_call | solution.py:326
  84.0 2.5 %collective-permute-start.25 = (bf16[128,512]{1,0:T(8,128)(2,1)S(1)}, bf16[128,512]{1,0:T(8,128)(2,1)S(1)}, u32[]{:S(2)}, u32[]{:S(2)}) collective-permute-start(bf16[128,512]{1,0:T(8,128)(2,1)S(1)} %get-tuple-element.56.refs_0_), channel_id=1, source_target_pairs={{0,24},{1,25},{2,26},{3,27},{4,28},{5,29},{6,30},{7,31},{8,16},{9,... | collective-permute-start | bytes 393224 | tf_op jit(solution)/shard_map/ppermute | solution.py:343
  86.6 1.9 %collective-permute-start.23 = (bf16[128,512]{1,0:T(8,128)(2,1)S(1)}, bf16[128,512]{1,0:T(8,128)(2,1)S(1)}, u32[]{:S(2)}, u32[]{:S(2)}) collective-permute-start(bf16[128,512]{1,0:T(8,128)(2,1)S(1)} %get-tuple-element.56.refs_0_), channel_id=1, source_target_pairs={{0,8},{1,9},{2,10},{3,11},{4,12},{5,13},{6,14},{7,15},{8,0},{9,1},... | collective-permute-start | bytes 393224 | tf_op jit(solution)/shard_map/ppermute | solution.py:343
  88.5 3.5 %factor_kernel.1.factor_ref = f32[128,128]{1,0:T(8,128)S(1)} custom-call(f32[256,256]{1,0:T(8,128)S(1)} %get-tuple-element.54.gram_ref, bf16[256,128]{1,0:T(8,128)(2,1)S(1)} %get-tuple-element.55.low_ref), custom_call_target="tpu_custom_call" | custom-call | tf_op jit(solution)/shard_map/factor_kernel/pallas_call | solution.py:326
  92.0 0.3 collective-permute-done.25.refs_3_
  92.4 5.9 %collective-permute-done.24.refs_2_ = bf16[128,512]{1,0:T(8,128)(2,1)S(1)} collective-permute-done((bf16[128,512]{1,0:T(8,128)(2,1)S(1)}, bf16[128,512]{1,0:T(8,128)(2,1)S(1)}, u32[]{:S(2)}, u32[]{:S(2)}) %collective-permute-start.24) | collective-permute-done | bytes 131104 | tf_op jit(solution)/shard_map/ppermute | solution.py:343
  98.2 0.8 coeffs_kernel.1
  99.1 1.2 collective-permute-done.26
  100.4 1.6 %collective-permute-start.29 = (bf16[1,128,128]{2,1,0:T(8,128)(2,1)S(1)}, bf16[1,128,128]{2,1,0:T(8,128)(2,1)S(1)}, u32[]{:S(2)}, u32[]{:S(2)}) collective-permute-start(bf16[1,128,128]{2,1,0:T(8,128)(2,1)S(1)} %add_convert_fusion.3), channel_id=1, source_target_pairs={{0,6},{1,7},{2,4},{3,5},{4,2},{5,3},{6,0},{7,1},{8,14},{9,15},{10,... | collective-permute-start | bytes 98312 | tf_op jit(solution)/shard_map/ppermute | solution.py:343
  102.0 0.3 collective-permute-start.28
  102.3 1.6 %collective-permute-start.27 = (bf16[1,128,128]{2,1,0:T(8,128)(2,1)S(1)}, bf16[1,128,128]{2,1,0:T(8,128)(2,1)S(1)}, u32[]{:S(2)}, u32[]{:S(2)}) collective-permute-start(bf16[1,128,128]{2,1,0:T(8,128)(2,1)S(1)} %add_convert_fusion.3), channel_id=1, source_target_pairs={{0,2},{1,3},{2,0},{3,1},{4,6},{5,7},{6,4},{7,5},{8,10},{9,11},{10,... | collective-permute-start | bytes 98312 | tf_op jit(solution)/shard_map/ppermute | solution.py:343
  103.9 1.3 %collective-permute-done.29 = bf16[1,128,128]{2,1,0:T(8,128)(2,1)S(1)} collective-permute-done((bf16[1,128,128]{2,1,0:T(8,128)(2,1)S(1)}, bf16[1,128,128]{2,1,0:T(8,128)(2,1)S(1)}, u32[]{:S(2)}, u32[]{:S(2)}) %collective-permute-start.29) | collective-permute-done | bytes 32800 | tf_op jit(solution)/shard_map/ppermute | solution.py:343
  105.3 0.6 collective-permute-done.28
  105.9 0.3 collective-permute-done.27
  106.3 1.2 collective-permute-done.30.other_ref
  107.6 0.8 project_kernel.1
  108.4 1.2 collective-permute-start.31
  109.5 1.3 %collective-permute-start.32 = (bf16[32,2048]{1,0:T(8,128)(2,1)S(1)}, bf16[32,2048]{1,0:T(8,128)(2,1)S(1)}, u32[]{:S(2)}, u32[]{:S(2)}) collective-permute-start(bf16[32,2048]{1,0:T(8,128)(2,1)S(1)} %get-tuple-element.61), channel_id=1, source_target_pairs={{0,7},{1,6},{2,5},{3,4},{4,3},{5,2},{6,1},{7,0},{8,15},{9,14},{10,... | collective-permute-start | bytes 393224 | tf_op jit(solution)/shard_map/ppermute | solution.py:343
  110.8 1.6 %collective-permute-start.33 = (bf16[32,2048]{1,0:T(8,128)(2,1)S(1)}, bf16[32,2048]{1,0:T(8,128)(2,1)S(1)}, u32[]{:S(2)}, u32[]{:S(2)}) collective-permute-start(bf16[32,2048]{1,0:T(8,128)(2,1)S(1)} %get-tuple-element.62), channel_id=1, source_target_pairs={{0,2},{1,3},{2,0},{3,1},{4,6},{5,7},{6,4},{7,5},{8,10},{9,11},{10,... | collective-permute-start | bytes 393224 | tf_op jit(solution)/shard_map/ppermute | solution.py:343
  112.5 1.7 %collective-permute-start.35 = (bf16[32,2048]{1,0:T(8,128)(2,1)S(1)}, bf16[32,2048]{1,0:T(8,128)(2,1)S(1)}, u32[]{:S(2)}, u32[]{:S(2)}) collective-permute-start(bf16[32,2048]{1,0:T(8,128)(2,1)S(1)} %get-tuple-element.64), channel_id=1, source_target_pairs={{0,3},{1,2},{2,1},{3,0},{4,7},{5,6},{6,5},{7,4},{8,11},{9,10},{10,... | collective-permute-start | bytes 393224 | tf_op jit(solution)/shard_map/ppermute | solution.py:343
  114.2 1.5 %collective-permute-done.31.refs_1_ = bf16[32,2048]{1,0:T(8,128)(2,1)S(1)} collective-permute-done((bf16[32,2048]{1,0:T(8,128)(2,1)S(1)}, bf16[32,2048]{1,0:T(8,128)(2,1)S(1)}, u32[]{:S(2)}, u32[]{:S(2)}) %collective-permute-start.31) | collective-permute-done | bytes 131104 | tf_op jit(solution)/shard_map/ppermute | solution.py:343
  115.7 1.3 %collective-permute-done.32.refs_2_ = bf16[32,2048]{1,0:T(8,128)(2,1)S(1)} collective-permute-done((bf16[32,2048]{1,0:T(8,128)(2,1)S(1)}, bf16[32,2048]{1,0:T(8,128)(2,1)S(1)}, u32[]{:S(2)}, u32[]{:S(2)}) %collective-permute-start.32) | collective-permute-done | bytes 131104 | tf_op jit(solution)/shard_map/ppermute | solution.py:343
  117.0 1.3 %collective-permute-start.37 = (bf16[32,2048]{1,0:T(8,128)(2,1)S(1)}, bf16[32,2048]{1,0:T(8,128)(2,1)S(1)}, u32[]{:S(2)}, u32[]{:S(2)}) collective-permute-start(bf16[32,2048]{1,0:T(8,128)(2,1)S(1)} %get-tuple-element.66), channel_id=1, source_target_pairs={{0,1},{1,0},{2,3},{3,2},{4,5},{5,4},{6,7},{7,6},{8,9},{9,8},{10,11... | collective-permute-start | bytes 393224 | tf_op jit(solution)/shard_map/ppermute | solution.py:343
  118.3 3.3 %collective-permute-done.33.refs_3_ = bf16[32,2048]{1,0:T(8,128)(2,1)S(1)} collective-permute-done((bf16[32,2048]{1,0:T(8,128)(2,1)S(1)}, bf16[32,2048]{1,0:T(8,128)(2,1)S(1)}, u32[]{:S(2)}, u32[]{:S(2)}) %collective-permute-start.33) | collective-permute-done | bytes 131104 | tf_op jit(solution)/shard_map/ppermute | solution.py:343
  121.6 1.2 collective-permute-done.35.refs_5_
  122.8 0.5 collective-permute-done.36.refs_6_
  123.2 1.0 whole_kernel.1
  (36 shorter events, 1.1 us)
Async XLA Ops:
  0.0 1.2 copy-start
  1.3 7.9 %collective-permute-start = (bf16[32,2048]{1,0:T(8,128)(2,1)S(1)}, bf16[32,2048]{1,0:T(8,128)(2,1)S(1)}, u32[]{:S(2)}, u32[]{:S(2)}) collective-permute-start(bf16[32,2048]{1,0:T(8,128)(2,1)S(1)} %get-tuple-element.37), channel_id=1, source_target_pairs={{0,6},{1,7},{2,4},{3,5},{4,2},{5,3},{6,0},{7,1},{8,14},{9,15},{10,... | collective-permute-start | bytes 393224 | tf_op jit(solution)/shard_map/ppermute | solution.py:343
  5.3 6.8 %collective-permute-start.1 = (bf16[32,2048]{1,0:T(8,128)(2,1)S(1)}, bf16[32,2048]{1,0:T(8,128)(2,1)S(1)}, u32[]{:S(2)}, u32[]{:S(2)}) collective-permute-start(bf16[32,2048]{1,0:T(8,128)(2,1)S(1)} %get-tuple-element.38), channel_id=1, source_target_pairs={{0,7},{1,6},{2,5},{3,4},{4,3},{5,2},{6,1},{7,0},{8,15},{9,14},{10,... | collective-permute-start | bytes 393224 | tf_op jit(solution)/shard_map/ppermute | solution.py:343
  5.3 10.2 %collective-permute-start.2 = (bf16[32,2048]{1,0:T(8,128)(2,1)S(1)}, bf16[32,2048]{1,0:T(8,128)(2,1)S(1)}, u32[]{:S(2)}, u32[]{:S(2)}) collective-permute-start(bf16[32,2048]{1,0:T(8,128)(2,1)S(1)} %get-tuple-element.39), channel_id=1, source_target_pairs={{0,2},{1,3},{2,0},{3,1},{4,6},{5,7},{6,4},{7,5},{8,10},{9,11},{10,... | collective-permute-start | bytes 393224 | tf_op jit(solution)/shard_map/ppermute | solution.py:343
  6.4 9.1 %collective-permute-start.3 = (bf16[32,2048]{1,0:T(8,128)(2,1)S(1)}, bf16[32,2048]{1,0:T(8,128)(2,1)S(1)}, u32[]{:S(2)}, u32[]{:S(2)}) collective-permute-start(bf16[32,2048]{1,0:T(8,128)(2,1)S(1)} %get-tuple-element.40), channel_id=1, source_target_pairs={{0,4},{1,5},{2,6},{3,7},{4,0},{5,1},{6,2},{7,3},{8,12},{9,13},{10,... | collective-permute-start | bytes 393224 | tf_op jit(solution)/shard_map/ppermute | solution.py:343
  7.9 8.7 %collective-permute-start.4 = (bf16[32,2048]{1,0:T(8,128)(2,1)S(1)}, bf16[32,2048]{1,0:T(8,128)(2,1)S(1)}, u32[]{:S(2)}, u32[]{:S(2)}) collective-permute-start(bf16[32,2048]{1,0:T(8,128)(2,1)S(1)} %get-tuple-element.41), channel_id=1, source_target_pairs={{0,3},{1,2},{2,1},{3,0},{4,7},{5,6},{6,5},{7,4},{8,11},{9,10},{10,... | collective-permute-start | bytes 393224 | tf_op jit(solution)/shard_map/ppermute | solution.py:343
  9.2 8.1 %collective-permute-start.5 = (bf16[32,2048]{1,0:T(8,128)(2,1)S(1)}, bf16[32,2048]{1,0:T(8,128)(2,1)S(1)}, u32[]{:S(2)}, u32[]{:S(2)}) collective-permute-start(bf16[32,2048]{1,0:T(8,128)(2,1)S(1)} %get-tuple-element.42), channel_id=1, source_target_pairs={{0,5},{1,4},{2,7},{3,6},{4,1},{5,0},{6,3},{7,2},{8,13},{9,12},{10,... | collective-permute-start | bytes 393224 | tf_op jit(solution)/shard_map/ppermute | solution.py:343
  12.0 5.3 %collective-permute-start.6 = (bf16[32,2048]{1,0:T(8,128)(2,1)S(1)}, bf16[32,2048]{1,0:T(8,128)(2,1)S(1)}, u32[]{:S(2)}, u32[]{:S(2)}) collective-permute-start(bf16[32,2048]{1,0:T(8,128)(2,1)S(1)} %get-tuple-element.43), channel_id=1, source_target_pairs={{0,1},{1,0},{2,3},{3,2},{4,5},{5,4},{6,7},{7,6},{8,9},{9,8},{10,11... | collective-permute-start | bytes 393224 | tf_op jit(solution)/shard_map/ppermute | solution.py:343
  17.8 1.4 %collective-permute-start.7 = (f32[3,64,128]{2,1,0:T(8,128)S(1)}, f32[3,64,128]{2,1,0:T(8,128)S(1)}, u32[]{:S(2)}, u32[]{:S(2)}) collective-permute-start(f32[3,64,128]{2,1,0:T(8,128)S(1)} %get-tuple-element.46), channel_id=1, source_target_pairs={{0,1},{1,0},{2,3},{3,2},{4,5},{5,4},{6,7},{7,6},{8,9},{9,8},{10,11... | collective-permute-start | bytes 294920 | tf_op jit(solution)/shard_map/ppermute | solution.py:343
  19.2 5.1 %collective-permute-start.10 = (bf16[3,64,128]{2,1,0:T(8,128)(2,1)S(1)}, bf16[3,64,128]{2,1,0:T(8,128)(2,1)S(1)}, u32[]{:S(2)}, u32[]{:S(2)}) collective-permute-start(bf16[3,64,128]{2,1,0:T(8,128)(2,1)S(1)} %add_convert_fusion.2), channel_id=1, source_target_pairs={{0,6},{1,7},{2,4},{3,5},{4,2},{5,3},{6,0},{7,1},{8,14},{9,15},{10,... | collective-permute-start | bytes 147464 | tf_op jit(solution)/shard_map/ppermute | solution.py:343
  21.8 4.1 %collective-permute-start.9 = (bf16[3,64,128]{2,1,0:T(8,128)(2,1)S(1)}, bf16[3,64,128]{2,1,0:T(8,128)(2,1)S(1)}, u32[]{:S(2)}, u32[]{:S(2)}) collective-permute-start(bf16[3,64,128]{2,1,0:T(8,128)(2,1)S(1)} %add_convert_fusion.2), channel_id=1, source_target_pairs={{0,4},{1,5},{2,6},{3,7},{4,0},{5,1},{6,2},{7,3},{8,12},{9,13},{10,... | collective-permute-start | bytes 147464 | tf_op jit(solution)/shard_map/ppermute | solution.py:343
  22.2 4.1 %collective-permute-start.8 = (bf16[3,64,128]{2,1,0:T(8,128)(2,1)S(1)}, bf16[3,64,128]{2,1,0:T(8,128)(2,1)S(1)}, u32[]{:S(2)}, u32[]{:S(2)}) collective-permute-start(bf16[3,64,128]{2,1,0:T(8,128)(2,1)S(1)} %add_convert_fusion.2), channel_id=1, source_target_pairs={{0,2},{1,3},{2,0},{3,1},{4,6},{5,7},{6,4},{7,5},{8,10},{9,11},{10,... | collective-permute-start | bytes 147464 | tf_op jit(solution)/shard_map/ppermute | solution.py:343
  26.4 1.4 %collective-permute-start.11 = (f32[3,64,128]{2,1,0:T(8,128)S(1)}, f32[3,64,128]{2,1,0:T(8,128)S(1)}, u32[]{:S(2)}, u32[]{:S(2)}) collective-permute-start(f32[3,64,128]{2,1,0:T(8,128)S(1)} %add_add_fusion.mine_ref), channel_id=1, source_target_pairs={{0,1},{1,0},{2,3},{3,2},{4,5},{5,4},{6,7},{7,6},{8,9},{9,8},{10,11... | collective-permute-start | bytes 294920 | tf_op jit(solution)/shard_map/ppermute | solution.py:343
  32.7 8.3 %collective-permute-start.12 = (bf16[128,512]{1,0:T(8,128)(2,1)S(1)}, bf16[128,512]{1,0:T(8,128)(2,1)S(1)}, u32[]{:S(2)}, u32[]{:S(2)}) collective-permute-start(bf16[128,512]{1,0:T(8,128)(2,1)S(1)} %get-tuple-element.48), channel_id=1, source_target_pairs={{0,24},{1,25},{2,26},{3,27},{4,28},{5,29},{6,30},{7,31},{8,16},{9,... | collective-permute-start | bytes 393224 | tf_op jit(solution)/shard_map/ppermute | solution.py:343
  36.4 11.4 %collective-permute-start.13 = (bf16[128,512]{1,0:T(8,128)(2,1)S(1)}, bf16[128,512]{1,0:T(8,128)(2,1)S(1)}, u32[]{:S(2)}, u32[]{:S(2)}) collective-permute-start(bf16[128,512]{1,0:T(8,128)(2,1)S(1)} %get-tuple-element.49), channel_id=1, source_target_pairs={{0,16},{1,17},{2,18},{3,19},{4,20},{5,21},{6,22},{7,23},{8,24},{9,... | collective-permute-start | bytes 393224 | tf_op jit(solution)/shard_map/ppermute | solution.py:343
  36.4 11.4 %collective-permute-start.14 = (bf16[128,512]{1,0:T(8,128)(2,1)S(1)}, bf16[128,512]{1,0:T(8,128)(2,1)S(1)}, u32[]{:S(2)}, u32[]{:S(2)}) collective-permute-start(bf16[128,512]{1,0:T(8,128)(2,1)S(1)} %get-tuple-element.50), channel_id=1, source_target_pairs={{0,8},{1,9},{2,10},{3,11},{4,12},{5,13},{6,14},{7,15},{8,0},{9,1},... | collective-permute-start | bytes 393224 | tf_op jit(solution)/shard_map/ppermute | solution.py:343
  48.2 1.5 %collective-permute-start.15 = (f32[6,64,128]{2,1,0:T(8,128)S(1)}, f32[6,64,128]{2,1,0:T(8,128)S(1)}, u32[]{:S(2)}, u32[]{:S(2)}) collective-permute-start(f32[6,64,128]{2,1,0:T(8,128)S(1)} %get-tuple-element.52), channel_id=1, source_target_pairs={{0,1},{1,0},{2,3},{3,2},{4,5},{5,4},{6,7},{7,6},{8,9},{9,8},{10,11... | collective-permute-start | bytes 589832 | tf_op jit(solution)/shard_map/ppermute | solution.py:343
  49.7 6.4 %collective-permute-start.18 = (bf16[6,64,128]{2,1,0:T(8,128)(2,1)S(1)}, bf16[6,64,128]{2,1,0:T(8,128)(2,1)S(1)}, u32[]{:S(2)}, u32[]{:S(2)}) collective-permute-start(bf16[6,64,128]{2,1,0:T(8,128)(2,1)S(1)} %add_convert_fusion.1), channel_id=1, source_target_pairs={{0,6},{1,7},{2,4},{3,5},{4,2},{5,3},{6,0},{7,1},{8,14},{9,15},{10,... | collective-permute-start | bytes 294920 | tf_op jit(solution)/shard_map/ppermute | solution.py:343
  51.3 6.3 %collective-permute-start.17 = (bf16[6,64,128]{2,1,0:T(8,128)(2,1)S(1)}, bf16[6,64,128]{2,1,0:T(8,128)(2,1)S(1)}, u32[]{:S(2)}, u32[]{:S(2)}) collective-permute-start(bf16[6,64,128]{2,1,0:T(8,128)(2,1)S(1)} %add_convert_fusion.1), channel_id=1, source_target_pairs={{0,4},{1,5},{2,6},{3,7},{4,0},{5,1},{6,2},{7,3},{8,12},{9,13},{10,... | collective-permute-start | bytes 294920 | tf_op jit(solution)/shard_map/ppermute | solution.py:343
  51.8 6.0 %collective-permute-start.16 = (bf16[6,64,128]{2,1,0:T(8,128)(2,1)S(1)}, bf16[6,64,128]{2,1,0:T(8,128)(2,1)S(1)}, u32[]{:S(2)}, u32[]{:S(2)}) collective-permute-start(bf16[6,64,128]{2,1,0:T(8,128)(2,1)S(1)} %add_convert_fusion.1), channel_id=1, source_target_pairs={{0,2},{1,3},{2,0},{3,1},{4,6},{5,7},{6,4},{7,5},{8,10},{9,11},{10,... | collective-permute-start | bytes 294920 | tf_op jit(solution)/shard_map/ppermute | solution.py:343
  57.8 8.0 %collective-permute-start.21 = (bf16[7,64,128]{2,1,0:T(8,128)(2,1)S(1)}, bf16[7,64,128]{2,1,0:T(8,128)(2,1)S(1)}, u32[]{:S(2)}, u32[]{:S(2)}) collective-permute-start(bf16[7,64,128]{2,1,0:T(8,128)(2,1)S(1)} %pad_maximum_fusion), channel_id=1, source_target_pairs={{0,24},{1,25},{2,26},{3,27},{4,28},{5,29},{6,30},{7,31},{8,16},{9,... | collective-permute-start | bytes 344072 | tf_op jit(solution)/shard_map/ppermute | solution.py:343
  60.4 9.2 %collective-permute-start.20 = (bf16[7,64,128]{2,1,0:T(8,128)(2,1)S(1)}, bf16[7,64,128]{2,1,0:T(8,128)(2,1)S(1)}, u32[]{:S(2)}, u32[]{:S(2)}) collective-permute-start(bf16[7,64,128]{2,1,0:T(8,128)(2,1)S(1)} %pad_maximum_fusion), channel_id=1, source_target_pairs={{0,16},{1,17},{2,18},{3,19},{4,20},{5,21},{6,22},{7,23},{8,24},{9,... | collective-permute-start | bytes 344072 | tf_op jit(solution)/shard_map/ppermute | solution.py:343
  60.4 9.2 %collective-permute-start.19 = (bf16[7,64,128]{2,1,0:T(8,128)(2,1)S(1)}, bf16[7,64,128]{2,1,0:T(8,128)(2,1)S(1)}, u32[]{:S(2)}, u32[]{:S(2)}) collective-permute-start(bf16[7,64,128]{2,1,0:T(8,128)(2,1)S(1)} %pad_maximum_fusion), channel_id=1, source_target_pairs={{0,8},{1,9},{2,10},{3,11},{4,12},{5,13},{6,14},{7,15},{8,0},{9,1},... | collective-permute-start | bytes 344072 | tf_op jit(solution)/shard_map/ppermute | solution.py:343
  69.7 1.7 %collective-permute-start.22 = (f32[10,64,128]{2,1,0:T(8,128)S(1)}, f32[10,64,128]{2,1,0:T(8,128)S(1)}, u32[]{:S(2)}, u32[]{:S(2)}) collective-permute-start(f32[10,64,128]{2,1,0:T(8,128)S(1)} %convert_dynamic-update-slice_fusion.mine_ref), channel_id=1, source_target_pairs={{0,1},{1,0},{2,3},{3,2},{4,5},{5,4},{6,7},{7,6},{8,9},{9,8},{10,11... | collective-permute-start | bytes 983048 | tf_op jit(solution)/shard_map/ppermute | solution.py:343
  84.0 8.3 %collective-permute-start.25 = (bf16[128,512]{1,0:T(8,128)(2,1)S(1)}, bf16[128,512]{1,0:T(8,128)(2,1)S(1)}, u32[]{:S(2)}, u32[]{:S(2)}) collective-permute-start(bf16[128,512]{1,0:T(8,128)(2,1)S(1)} %get-tuple-element.56.refs_0_), channel_id=1, source_target_pairs={{0,24},{1,25},{2,26},{3,27},{4,28},{5,29},{6,30},{7,31},{8,16},{9,... | collective-permute-start | bytes 393224 | tf_op jit(solution)/shard_map/ppermute | solution.py:343
  86.6 11.6 %collective-permute-start.24 = (bf16[128,512]{1,0:T(8,128)(2,1)S(1)}, bf16[128,512]{1,0:T(8,128)(2,1)S(1)}, u32[]{:S(2)}, u32[]{:S(2)}) collective-permute-start(bf16[128,512]{1,0:T(8,128)(2,1)S(1)} %get-tuple-element.56.refs_0_), channel_id=1, source_target_pairs={{0,16},{1,17},{2,18},{3,19},{4,20},{5,21},{6,22},{7,23},{8,24},{9,... | collective-permute-start | bytes 393224 | tf_op jit(solution)/shard_map/ppermute | solution.py:343
  86.6 11.6 %collective-permute-start.23 = (bf16[128,512]{1,0:T(8,128)(2,1)S(1)}, bf16[128,512]{1,0:T(8,128)(2,1)S(1)}, u32[]{:S(2)}, u32[]{:S(2)}) collective-permute-start(bf16[128,512]{1,0:T(8,128)(2,1)S(1)} %get-tuple-element.56.refs_0_), channel_id=1, source_target_pairs={{0,8},{1,9},{2,10},{3,11},{4,12},{5,13},{6,14},{7,15},{8,0},{9,1},... | collective-permute-start | bytes 393224 | tf_op jit(solution)/shard_map/ppermute | solution.py:343
  99.1 1.3 %collective-permute-start.26 = (f32[1,128,128]{2,1,0:T(8,128)S(1)}, f32[1,128,128]{2,1,0:T(8,128)S(1)}, u32[]{:S(2)}, u32[]{:S(2)}) collective-permute-start(f32[1,128,128]{2,1,0:T(8,128)S(1)} %get-tuple-element.58), channel_id=1, source_target_pairs={{0,1},{1,0},{2,3},{3,2},{4,5},{5,4},{6,7},{7,6},{8,9},{9,8},{10,11... | collective-permute-start | bytes 196616 | tf_op jit(solution)/shard_map/ppermute | solution.py:343
  100.4 4.9 %collective-permute-start.29 = (bf16[1,128,128]{2,1,0:T(8,128)(2,1)S(1)}, bf16[1,128,128]{2,1,0:T(8,128)(2,1)S(1)}, u32[]{:S(2)}, u32[]{:S(2)}) collective-permute-start(bf16[1,128,128]{2,1,0:T(8,128)(2,1)S(1)} %add_convert_fusion.3), channel_id=1, source_target_pairs={{0,6},{1,7},{2,4},{3,5},{4,2},{5,3},{6,0},{7,1},{8,14},{9,15},{10,... | collective-permute-start | bytes 98312 | tf_op jit(solution)/shard_map/ppermute | solution.py:343
  102.0 3.9 %collective-permute-start.28 = (bf16[1,128,128]{2,1,0:T(8,128)(2,1)S(1)}, bf16[1,128,128]{2,1,0:T(8,128)(2,1)S(1)}, u32[]{:S(2)}, u32[]{:S(2)}) collective-permute-start(bf16[1,128,128]{2,1,0:T(8,128)(2,1)S(1)} %add_convert_fusion.3), channel_id=1, source_target_pairs={{0,4},{1,5},{2,6},{3,7},{4,0},{5,1},{6,2},{7,3},{8,12},{9,13},{10,... | collective-permute-start | bytes 98312 | tf_op jit(solution)/shard_map/ppermute | solution.py:343
  102.3 3.9 %collective-permute-start.27 = (bf16[1,128,128]{2,1,0:T(8,128)(2,1)S(1)}, bf16[1,128,128]{2,1,0:T(8,128)(2,1)S(1)}, u32[]{:S(2)}, u32[]{:S(2)}) collective-permute-start(bf16[1,128,128]{2,1,0:T(8,128)(2,1)S(1)} %add_convert_fusion.3), channel_id=1, source_target_pairs={{0,2},{1,3},{2,0},{3,1},{4,6},{5,7},{6,4},{7,5},{8,10},{9,11},{10,... | collective-permute-start | bytes 98312 | tf_op jit(solution)/shard_map/ppermute | solution.py:343
  106.2 1.3 %collective-permute-start.30 = (f32[1,128,128]{2,1,0:T(8,128)S(1)}, f32[1,128,128]{2,1,0:T(8,128)S(1)}, u32[]{:S(2)}, u32[]{:S(2)}) collective-permute-start(f32[1,128,128]{2,1,0:T(8,128)S(1)} %add_add_fusion.1.mine_ref), channel_id=1, source_target_pairs={{0,1},{1,0},{2,3},{3,2},{4,5},{5,4},{6,7},{7,6},{8,9},{9,8},{10,11... | collective-permute-start | bytes 196616 | tf_op jit(solution)/shard_map/ppermute | solution.py:343
  108.4 7.3 %collective-permute-start.31 = (bf16[32,2048]{1,0:T(8,128)(2,1)S(1)}, bf16[32,2048]{1,0:T(8,128)(2,1)S(1)}, u32[]{:S(2)}, u32[]{:S(2)}) collective-permute-start(bf16[32,2048]{1,0:T(8,128)(2,1)S(1)} %get-tuple-element.60), channel_id=1, source_target_pairs={{0,6},{1,7},{2,4},{3,5},{4,2},{5,3},{6,0},{7,1},{8,14},{9,15},{10,... | collective-permute-start | bytes 393224 | tf_op jit(solution)/shard_map/ppermute | solution.py:343
  109.5 7.4 %collective-permute-start.32 = (bf16[32,2048]{1,0:T(8,128)(2,1)S(1)}, bf16[32,2048]{1,0:T(8,128)(2,1)S(1)}, u32[]{:S(2)}, u32[]{:S(2)}) collective-permute-start(bf16[32,2048]{1,0:T(8,128)(2,1)S(1)} %get-tuple-element.61), channel_id=1, source_target_pairs={{0,7},{1,6},{2,5},{3,4},{4,3},{5,2},{6,1},{7,0},{8,15},{9,14},{10,... | collective-permute-start | bytes 393224 | tf_op jit(solution)/shard_map/ppermute | solution.py:343
  110.8 10.7 %collective-permute-start.33 = (bf16[32,2048]{1,0:T(8,128)(2,1)S(1)}, bf16[32,2048]{1,0:T(8,128)(2,1)S(1)}, u32[]{:S(2)}, u32[]{:S(2)}) collective-permute-start(bf16[32,2048]{1,0:T(8,128)(2,1)S(1)} %get-tuple-element.62), channel_id=1, source_target_pairs={{0,2},{1,3},{2,0},{3,1},{4,6},{5,7},{6,4},{7,5},{8,10},{9,11},{10,... | collective-permute-start | bytes 393224 | tf_op jit(solution)/shard_map/ppermute | solution.py:343
  112.5 9.1 %collective-permute-start.34 = (bf16[32,2048]{1,0:T(8,128)(2,1)S(1)}, bf16[32,2048]{1,0:T(8,128)(2,1)S(1)}, u32[]{:S(2)}, u32[]{:S(2)}) collective-permute-start(bf16[32,2048]{1,0:T(8,128)(2,1)S(1)} %get-tuple-element.63), channel_id=1, source_target_pairs={{0,4},{1,5},{2,6},{3,7},{4,0},{5,1},{6,2},{7,3},{8,12},{9,13},{10,... | collective-permute-start | bytes 393224 | tf_op jit(solution)/shard_map/ppermute | solution.py:343
  112.5 10.3 %collective-permute-start.35 = (bf16[32,2048]{1,0:T(8,128)(2,1)S(1)}, bf16[32,2048]{1,0:T(8,128)(2,1)S(1)}, u32[]{:S(2)}, u32[]{:S(2)}) collective-permute-start(bf16[32,2048]{1,0:T(8,128)(2,1)S(1)} %get-tuple-element.64), channel_id=1, source_target_pairs={{0,3},{1,2},{2,1},{3,0},{4,7},{5,6},{6,5},{7,4},{8,11},{9,10},{10,... | collective-permute-start | bytes 393224 | tf_op jit(solution)/shard_map/ppermute | solution.py:343
  115.7 7.6 %collective-permute-start.36 = (bf16[32,2048]{1,0:T(8,128)(2,1)S(1)}, bf16[32,2048]{1,0:T(8,128)(2,1)S(1)}, u32[]{:S(2)}, u32[]{:S(2)}) collective-permute-start(bf16[32,2048]{1,0:T(8,128)(2,1)S(1)} %get-tuple-element.65), channel_id=1, source_target_pairs={{0,5},{1,4},{2,7},{3,6},{4,1},{5,0},{6,3},{7,2},{8,13},{9,12},{10,... | collective-permute-start | bytes 393224 | tf_op jit(solution)/shard_map/ppermute | solution.py:343
  117.0 6.3 %collective-permute-start.37 = (bf16[32,2048]{1,0:T(8,128)(2,1)S(1)}, bf16[32,2048]{1,0:T(8,128)(2,1)S(1)}, u32[]{:S(2)}, u32[]{:S(2)}) collective-permute-start(bf16[32,2048]{1,0:T(8,128)(2,1)S(1)} %get-tuple-element.66), channel_id=1, source_target_pairs={{0,1},{1,0},{2,3},{3,2},{4,5},{5,4},{6,7},{7,6},{8,9},{9,8},{10,11... | collective-permute-start | bytes 393224 | tf_op jit(solution)/shard_map/ppermute | solution.py:343

commit v3 on v2

--- a/solution.py
+++ b/solution.py
@@ -60,6 +60,7 @@
     sub = iota2((TILE, RANK), 0)
     count = len(sets[0])
     early = [None] * len(sets)
+    pivots = [[] for _ in sets]
     for t in range(count):
         g = TILE * (first + t)
         spread, coming = [], []
@@ -70,10 +71,12 @@
             spread.append(cols)
             near = (t, t + 1) if ahead and t + 1 < count else ()
             coming.append({i: [lanes_of(tiles[i], g + TILE + j) for j in range(TILE)] for i in near})
+            pivots[n].append(jnp.zeros((TILE, RANK), f32))
         for k in range(TILE):
             here = lane == g + k
-            for tiles, cols, look in zip(sets, spread, coming):
+            for tiles, cols, look, held in zip(sets, spread, coming, pivots):
                 pivot_row = [rows_of(cols[t][j], k) if j >= k else None for j in range(TILE)]
+                held[t] = jnp.where(sub == k, pivot_row[k], held[t])
                 inv = 1.0 / pivot_row[k]
                 scaled = [pivot_row[j] * inv if j > k else None for j in range(TILE)]
                 row = jnp.where(here, 1.0, rows_of(tiles[t], k)) * inv
@@ -91,7 +94,7 @@
                     if i in look:
                         look[i] = [x - col * y for x, y in zip(look[i], look_row)]
         early = [look.get(t + 1) for look in coming]
-    return sets
+    return list(zip(sets, pivots))
 
 
 def inverse_factors(matrices):
@@ -102,66 +105,76 @@
     for lo in range(0, RANK, size):
         hi = lo + size
         sets = [[rest[TILE * t : TILE * t + TILE, :] for t in range(size // TILE)] for rest in rests]
-        for n, tiles in enumerate(eliminate(sets, lo // TILE, alone)):
+        r = iota2((size, RANK), 0) + lo
+        c = iota2((size, RANK), 1)
+        for n, (tiles, pivots) in enumerate(eliminate(sets, lo // TILE, alone)):
             panel = jnp.concatenate(tiles, 0)
-            done[n].append(panel)
+            pivots = jnp.concatenate(pivots, 0)
+            unit = jnp.where(r > c, panel, jnp.where(r == c, 1.0, 0.0))
+            done[n].append((unit * lax.rsqrt(pivots), pivots))
             if hi == RANK:
                 continue
-            r = iota2((size, RANK), 0) + lo
-            c = iota2((size, RANK), 1)
-            pivots = jnp.sum(jnp.where(r == c, panel, 0.0), 1, keepdims=True)
             rows = jnp.where(r == c, 1.0, jnp.where((c > r) & (c < hi), 0.0, panel))
             tail = rests[n][size:, :]
-            c = iota2(tail.shape, 1)
-            tail = jnp.where((c >= lo) & (c < hi), 0.0, tail)
+            at = iota2(tail.shape, 1)
+            tail = jnp.where((at >= lo) & (at < hi), 0.0, tail)
             rests[n] = tail - dot(panel * (1.0 / pivots), rows, 0, 0)[hi:, :]
-    results = []
-    for panels in done:
-        x = jnp.concatenate(panels, 0)
-        r = iota2((RANK, RANK), 0)
-        c = iota2((RANK, RANK), 1)
-        pivots = jnp.sum(jnp.where(r == c, x, 0.0), 1, keepdims=True)
-        unit = jnp.where(r > c, x, jnp.where(r == c, 1.0, 0.0))
-        results.append((unit * lax.rsqrt(pivots), pivots))
-    return results
+    return [tuple(jnp.concatenate(x, 0) for x in zip(*panels)) for panels in done]
 
 
 def diagonal_of(x):
     return jnp.sum(jnp.where(iota2(x.shape, 0) == iota2(x.shape, 1), x, 0.0), 1, keepdims=True)
 
 
-def leading_spaces(grams, work):
+def unit_scale(blocks):
+    largest = diagonal_of(blocks[0])
+    for x in blocks[1:]:
+        largest = jnp.maximum(largest, diagonal_of(x))
+    return 1.0 / jnp.max(largest, keepdims=True)
+
+
+def leading_spaces(grams, scale, work, careful, sound_ref):
     for gram, (gram_ref, imaged_ref, _) in zip(grams, work):
-        largest = jnp.maximum(diagonal_of(gram[:RANK, :RANK]), diagonal_of(gram[RANK:, RANK:]))
-        gram = gram * (1.0 / jnp.max(largest, keepdims=True))
-        gram_ref[...] = gram
-        imaged = gram[:, :RANK]
-        for step in range(SWEEPS - 1):
-            imaged = dot_split(gram, imaged, 1, 0)
-        imaged_ref[...] = imaged
-
-    def attempt(step):
+        gram_ref[...] = gram * scale
+        imaged_ref[...] = gram_ref[:, :RANK]
+    count = jnp.where(careful, SWEEPS, 1)
+
+    def sweep(step, carry):
+        @pl.when(jnp.logical_not(careful))
+        def _():
+            images = [imaged_ref[...] for _, imaged_ref, _ in work]
+            for again in range(SWEEPS - 1):
+                images = [dot_split(gram_ref[...], x, 1, 0) for x, (gram_ref, _, _) in zip(images, work)]
+            for x, (_, imaged_ref, _) in zip(images, work):
+                imaged_ref[...] = x
+
         inners = [dot(imaged_ref[...], imaged_ref[...], 0, 0) for _, imaged_ref, _ in work]
-        share = None
         for inner, (factor, pivots), (_, imaged_ref, frame_ref) in zip(inners, inverse_factors(inners), work):
             frame_ref[...] = dot(imaged_ref[...], factor, 1, 1)
-            ratio = pivots / diagonal_of(inner)
-            share = ratio if share is None else jnp.where(ratio < share, ratio, share)
-        good = jnp.logical_and(step == 0, jnp.min(share) > PIVOT_SHARE)
-        last = jnp.logical_or(good, step == SWEEPS)
-
-        @pl.when(jnp.logical_not(last))
+            sound_ref[...] = jnp.where(pivots > PIVOT_SHARE * diagonal_of(inner), sound_ref[...], 0.0)
+
+        @pl.when(step + 1 < count)
         def _():
             for gram_ref, imaged_ref, frame_ref in work:
-                first = gram_ref[:, :RANK]
-                imaged_ref[...] = jnp.where(step == 0, first, dot(gram_ref[...], frame_ref[...], 1, 0))
-
-        return jnp.where(last, SWEEPS + 1, step + 1)
-
-    lax.while_loop(lambda step: step <= SWEEPS, attempt, jnp.int32(0))
+                imaged_ref[...] = dot(gram_ref[...], frame_ref[...], 1, 0)
+
+        return carry
+
+    lax.fori_loop(0, count, sweep, 0)
     return [frame_ref[...].astype(bf16) for _, _, frame_ref in work]
 
 
+def until_sound(sound_ref, attempt):
+    def once(mode):
+        sound_ref[...] = jnp.ones(sound_ref.shape, f32)
+        attempt(mode == 1)
+        sound = jnp.min(sound_ref[...]) > 0.5
+        return jnp.where(jnp.logical_or(mode == 1, sound), 2, 1)
+
+    lax.while_loop(lambda mode: mode < 2, once, jnp.int32(0))
+
+
+sound_shape = [pltpu.VMEM((RANK, RANK), f32)]
 work_shapes = [pltpu.VMEM((2 * RANK, 2 * RANK), f32)] + [pltpu.VMEM((2 * RANK, RANK), f32)] * 2
 
 
@@ -219,13 +232,19 @@
 
 
 def node_kernel(pos_ref, mine_ref, other_ref, rows_ref, *refs):
-    nodes, low_ref, work = refs[:PLANES], refs[PLANES], refs[PLANES + 1 :]
+    nodes, low_ref, sound_ref, work = refs[:PLANES], refs[PLANES], refs[PLANES + 1], refs[PLANES + 2 :]
     core, z = place(pos_ref)
-    (low,) = leading_spaces([plane_gram(mine_ref, other_ref, core)], [work])
-    low_ref[...] = low
     width = nodes[0].shape[1]
-    for ref, m in zip(nodes, TREE_ORDER):
-        ref[...] = dot_low(low, rows_ref[:, chunk(z, m, width)], 0, 0).astype(bf16)
+
+    def attempt(careful):
+        gram = plane_gram(mine_ref, other_ref, core)
+        scale = unit_scale([gram[:RANK, :RANK], gram[RANK:, RANK:]])
+        (low,) = leading_spaces([gram], scale, [work], careful, sound_ref)
+        low_ref[...] = low
+        for ref, m in zip(nodes, TREE_ORDER):
+            ref[...] = dot_low(low, rows_ref[:, chunk(z, m, width)], 0, 0).astype(bf16)
+
+    until_sound(sound_ref, attempt)
 
 
 def reduced(gram, low):
@@ -252,33 +271,37 @@
 
 def top_kernel(pos_ref, mine_ref, other_ref, *refs):
     nodes, (top_ref, gram_ref, low_ref), refs = refs[:PLANES], refs[PLANES : PLANES + 3], refs[PLANES + 3 :]
-    all_ref, diag_ref, work = refs[0], refs[1], [refs[2:5], refs[5:8]]
+    all_ref, diag_ref, sound_ref, work = refs[0], refs[1], refs[2], [refs[3:6], refs[6:9]]
     core, z = place(pos_ref)
     for ref, m in zip(nodes, TREE_ORDER):
         all_ref[z ^ m] = ref[...]
         diag_ref[z ^ m] = joined(mine_ref, other_ref, core, len(PAIRS) + m)
-    cross = {pair: joined(mine_ref, other_ref, core, b) for b, pair in enumerate(PAIRS)}
-    gram_a = square(diag_ref[0], cross[0, 1], diag_ref[1])
-    gram_b = square(diag_ref[2], cross[2, 3], diag_ref[3])
-    low_a, low_b = leading_spaces([gram_a, gram_b], work)
-    between = jnp.concatenate(
-        [
-            jnp.concatenate([cross[0, 2], cross[1, 2]], 1),
-            jnp.concatenate([cross[0, 3], cross[1, 3]], 1),
-        ],
-        0,
-    )
-    gram = square(
-        reduced(gram_a, low_a),
-        dot_split(low_b, dot_split(between, low_a, 1, 0), 0, 0),
-        reduced(gram_b, low_b),
-    )
-    gram_ref[...] = gram
-    (low,) = leading_spaces([gram], work[:1])
-    low_ref[...] = low
-    node_a = dot_low(low_a, jnp.concatenate([all_ref[0], all_ref[1]], 0), 0, 0).astype(bf16)
-    node_b = dot_low(low_b, jnp.concatenate([all_ref[2], all_ref[3]], 0), 0, 0).astype(bf16)
-    top_ref[...] = dot_low(low, jnp.concatenate([node_a, node_b], 0), 0, 0).astype(bf16)
+
+    def attempt(careful):
+        cross = {pair: joined(mine_ref, other_ref, core, b) for b, pair in enumerate(PAIRS)}
+        scale = unit_scale([diag_ref[y] for y in range(PLANES)])
+        grams = [square(diag_ref[i], cross[i, j], diag_ref[j]) for i, j in ((0, 1), (2, 3))]
+        low_a, low_b = leading_spaces(grams, scale, work, careful, sound_ref)
+        between = jnp.concatenate(
+            [
+                jnp.concatenate([cross[0, 2], cross[1, 2]], 1),
+                jnp.concatenate([cross[0, 3], cross[1, 3]], 1),
+            ],
+            0,
+        )
+        gram = square(
+            reduced(grams[0], low_a),
+            dot_split(low_b, dot_split(between, low_a, 1, 0), 0, 0),
+            reduced(grams[1], low_b),
+        )
+        gram_ref[...] = gram
+        node_a = dot_low(low_a, jnp.concatenate([all_ref[0], all_ref[1]], 0), 0, 0).astype(bf16)
+        node_b = dot_low(low_b, jnp.concatenate([all_ref[2], all_ref[3]], 0), 0, 0).astype(bf16)
+        (low,) = leading_spaces([gram], scale, work[:1], careful, sound_ref)
+        low_ref[...] = low
+        top_ref[...] = dot_low(low, jnp.concatenate([node_a, node_b], 0), 0, 0).astype(bf16)
+
+    until_sound(sound_ref, attempt)
 
 
 def factor_kernel(gram_ref, low_ref, factor_ref):
@@ -368,7 +391,7 @@
         node_kernel,
         [((RANK, part), bf16)] * PLANES + [((2 * RANK, RANK), bf16)],
         pos, mine, other, rows,
-        scratch=work_shapes,
+        scratch=sound_shape + work_shapes,
     )
     nodes = swap_all(nodes, TREE_ORDER, PLANE)
     (diag,) = kernel(diag_kernel, [((1, half, RANK), bf16)], pos, mine, other, low)
@@ -386,7 +409,9 @@
         top_kernel,
         [((RANK, part), bf16), ((2 * RANK, 2 * RANK), f32), ((2 * RANK, RANK), bf16)],
         pos, mine, swap(mine, 1), *nodes,
-        scratch=[pltpu.VMEM((PLANES, RANK, part), bf16), pltpu.VMEM((PLANES, RANK, RANK), f32)] + work_shapes * 2,
+        scratch=[pltpu.VMEM((PLANES, RANK, part), bf16), pltpu.VMEM((PLANES, RANK, RANK), f32)]
+        + sound_shape
+        + work_shapes * 2,
     )
     tops = swap_all([top] * PLANES, range(PLANES), PLANE)
     (factor,) = kernel(factor_kernel, [((RANK, RANK), f32)], gram, low, scalar=False)

time: 124 us -> 124 us (level)
  no operation moved by 1% of the time
where the time goes in v3:
time: 124 us; the launch traced here: 123 us
  waiting for transfers between devices  58.6 us (47%)
  starting transfers between devices  38.9 us (31%)
  Pallas kernels  24.3 us (20%)
    ppermute x38, waiting for transfers between devices, swap(): return lax.ppermute(x, 'cols', [(i, i ^ apart) for i in range(count)])  58.6 us
    ppermute x38, starting transfers between devices, swap(): return lax.ppermute(x, 'cols', [(i, i ^ apart) for i in range(count)])  38.9 us
    pallas_call x10, Pallas kernels, kernel(): pl.pallas_call(fn, out_shape=[jax.ShapeDtypeStruct(s, d) for s, d in shap...  24.3 us
  transfers between devices with their start and end apart: 38, of which 31 were waited for; matrix products, arithmetic and copies ran while one was open for 0% of the time, Pallas kernels for 3%

profile of v3, /device:TPU:0, one launch (start us, length us, event | category | flops | bytes accessed | tf_op | source)
XLA Modules:
  0.0 123.5 jit_solution(13170816974931261894)
XLA Ops:
  0.0 1.2 copy-done
  1.3 4.0 %collective-permute-start = (bf16[32,2048]{1,0:T(8,128)(2,1)S(1)}, bf16[32,2048]{1,0:T(8,128)(2,1)S(1)}, u32[]{:S(2)}, u32[]{:S(2)}) collective-permute-start(bf16[32,2048]{1,0:T(8,128)(2,1)S(1)} %get-tuple-element.37), channel_id=1, source_target_pairs={{0,6},{1,7},{2,4},{3,5},{4,2},{5,3},{6,0},{7,1},{8,14},{9,15},{10,... | collective-permute-start | bytes 393224 | tf_op jit(solution)/shard_map/ppermute | solution.py:366
  5.3 1.1 collective-permute-start.2
  6.4 1.5 %collective-permute-start.3 = (bf16[32,2048]{1,0:T(8,128)(2,1)S(1)}, bf16[32,2048]{1,0:T(8,128)(2,1)S(1)}, u32[]{:S(2)}, u32[]{:S(2)}) collective-permute-start(bf16[32,2048]{1,0:T(8,128)(2,1)S(1)} %get-tuple-element.40), channel_id=1, source_target_pairs={{0,4},{1,5},{2,6},{3,7},{4,0},{5,1},{6,2},{7,3},{8,12},{9,13},{10,... | collective-permute-start | bytes 393224 | tf_op jit(solution)/shard_map/ppermute | solution.py:366
  7.9 0.6 collective-permute-start.4
  8.5 0.7 collective-permute-done.refs_1_
  9.2 2.8 %collective-permute-done.1.refs_2_ = bf16[32,2048]{1,0:T(8,128)(2,1)S(1)} collective-permute-done((bf16[32,2048]{1,0:T(8,128)(2,1)S(1)}, bf16[32,2048]{1,0:T(8,128)(2,1)S(1)}, u32[]{:S(2)}, u32[]{:S(2)}) %collective-permute-start.1) | collective-permute-done | bytes 131104 | tf_op jit(solution)/shard_map/ppermute | solution.py:366
  12.0 3.4 %collective-permute-done.2.refs_3_ = bf16[32,2048]{1,0:T(8,128)(2,1)S(1)} collective-permute-done((bf16[32,2048]{1,0:T(8,128)(2,1)S(1)}, bf16[32,2048]{1,0:T(8,128)(2,1)S(1)}, u32[]{:S(2)}, u32[]{:S(2)}) %collective-permute-start.2) | collective-permute-done | bytes 131104 | tf_op jit(solution)/shard_map/ppermute | solution.py:366
  15.5 1.1 collective-permute-done.4.refs_5_
  16.6 0.7 collective-permute-done.5.refs_6_
  17.3 0.5 gram_kernel.1
  18.0 1.2 collective-permute-done.7
  19.2 2.6 %collective-permute-start.10 = (bf16[3,64,128]{2,1,0:T(8,128)(2,1)S(1)}, bf16[3,64,128]{2,1,0:T(8,128)(2,1)S(1)}, u32[]{:S(2)}, u32[]{:S(2)}) collective-permute-start(bf16[3,64,128]{2,1,0:T(8,128)(2,1)S(1)} %add_convert_fusion.2), channel_id=1, source_target_pairs={{0,6},{1,7},{2,4},{3,5},{4,2},{5,3},{6,0},{7,1},{8,14},{9,15},{10,... | collective-permute-start | bytes 147464 | tf_op jit(solution)/shard_map/ppermute | solution.py:366
  21.8 0.5 collective-permute-start.9
  22.2 0.5 collective-permute-start.8
  22.8 1.5 %collective-permute-done.10 = bf16[3,64,128]{2,1,0:T(8,128)(2,1)S(1)} collective-permute-done((bf16[3,64,128]{2,1,0:T(8,128)(2,1)S(1)}, bf16[3,64,128]{2,1,0:T(8,128)(2,1)S(1)}, u32[]{:S(2)}, u32[]{:S(2)}) %collective-permute-start.10) | collective-permute-done | bytes 49184 | tf_op jit(solution)/shard_map/ppermute | solution.py:366
  24.3 1.6 %collective-permute-done.9 = bf16[3,64,128]{2,1,0:T(8,128)(2,1)S(1)} collective-permute-done((bf16[3,64,128]{2,1,0:T(8,128)(2,1)S(1)}, bf16[3,64,128]{2,1,0:T(8,128)(2,1)S(1)}, u32[]{:S(2)}, u32[]{:S(2)}) %collective-permute-start.9) | collective-permute-done | bytes 49184 | tf_op jit(solution)/shard_map/ppermute | solution.py:366
  25.9 0.5 collective-permute-done.8
  26.4 1.3 %collective-permute-done.11.other_ref = f32[3,64,128]{2,1,0:T(8,128)S(1)} collective-permute-done((f32[3,64,128]{2,1,0:T(8,128)S(1)}, f32[3,64,128]{2,1,0:T(8,128)S(1)}, u32[]{:S(2)}, u32[]{:S(2)}) %collective-permute-start.11) | collective-permute-done | bytes 98336 | tf_op jit(solution)/shard_map/ppermute | solution.py:366
  27.7 4.8 %node_kernel.1 = (bf16[128,512]{1,0:T(8,128)(2,1)S(1)}, bf16[128,512]{1,0:T(8,128)(2,1)S(1)}, bf16[128,512]{1,0:T(8,128)(2,1)S(1)}, bf16[128,512]{1,0:T(8,128)(2,1)S(1)}, bf16[256,128]{1,0:T(8,128)(2,1)S(1)}) custom-call(s32[1]{0:T(128)} %bitcast.pos_ref, f32[3,64,128]{2,1,0:T(8,128)S(1)} %add_add_fusion.mine_ref, ...), custom_call_target="tpu_custom_call" | custom-call | tf_op jit(solution)/shard_map/node_kernel/pallas_call | solution.py:349
  32.5 3.7 %collective-permute-start.12 = (bf16[128,512]{1,0:T(8,128)(2,1)S(1)}, bf16[128,512]{1,0:T(8,128)(2,1)S(1)}, u32[]{:S(2)}, u32[]{:S(2)}) collective-permute-start(bf16[128,512]{1,0:T(8,128)(2,1)S(1)} %get-tuple-element.48), channel_id=1, source_target_pairs={{0,24},{1,25},{2,26},{3,27},{4,28},{5,29},{6,30},{7,31},{8,16},{9,... | collective-permute-start | bytes 393224 | tf_op jit(solution)/shard_map/ppermute | solution.py:366
  36.2 0.8 collective-permute-start.14
  37.0 3.8 %collective-permute-done.12.refs_1_ = bf16[128,512]{1,0:T(8,128)(2,1)S(1)} collective-permute-done((bf16[128,512]{1,0:T(8,128)(2,1)S(1)}, bf16[128,512]{1,0:T(8,128)(2,1)S(1)}, u32[]{:S(2)}, u32[]{:S(2)}) %collective-permute-start.12) | collective-permute-done | bytes 131104 | tf_op jit(solution)/shard_map/ppermute | solution.py:366
  40.8 6.8 %collective-permute-done.13.refs_2_ = bf16[128,512]{1,0:T(8,128)(2,1)S(1)} collective-permute-done((bf16[128,512]{1,0:T(8,128)(2,1)S(1)}, bf16[128,512]{1,0:T(8,128)(2,1)S(1)}, u32[]{:S(2)}, u32[]{:S(2)}) %collective-permute-start.13) | collective-permute-done | bytes 131104 | tf_op jit(solution)/shard_map/ppermute | solution.py:366
  47.6 0.4 cross_kernel.1
  48.1 1.4 %collective-permute-done.15 = f32[6,64,128]{2,1,0:T(8,128)S(1)} collective-permute-done((f32[6,64,128]{2,1,0:T(8,128)S(1)}, f32[6,64,128]{2,1,0:T(8,128)S(1)}, u32[]{:S(2)}, u32[]{:S(2)}) %collective-permute-start.15) | collective-permute-done | bytes 196640 | tf_op jit(solution)/shard_map/ppermute | solution.py:366
  49.6 1.6 %collective-permute-start.18 = (bf16[6,64,128]{2,1,0:T(8,128)(2,1)S(1)}, bf16[6,64,128]{2,1,0:T(8,128)(2,1)S(1)}, u32[]{:S(2)}, u32[]{:S(2)}) collective-permute-start(bf16[6,64,128]{2,1,0:T(8,128)(2,1)S(1)} %add_convert_fusion.1), channel_id=1, source_target_pairs={{0,6},{1,7},{2,4},{3,5},{4,2},{5,3},{6,0},{7,1},{8,14},{9,15},{10,... | collective-permute-start | bytes 294920 | tf_op jit(solution)/shard_map/ppermute | solution.py:366
  51.1 0.5 collective-permute-start.17
  51.7 1.5 %collective-permute-start.16 = (bf16[6,64,128]{2,1,0:T(8,128)(2,1)S(1)}, bf16[6,64,128]{2,1,0:T(8,128)(2,1)S(1)}, u32[]{:S(2)}, u32[]{:S(2)}) collective-permute-start(bf16[6,64,128]{2,1,0:T(8,128)(2,1)S(1)} %add_convert_fusion.1), channel_id=1, source_target_pairs={{0,2},{1,3},{2,0},{3,1},{4,6},{5,7},{6,4},{7,5},{8,10},{9,11},{10,... | collective-permute-start | bytes 294920 | tf_op jit(solution)/shard_map/ppermute | solution.py:366
  53.1 0.4 diag_kernel.1
  53.6 2.4 %collective-permute-done.18 = bf16[6,64,128]{2,1,0:T(8,128)(2,1)S(1)} collective-permute-done((bf16[6,64,128]{2,1,0:T(8,128)(2,1)S(1)}, bf16[6,64,128]{2,1,0:T(8,128)(2,1)S(1)}, u32[]{:S(2)}, u32[]{:S(2)}) %collective-permute-start.18) | collective-permute-done | bytes 98336 | tf_op jit(solution)/shard_map/ppermute | solution.py:366
  56.0 1.5 %collective-permute-done.17 = bf16[6,64,128]{2,1,0:T(8,128)(2,1)S(1)} collective-permute-done((bf16[6,64,128]{2,1,0:T(8,128)(2,1)S(1)}, bf16[6,64,128]{2,1,0:T(8,128)(2,1)S(1)}, u32[]{:S(2)}, u32[]{:S(2)}) %collective-permute-start.17) | collective-permute-done | bytes 98336 | tf_op jit(solution)/shard_map/ppermute | solution.py:366
  57.7 2.6 %collective-permute-start.21 = (bf16[7,64,128]{2,1,0:T(8,128)(2,1)S(1)}, bf16[7,64,128]{2,1,0:T(8,128)(2,1)S(1)}, u32[]{:S(2)}, u32[]{:S(2)}) collective-permute-start(bf16[7,64,128]{2,1,0:T(8,128)(2,1)S(1)} %pad_maximum_fusion), channel_id=1, source_target_pairs={{0,24},{1,25},{2,26},{3,27},{4,28},{5,29},{6,30},{7,31},{8,16},{9,... | collective-permute-start | bytes 344072 | tf_op jit(solution)/shard_map/ppermute | solution.py:366
  60.3 1.9 %collective-permute-start.19 = (bf16[7,64,128]{2,1,0:T(8,128)(2,1)S(1)}, bf16[7,64,128]{2,1,0:T(8,128)(2,1)S(1)}, u32[]{:S(2)}, u32[]{:S(2)}) collective-permute-start(bf16[7,64,128]{2,1,0:T(8,128)(2,1)S(1)} %pad_maximum_fusion), channel_id=1, source_target_pairs={{0,8},{1,9},{2,10},{3,11},{4,12},{5,13},{6,14},{7,15},{8,0},{9,1},... | collective-permute-start | bytes 344072 | tf_op jit(solution)/shard_map/ppermute | solution.py:366
  62.1 3.5 %collective-permute-done.21 = bf16[7,64,128]{2,1,0:T(8,128)(2,1)S(1)} collective-permute-done((bf16[7,64,128]{2,1,0:T(8,128)(2,1)S(1)}, bf16[7,64,128]{2,1,0:T(8,128)(2,1)S(1)}, u32[]{:S(2)}, u32[]{:S(2)}) %collective-permute-start.21) | collective-permute-done | bytes 114720 | tf_op jit(solution)/shard_map/ppermute | solution.py:366
  65.7 3.7 %collective-permute-done.20 = bf16[7,64,128]{2,1,0:T(8,128)(2,1)S(1)} collective-permute-done((bf16[7,64,128]{2,1,0:T(8,128)(2,1)S(1)}, bf16[7,64,128]{2,1,0:T(8,128)(2,1)S(1)}, u32[]{:S(2)}, u32[]{:S(2)}) %collective-permute-start.20) | collective-permute-done | bytes 114720 | tf_op jit(solution)/shard_map/ppermute | solution.py:366
  69.6 1.6 %collective-permute-done.22.other_ref = f32[10,64,128]{2,1,0:T(8,128)S(1)} collective-permute-done((f32[10,64,128]{2,1,0:T(8,128)S(1)}, f32[10,64,128]{2,1,0:T(8,128)S(1)}, u32[]{:S(2)}, u32[]{:S(2)}) %collective-permute-start.22) | collective-permute-done | bytes 327712 | tf_op jit(solution)/shard_map/ppermute | solution.py:366
  71.2 12.0 %top_kernel.1 = (bf16[128,512]{1,0:T(8,128)(2,1)S(1)}, f32[256,256]{1,0:T(8,128)S(1)}, bf16[256,128]{1,0:T(8,128)(2,1)S(1)}) custom-call(s32[1]{0:T(128)} %bitcast.pos_ref, f32[10,64,128]{2,1,0:T(8,128)S(1)} %convert_dynamic-update-slice_fusion.mine_ref, f32[10,64,128]{2,1,0:T(8,128)S(1)} %collective-permute-done.22.other_ref, ...), custom_call_target="tpu_custom_call" | custom-call | tf_op jit(solution)/shard_map/top_kernel/pallas_call | solution.py:349
  83.2 2.6 %collective-permute-start.25 = (bf16[128,512]{1,0:T(8,128)(2,1)S(1)}, bf16[128,512]{1,0:T(8,128)(2,1)S(1)}, u32[]{:S(2)}, u32[]{:S(2)}) collective-permute-start(bf16[128,512]{1,0:T(8,128)(2,1)S(1)} %get-tuple-element.56.refs_0_), channel_id=1, source_target_pairs={{0,24},{1,25},{2,26},{3,27},{4,28},{5,29},{6,30},{7,31},{8,16},{9,... | collective-permute-start | bytes 393224 | tf_op jit(solution)/shard_map/ppermute | solution.py:366
  85.8 1.9 %collective-permute-start.23 = (bf16[128,512]{1,0:T(8,128)(2,1)S(1)}, bf16[128,512]{1,0:T(8,128)(2,1)S(1)}, u32[]{:S(2)}, u32[]{:S(2)}) collective-permute-start(bf16[128,512]{1,0:T(8,128)(2,1)S(1)} %get-tuple-element.56.refs_0_), channel_id=1, source_target_pairs={{0,8},{1,9},{2,10},{3,11},{4,12},{5,13},{6,14},{7,15},{8,0},{9,1},... | collective-permute-start | bytes 393224 | tf_op jit(solution)/shard_map/ppermute | solution.py:366
  87.7 3.4 %factor_kernel.1.factor_ref = f32[128,128]{1,0:T(8,128)S(1)} custom-call(f32[256,256]{1,0:T(8,128)S(1)} %get-tuple-element.54.gram_ref, bf16[256,128]{1,0:T(8,128)(2,1)S(1)} %get-tuple-element.55.low_ref), custom_call_target="tpu_custom_call" | custom-call | tf_op jit(solution)/shard_map/factor_kernel/pallas_call | solution.py:349
  91.1 0.5 collective-permute-done.25.refs_3_
  91.5 5.9 %collective-permute-done.24.refs_2_ = bf16[128,512]{1,0:T(8,128)(2,1)S(1)} collective-permute-done((bf16[128,512]{1,0:T(8,128)(2,1)S(1)}, bf16[128,512]{1,0:T(8,128)(2,1)S(1)}, u32[]{:S(2)}, u32[]{:S(2)}) %collective-permute-start.24) | collective-permute-done | bytes 131104 | tf_op jit(solution)/shard_map/ppermute | solution.py:366
  97.4 0.8 coeffs_kernel.1
  98.3 1.2 %collective-permute-done.26 = f32[1,128,128]{2,1,0:T(8,128)S(1)} collective-permute-done((f32[1,128,128]{2,1,0:T(8,128)S(1)}, f32[1,128,128]{2,1,0:T(8,128)S(1)}, u32[]{:S(2)}, u32[]{:S(2)}) %collective-permute-start.26) | collective-permute-done | bytes 65568 | tf_op jit(solution)/shard_map/ppermute | solution.py:366
  99.6 1.6 %collective-permute-start.29 = (bf16[1,128,128]{2,1,0:T(8,128)(2,1)S(1)}, bf16[1,128,128]{2,1,0:T(8,128)(2,1)S(1)}, u32[]{:S(2)}, u32[]{:S(2)}) collective-permute-start(bf16[1,128,128]{2,1,0:T(8,128)(2,1)S(1)} %add_convert_fusion.3), channel_id=1, source_target_pairs={{0,6},{1,7},{2,4},{3,5},{4,2},{5,3},{6,0},{7,1},{8,14},{9,15},{10,... | collective-permute-start | bytes 98312 | tf_op jit(solution)/shard_map/ppermute | solution.py:366
  101.2 0.3 collective-permute-start.28
  101.5 1.6 %collective-permute-start.27 = (bf16[1,128,128]{2,1,0:T(8,128)(2,1)S(1)}, bf16[1,128,128]{2,1,0:T(8,128)(2,1)S(1)}, u32[]{:S(2)}, u32[]{:S(2)}) collective-permute-start(bf16[1,128,128]{2,1,0:T(8,128)(2,1)S(1)} %add_convert_fusion.3), channel_id=1, source_target_pairs={{0,2},{1,3},{2,0},{3,1},{4,6},{5,7},{6,4},{7,5},{8,10},{9,11},{10,... | collective-permute-start | bytes 98312 | tf_op jit(solution)/shard_map/ppermute | solution.py:366
  103.1 1.3 %collective-permute-done.29 = bf16[1,128,128]{2,1,0:T(8,128)(2,1)S(1)} collective-permute-done((bf16[1,128,128]{2,1,0:T(8,128)(2,1)S(1)}, bf16[1,128,128]{2,1,0:T(8,128)(2,1)S(1)}, u32[]{:S(2)}, u32[]{:S(2)}) %collective-permute-start.29) | collective-permute-done | bytes 32800 | tf_op jit(solution)/shard_map/ppermute | solution.py:366
  104.4 0.6 collective-permute-done.28
  105.1 0.3 collective-permute-done.27
  105.5 1.2 %collective-permute-done.30.other_ref = f32[1,128,128]{2,1,0:T(8,128)S(1)} collective-permute-done((f32[1,128,128]{2,1,0:T(8,128)S(1)}, f32[1,128,128]{2,1,0:T(8,128)S(1)}, u32[]{:S(2)}, u32[]{:S(2)}) %collective-permute-start.30) | collective-permute-done | bytes 65568 | tf_op jit(solution)/shard_map/ppermute | solution.py:366
  106.7 0.8 project_kernel.1
  107.5 1.2 collective-permute-start.31
  108.7 1.3 %collective-permute-start.32 = (bf16[32,2048]{1,0:T(8,128)(2,1)S(1)}, bf16[32,2048]{1,0:T(8,128)(2,1)S(1)}, u32[]{:S(2)}, u32[]{:S(2)}) collective-permute-start(bf16[32,2048]{1,0:T(8,128)(2,1)S(1)} %get-tuple-element.61), channel_id=1, source_target_pairs={{0,7},{1,6},{2,5},{3,4},{4,3},{5,2},{6,1},{7,0},{8,15},{9,14},{10,... | collective-permute-start | bytes 393224 | tf_op jit(solution)/shard_map/ppermute | solution.py:366
  110.0 1.6 %collective-permute-start.33 = (bf16[32,2048]{1,0:T(8,128)(2,1)S(1)}, bf16[32,2048]{1,0:T(8,128)(2,1)S(1)}, u32[]{:S(2)}, u32[]{:S(2)}) collective-permute-start(bf16[32,2048]{1,0:T(8,128)(2,1)S(1)} %get-tuple-element.62), channel_id=1, source_target_pairs={{0,2},{1,3},{2,0},{3,1},{4,6},{5,7},{6,4},{7,5},{8,10},{9,11},{10,... | collective-permute-start | bytes 393224 | tf_op jit(solution)/shard_map/ppermute | solution.py:366
  111.7 1.7 %collective-permute-start.35 = (bf16[32,2048]{1,0:T(8,128)(2,1)S(1)}, bf16[32,2048]{1,0:T(8,128)(2,1)S(1)}, u32[]{:S(2)}, u32[]{:S(2)}) collective-permute-start(bf16[32,2048]{1,0:T(8,128)(2,1)S(1)} %get-tuple-element.64), channel_id=1, source_target_pairs={{0,3},{1,2},{2,1},{3,0},{4,7},{5,6},{6,5},{7,4},{8,11},{9,10},{10,... | collective-permute-start | bytes 393224 | tf_op jit(solution)/shard_map/ppermute | solution.py:366
  113.4 1.4 %collective-permute-done.31.refs_1_ = bf16[32,2048]{1,0:T(8,128)(2,1)S(1)} collective-permute-done((bf16[32,2048]{1,0:T(8,128)(2,1)S(1)}, bf16[32,2048]{1,0:T(8,128)(2,1)S(1)}, u32[]{:S(2)}, u32[]{:S(2)}) %collective-permute-start.31) | collective-permute-done | bytes 131104 | tf_op jit(solution)/shard_map/ppermute | solution.py:366
  114.9 1.3 %collective-permute-done.32.refs_2_ = bf16[32,2048]{1,0:T(8,128)(2,1)S(1)} collective-permute-done((bf16[32,2048]{1,0:T(8,128)(2,1)S(1)}, bf16[32,2048]{1,0:T(8,128)(2,1)S(1)}, u32[]{:S(2)}, u32[]{:S(2)}) %collective-permute-start.32) | collective-permute-done | bytes 131104 | tf_op jit(solution)/shard_map/ppermute | solution.py:366
  116.2 1.3 %collective-permute-start.37 = (bf16[32,2048]{1,0:T(8,128)(2,1)S(1)}, bf16[32,2048]{1,0:T(8,128)(2,1)S(1)}, u32[]{:S(2)}, u32[]{:S(2)}) collective-permute-start(bf16[32,2048]{1,0:T(8,128)(2,1)S(1)} %get-tuple-element.66), channel_id=1, source_target_pairs={{0,1},{1,0},{2,3},{3,2},{4,5},{5,4},{6,7},{7,6},{8,9},{9,8},{10,11... | collective-permute-start | bytes 393224 | tf_op jit(solution)/shard_map/ppermute | solution.py:366
  117.5 3.3 %collective-permute-done.33.refs_3_ = bf16[32,2048]{1,0:T(8,128)(2,1)S(1)} collective-permute-done((bf16[32,2048]{1,0:T(8,128)(2,1)S(1)}, bf16[32,2048]{1,0:T(8,128)(2,1)S(1)}, u32[]{:S(2)}, u32[]{:S(2)}) %collective-permute-start.33) | collective-permute-done | bytes 131104 | tf_op jit(solution)/shard_map/ppermute | solution.py:366
  120.7 1.2 collective-permute-done.35.refs_5_
  122.0 0.4 collective-permute-done.36.refs_6_
  122.4 1.0 whole_kernel.1
  (36 shorter events, 1.1 us)
Async XLA Ops:
  0.0 1.2 copy-start
  1.3 7.9 %collective-permute-start = (bf16[32,2048]{1,0:T(8,128)(2,1)S(1)}, bf16[32,2048]{1,0:T(8,128)(2,1)S(1)}, u32[]{:S(2)}, u32[]{:S(2)}) collective-permute-start(bf16[32,2048]{1,0:T(8,128)(2,1)S(1)} %get-tuple-element.37), channel_id=1, source_target_pairs={{0,6},{1,7},{2,4},{3,5},{4,2},{5,3},{6,0},{7,1},{8,14},{9,15},{10,... | collective-permute-start | bytes 393224 | tf_op jit(solution)/shard_map/ppermute | solution.py:366
  5.3 6.8 %collective-permute-start.1 = (bf16[32,2048]{1,0:T(8,128)(2,1)S(1)}, bf16[32,2048]{1,0:T(8,128)(2,1)S(1)}, u32[]{:S(2)}, u32[]{:S(2)}) collective-permute-start(bf16[32,2048]{1,0:T(8,128)(2,1)S(1)} %get-tuple-element.38), channel_id=1, source_target_pairs={{0,7},{1,6},{2,5},{3,4},{4,3},{5,2},{6,1},{7,0},{8,15},{9,14},{10,... | collective-permute-start | bytes 393224 | tf_op jit(solution)/shard_map/ppermute | solution.py:366
  5.3 10.2 %collective-permute-start.2 = (bf16[32,2048]{1,0:T(8,128)(2,1)S(1)}, bf16[32,2048]{1,0:T(8,128)(2,1)S(1)}, u32[]{:S(2)}, u32[]{:S(2)}) collective-permute-start(bf16[32,2048]{1,0:T(8,128)(2,1)S(1)} %get-tuple-element.39), channel_id=1, source_target_pairs={{0,2},{1,3},{2,0},{3,1},{4,6},{5,7},{6,4},{7,5},{8,10},{9,11},{10,... | collective-permute-start | bytes 393224 | tf_op jit(solution)/shard_map/ppermute | solution.py:366
  6.4 9.1 %collective-permute-start.3 = (bf16[32,2048]{1,0:T(8,128)(2,1)S(1)}, bf16[32,2048]{1,0:T(8,128)(2,1)S(1)}, u32[]{:S(2)}, u32[]{:S(2)}) collective-permute-start(bf16[32,2048]{1,0:T(8,128)(2,1)S(1)} %get-tuple-element.40), channel_id=1, source_target_pairs={{0,4},{1,5},{2,6},{3,7},{4,0},{5,1},{6,2},{7,3},{8,12},{9,13},{10,... | collective-permute-start | bytes 393224 | tf_op jit(solution)/shard_map/ppermute | solution.py:366
  7.9 8.7 %collective-permute-start.4 = (bf16[32,2048]{1,0:T(8,128)(2,1)S(1)}, bf16[32,2048]{1,0:T(8,128)(2,1)S(1)}, u32[]{:S(2)}, u32[]{:S(2)}) collective-permute-start(bf16[32,2048]{1,0:T(8,128)(2,1)S(1)} %get-tuple-element.41), channel_id=1, source_target_pairs={{0,3},{1,2},{2,1},{3,0},{4,7},{5,6},{6,5},{7,4},{8,11},{9,10},{10,... | collective-permute-start | bytes 393224 | tf_op jit(solution)/shard_map/ppermute | solution.py:366
  9.2 8.1 %collective-permute-start.5 = (bf16[32,2048]{1,0:T(8,128)(2,1)S(1)}, bf16[32,2048]{1,0:T(8,128)(2,1)S(1)}, u32[]{:S(2)}, u32[]{:S(2)}) collective-permute-start(bf16[32,2048]{1,0:T(8,128)(2,1)S(1)} %get-tuple-element.42), channel_id=1, source_target_pairs={{0,5},{1,4},{2,7},{3,6},{4,1},{5,0},{6,3},{7,2},{8,13},{9,12},{10,... | collective-permute-start | bytes 393224 | tf_op jit(solution)/shard_map/ppermute | solution.py:366
  12.0 5.3 %collective-permute-start.6 = (bf16[32,2048]{1,0:T(8,128)(2,1)S(1)}, bf16[32,2048]{1,0:T(8,128)(2,1)S(1)}, u32[]{:S(2)}, u32[]{:S(2)}) collective-permute-start(bf16[32,2048]{1,0:T(8,128)(2,1)S(1)} %get-tuple-element.43), channel_id=1, source_target_pairs={{0,1},{1,0},{2,3},{3,2},{4,5},{5,4},{6,7},{7,6},{8,9},{9,8},{10,11... | collective-permute-start | bytes 393224 | tf_op jit(solution)/shard_map/ppermute | solution.py:366
  17.8 1.4 %collective-permute-start.7 = (f32[3,64,128]{2,1,0:T(8,128)S(1)}, f32[3,64,128]{2,1,0:T(8,128)S(1)}, u32[]{:S(2)}, u32[]{:S(2)}) collective-permute-start(f32[3,64,128]{2,1,0:T(8,128)S(1)} %get-tuple-element.46), channel_id=1, source_target_pairs={{0,1},{1,0},{2,3},{3,2},{4,5},{5,4},{6,7},{7,6},{8,9},{9,8},{10,11... | collective-permute-start | bytes 294920 | tf_op jit(solution)/shard_map/ppermute | solution.py:366
  19.2 5.1 %collective-permute-start.10 = (bf16[3,64,128]{2,1,0:T(8,128)(2,1)S(1)}, bf16[3,64,128]{2,1,0:T(8,128)(2,1)S(1)}, u32[]{:S(2)}, u32[]{:S(2)}) collective-permute-start(bf16[3,64,128]{2,1,0:T(8,128)(2,1)S(1)} %add_convert_fusion.2), channel_id=1, source_target_pairs={{0,6},{1,7},{2,4},{3,5},{4,2},{5,3},{6,0},{7,1},{8,14},{9,15},{10,... | collective-permute-start | bytes 147464 | tf_op jit(solution)/shard_map/ppermute | solution.py:366
  21.8 4.1 %collective-permute-start.9 = (bf16[3,64,128]{2,1,0:T(8,128)(2,1)S(1)}, bf16[3,64,128]{2,1,0:T(8,128)(2,1)S(1)}, u32[]{:S(2)}, u32[]{:S(2)}) collective-permute-start(bf16[3,64,128]{2,1,0:T(8,128)(2,1)S(1)} %add_convert_fusion.2), channel_id=1, source_target_pairs={{0,4},{1,5},{2,6},{3,7},{4,0},{5,1},{6,2},{7,3},{8,12},{9,13},{10,... | collective-permute-start | bytes 147464 | tf_op jit(solution)/shard_map/ppermute | solution.py:366
  22.2 4.1 %collective-permute-start.8 = (bf16[3,64,128]{2,1,0:T(8,128)(2,1)S(1)}, bf16[3,64,128]{2,1,0:T(8,128)(2,1)S(1)}, u32[]{:S(2)}, u32[]{:S(2)}) collective-permute-start(bf16[3,64,128]{2,1,0:T(8,128)(2,1)S(1)} %add_convert_fusion.2), channel_id=1, source_target_pairs={{0,2},{1,3},{2,0},{3,1},{4,6},{5,7},{6,4},{7,5},{8,10},{9,11},{10,... | collective-permute-start | bytes 147464 | tf_op jit(solution)/shard_map/ppermute | solution.py:366
  26.4 1.4 %collective-permute-start.11 = (f32[3,64,128]{2,1,0:T(8,128)S(1)}, f32[3,64,128]{2,1,0:T(8,128)S(1)}, u32[]{:S(2)}, u32[]{:S(2)}) collective-permute-start(f32[3,64,128]{2,1,0:T(8,128)S(1)} %add_add_fusion.mine_ref), channel_id=1, source_target_pairs={{0,1},{1,0},{2,3},{3,2},{4,5},{5,4},{6,7},{7,6},{8,9},{9,8},{10,11... | collective-permute-start | bytes 294920 | tf_op jit(solution)/shard_map/ppermute | solution.py:366
  32.5 8.3 %collective-permute-start.12 = (bf16[128,512]{1,0:T(8,128)(2,1)S(1)}, bf16[128,512]{1,0:T(8,128)(2,1)S(1)}, u32[]{:S(2)}, u32[]{:S(2)}) collective-permute-start(bf16[128,512]{1,0:T(8,128)(2,1)S(1)} %get-tuple-element.48), channel_id=1, source_target_pairs={{0,24},{1,25},{2,26},{3,27},{4,28},{5,29},{6,30},{7,31},{8,16},{9,... | collective-permute-start | bytes 393224 | tf_op jit(solution)/shard_map/ppermute | solution.py:366
  36.2 11.4 %collective-permute-start.13 = (bf16[128,512]{1,0:T(8,128)(2,1)S(1)}, bf16[128,512]{1,0:T(8,128)(2,1)S(1)}, u32[]{:S(2)}, u32[]{:S(2)}) collective-permute-start(bf16[128,512]{1,0:T(8,128)(2,1)S(1)} %get-tuple-element.49), channel_id=1, source_target_pairs={{0,16},{1,17},{2,18},{3,19},{4,20},{5,21},{6,22},{7,23},{8,24},{9,... | collective-permute-start | bytes 393224 | tf_op jit(solution)/shard_map/ppermute | solution.py:366
  36.2 11.4 %collective-permute-start.14 = (bf16[128,512]{1,0:T(8,128)(2,1)S(1)}, bf16[128,512]{1,0:T(8,128)(2,1)S(1)}, u32[]{:S(2)}, u32[]{:S(2)}) collective-permute-start(bf16[128,512]{1,0:T(8,128)(2,1)S(1)} %get-tuple-element.50), channel_id=1, source_target_pairs={{0,8},{1,9},{2,10},{3,11},{4,12},{5,13},{6,14},{7,15},{8,0},{9,1},... | collective-permute-start | bytes 393224 | tf_op jit(solution)/shard_map/ppermute | solution.py:366
  48.0 1.5 %collective-permute-start.15 = (f32[6,64,128]{2,1,0:T(8,128)S(1)}, f32[6,64,128]{2,1,0:T(8,128)S(1)}, u32[]{:S(2)}, u32[]{:S(2)}) collective-permute-start(f32[6,64,128]{2,1,0:T(8,128)S(1)} %get-tuple-element.52), channel_id=1, source_target_pairs={{0,1},{1,0},{2,3},{3,2},{4,5},{5,4},{6,7},{7,6},{8,9},{9,8},{10,11... | collective-permute-start | bytes 589832 | tf_op jit(solution)/shard_map/ppermute | solution.py:366
  49.6 6.4 %collective-permute-start.18 = (bf16[6,64,128]{2,1,0:T(8,128)(2,1)S(1)}, bf16[6,64,128]{2,1,0:T(8,128)(2,1)S(1)}, u32[]{:S(2)}, u32[]{:S(2)}) collective-permute-start(bf16[6,64,128]{2,1,0:T(8,128)(2,1)S(1)} %add_convert_fusion.1), channel_id=1, source_target_pairs={{0,6},{1,7},{2,4},{3,5},{4,2},{5,3},{6,0},{7,1},{8,14},{9,15},{10,... | collective-permute-start | bytes 294920 | tf_op jit(solution)/shard_map/ppermute | solution.py:366
  51.1 6.3 %collective-permute-start.17 = (bf16[6,64,128]{2,1,0:T(8,128)(2,1)S(1)}, bf16[6,64,128]{2,1,0:T(8,128)(2,1)S(1)}, u32[]{:S(2)}, u32[]{:S(2)}) collective-permute-start(bf16[6,64,128]{2,1,0:T(8,128)(2,1)S(1)} %add_convert_fusion.1), channel_id=1, source_target_pairs={{0,4},{1,5},{2,6},{3,7},{4,0},{5,1},{6,2},{7,3},{8,12},{9,13},{10,... | collective-permute-start | bytes 294920 | tf_op jit(solution)/shard_map/ppermute | solution.py:366
  51.7 6.0 %collective-permute-start.16 = (bf16[6,64,128]{2,1,0:T(8,128)(2,1)S(1)}, bf16[6,64,128]{2,1,0:T(8,128)(2,1)S(1)}, u32[]{:S(2)}, u32[]{:S(2)}) collective-permute-start(bf16[6,64,128]{2,1,0:T(8,128)(2,1)S(1)} %add_convert_fusion.1), channel_id=1, source_target_pairs={{0,2},{1,3},{2,0},{3,1},{4,6},{5,7},{6,4},{7,5},{8,10},{9,11},{10,... | collective-permute-start | bytes 294920 | tf_op jit(solution)/shard_map/ppermute | solution.py:366
  57.7 8.0 %collective-permute-start.21 = (bf16[7,64,128]{2,1,0:T(8,128)(2,1)S(1)}, bf16[7,64,128]{2,1,0:T(8,128)(2,1)S(1)}, u32[]{:S(2)}, u32[]{:S(2)}) collective-permute-start(bf16[7,64,128]{2,1,0:T(8,128)(2,1)S(1)} %pad_maximum_fusion), channel_id=1, source_target_pairs={{0,24},{1,25},{2,26},{3,27},{4,28},{5,29},{6,30},{7,31},{8,16},{9,... | collective-permute-start | bytes 344072 | tf_op jit(solution)/shard_map/ppermute | solution.py:366
  60.3 9.1 %collective-permute-start.20 = (bf16[7,64,128]{2,1,0:T(8,128)(2,1)S(1)}, bf16[7,64,128]{2,1,0:T(8,128)(2,1)S(1)}, u32[]{:S(2)}, u32[]{:S(2)}) collective-permute-start(bf16[7,64,128]{2,1,0:T(8,128)(2,1)S(1)} %pad_maximum_fusion), channel_id=1, source_target_pairs={{0,16},{1,17},{2,18},{3,19},{4,20},{5,21},{6,22},{7,23},{8,24},{9,... | collective-permute-start | bytes 344072 | tf_op jit(solution)/shard_map/ppermute | solution.py:366
  60.3 9.1 %collective-permute-start.19 = (bf16[7,64,128]{2,1,0:T(8,128)(2,1)S(1)}, bf16[7,64,128]{2,1,0:T(8,128)(2,1)S(1)}, u32[]{:S(2)}, u32[]{:S(2)}) collective-permute-start(bf16[7,64,128]{2,1,0:T(8,128)(2,1)S(1)} %pad_maximum_fusion), channel_id=1, source_target_pairs={{0,8},{1,9},{2,10},{3,11},{4,12},{5,13},{6,14},{7,15},{8,0},{9,1},... | collective-permute-start | bytes 344072 | tf_op jit(solution)/shard_map/ppermute | solution.py:366
  69.5 1.7 %collective-permute-start.22 = (f32[10,64,128]{2,1,0:T(8,128)S(1)}, f32[10,64,128]{2,1,0:T(8,128)S(1)}, u32[]{:S(2)}, u32[]{:S(2)}) collective-permute-start(f32[10,64,128]{2,1,0:T(8,128)S(1)} %convert_dynamic-update-slice_fusion.mine_ref), channel_id=1, source_target_pairs={{0,1},{1,0},{2,3},{3,2},{4,5},{5,4},{6,7},{7,6},{8,9},{9,8},{10,11... | collective-permute-start | bytes 983048 | tf_op jit(solution)/shard_map/ppermute | solution.py:366
  83.2 8.3 %collective-permute-start.25 = (bf16[128,512]{1,0:T(8,128)(2,1)S(1)}, bf16[128,512]{1,0:T(8,128)(2,1)S(1)}, u32[]{:S(2)}, u32[]{:S(2)}) collective-permute-start(bf16[128,512]{1,0:T(8,128)(2,1)S(1)} %get-tuple-element.56.refs_0_), channel_id=1, source_target_pairs={{0,24},{1,25},{2,26},{3,27},{4,28},{5,29},{6,30},{7,31},{8,16},{9,... | collective-permute-start | bytes 393224 | tf_op jit(solution)/shard_map/ppermute | solution.py:366
  85.8 11.6 %collective-permute-start.24 = (bf16[128,512]{1,0:T(8,128)(2,1)S(1)}, bf16[128,512]{1,0:T(8,128)(2,1)S(1)}, u32[]{:S(2)}, u32[]{:S(2)}) collective-permute-start(bf16[128,512]{1,0:T(8,128)(2,1)S(1)} %get-tuple-element.56.refs_0_), channel_id=1, source_target_pairs={{0,16},{1,17},{2,18},{3,19},{4,20},{5,21},{6,22},{7,23},{8,24},{9,... | collective-permute-start | bytes 393224 | tf_op jit(solution)/shard_map/ppermute | solution.py:366
  85.8 11.6 %collective-permute-start.23 = (bf16[128,512]{1,0:T(8,128)(2,1)S(1)}, bf16[128,512]{1,0:T(8,128)(2,1)S(1)}, u32[]{:S(2)}, u32[]{:S(2)}) collective-permute-start(bf16[128,512]{1,0:T(8,128)(2,1)S(1)} %get-tuple-element.56.refs_0_), channel_id=1, source_target_pairs={{0,8},{1,9},{2,10},{3,11},{4,12},{5,13},{6,14},{7,15},{8,0},{9,1},... | collective-permute-start | bytes 393224 | tf_op jit(solution)/shard_map/ppermute | solution.py:366
  98.2 1.3 %collective-permute-start.26 = (f32[1,128,128]{2,1,0:T(8,128)S(1)}, f32[1,128,128]{2,1,0:T(8,128)S(1)}, u32[]{:S(2)}, u32[]{:S(2)}) collective-permute-start(f32[1,128,128]{2,1,0:T(8,128)S(1)} %get-tuple-element.58), channel_id=1, source_target_pairs={{0,1},{1,0},{2,3},{3,2},{4,5},{5,4},{6,7},{7,6},{8,9},{9,8},{10,11... | collective-permute-start | bytes 196616 | tf_op jit(solution)/shard_map/ppermute | solution.py:366
  99.6 4.9 %collective-permute-start.29 = (bf16[1,128,128]{2,1,0:T(8,128)(2,1)S(1)}, bf16[1,128,128]{2,1,0:T(8,128)(2,1)S(1)}, u32[]{:S(2)}, u32[]{:S(2)}) collective-permute-start(bf16[1,128,128]{2,1,0:T(8,128)(2,1)S(1)} %add_convert_fusion.3), channel_id=1, source_target_pairs={{0,6},{1,7},{2,4},{3,5},{4,2},{5,3},{6,0},{7,1},{8,14},{9,15},{10,... | collective-permute-start | bytes 98312 | tf_op jit(solution)/shard_map/ppermute | solution.py:366
  101.2 3.9 %collective-permute-start.28 = (bf16[1,128,128]{2,1,0:T(8,128)(2,1)S(1)}, bf16[1,128,128]{2,1,0:T(8,128)(2,1)S(1)}, u32[]{:S(2)}, u32[]{:S(2)}) collective-permute-start(bf16[1,128,128]{2,1,0:T(8,128)(2,1)S(1)} %add_convert_fusion.3), channel_id=1, source_target_pairs={{0,4},{1,5},{2,6},{3,7},{4,0},{5,1},{6,2},{7,3},{8,12},{9,13},{10,... | collective-permute-start | bytes 98312 | tf_op jit(solution)/shard_map/ppermute | solution.py:366
  101.5 3.9 %collective-permute-start.27 = (bf16[1,128,128]{2,1,0:T(8,128)(2,1)S(1)}, bf16[1,128,128]{2,1,0:T(8,128)(2,1)S(1)}, u32[]{:S(2)}, u32[]{:S(2)}) collective-permute-start(bf16[1,128,128]{2,1,0:T(8,128)(2,1)S(1)} %add_convert_fusion.3), channel_id=1, source_target_pairs={{0,2},{1,3},{2,0},{3,1},{4,6},{5,7},{6,4},{7,5},{8,10},{9,11},{10,... | collective-permute-start | bytes 98312 | tf_op jit(solution)/shard_map/ppermute | solution.py:366
  105.4 1.3 %collective-permute-start.30 = (f32[1,128,128]{2,1,0:T(8,128)S(1)}, f32[1,128,128]{2,1,0:T(8,128)S(1)}, u32[]{:S(2)}, u32[]{:S(2)}) collective-permute-start(f32[1,128,128]{2,1,0:T(8,128)S(1)} %add_add_fusion.1.mine_ref), channel_id=1, source_target_pairs={{0,1},{1,0},{2,3},{3,2},{4,5},{5,4},{6,7},{7,6},{8,9},{9,8},{10,11... | collective-permute-start | bytes 196616 | tf_op jit(solution)/shard_map/ppermute | solution.py:366
  107.5 7.3 %collective-permute-start.31 = (bf16[32,2048]{1,0:T(8,128)(2,1)S(1)}, bf16[32,2048]{1,0:T(8,128)(2,1)S(1)}, u32[]{:S(2)}, u32[]{:S(2)}) collective-permute-start(bf16[32,2048]{1,0:T(8,128)(2,1)S(1)} %get-tuple-element.60), channel_id=1, source_target_pairs={{0,6},{1,7},{2,4},{3,5},{4,2},{5,3},{6,0},{7,1},{8,14},{9,15},{10,... | collective-permute-start | bytes 393224 | tf_op jit(solution)/shard_map/ppermute | solution.py:366
  108.7 7.4 %collective-permute-start.32 = (bf16[32,2048]{1,0:T(8,128)(2,1)S(1)}, bf16[32,2048]{1,0:T(8,128)(2,1)S(1)}, u32[]{:S(2)}, u32[]{:S(2)}) collective-permute-start(bf16[32,2048]{1,0:T(8,128)(2,1)S(1)} %get-tuple-element.61), channel_id=1, source_target_pairs={{0,7},{1,6},{2,5},{3,4},{4,3},{5,2},{6,1},{7,0},{8,15},{9,14},{10,... | collective-permute-start | bytes 393224 | tf_op jit(solution)/shard_map/ppermute | solution.py:366
  110.0 10.7 %collective-permute-start.33 = (bf16[32,2048]{1,0:T(8,128)(2,1)S(1)}, bf16[32,2048]{1,0:T(8,128)(2,1)S(1)}, u32[]{:S(2)}, u32[]{:S(2)}) collective-permute-start(bf16[32,2048]{1,0:T(8,128)(2,1)S(1)} %get-tuple-element.62), channel_id=1, source_target_pairs={{0,2},{1,3},{2,0},{3,1},{4,6},{5,7},{6,4},{7,5},{8,10},{9,11},{10,... | collective-permute-start | bytes 393224 | tf_op jit(solution)/shard_map/ppermute | solution.py:366
  111.6 9.1 %collective-permute-start.34 = (bf16[32,2048]{1,0:T(8,128)(2,1)S(1)}, bf16[32,2048]{1,0:T(8,128)(2,1)S(1)}, u32[]{:S(2)}, u32[]{:S(2)}) collective-permute-start(bf16[32,2048]{1,0:T(8,128)(2,1)S(1)} %get-tuple-element.63), channel_id=1, source_target_pairs={{0,4},{1,5},{2,6},{3,7},{4,0},{5,1},{6,2},{7,3},{8,12},{9,13},{10,... | collective-permute-start | bytes 393224 | tf_op jit(solution)/shard_map/ppermute | solution.py:366
  111.7 10.3 %collective-permute-start.35 = (bf16[32,2048]{1,0:T(8,128)(2,1)S(1)}, bf16[32,2048]{1,0:T(8,128)(2,1)S(1)}, u32[]{:S(2)}, u32[]{:S(2)}) collective-permute-start(bf16[32,2048]{1,0:T(8,128)(2,1)S(1)} %get-tuple-element.64), channel_id=1, source_target_pairs={{0,3},{1,2},{2,1},{3,0},{4,7},{5,6},{6,5},{7,4},{8,11},{9,10},{10,... | collective-permute-start | bytes 393224 | tf_op jit(solution)/shard_map/ppermute | solution.py:366
  114.8 7.6 %collective-permute-start.36 = (bf16[32,2048]{1,0:T(8,128)(2,1)S(1)}, bf16[32,2048]{1,0:T(8,128)(2,1)S(1)}, u32[]{:S(2)}, u32[]{:S(2)}) collective-permute-start(bf16[32,2048]{1,0:T(8,128)(2,1)S(1)} %get-tuple-element.65), channel_id=1, source_target_pairs={{0,5},{1,4},{2,7},{3,6},{4,1},{5,0},{6,3},{7,2},{8,13},{9,12},{10,... | collective-permute-start | bytes 393224 | tf_op jit(solution)/shard_map/ppermute | solution.py:366
  116.2 6.3 %collective-permute-start.37 = (bf16[32,2048]{1,0:T(8,128)(2,1)S(1)}, bf16[32,2048]{1,0:T(8,128)(2,1)S(1)}, u32[]{:S(2)}, u32[]{:S(2)}) collective-permute-start(bf16[32,2048]{1,0:T(8,128)(2,1)S(1)} %get-tuple-element.66), channel_id=1, source_target_pairs={{0,1},{1,0},{2,3},{3,2},{4,5},{5,4},{6,7},{7,6},{8,9},{9,8},{10,11... | collective-permute-start | bytes 393224 | tf_op jit(solution)/shard_map/ppermute | solution.py:366

commit v4 on v3

--- a/solution.py
+++ b/solution.py
@@ -13,7 +13,7 @@
 TILE = 8
 PANEL = 64
 PLANE_ORDER = (0, 6, 7, 2, 4, 3, 5, 1)
-TREE_ORDER = (0, 3, 2, 1)
+MIDDLE = (1, 2)
 PIVOT_SHARE = 2e-4
 
 precise = lax.Precision.HIGHEST
@@ -164,12 +164,12 @@
     return [frame_ref[...].astype(bf16) for _, _, frame_ref in work]
 
 
-def until_sound(sound_ref, attempt):
+def until_sound(sound_ref, attempt, idle=False):
     def once(mode):
         sound_ref[...] = jnp.ones(sound_ref.shape, f32)
         attempt(mode == 1)
         sound = jnp.min(sound_ref[...]) > 0.5
-        return jnp.where(jnp.logical_or(mode == 1, sound), 2, 1)
+        return jnp.where(jnp.logical_or(jnp.logical_or(mode == 1, idle), sound), 2, 1)
 
     lax.while_loop(lambda mode: mode < 2, once, jnp.int32(0))
 
@@ -200,6 +200,14 @@
 
 def chunk(z, m, width):
     return pl.ds(pl.multiple_of((z ^ m) * width, width), width)
+
+
+def in_middle(z):
+    return jnp.logical_or(z == MIDDLE[0], z == MIDDLE[1])
+
+
+def side(z, far, width):
+    return pl.ds(pl.multiple_of(((z // 2) ^ far) * width, width), width)
 
 
 def member(pos_ref):
@@ -232,17 +240,17 @@
 
 
 def node_kernel(pos_ref, mine_ref, other_ref, rows_ref, *refs):
-    nodes, low_ref, sound_ref, work = refs[:PLANES], refs[PLANES], refs[PLANES + 1], refs[PLANES + 2 :]
+    sides, low_ref, sound_ref, work = refs[:2], refs[2], refs[3], refs[4:]
     core, z = place(pos_ref)
-    width = nodes[0].shape[1]
+    width = sides[0].shape[1]
 
     def attempt(careful):
         gram = plane_gram(mine_ref, other_ref, core)
         scale = unit_scale([gram[:RANK, :RANK], gram[RANK:, RANK:]])
         (low,) = leading_spaces([gram], scale, [work], careful, sound_ref)
         low_ref[...] = low
-        for ref, m in zip(nodes, TREE_ORDER):
-            ref[...] = dot_low(low, rows_ref[:, chunk(z, m, width)], 0, 0).astype(bf16)
+        for far, ref in enumerate(sides):
+            ref[...] = dot_low(low, rows_ref[:, side(z, far, width)], 0, 0).astype(bf16)
 
     until_sound(sound_ref, attempt)
 
@@ -264,7 +272,7 @@
 def cross_kernel(pos_ref, *refs):
     nodes, (mine_ref, theirs_ref, all_ref) = refs[:PLANES], refs[PLANES:]
     core, z = place(pos_ref)
-    for ref, m in zip(nodes, TREE_ORDER):
+    for m, ref in enumerate(nodes):
         all_ref[z ^ m] = ref[...]
     split([dot_low(all_ref[j], all_ref[i], 1, 1) for i, j in PAIRS], core, mine_ref, theirs_ref)
 
@@ -273,7 +281,7 @@
     nodes, (top_ref, gram_ref, low_ref), refs = refs[:PLANES], refs[PLANES : PLANES + 3], refs[PLANES + 3 :]
     all_ref, diag_ref, sound_ref, work = refs[0], refs[1], refs[2], [refs[3:6], refs[6:9]]
     core, z = place(pos_ref)
-    for ref, m in zip(nodes, TREE_ORDER):
+    for m, ref in enumerate(nodes):
         all_ref[z ^ m] = ref[...]
         diag_ref[z ^ m] = joined(mine_ref, other_ref, core, len(PAIRS) + m)
 
@@ -301,35 +309,40 @@
         low_ref[...] = low
         top_ref[...] = dot_low(low, jnp.concatenate([node_a, node_b], 0), 0, 0).astype(bf16)
 
-    until_sound(sound_ref, attempt)
+    until_sound(sound_ref, attempt, jnp.logical_not(in_middle(z)))
 
 
 def factor_kernel(gram_ref, low_ref, factor_ref):
     factor_ref[...] = inverse_factors([reduced(gram_ref[...], low_ref[...])])[0][0]
 
 
-def coeffs_kernel(pos_ref, rows_ref, factor_ref, *refs):
+def halves_of_top(z, own_ref, near_ref, far_outer_ref, far_ref):
+    middle = in_middle(z)
+    return jnp.where(middle, own_ref[...], near_ref[...]), jnp.where(middle, far_ref[...], far_outer_ref[...])
+
+
+def coeffs_kernel(pos_ref, rows_ref, *refs):
     tops, (mine_ref, theirs_ref) = refs[:PLANES], refs[PLANES:]
     core, z = place(pos_ref)
-    width = tops[0].shape[1]
-    total = None
-    for m, ref in enumerate(tops):
-        part = dot_low(rows_ref[:, chunk(z, m, width)], ref[...], 1, 1)
-        total = part if total is None else total + part
-    split([dot(total, factor_ref[...], 1, 1)], core, mine_ref, theirs_ref)
-
-
-def project_kernel(pos_ref, mine_ref, other_ref, factor_ref, *refs):
+    near, far = halves_of_top(z, *tops)
+    width = near.shape[1]
+    total = dot_low(rows_ref[:, side(z, 0, width)], near, 1, 1)
+    total = total + dot_low(rows_ref[:, side(z, 1, width)], far, 1, 1)
+    split([total], core, mine_ref, theirs_ref)
+
+
+def project_kernel(pos_ref, mine_ref, other_ref, own_factor_ref, factor_ref, *refs):
     tops, outs, solved_ref = refs[:PLANES], refs[PLANES:-1], refs[-1]
     core, z = place(pos_ref)
-    height, width = outs[0].shape[0], tops[0].shape[1]
-    solved_ref[...] = dot(joined(mine_ref, other_ref, core, 0), factor_ref[...], 1, 0)
+    factor = jnp.where(in_middle(z), own_factor_ref[...], factor_ref[...])
+    height = outs[0].shape[0]
+    solved_ref[...] = dot(dot(joined(mine_ref, other_ref, core, 0), factor, 1, 1), factor, 1, 0)
     solved = [solved_ref[chunk(member(pos_ref), m, height), :] for m in PLANE_ORDER]
     solved = jnp.concatenate(solved, 0).astype(bf16)
-    for m, ref in enumerate(tops):
-        made = dot_low(solved, ref[...], 1, 0).astype(bf16)
+    for far, top in enumerate(halves_of_top(z, *tops)):
+        made = dot_low(solved, top, 1, 0).astype(bf16)
         for k in range(PLANE):
-            outs[k][:, chunk(z, m, width)] = made[k * height : (k + 1) * height, :]
+            outs[k][:, side(z, far, top.shape[1])] = made[k * height : (k + 1) * height, :]
 
 
 def whole_kernel(pos_ref, *refs):
@@ -368,6 +381,10 @@
     def swap_all(parts, order, unit=1):
         return [x if m == 0 else swap(x, unit * m) for x, m in zip(parts, order)]
 
+    def send(x, apart, from_middle):
+        starts = [i for i in range(count) if (i // PLANE % PLANES in MIDDLE) == from_middle]
+        return lax.ppermute(x, "cols", [(i, i ^ apart * PLANE) for i in starts])
+
     def sum4(parts):
         parts = [p.astype(f32) for p in parts]
         return (parts[0] + parts[1]) + (parts[2] + parts[3])
@@ -377,7 +394,7 @@
 
     block, total = mortality.shape
     height, width = block * PLANE, total // PLANE
-    part = width // PLANES
+    part = width // len(MIDDLE)
     half = RANK // 2
 
     parts = kernel(parts_kernel, [((block, width), bf16)] * PLANE, pos, mortality)
@@ -387,13 +404,13 @@
     )
     mine = plane_sum(mine, theirs)
     other = swap(mine, 1)
-    *nodes, low = kernel(
+    near, far, low = kernel(
         node_kernel,
-        [((RANK, part), bf16)] * PLANES + [((2 * RANK, RANK), bf16)],
+        [((RANK, part), bf16)] * 2 + [((2 * RANK, RANK), bf16)],
         pos, mine, other, rows,
         scratch=sound_shape + work_shapes,
     )
-    nodes = swap_all(nodes, TREE_ORDER, PLANE)
+    nodes = [near, send(near, 1, False), send(far, 2, False), send(far, 3, True)]
     (diag,) = kernel(diag_kernel, [((1, half, RANK), bf16)], pos, mine, other, low)
 
     mine, theirs = kernel(
@@ -403,8 +420,12 @@
         scratch=[pltpu.VMEM((PLANES, RANK, part), bf16)],
     )
     mine = plane_sum(mine, theirs)
-    both = swap_all([jnp.concatenate([mine.astype(bf16), diag], 0)] * PLANES, range(PLANES), PLANE)
-    mine = jnp.concatenate([sum4([x[: len(PAIRS)] for x in both])] + [x[len(PAIRS) :].astype(f32) for x in both], 0)
+    diags = [diag, send(diag, 1, False), send(diag, 2, False)]
+    mine, diags = lax.optimization_barrier((mine, diags))
+    both = jnp.concatenate([mine.astype(bf16), diags[0]], 0)
+    beyond = send(both, 3, True)
+    mine = both[: len(PAIRS)].astype(f32) + beyond[: len(PAIRS)].astype(f32)
+    mine = jnp.concatenate([mine] + [x.astype(f32) for x in diags + [beyond[len(PAIRS) :]]], 0)
     top, gram, low = kernel(
         top_kernel,
         [((RANK, part), bf16), ((2 * RANK, 2 * RANK), f32), ((2 * RANK, RANK), bf16)],
@@ -413,15 +434,18 @@
         + sound_shape
         + work_shapes * 2,
     )
-    tops = swap_all([top] * PLANES, range(PLANES), PLANE)
+    tops = [top, send(top, 1, True), send(top, 2, True), send(top, 3, True)]
     (factor,) = kernel(factor_kernel, [((RANK, RANK), f32)], gram, low, scalar=False)
 
-    mine, theirs = kernel(coeffs_kernel, [((1, height // 2, RANK), f32)] * 2, pos, rows, factor, *tops)
+    near_factor = send(factor, 1, True)
+    factor, tops = lax.optimization_barrier((factor, tops))
+
+    mine, theirs = kernel(coeffs_kernel, [((1, height // 2, RANK), f32)] * 2, pos, rows, *tops)
     mine = plane_sum(mine, theirs)
     outs = kernel(
         project_kernel,
         [((block, width), bf16)] * PLANE,
-        pos, mine, swap(mine, 1), factor, *tops,
+        pos, mine, swap(mine, 1), factor, near_factor, *tops,
         scratch=[pltpu.VMEM((height, RANK), f32)],
     )
     (result,) = kernel(whole_kernel, [((block, total), bf16)], pos, *swap_all(outs, PLANE_ORDER))

time: 124 us -> 133 us (1.073)
  starting transfers between devices: 38.9 us -> 45.4 us
  waiting for transfers between devices: 58.6 us -> 61.1 us
    ppermute x0 -> x10, waiting for transfers between devices: none -> 33 us  [send(): return lax.ppermute(x, 'cols', [(i, i ^ apart * PLANE) for i in starts])]
    ppermute x38 -> x29, waiting for transfers between devices: 58.6 us -> 28.1 us  [swap(): return lax.ppermute(x, 'cols', [(i, i ^ apart) for i in range(count)])]
    ppermute x0 -> x10, starting transfers between devices: none -> 20.6 us  [send(): return lax.ppermute(x, 'cols', [(i, i ^ apart * PLANE) for i in starts])]
    ppermute x38 -> x29, starting transfers between devices: 38.9 us -> 24.8 us  [swap(): return lax.ppermute(x, 'cols', [(i, i ^ apart) for i in range(count)])]
  transfers between devices with their start and end apart: 38 -> 39, of which waited for: 31 -> 25; matrix products, arithmetic and copies ran while one was open for 0% -> 0% of each run, Pallas kernels for 3% -> 3%
where the time goes in v4:
time: 133 us; the launch traced here: 132 us
  waiting for transfers between devices  61.1 us (46%)
  starting transfers between devices  45.4 us (34%)
  Pallas kernels  24.2 us (18%)
    ppermute x10, waiting for transfers between devices, send(): return lax.ppermute(x, 'cols', [(i, i ^ apart * PLANE) for i in starts])  33 us
    ppermute x29, waiting for transfers between devices, swap(): return lax.ppermute(x, 'cols', [(i, i ^ apart) for i in range(count)])  28.1 us
    ppermute x29, starting transfers between devices, swap(): return lax.ppermute(x, 'cols', [(i, i ^ apart) for i in range(count)])  24.8 us
    pallas_call x10, Pallas kernels, kernel(): pl.pallas_call(fn, out_shape=[jax.ShapeDtypeStruct(s, d) for s, d in shap...  24.2 us
    ppermute x10, starting transfers between devices, send(): return lax.ppermute(x, 'cols', [(i, i ^ apart * PLANE) for i in starts])  20.6 us
  transfers between devices with their start and end apart: 39, of which 25 were waited for; matrix products, arithmetic and copies ran while one was open for 0% of the time, Pallas kernels for 3%

profile of v4, /device:TPU:0, one launch (start us, length us, event | category | flops | bytes accessed | tf_op | source)
XLA Modules:
  0.0 132.4 jit_solution(11150380395784166015)
XLA Ops:
  0.0 1.2 copy-done
  1.3 4.0 %collective-permute-start = (bf16[32,2048]{1,0:T(8,128)(2,1)S(1)}, bf16[32,2048]{1,0:T(8,128)(2,1)S(1)}, u32[]{:S(2)}, u32[]{:S(2)}) collective-permute-start(bf16[32,2048]{1,0:T(8,128)(2,1)S(1)} %get-tuple-element.44), channel_id=1, source_target_pairs={{0,6},{1,7},{2,4},{3,5},{4,2},{5,3},{6,0},{7,1},{8,14},{9,15},{10,... | collective-permute-start | bytes 393224 | tf_op jit(solution)/shard_map/ppermute | solution.py:379
  5.3 1.1 collective-permute-start.2
  6.4 1.5 %collective-permute-start.3 = (bf16[32,2048]{1,0:T(8,128)(2,1)S(1)}, bf16[32,2048]{1,0:T(8,128)(2,1)S(1)}, u32[]{:S(2)}, u32[]{:S(2)}) collective-permute-start(bf16[32,2048]{1,0:T(8,128)(2,1)S(1)} %get-tuple-element.47), channel_id=1, source_target_pairs={{0,4},{1,5},{2,6},{3,7},{4,0},{5,1},{6,2},{7,3},{8,12},{9,13},{10,... | collective-permute-start | bytes 393224 | tf_op jit(solution)/shard_map/ppermute | solution.py:379
  7.9 0.6 collective-permute-start.4
  8.5 0.7 collective-permute-done.refs_1_
  9.2 2.8 %collective-permute-done.1.refs_2_ = bf16[32,2048]{1,0:T(8,128)(2,1)S(1)} collective-permute-done((bf16[32,2048]{1,0:T(8,128)(2,1)S(1)}, bf16[32,2048]{1,0:T(8,128)(2,1)S(1)}, u32[]{:S(2)}, u32[]{:S(2)}) %collective-permute-start.1) | collective-permute-done | bytes 131104 | tf_op jit(solution)/shard_map/ppermute | solution.py:379
  12.0 3.4 %collective-permute-done.2.refs_3_ = bf16[32,2048]{1,0:T(8,128)(2,1)S(1)} collective-permute-done((bf16[32,2048]{1,0:T(8,128)(2,1)S(1)}, bf16[32,2048]{1,0:T(8,128)(2,1)S(1)}, u32[]{:S(2)}, u32[]{:S(2)}) %collective-permute-start.2) | collective-permute-done | bytes 131104 | tf_op jit(solution)/shard_map/ppermute | solution.py:379
  15.5 1.1 collective-permute-done.4.refs_5_
  16.6 0.7 collective-permute-done.5.refs_6_
  17.3 0.5 gram_kernel.1
  17.8 0.2 collective-permute-start.7
  18.0 1.2 collective-permute-done.7
  19.2 2.6 %collective-permute-start.10 = (bf16[3,64,128]{2,1,0:T(8,128)(2,1)S(1)}, bf16[3,64,128]{2,1,0:T(8,128)(2,1)S(1)}, u32[]{:S(2)}, u32[]{:S(2)}) collective-permute-start(bf16[3,64,128]{2,1,0:T(8,128)(2,1)S(1)} %add_convert_fusion.1), channel_id=1, source_target_pairs={{0,6},{1,7},{2,4},{3,5},{4,2},{5,3},{6,0},{7,1},{8,14},{9,15},{10,... | collective-permute-start | bytes 147464 | tf_op jit(solution)/shard_map/ppermute | solution.py:379
  21.8 0.5 collective-permute-start.9
  22.2 0.5 collective-permute-start.8
  22.8 1.5 %collective-permute-done.10 = bf16[3,64,128]{2,1,0:T(8,128)(2,1)S(1)} collective-permute-done((bf16[3,64,128]{2,1,0:T(8,128)(2,1)S(1)}, bf16[3,64,128]{2,1,0:T(8,128)(2,1)S(1)}, u32[]{:S(2)}, u32[]{:S(2)}) %collective-permute-start.10) | collective-permute-done | bytes 49184 | tf_op jit(solution)/shard_map/ppermute | solution.py:379
  24.3 1.6 %collective-permute-done.9 = bf16[3,64,128]{2,1,0:T(8,128)(2,1)S(1)} collective-permute-done((bf16[3,64,128]{2,1,0:T(8,128)(2,1)S(1)}, bf16[3,64,128]{2,1,0:T(8,128)(2,1)S(1)}, u32[]{:S(2)}, u32[]{:S(2)}) %collective-permute-start.9) | collective-permute-done | bytes 49184 | tf_op jit(solution)/shard_map/ppermute | solution.py:379
  25.9 0.5 collective-permute-done.8
  26.4 1.3 collective-permute-done.11.other_ref
  27.7 4.8 %node_kernel.1 = (bf16[128,1024]{1,0:T(8,128)(2,1)S(1)}, bf16[128,1024]{1,0:T(8,128)(2,1)S(1)}, bf16[256,128]{1,0:T(8,128)(2,1)S(1)}) custom-call(s32[1]{0:T(128)} %bitcast.pos_ref, f32[3,64,128]{2,1,0:T(8,128)S(1)} %add_add_fusion.1.mine_ref, f32[3,64,128]{2,1,0:T(8,128)S(1)} %collective-permute-done.11.other_ref, ...), custom_call_target="tpu_custom_call" | custom-call | tf_op jit(solution)/shard_map/node_kernel/pallas_call | solution.py:362
  32.5 0.7 collective-permute-start.14
  33.2 6.2 %collective-permute-start.13 = (bf16[128,1024]{1,0:T(8,128)(2,1)S(1)}, bf16[128,1024]{1,0:T(8,128)(2,1)S(1)}, u32[]{:S(2)}, u32[]{:S(2)}) collective-permute-start(bf16[128,1024]{1,0:T(8,128)(2,1)S(1)} %get-tuple-element.55), channel_id=1, source_target_pairs={{0,16},{1,17},{2,18},{3,19},{4,20},{5,21},{6,22},{7,23},{24,8},{25... | collective-permute-start | bytes 786440 | tf_op jit(solution)/shard_map/ppermute | solution.py:386
  39.4 1.4 %collective-permute-start.12 = (bf16[128,1024]{1,0:T(8,128)(2,1)S(1)}, bf16[128,1024]{1,0:T(8,128)(2,1)S(1)}, u32[]{:S(2)}, u32[]{:S(2)}) collective-permute-start(bf16[128,1024]{1,0:T(8,128)(2,1)S(1)} %get-tuple-element.54.refs_0_), channel_id=1, source_target_pairs={{0,8},{1,9},{2,10},{3,11},{4,12},{5,13},{6,14},{7,15},{24,16},{25,... | collective-permute-start | bytes 786440 | tf_op jit(solution)/shard_map/ppermute | solution.py:386
  40.8 5.2 %collective-permute-done.13.refs_2_ = bf16[128,1024]{1,0:T(8,128)(2,1)S(1)} collective-permute-done((bf16[128,1024]{1,0:T(8,128)(2,1)S(1)}, bf16[128,1024]{1,0:T(8,128)(2,1)S(1)}, u32[]{:S(2)}, u32[]{:S(2)}) %collective-permute-start.13) | collective-permute-done | bytes 262176 | tf_op jit(solution)/shard_map/ppermute | solution.py:386
  46.1 4.6 %collective-permute-done.12.refs_1_ = bf16[128,1024]{1,0:T(8,128)(2,1)S(1)} collective-permute-done((bf16[128,1024]{1,0:T(8,128)(2,1)S(1)}, bf16[128,1024]{1,0:T(8,128)(2,1)S(1)}, u32[]{:S(2)}, u32[]{:S(2)}) %collective-permute-start.12) | collective-permute-done | bytes 262176 | tf_op jit(solution)/shard_map/ppermute | solution.py:386
  50.7 0.7 cross_kernel.1
  51.4 1.4 %collective-permute-done.15 = f32[6,64,128]{2,1,0:T(8,128)S(1)} collective-permute-done((f32[6,64,128]{2,1,0:T(8,128)S(1)}, f32[6,64,128]{2,1,0:T(8,128)S(1)}, u32[]{:S(2)}, u32[]{:S(2)}) %collective-permute-start.15) | collective-permute-done | bytes 196640 | tf_op jit(solution)/shard_map/ppermute | solution.py:379
  52.9 1.6 %collective-permute-start.18 = (bf16[6,64,128]{2,1,0:T(8,128)(2,1)S(1)}, bf16[6,64,128]{2,1,0:T(8,128)(2,1)S(1)}, u32[]{:S(2)}, u32[]{:S(2)}) collective-permute-start(bf16[6,64,128]{2,1,0:T(8,128)(2,1)S(1)} %add_convert_fusion), channel_id=1, source_target_pairs={{0,6},{1,7},{2,4},{3,5},{4,2},{5,3},{6,0},{7,1},{8,14},{9,15},{10,... | collective-permute-start | bytes 294920 | tf_op jit(solution)/shard_map/ppermute | solution.py:379
  54.4 0.5 collective-permute-start.17
  54.9 1.5 %collective-permute-start.16 = (bf16[6,64,128]{2,1,0:T(8,128)(2,1)S(1)}, bf16[6,64,128]{2,1,0:T(8,128)(2,1)S(1)}, u32[]{:S(2)}, u32[]{:S(2)}) collective-permute-start(bf16[6,64,128]{2,1,0:T(8,128)(2,1)S(1)} %add_convert_fusion), channel_id=1, source_target_pairs={{0,2},{1,3},{2,0},{3,1},{4,6},{5,7},{6,4},{7,5},{8,10},{9,11},{10,... | collective-permute-start | bytes 294920 | tf_op jit(solution)/shard_map/ppermute | solution.py:379
  56.4 0.4 diag_kernel.1
  56.9 5.4 %collective-permute-start.20 = (bf16[1,64,128]{2,1,0:T(8,128)(2,1)S(1)}, bf16[1,64,128]{2,1,0:T(8,128)(2,1)S(1)}, u32[]{:S(2)}, u32[]{:S(2)}) collective-permute-start(bf16[1,64,128]{2,1,0:T(8,128)(2,1)S(1)} %diag_kernel.1), channel_id=1, source_target_pairs={{0,16},{1,17},{2,18},{3,19},{4,20},{5,21},{6,22},{7,23},{24,8},{25... | collective-permute-start | bytes 49160 | tf_op jit(solution)/shard_map/ppermute | solution.py:386
  62.3 1.3 collective-permute-start.19
  63.7 1.3 collective-permute-done.19
  65.0 0.8 collective-permute-start.21
  66.0 1.6 %collective-permute-done.22.other_ref = f32[10,64,128]{2,1,0:T(8,128)S(1)} collective-permute-done((f32[10,64,128]{2,1,0:T(8,128)S(1)}, f32[10,64,128]{2,1,0:T(8,128)S(1)}, u32[]{:S(2)}, u32[]{:S(2)}) %collective-permute-start.22) | collective-permute-done | bytes 327712 | tf_op jit(solution)/shard_map/ppermute | solution.py:379
  67.7 11.7 %top_kernel.1 = (bf16[128,1024]{1,0:T(8,128)(2,1)S(1)}, f32[256,256]{1,0:T(8,128)S(1)}, bf16[256,128]{1,0:T(8,128)(2,1)S(1)}) custom-call(s32[1]{0:T(128)} %bitcast.pos_ref, f32[10,64,128]{2,1,0:T(8,128)S(1)} %convert_dynamic-update-slice_fusion.mine_ref, f32[10,64,128]{2,1,0:T(8,128)S(1)} %collective-permute-done.22.other_ref, ...), custom_call_target="tpu_custom_call" | custom-call | tf_op jit(solution)/shard_map/top_kernel/pallas_call | solution.py:362
  79.4 0.7 collective-permute-start.25
  80.1 1.3 collective-permute-start.24
  81.4 1.5 %collective-permute-start.23 = (bf16[128,1024]{1,0:T(8,128)(2,1)S(1)}, bf16[128,1024]{1,0:T(8,128)(2,1)S(1)}, u32[]{:S(2)}, u32[]{:S(2)}) collective-permute-start(bf16[128,1024]{1,0:T(8,128)(2,1)S(1)} %get-tuple-element.66.refs_0_), channel_id=1, source_target_pairs={{8,0},{9,1},{10,2},{11,3},{12,4},{13,5},{14,6},{15,7},{16,24},{17,... | collective-permute-start | bytes 786440 | tf_op jit(solution)/shard_map/ppermute | solution.py:386
  82.9 3.4 %factor_kernel.1.own_factor_ref = f32[128,128]{1,0:T(8,128)S(1)} custom-call(f32[256,256]{1,0:T(8,128)S(1)} %get-tuple-element.63.gram_ref, bf16[256,128]{1,0:T(8,128)(2,1)S(1)} %get-tuple-element.64.low_ref), custom_call_target="tpu_custom_call" | custom-call | tf_op jit(solution)/shard_map/factor_kernel/pallas_call | solution.py:362
  86.3 16.6 %collective-permute-done.24.refs_2_ = bf16[128,1024]{1,0:T(8,128)(2,1)S(1)} collective-permute-done((bf16[128,1024]{1,0:T(8,128)(2,1)S(1)}, bf16[128,1024]{1,0:T(8,128)(2,1)S(1)}, u32[]{:S(2)}, u32[]{:S(2)}) %collective-permute-start.24) | collective-permute-done | bytes 262176 | tf_op jit(solution)/shard_map/ppermute | solution.py:386
  102.9 1.6 %collective-permute-done.23.refs_1_ = bf16[128,1024]{1,0:T(8,128)(2,1)S(1)} collective-permute-done((bf16[128,1024]{1,0:T(8,128)(2,1)S(1)}, bf16[128,1024]{1,0:T(8,128)(2,1)S(1)}, u32[]{:S(2)}, u32[]{:S(2)}) %collective-permute-start.23) | collective-permute-done | bytes 262176 | tf_op jit(solution)/shard_map/ppermute | solution.py:386
  104.5 0.4 coeffs_kernel.1
  105.0 1.2 collective-permute-done.26
  106.3 1.6 %collective-permute-start.29 = (bf16[1,128,128]{2,1,0:T(8,128)(2,1)S(1)}, bf16[1,128,128]{2,1,0:T(8,128)(2,1)S(1)}, u32[]{:S(2)}, u32[]{:S(2)}) collective-permute-start(bf16[1,128,128]{2,1,0:T(8,128)(2,1)S(1)} %add_convert_fusion.2), channel_id=1, source_target_pairs={{0,6},{1,7},{2,4},{3,5},{4,2},{5,3},{6,0},{7,1},{8,14},{9,15},{10,... | collective-permute-start | bytes 98312 | tf_op jit(solution)/shard_map/ppermute | solution.py:379
  107.9 0.5 collective-permute-start.28
  108.4 1.5 %collective-permute-start.27 = (bf16[1,128,128]{2,1,0:T(8,128)(2,1)S(1)}, bf16[1,128,128]{2,1,0:T(8,128)(2,1)S(1)}, u32[]{:S(2)}, u32[]{:S(2)}) collective-permute-start(bf16[1,128,128]{2,1,0:T(8,128)(2,1)S(1)} %add_convert_fusion.2), channel_id=1, source_target_pairs={{0,2},{1,3},{2,0},{3,1},{4,6},{5,7},{6,4},{7,5},{8,10},{9,11},{10,... | collective-permute-start | bytes 98312 | tf_op jit(solution)/shard_map/ppermute | solution.py:379
  109.9 1.3 collective-permute-start.31
  111.2 0.6 collective-permute-done.28
  111.8 0.5 collective-permute-done.27
  112.4 3.6 %collective-permute-done.31.factor_ref = f32[128,128]{1,0:T(8,128)S(1)} collective-permute-done((f32[128,128]{1,0:T(8,128)S(1)}, f32[128,128]{1,0:T(8,128)S(1)}, u32[]{:S(2)}, u32[]{:S(2)}) %collective-permute-start.31) | collective-permute-done | bytes 65568 | tf_op jit(solution)/shard_map/ppermute | solution.py:386
  116.0 1.1 project_kernel.1
  117.1 1.6 %collective-permute-start.32 = (bf16[32,2048]{1,0:T(8,128)(2,1)S(1)}, bf16[32,2048]{1,0:T(8,128)(2,1)S(1)}, u32[]{:S(2)}, u32[]{:S(2)}) collective-permute-start(bf16[32,2048]{1,0:T(8,128)(2,1)S(1)} %get-tuple-element.74), channel_id=1, source_target_pairs={{0,6},{1,7},{2,4},{3,5},{4,2},{5,3},{6,0},{7,1},{8,14},{9,15},{10,... | collective-permute-start | bytes 393224 | tf_op jit(solution)/shard_map/ppermute | solution.py:379
  118.7 1.5 %collective-permute-start.34 = (bf16[32,2048]{1,0:T(8,128)(2,1)S(1)}, bf16[32,2048]{1,0:T(8,128)(2,1)S(1)}, u32[]{:S(2)}, u32[]{:S(2)}) collective-permute-start(bf16[32,2048]{1,0:T(8,128)(2,1)S(1)} %get-tuple-element.76), channel_id=1, source_target_pairs={{0,2},{1,3},{2,0},{3,1},{4,6},{5,7},{6,4},{7,5},{8,10},{9,11},{10,... | collective-permute-start | bytes 393224 | tf_op jit(solution)/shard_map/ppermute | solution.py:379
  120.2 0.5 collective-permute-start.35
  120.6 2.2 %collective-permute-start.36 = (bf16[32,2048]{1,0:T(8,128)(2,1)S(1)}, bf16[32,2048]{1,0:T(8,128)(2,1)S(1)}, u32[]{:S(2)}, u32[]{:S(2)}) collective-permute-start(bf16[32,2048]{1,0:T(8,128)(2,1)S(1)} %get-tuple-element.78), channel_id=1, source_target_pairs={{0,3},{1,2},{2,1},{3,0},{4,7},{5,6},{6,5},{7,4},{8,11},{9,10},{10,... | collective-permute-start | bytes 393224 | tf_op jit(solution)/shard_map/ppermute | solution.py:379
  122.8 0.7 collective-permute-done.32.refs_1_
  123.5 1.9 %collective-permute-done.33.refs_2_ = bf16[32,2048]{1,0:T(8,128)(2,1)S(1)} collective-permute-done((bf16[32,2048]{1,0:T(8,128)(2,1)S(1)}, bf16[32,2048]{1,0:T(8,128)(2,1)S(1)}, u32[]{:S(2)}, u32[]{:S(2)}) %collective-permute-start.33) | collective-permute-done | bytes 131104 | tf_op jit(solution)/shard_map/ppermute | solution.py:379
  125.4 0.7 collective-permute-start.38
  126.1 3.9 %collective-permute-done.34.refs_3_ = bf16[32,2048]{1,0:T(8,128)(2,1)S(1)} collective-permute-done((bf16[32,2048]{1,0:T(8,128)(2,1)S(1)}, bf16[32,2048]{1,0:T(8,128)(2,1)S(1)}, u32[]{:S(2)}, u32[]{:S(2)}) %collective-permute-start.34) | collective-permute-done | bytes 131104 | tf_op jit(solution)/shard_map/ppermute | solution.py:379
  130.0 1.3 %collective-permute-done.37.refs_6_ = bf16[32,2048]{1,0:T(8,128)(2,1)S(1)} collective-permute-done((bf16[32,2048]{1,0:T(8,128)(2,1)S(1)}, bf16[32,2048]{1,0:T(8,128)(2,1)S(1)}, u32[]{:S(2)}, u32[]{:S(2)}) %collective-permute-start.37) | collective-permute-done | bytes 131104 | tf_op jit(solution)/shard_map/ppermute | solution.py:379
  131.4 1.0 whole_kernel.1
  (38 shorter events, 0.7 us)
Async XLA Ops:
  0.0 1.2 copy-start
  1.3 7.9 %collective-permute-start = (bf16[32,2048]{1,0:T(8,128)(2,1)S(1)}, bf16[32,2048]{1,0:T(8,128)(2,1)S(1)}, u32[]{:S(2)}, u32[]{:S(2)}) collective-permute-start(bf16[32,2048]{1,0:T(8,128)(2,1)S(1)} %get-tuple-element.44), channel_id=1, source_target_pairs={{0,6},{1,7},{2,4},{3,5},{4,2},{5,3},{6,0},{7,1},{8,14},{9,15},{10,... | collective-permute-start | bytes 393224 | tf_op jit(solution)/shard_map/ppermute | solution.py:379
  5.3 6.8 %collective-permute-start.1 = (bf16[32,2048]{1,0:T(8,128)(2,1)S(1)}, bf16[32,2048]{1,0:T(8,128)(2,1)S(1)}, u32[]{:S(2)}, u32[]{:S(2)}) collective-permute-start(bf16[32,2048]{1,0:T(8,128)(2,1)S(1)} %get-tuple-element.45), channel_id=1, source_target_pairs={{0,7},{1,6},{2,5},{3,4},{4,3},{5,2},{6,1},{7,0},{8,15},{9,14},{10,... | collective-permute-start | bytes 393224 | tf_op jit(solution)/shard_map/ppermute | solution.py:379
  5.3 10.2 %collective-permute-start.2 = (bf16[32,2048]{1,0:T(8,128)(2,1)S(1)}, bf16[32,2048]{1,0:T(8,128)(2,1)S(1)}, u32[]{:S(2)}, u32[]{:S(2)}) collective-permute-start(bf16[32,2048]{1,0:T(8,128)(2,1)S(1)} %get-tuple-element.46), channel_id=1, source_target_pairs={{0,2},{1,3},{2,0},{3,1},{4,6},{5,7},{6,4},{7,5},{8,10},{9,11},{10,... | collective-permute-start | bytes 393224 | tf_op jit(solution)/shard_map/ppermute | solution.py:379
  6.4 9.1 %collective-permute-start.3 = (bf16[32,2048]{1,0:T(8,128)(2,1)S(1)}, bf16[32,2048]{1,0:T(8,128)(2,1)S(1)}, u32[]{:S(2)}, u32[]{:S(2)}) collective-permute-start(bf16[32,2048]{1,0:T(8,128)(2,1)S(1)} %get-tuple-element.47), channel_id=1, source_target_pairs={{0,4},{1,5},{2,6},{3,7},{4,0},{5,1},{6,2},{7,3},{8,12},{9,13},{10,... | collective-permute-start | bytes 393224 | tf_op jit(solution)/shard_map/ppermute | solution.py:379
  7.9 8.7 %collective-permute-start.4 = (bf16[32,2048]{1,0:T(8,128)(2,1)S(1)}, bf16[32,2048]{1,0:T(8,128)(2,1)S(1)}, u32[]{:S(2)}, u32[]{:S(2)}) collective-permute-start(bf16[32,2048]{1,0:T(8,128)(2,1)S(1)} %get-tuple-element.48), channel_id=1, source_target_pairs={{0,3},{1,2},{2,1},{3,0},{4,7},{5,6},{6,5},{7,4},{8,11},{9,10},{10,... | collective-permute-start | bytes 393224 | tf_op jit(solution)/shard_map/ppermute | solution.py:379
  9.2 8.1 %collective-permute-start.5 = (bf16[32,2048]{1,0:T(8,128)(2,1)S(1)}, bf16[32,2048]{1,0:T(8,128)(2,1)S(1)}, u32[]{:S(2)}, u32[]{:S(2)}) collective-permute-start(bf16[32,2048]{1,0:T(8,128)(2,1)S(1)} %get-tuple-element.49), channel_id=1, source_target_pairs={{0,5},{1,4},{2,7},{3,6},{4,1},{5,0},{6,3},{7,2},{8,13},{9,12},{10,... | collective-permute-start | bytes 393224 | tf_op jit(solution)/shard_map/ppermute | solution.py:379
  12.0 5.3 %collective-permute-start.6 = (bf16[32,2048]{1,0:T(8,128)(2,1)S(1)}, bf16[32,2048]{1,0:T(8,128)(2,1)S(1)}, u32[]{:S(2)}, u32[]{:S(2)}) collective-permute-start(bf16[32,2048]{1,0:T(8,128)(2,1)S(1)} %get-tuple-element.50), channel_id=1, source_target_pairs={{0,1},{1,0},{2,3},{3,2},{4,5},{5,4},{6,7},{7,6},{8,9},{9,8},{10,11... | collective-permute-start | bytes 393224 | tf_op jit(solution)/shard_map/ppermute | solution.py:379
  17.8 1.4 %collective-permute-start.7 = (f32[3,64,128]{2,1,0:T(8,128)S(1)}, f32[3,64,128]{2,1,0:T(8,128)S(1)}, u32[]{:S(2)}, u32[]{:S(2)}) collective-permute-start(f32[3,64,128]{2,1,0:T(8,128)S(1)} %get-tuple-element.53), channel_id=1, source_target_pairs={{0,1},{1,0},{2,3},{3,2},{4,5},{5,4},{6,7},{7,6},{8,9},{9,8},{10,11... | collective-permute-start | bytes 294920 | tf_op jit(solution)/shard_map/ppermute | solution.py:379
  19.2 5.1 %collective-permute-start.10 = (bf16[3,64,128]{2,1,0:T(8,128)(2,1)S(1)}, bf16[3,64,128]{2,1,0:T(8,128)(2,1)S(1)}, u32[]{:S(2)}, u32[]{:S(2)}) collective-permute-start(bf16[3,64,128]{2,1,0:T(8,128)(2,1)S(1)} %add_convert_fusion.1), channel_id=1, source_target_pairs={{0,6},{1,7},{2,4},{3,5},{4,2},{5,3},{6,0},{7,1},{8,14},{9,15},{10,... | collective-permute-start | bytes 147464 | tf_op jit(solution)/shard_map/ppermute | solution.py:379
  21.8 4.1 %collective-permute-start.9 = (bf16[3,64,128]{2,1,0:T(8,128)(2,1)S(1)}, bf16[3,64,128]{2,1,0:T(8,128)(2,1)S(1)}, u32[]{:S(2)}, u32[]{:S(2)}) collective-permute-start(bf16[3,64,128]{2,1,0:T(8,128)(2,1)S(1)} %add_convert_fusion.1), channel_id=1, source_target_pairs={{0,4},{1,5},{2,6},{3,7},{4,0},{5,1},{6,2},{7,3},{8,12},{9,13},{10,... | collective-permute-start | bytes 147464 | tf_op jit(solution)/shard_map/ppermute | solution.py:379
  22.2 4.1 %collective-permute-start.8 = (bf16[3,64,128]{2,1,0:T(8,128)(2,1)S(1)}, bf16[3,64,128]{2,1,0:T(8,128)(2,1)S(1)}, u32[]{:S(2)}, u32[]{:S(2)}) collective-permute-start(bf16[3,64,128]{2,1,0:T(8,128)(2,1)S(1)} %add_convert_fusion.1), channel_id=1, source_target_pairs={{0,2},{1,3},{2,0},{3,1},{4,6},{5,7},{6,4},{7,5},{8,10},{9,11},{10,... | collective-permute-start | bytes 147464 | tf_op jit(solution)/shard_map/ppermute | solution.py:379
  26.4 1.4 %collective-permute-start.11 = (f32[3,64,128]{2,1,0:T(8,128)S(1)}, f32[3,64,128]{2,1,0:T(8,128)S(1)}, u32[]{:S(2)}, u32[]{:S(2)}) collective-permute-start(f32[3,64,128]{2,1,0:T(8,128)S(1)} %add_add_fusion.1.mine_ref), channel_id=1, source_target_pairs={{0,1},{1,0},{2,3},{3,2},{4,5},{5,4},{6,7},{7,6},{8,9},{9,8},{10,11... | collective-permute-start | bytes 294920 | tf_op jit(solution)/shard_map/ppermute | solution.py:379
  32.5 8.3 %collective-permute-start.14 = (bf16[128,1024]{1,0:T(8,128)(2,1)S(1)}, bf16[128,1024]{1,0:T(8,128)(2,1)S(1)}, u32[]{:S(2)}, u32[]{:S(2)}) collective-permute-start(bf16[128,1024]{1,0:T(8,128)(2,1)S(1)} %get-tuple-element.55), channel_id=1, source_target_pairs={{8,16},{9,17},{10,18},{11,19},{12,20},{13,21},{14,22},{15,23},{16,... | collective-permute-start | bytes 786440 | tf_op jit(solution)/shard_map/ppermute | solution.py:386
  33.2 12.9 %collective-permute-start.13 = (bf16[128,1024]{1,0:T(8,128)(2,1)S(1)}, bf16[128,1024]{1,0:T(8,128)(2,1)S(1)}, u32[]{:S(2)}, u32[]{:S(2)}) collective-permute-start(bf16[128,1024]{1,0:T(8,128)(2,1)S(1)} %get-tuple-element.55), channel_id=1, source_target_pairs={{0,16},{1,17},{2,18},{3,19},{4,20},{5,21},{6,22},{7,23},{24,8},{25... | collective-permute-start | bytes 786440 | tf_op jit(solution)/shard_map/ppermute | solution.py:386
  39.4 11.2 %collective-permute-start.12 = (bf16[128,1024]{1,0:T(8,128)(2,1)S(1)}, bf16[128,1024]{1,0:T(8,128)(2,1)S(1)}, u32[]{:S(2)}, u32[]{:S(2)}) collective-permute-start(bf16[128,1024]{1,0:T(8,128)(2,1)S(1)} %get-tuple-element.54.refs_0_), channel_id=1, source_target_pairs={{0,8},{1,9},{2,10},{3,11},{4,12},{5,13},{6,14},{7,15},{24,16},{25,... | collective-permute-start | bytes 786440 | tf_op jit(solution)/shard_map/ppermute | solution.py:386
  51.3 1.5 %collective-permute-start.15 = (f32[6,64,128]{2,1,0:T(8,128)S(1)}, f32[6,64,128]{2,1,0:T(8,128)S(1)}, u32[]{:S(2)}, u32[]{:S(2)}) collective-permute-start(f32[6,64,128]{2,1,0:T(8,128)S(1)} %get-tuple-element.57), channel_id=1, source_target_pairs={{0,1},{1,0},{2,3},{3,2},{4,5},{5,4},{6,7},{7,6},{8,9},{9,8},{10,11... | collective-permute-start | bytes 589832 | tf_op jit(solution)/shard_map/ppermute | solution.py:379
  52.9 10.7 %collective-permute-start.18 = (bf16[6,64,128]{2,1,0:T(8,128)(2,1)S(1)}, bf16[6,64,128]{2,1,0:T(8,128)(2,1)S(1)}, u32[]{:S(2)}, u32[]{:S(2)}) collective-permute-start(bf16[6,64,128]{2,1,0:T(8,128)(2,1)S(1)} %add_convert_fusion), channel_id=1, source_target_pairs={{0,6},{1,7},{2,4},{3,5},{4,2},{5,3},{6,0},{7,1},{8,14},{9,15},{10,... | collective-permute-start | bytes 294920 | tf_op jit(solution)/shard_map/ppermute | solution.py:379
  54.4 9.1 %collective-permute-start.17 = (bf16[6,64,128]{2,1,0:T(8,128)(2,1)S(1)}, bf16[6,64,128]{2,1,0:T(8,128)(2,1)S(1)}, u32[]{:S(2)}, u32[]{:S(2)}) collective-permute-start(bf16[6,64,128]{2,1,0:T(8,128)(2,1)S(1)} %add_convert_fusion), channel_id=1, source_target_pairs={{0,4},{1,5},{2,6},{3,7},{4,0},{5,1},{6,2},{7,3},{8,12},{9,13},{10,... | collective-permute-start | bytes 294920 | tf_op jit(solution)/shard_map/ppermute | solution.py:379
  54.9 8.6 %collective-permute-start.16 = (bf16[6,64,128]{2,1,0:T(8,128)(2,1)S(1)}, bf16[6,64,128]{2,1,0:T(8,128)(2,1)S(1)}, u32[]{:S(2)}, u32[]{:S(2)}) collective-permute-start(bf16[6,64,128]{2,1,0:T(8,128)(2,1)S(1)} %add_convert_fusion), channel_id=1, source_target_pairs={{0,2},{1,3},{2,0},{3,1},{4,6},{5,7},{6,4},{7,5},{8,10},{9,11},{10,... | collective-permute-start | bytes 294920 | tf_op jit(solution)/shard_map/ppermute | solution.py:379
  56.9 6.8 %collective-permute-start.20 = (bf16[1,64,128]{2,1,0:T(8,128)(2,1)S(1)}, bf16[1,64,128]{2,1,0:T(8,128)(2,1)S(1)}, u32[]{:S(2)}, u32[]{:S(2)}) collective-permute-start(bf16[1,64,128]{2,1,0:T(8,128)(2,1)S(1)} %diag_kernel.1), channel_id=1, source_target_pairs={{0,16},{1,17},{2,18},{3,19},{4,20},{5,21},{6,22},{7,23},{24,8},{25... | collective-permute-start | bytes 49160 | tf_op jit(solution)/shard_map/ppermute | solution.py:386
  62.3 2.7 %collective-permute-start.19 = (bf16[1,64,128]{2,1,0:T(8,128)(2,1)S(1)}, bf16[1,64,128]{2,1,0:T(8,128)(2,1)S(1)}, u32[]{:S(2)}, u32[]{:S(2)}) collective-permute-start(bf16[1,64,128]{2,1,0:T(8,128)(2,1)S(1)} %diag_kernel.1), channel_id=1, source_target_pairs={{0,8},{1,9},{2,10},{3,11},{4,12},{5,13},{6,14},{7,15},{24,16},{25,... | collective-permute-start | bytes 49160 | tf_op jit(solution)/shard_map/ppermute | solution.py:386
  65.0 0.9 collective-permute-start.21
  66.0 1.7 %collective-permute-start.22 = (f32[10,64,128]{2,1,0:T(8,128)S(1)}, f32[10,64,128]{2,1,0:T(8,128)S(1)}, u32[]{:S(2)}, u32[]{:S(2)}) collective-permute-start(f32[10,64,128]{2,1,0:T(8,128)S(1)} %convert_dynamic-update-slice_fusion.mine_ref), channel_id=1, source_target_pairs={{0,1},{1,0},{2,3},{3,2},{4,5},{5,4},{6,7},{7,6},{8,9},{9,8},{10,11... | collective-permute-start | bytes 983048 | tf_op jit(solution)/shard_map/ppermute | solution.py:379
  79.4 6.9 %collective-permute-start.25 = (bf16[128,1024]{1,0:T(8,128)(2,1)S(1)}, bf16[128,1024]{1,0:T(8,128)(2,1)S(1)}, u32[]{:S(2)}, u32[]{:S(2)}) collective-permute-start(bf16[128,1024]{1,0:T(8,128)(2,1)S(1)} %get-tuple-element.66.refs_0_), channel_id=1, source_target_pairs={{8,16},{9,17},{10,18},{11,19},{12,20},{13,21},{14,22},{15,23},{16,... | collective-permute-start | bytes 786440 | tf_op jit(solution)/shard_map/ppermute | solution.py:386
  80.1 22.8 %collective-permute-start.24 = (bf16[128,1024]{1,0:T(8,128)(2,1)S(1)}, bf16[128,1024]{1,0:T(8,128)(2,1)S(1)}, u32[]{:S(2)}, u32[]{:S(2)}) collective-permute-start(bf16[128,1024]{1,0:T(8,128)(2,1)S(1)} %get-tuple-element.66.refs_0_), channel_id=1, source_target_pairs={{8,24},{9,25},{10,26},{11,27},{12,28},{13,29},{14,30},{15,31},{16,... | collective-permute-start | bytes 786440 | tf_op jit(solution)/shard_map/ppermute | solution.py:386
  81.4 23.2 %collective-permute-start.23 = (bf16[128,1024]{1,0:T(8,128)(2,1)S(1)}, bf16[128,1024]{1,0:T(8,128)(2,1)S(1)}, u32[]{:S(2)}, u32[]{:S(2)}) collective-permute-start(bf16[128,1024]{1,0:T(8,128)(2,1)S(1)} %get-tuple-element.66.refs_0_), channel_id=1, source_target_pairs={{8,0},{9,1},{10,2},{11,3},{12,4},{13,5},{14,6},{15,7},{16,24},{17,... | collective-permute-start | bytes 786440 | tf_op jit(solution)/shard_map/ppermute | solution.py:386
  105.0 1.3 collective-permute-start.26
  106.3 4.9 %collective-permute-start.29 = (bf16[1,128,128]{2,1,0:T(8,128)(2,1)S(1)}, bf16[1,128,128]{2,1,0:T(8,128)(2,1)S(1)}, u32[]{:S(2)}, u32[]{:S(2)}) collective-permute-start(bf16[1,128,128]{2,1,0:T(8,128)(2,1)S(1)} %add_convert_fusion.2), channel_id=1, source_target_pairs={{0,6},{1,7},{2,4},{3,5},{4,2},{5,3},{6,0},{7,1},{8,14},{9,15},{10,... | collective-permute-start | bytes 98312 | tf_op jit(solution)/shard_map/ppermute | solution.py:379
  107.9 3.9 %collective-permute-start.28 = (bf16[1,128,128]{2,1,0:T(8,128)(2,1)S(1)}, bf16[1,128,128]{2,1,0:T(8,128)(2,1)S(1)}, u32[]{:S(2)}, u32[]{:S(2)}) collective-permute-start(bf16[1,128,128]{2,1,0:T(8,128)(2,1)S(1)} %add_convert_fusion.2), channel_id=1, source_target_pairs={{0,4},{1,5},{2,6},{3,7},{4,0},{5,1},{6,2},{7,3},{8,12},{9,13},{10,... | collective-permute-start | bytes 98312 | tf_op jit(solution)/shard_map/ppermute | solution.py:379
  108.4 3.9 %collective-permute-start.27 = (bf16[1,128,128]{2,1,0:T(8,128)(2,1)S(1)}, bf16[1,128,128]{2,1,0:T(8,128)(2,1)S(1)}, u32[]{:S(2)}, u32[]{:S(2)}) collective-permute-start(bf16[1,128,128]{2,1,0:T(8,128)(2,1)S(1)} %add_convert_fusion.2), channel_id=1, source_target_pairs={{0,2},{1,3},{2,0},{3,1},{4,6},{5,7},{6,4},{7,5},{8,10},{9,11},{10,... | collective-permute-start | bytes 98312 | tf_op jit(solution)/shard_map/ppermute | solution.py:379
  109.9 6.1 %collective-permute-start.31 = (f32[128,128]{1,0:T(8,128)S(1)}, f32[128,128]{1,0:T(8,128)S(1)}, u32[]{:S(2)}, u32[]{:S(2)}) collective-permute-start(f32[128,128]{1,0:T(8,128)S(1)} %factor_kernel.1.own_factor_ref), channel_id=1, source_target_pairs={{8,0},{9,1},{10,2},{11,3},{12,4},{13,5},{14,6},{15,7},{16,24},{17,... | collective-permute-start | bytes 196616 | tf_op jit(solution)/shard_map/ppermute | solution.py:386
  112.3 3.7 %collective-permute-start.30 = (f32[1,128,128]{2,1,0:T(8,128)S(1)}, f32[1,128,128]{2,1,0:T(8,128)S(1)}, u32[]{:S(2)}, u32[]{:S(2)}) collective-permute-start(f32[1,128,128]{2,1,0:T(8,128)S(1)} %add_add_fusion.2.mine_ref), channel_id=1, source_target_pairs={{0,1},{1,0},{2,3},{3,2},{4,5},{5,4},{6,7},{7,6},{8,9},{9,8},{10,11... | collective-permute-start | bytes 196616 | tf_op jit(solution)/shard_map/ppermute | solution.py:379
  117.1 6.4 %collective-permute-start.32 = (bf16[32,2048]{1,0:T(8,128)(2,1)S(1)}, bf16[32,2048]{1,0:T(8,128)(2,1)S(1)}, u32[]{:S(2)}, u32[]{:S(2)}) collective-permute-start(bf16[32,2048]{1,0:T(8,128)(2,1)S(1)} %get-tuple-element.74), channel_id=1, source_target_pairs={{0,6},{1,7},{2,4},{3,5},{4,2},{5,3},{6,0},{7,1},{8,14},{9,15},{10,... | collective-permute-start | bytes 393224 | tf_op jit(solution)/shard_map/ppermute | solution.py:379
  118.7 6.8 %collective-permute-start.33 = (bf16[32,2048]{1,0:T(8,128)(2,1)S(1)}, bf16[32,2048]{1,0:T(8,128)(2,1)S(1)}, u32[]{:S(2)}, u32[]{:S(2)}) collective-permute-start(bf16[32,2048]{1,0:T(8,128)(2,1)S(1)} %get-tuple-element.75), channel_id=1, source_target_pairs={{0,7},{1,6},{2,5},{3,4},{4,3},{5,2},{6,1},{7,0},{8,15},{9,14},{10,... | collective-permute-start | bytes 393224 | tf_op jit(solution)/shard_map/ppermute | solution.py:379
  118.7 11.4 %collective-permute-start.34 = (bf16[32,2048]{1,0:T(8,128)(2,1)S(1)}, bf16[32,2048]{1,0:T(8,128)(2,1)S(1)}, u32[]{:S(2)}, u32[]{:S(2)}) collective-permute-start(bf16[32,2048]{1,0:T(8,128)(2,1)S(1)} %get-tuple-element.76), channel_id=1, source_target_pairs={{0,2},{1,3},{2,0},{3,1},{4,6},{5,7},{6,4},{7,5},{8,10},{9,11},{10,... | collective-permute-start | bytes 393224 | tf_op jit(solution)/shard_map/ppermute | solution.py:379
  120.2 9.9 %collective-permute-start.35 = (bf16[32,2048]{1,0:T(8,128)(2,1)S(1)}, bf16[32,2048]{1,0:T(8,128)(2,1)S(1)}, u32[]{:S(2)}, u32[]{:S(2)}) collective-permute-start(bf16[32,2048]{1,0:T(8,128)(2,1)S(1)} %get-tuple-element.77), channel_id=1, source_target_pairs={{0,4},{1,5},{2,6},{3,7},{4,0},{5,1},{6,2},{7,3},{8,12},{9,13},{10,... | collective-permute-start | bytes 393224 | tf_op jit(solution)/shard_map/ppermute | solution.py:379
  120.6 9.4 %collective-permute-start.36 = (bf16[32,2048]{1,0:T(8,128)(2,1)S(1)}, bf16[32,2048]{1,0:T(8,128)(2,1)S(1)}, u32[]{:S(2)}, u32[]{:S(2)}) collective-permute-start(bf16[32,2048]{1,0:T(8,128)(2,1)S(1)} %get-tuple-element.78), channel_id=1, source_target_pairs={{0,3},{1,2},{2,1},{3,0},{4,7},{5,6},{6,5},{7,4},{8,11},{9,10},{10,... | collective-permute-start | bytes 393224 | tf_op jit(solution)/shard_map/ppermute | solution.py:379
  123.5 7.9 %collective-permute-start.37 = (bf16[32,2048]{1,0:T(8,128)(2,1)S(1)}, bf16[32,2048]{1,0:T(8,128)(2,1)S(1)}, u32[]{:S(2)}, u32[]{:S(2)}) collective-permute-start(bf16[32,2048]{1,0:T(8,128)(2,1)S(1)} %get-tuple-element.79), channel_id=1, source_target_pairs={{0,5},{1,4},{2,7},{3,6},{4,1},{5,0},{6,3},{7,2},{8,13},{9,12},{10,... | collective-permute-start | bytes 393224 | tf_op jit(solution)/shard_map/ppermute | solution.py:379
  125.4 5.9 %collective-permute-start.38 = (bf16[32,2048]{1,0:T(8,128)(2,1)S(1)}, bf16[32,2048]{1,0:T(8,128)(2,1)S(1)}, u32[]{:S(2)}, u32[]{:S(2)}) collective-permute-start(bf16[32,2048]{1,0:T(8,128)(2,1)S(1)} %get-tuple-element.80), channel_id=1, source_target_pairs={{0,1},{1,0},{2,3},{3,2},{4,5},{5,4},{6,7},{7,6},{8,9},{9,8},{10,11... | collective-permute-start | bytes 393224 | tf_op jit(solution)/shard_map/ppermute | solution.py:379

commit v5 on v3

--- a/solution.py
+++ b/solution.py
@@ -1,3 +1,5 @@
+import functools
+
 import jax
 import jax.numpy as jnp
 from jax import lax
@@ -12,7 +14,7 @@
 PLANES = 2**LEVELS // PLANE
 TILE = 8
 PANEL = 64
-PLANE_ORDER = (0, 6, 7, 2, 4, 3, 5, 1)
+PLANE_ORDER = (6, 7, 2, 4, 3, 5, 1, 0)
 TREE_ORDER = (0, 3, 2, 1)
 PIVOT_SHARE = 2e-4
 
@@ -192,7 +194,7 @@
 
 
 def joined(mine_ref, other_ref, core, b):
-    mine, other = mine_ref[b], other_ref[b]
+    mine, other = mine_ref[b].astype(f32), other_ref[b].astype(f32)
     low = jnp.where(core == 1, other, mine)
     high = jnp.where(core == 1, mine, other)
     return jnp.concatenate([low, high], 0)
@@ -206,10 +208,17 @@
     return pos_ref[0] % PLANE
 
 
-def parts_kernel(pos_ref, x_ref, *refs):
-    width = refs[0].shape[1]
-    for ref, m in zip(refs, PLANE_ORDER):
-        ref[...] = x_ref[:, chunk(member(pos_ref), m, width)]
+def copy_all(copies):
+    for c in copies:
+        c.start()
+    for c in copies:
+        c.wait()
+
+
+def parts_kernel(order, pos_ref, x_ref, *refs):
+    parts, sems = refs[:-1], refs[-1]
+    where = [x_ref.at[:, chunk(member(pos_ref), m, parts[0].shape[1])] for m in order]
+    copy_all([pltpu.make_async_copy(w, part, sems.at[k]) for k, (w, part) in enumerate(zip(where, parts))])
 
 
 def gram_kernel(pos_ref, *refs):
@@ -332,30 +341,53 @@
             outs[k][:, chunk(z, m, width)] = made[k * height : (k + 1) * height, :]
 
 
-def whole_kernel(pos_ref, *refs):
-    parts, out_ref = refs[:PLANE], refs[PLANE]
-    width = parts[0].shape[1]
-    for ref, m in zip(parts, PLANE_ORDER):
-        out_ref[:, chunk(member(pos_ref), m, width)] = ref[...]
+def whole_kernel(order, pos_ref, *refs):
+    parts, out_ref, sems = refs[: len(order)], refs[-2], refs[-1]
+    where = [out_ref.at[:, chunk(member(pos_ref), m, parts[0].shape[1])] for m in order]
+    copy_all([pltpu.make_async_copy(part, w, sems.at[k]) for k, (w, part) in enumerate(zip(where, parts))])
 
 
 smem = pl.BlockSpec(memory_space=pltpu.SMEM)
 vmem = pl.BlockSpec(memory_space=pltpu.VMEM)
+hbm = pl.BlockSpec(memory_space=pltpu.HBM)
 
 
 def kernel(fn, outs, *args, scratch=(), scalar=True):
-    single = not isinstance(outs, (list, tuple))
-    shapes = [outs] if single else list(outs)
-    res = pl.pallas_call(
+    return pl.pallas_call(
         fn,
-        out_shape=[jax.ShapeDtypeStruct(s, d) for s, d in shapes] if not single else None,
+        out_shape=[jax.ShapeDtypeStruct(s, d) for s, d in outs],
         in_specs=[smem if scalar and i == 0 else vmem for i in range(len(args))],
-        out_specs=[vmem for _ in shapes],
+        out_specs=[vmem for _ in outs],
         scratch_shapes=list(scratch),
         compiler_params=pltpu.CompilerParams(vmem_limit_bytes=40 * 2**20),
         name=fn.__name__,
     )(*args)
-    return res
+
+
+def read_parts(order, pos, x, width):
+    return pl.pallas_call(
+        functools.partial(parts_kernel, order),
+        out_shape=[jax.ShapeDtypeStruct((x.shape[0], width), x.dtype) for _ in order],
+        in_specs=[smem, hbm],
+        out_specs=[vmem for _ in order],
+        scratch_shapes=[pltpu.SemaphoreType.DMA((len(order),))],
+        compiler_params=pltpu.CompilerParams(vmem_limit_bytes=40 * 2**20),
+        name="parts_kernel",
+    )(pos, pltpu.with_memory_space_constraint(x, pltpu.HBM))
+
+
+def write_parts(order, pos, parts, shape, before=None):
+    earlier = [] if before is None else [before]
+    return pl.pallas_call(
+        functools.partial(whole_kernel, order),
+        out_shape=jax.ShapeDtypeStruct(shape, parts[0].dtype),
+        in_specs=[smem] + [vmem] * len(parts) + [hbm] * len(earlier),
+        out_specs=hbm,
+        scratch_shapes=[pltpu.SemaphoreType.DMA((len(order),))],
+        input_output_aliases={} if before is None else {len(parts) + 1: 0},
+        compiler_params=pltpu.CompilerParams(vmem_limit_bytes=40 * 2**20),
+        name="whole_kernel",
+    )(pos, *parts, *earlier)
 
 
 def body(mortality):
@@ -373,14 +405,17 @@
         return (parts[0] + parts[1]) + (parts[2] + parts[3])
 
     def plane_sum(mine, theirs):
-        return sum4(swap_all([(mine + swap(theirs, 1)).astype(bf16)] * 4, range(4), 2))
+        return sum4(swap_all([(mine + swap(theirs, 1)).astype(bf16)] * 4, range(4), 2)).astype(bf16)
 
     block, total = mortality.shape
     height, width = block * PLANE, total // PLANE
     part = width // PLANES
     half = RANK // 2
 
-    parts = kernel(parts_kernel, [((block, width), bf16)] * PLANE, pos, mortality)
+    early, late = PLANE_ORDER[:4], PLANE_ORDER[4:]
+    parts = read_parts(early, pos, mortality, width)
+    parts, after = lax.optimization_barrier((parts, pos))
+    parts = parts + read_parts(late, after, mortality, width)
     parts = swap_all(parts, PLANE_ORDER)
     rows, mine, theirs = kernel(
         gram_kernel, [((height, width), bf16)] + [((3, half, RANK), f32)] * 2, pos, *parts
@@ -403,8 +438,9 @@
         scratch=[pltpu.VMEM((PLANES, RANK, part), bf16)],
     )
     mine = plane_sum(mine, theirs)
-    both = swap_all([jnp.concatenate([mine.astype(bf16), diag], 0)] * PLANES, range(PLANES), PLANE)
-    mine = jnp.concatenate([sum4([x[: len(PAIRS)] for x in both])] + [x[len(PAIRS) :].astype(f32) for x in both], 0)
+    both = swap_all([jnp.concatenate([mine, diag], 0)] * PLANES, range(PLANES), PLANE)
+    total_cross = sum4([x[: len(PAIRS)] for x in both]).astype(bf16)
+    mine = jnp.concatenate([total_cross] + [x[len(PAIRS) :] for x in both], 0)
     top, gram, low = kernel(
         top_kernel,
         [((RANK, part), bf16), ((2 * RANK, 2 * RANK), f32), ((2 * RANK, RANK), bf16)],
@@ -424,8 +460,10 @@
         pos, mine, swap(mine, 1), factor, *tops,
         scratch=[pltpu.VMEM((height, RANK), f32)],
     )
-    (result,) = kernel(whole_kernel, [((block, total), bf16)], pos, *swap_all(outs, PLANE_ORDER))
-    return result
+    outs = swap_all(outs, PLANE_ORDER)
+    early, late = PLANE_ORDER[:3] + PLANE_ORDER[-1:], PLANE_ORDER[3:-1]
+    result = write_parts(early, pos, outs[:3] + outs[-1:], (block, total))
+    return write_parts(late, pos, outs[3:-1], (block, total), result)
 
 
 def solution(mesh):

time: 124 us -> 124 us (level)
  Pallas kernels: 24.3 us -> 27 us
  waiting for transfers between devices: 58.6 us -> 56.6 us
    pallas_call x10 -> x12, Pallas kernels: 24.3 us -> 27 us  [the longest x8 23.1 us: kernel(): pl.pallas_call(fn, out_shape=[jax.ShapeDtypeStruct(s, d) for s, d in outs...]
    ppermute x38, waiting for transfers between devices: 58.6 us -> 56.6 us  [swap(): return lax.ppermute(x, 'cols', [(i, i ^ apart) for i in range(count)])]
  transfers between devices with their start and end apart: 38 -> 38, of which waited for: 31 -> 28; matrix products, arithmetic and copies ran while one was open for 0% -> 0% of each run, Pallas kernels for 3% -> 5%
where the time goes in v5:
time: 124 us
  waiting for transfers between devices  56.6 us (46%)
  starting transfers between devices  39.8 us (32%)
  Pallas kernels  27 us (22%)
    ppermute x38, waiting for transfers between devices, swap(): return lax.ppermute(x, 'cols', [(i, i ^ apart) for i in range(count)])  56.6 us
    ppermute x38, starting transfers between devices, swap(): return lax.ppermute(x, 'cols', [(i, i ^ apart) for i in range(count)])  39.8 us
    pallas_call x8, Pallas kernels, kernel(): pl.pallas_call(fn, out_shape=[jax.ShapeDtypeStruct(s, d) for s, d in outs...  23.1 us
  transfers between devices with their start and end apart: 38, of which 28 were waited for; matrix products, arithmetic and copies ran while one was open for 0% of the time, Pallas kernels for 5%

profile of v5, /device:TPU:0, one launch (start us, length us, event | category | flops | bytes accessed | tf_op | source)
XLA Modules:
  0.0 124.1 jit_solution(4750935815312139441)
XLA Ops:
  0.0 1.1 parts_kernel.2
  1.1 4.0 %collective-permute-start = (bf16[32,2048]{1,0:T(8,128)(2,1)S(1)}, bf16[32,2048]{1,0:T(8,128)(2,1)S(1)}, u32[]{:S(2)}, u32[]{:S(2)}) collective-permute-start(bf16[32,2048]{1,0:T(8,128)(2,1)S(1)} %get-tuple-element.45), channel_id=1, source_target_pairs={{0,6},{1,7},{2,4},{3,5},{4,2},{5,3},{6,0},{7,1},{8,14},{9,15},{10,... | collective-permute-start | bytes 393224 | tf_op jit(solution)/shard_map/ppermute | solution.py:398
  5.1 1.1 collective-permute-start.2
  6.2 1.5 %collective-permute-start.3 = (bf16[32,2048]{1,0:T(8,128)(2,1)S(1)}, bf16[32,2048]{1,0:T(8,128)(2,1)S(1)}, u32[]{:S(2)}, u32[]{:S(2)}) collective-permute-start(bf16[32,2048]{1,0:T(8,128)(2,1)S(1)} %get-tuple-element.48), channel_id=1, source_target_pairs={{0,4},{1,5},{2,6},{3,7},{4,0},{5,1},{6,2},{7,3},{8,12},{9,13},{10,... | collective-permute-start | bytes 393224 | tf_op jit(solution)/shard_map/ppermute | solution.py:398
  7.7 1.1 parts_kernel.3
  8.9 0.6 collective-permute-start.4
  9.5 0.6 collective-permute-start.5
  10.1 1.8 %collective-permute-done.1.refs_1_ = bf16[32,2048]{1,0:T(8,128)(2,1)S(1)} collective-permute-done((bf16[32,2048]{1,0:T(8,128)(2,1)S(1)}, bf16[32,2048]{1,0:T(8,128)(2,1)S(1)}, u32[]{:S(2)}, u32[]{:S(2)}) %collective-permute-start.1) | collective-permute-done | bytes 131104 | tf_op jit(solution)/shard_map/ppermute | solution.py:398
  11.9 3.4 %collective-permute-done.2.refs_2_ = bf16[32,2048]{1,0:T(8,128)(2,1)S(1)} collective-permute-done((bf16[32,2048]{1,0:T(8,128)(2,1)S(1)}, bf16[32,2048]{1,0:T(8,128)(2,1)S(1)}, u32[]{:S(2)}, u32[]{:S(2)}) %collective-permute-start.2) | collective-permute-done | bytes 131104 | tf_op jit(solution)/shard_map/ppermute | solution.py:398
  15.3 1.1 collective-permute-done.4.refs_4_
  16.4 0.7 collective-permute-done.5.refs_5_
  17.1 0.5 gram_kernel.1
  17.9 1.2 collective-permute-done.7
  19.1 2.6 %collective-permute-start.10 = (bf16[3,64,128]{2,1,0:T(8,128)(2,1)S(1)}, bf16[3,64,128]{2,1,0:T(8,128)(2,1)S(1)}, u32[]{:S(2)}, u32[]{:S(2)}) collective-permute-start(bf16[3,64,128]{2,1,0:T(8,128)(2,1)S(1)} %add_convert_fusion.4), channel_id=1, source_target_pairs={{0,6},{1,7},{2,4},{3,5},{4,2},{5,3},{6,0},{7,1},{8,14},{9,15},{10,... | collective-permute-start | bytes 147464 | tf_op jit(solution)/shard_map/ppermute | solution.py:398
  21.6 0.4 collective-permute-start.9
  22.1 0.5 collective-permute-start.8
  22.6 1.5 %collective-permute-done.10 = bf16[3,64,128]{2,1,0:T(8,128)(2,1)S(1)} collective-permute-done((bf16[3,64,128]{2,1,0:T(8,128)(2,1)S(1)}, bf16[3,64,128]{2,1,0:T(8,128)(2,1)S(1)}, u32[]{:S(2)}, u32[]{:S(2)}) %collective-permute-start.10) | collective-permute-done | bytes 49184 | tf_op jit(solution)/shard_map/ppermute | solution.py:398
  24.1 1.6 %collective-permute-done.9 = bf16[3,64,128]{2,1,0:T(8,128)(2,1)S(1)} collective-permute-done((bf16[3,64,128]{2,1,0:T(8,128)(2,1)S(1)}, bf16[3,64,128]{2,1,0:T(8,128)(2,1)S(1)}, u32[]{:S(2)}, u32[]{:S(2)}) %collective-permute-start.9) | collective-permute-done | bytes 49184 | tf_op jit(solution)/shard_map/ppermute | solution.py:398
  25.7 0.4 collective-permute-done.8
  26.3 1.2 collective-permute-done.11.other_ref
  27.5 4.8 %node_kernel.1 = (bf16[128,512]{1,0:T(8,128)(2,1)S(1)}, bf16[128,512]{1,0:T(8,128)(2,1)S(1)}, bf16[128,512]{1,0:T(8,128)(2,1)S(1)}, bf16[128,512]{1,0:T(8,128)(2,1)S(1)}, bf16[256,128]{1,0:T(8,128)(2,1)S(1)}) custom-call(s32[1]{0:T(128)} %bitcast.pos_ref, bf16[3,64,128]{2,1,0:T(8,128)(2,1)S(1)} %add_convert_fusion.3.mine_ref, ...), custom_call_target="tpu_custom_call" | custom-call | tf_op jit(solution)/shard_map/node_kernel/pallas_call | solution.py:356
  32.3 3.7 %collective-permute-start.12 = (bf16[128,512]{1,0:T(8,128)(2,1)S(1)}, bf16[128,512]{1,0:T(8,128)(2,1)S(1)}, u32[]{:S(2)}, u32[]{:S(2)}) collective-permute-start(bf16[128,512]{1,0:T(8,128)(2,1)S(1)} %get-tuple-element.58), channel_id=1, source_target_pairs={{0,24},{1,25},{2,26},{3,27},{4,28},{5,29},{6,30},{7,31},{8,16},{9,... | collective-permute-start | bytes 393224 | tf_op jit(solution)/shard_map/ppermute | solution.py:398
  36.0 0.8 collective-permute-start.14
  36.7 3.8 %collective-permute-done.12.refs_1_ = bf16[128,512]{1,0:T(8,128)(2,1)S(1)} collective-permute-done((bf16[128,512]{1,0:T(8,128)(2,1)S(1)}, bf16[128,512]{1,0:T(8,128)(2,1)S(1)}, u32[]{:S(2)}, u32[]{:S(2)}) %collective-permute-start.12) | collective-permute-done | bytes 131104 | tf_op jit(solution)/shard_map/ppermute | solution.py:398
  40.6 6.8 %collective-permute-done.13.refs_2_ = bf16[128,512]{1,0:T(8,128)(2,1)S(1)} collective-permute-done((bf16[128,512]{1,0:T(8,128)(2,1)S(1)}, bf16[128,512]{1,0:T(8,128)(2,1)S(1)}, u32[]{:S(2)}, u32[]{:S(2)}) %collective-permute-start.13) | collective-permute-done | bytes 131104 | tf_op jit(solution)/shard_map/ppermute | solution.py:398
  47.4 0.4 cross_kernel.1
  47.9 1.4 %collective-permute-done.15 = f32[6,64,128]{2,1,0:T(8,128)S(1)} collective-permute-done((f32[6,64,128]{2,1,0:T(8,128)S(1)}, f32[6,64,128]{2,1,0:T(8,128)S(1)}, u32[]{:S(2)}, u32[]{:S(2)}) %collective-permute-start.15) | collective-permute-done | bytes 196640 | tf_op jit(solution)/shard_map/ppermute | solution.py:398
  49.3 1.6 %collective-permute-start.18 = (bf16[6,64,128]{2,1,0:T(8,128)(2,1)S(1)}, bf16[6,64,128]{2,1,0:T(8,128)(2,1)S(1)}, u32[]{:S(2)}, u32[]{:S(2)}) collective-permute-start(bf16[6,64,128]{2,1,0:T(8,128)(2,1)S(1)} %add_convert_fusion.2), channel_id=1, source_target_pairs={{0,6},{1,7},{2,4},{3,5},{4,2},{5,3},{6,0},{7,1},{8,14},{9,15},{10,... | collective-permute-start | bytes 294920 | tf_op jit(solution)/shard_map/ppermute | solution.py:398
  50.9 0.5 collective-permute-start.17
  51.4 1.5 %collective-permute-start.16 = (bf16[6,64,128]{2,1,0:T(8,128)(2,1)S(1)}, bf16[6,64,128]{2,1,0:T(8,128)(2,1)S(1)}, u32[]{:S(2)}, u32[]{:S(2)}) collective-permute-start(bf16[6,64,128]{2,1,0:T(8,128)(2,1)S(1)} %add_convert_fusion.2), channel_id=1, source_target_pairs={{0,2},{1,3},{2,0},{3,1},{4,6},{5,7},{6,4},{7,5},{8,10},{9,11},{10,... | collective-permute-start | bytes 294920 | tf_op jit(solution)/shard_map/ppermute | solution.py:398
  52.9 0.4 diag_kernel.1
  53.4 2.4 %collective-permute-done.18 = bf16[6,64,128]{2,1,0:T(8,128)(2,1)S(1)} collective-permute-done((bf16[6,64,128]{2,1,0:T(8,128)(2,1)S(1)}, bf16[6,64,128]{2,1,0:T(8,128)(2,1)S(1)}, u32[]{:S(2)}, u32[]{:S(2)}) %collective-permute-start.18) | collective-permute-done | bytes 98336 | tf_op jit(solution)/shard_map/ppermute | solution.py:398
  55.8 1.5 %collective-permute-done.17 = bf16[6,64,128]{2,1,0:T(8,128)(2,1)S(1)} collective-permute-done((bf16[6,64,128]{2,1,0:T(8,128)(2,1)S(1)}, bf16[6,64,128]{2,1,0:T(8,128)(2,1)S(1)}, u32[]{:S(2)}, u32[]{:S(2)}) %collective-permute-start.17) | collective-permute-done | bytes 98336 | tf_op jit(solution)/shard_map/ppermute | solution.py:398
  57.5 2.6 %collective-permute-start.21 = (bf16[7,64,128]{2,1,0:T(8,128)(2,1)S(1)}, bf16[7,64,128]{2,1,0:T(8,128)(2,1)S(1)}, u32[]{:S(2)}, u32[]{:S(2)}) collective-permute-start(bf16[7,64,128]{2,1,0:T(8,128)(2,1)S(1)} %pad_maximum_fusion), channel_id=1, source_target_pairs={{0,24},{1,25},{2,26},{3,27},{4,28},{5,29},{6,30},{7,31},{8,16},{9,... | collective-permute-start | bytes 344072 | tf_op jit(solution)/shard_map/ppermute | solution.py:398
  60.0 1.9 %collective-permute-start.19 = (bf16[7,64,128]{2,1,0:T(8,128)(2,1)S(1)}, bf16[7,64,128]{2,1,0:T(8,128)(2,1)S(1)}, u32[]{:S(2)}, u32[]{:S(2)}) collective-permute-start(bf16[7,64,128]{2,1,0:T(8,128)(2,1)S(1)} %pad_maximum_fusion), channel_id=1, source_target_pairs={{0,8},{1,9},{2,10},{3,11},{4,12},{5,13},{6,14},{7,15},{8,0},{9,1},... | collective-permute-start | bytes 344072 | tf_op jit(solution)/shard_map/ppermute | solution.py:398
  61.9 3.5 %collective-permute-done.21 = bf16[7,64,128]{2,1,0:T(8,128)(2,1)S(1)} collective-permute-done((bf16[7,64,128]{2,1,0:T(8,128)(2,1)S(1)}, bf16[7,64,128]{2,1,0:T(8,128)(2,1)S(1)}, u32[]{:S(2)}, u32[]{:S(2)}) %collective-permute-start.21) | collective-permute-done | bytes 114720 | tf_op jit(solution)/shard_map/ppermute | solution.py:398
  65.5 3.7 %collective-permute-done.20 = bf16[7,64,128]{2,1,0:T(8,128)(2,1)S(1)} collective-permute-done((bf16[7,64,128]{2,1,0:T(8,128)(2,1)S(1)}, bf16[7,64,128]{2,1,0:T(8,128)(2,1)S(1)}, u32[]{:S(2)}, u32[]{:S(2)}) %collective-permute-start.20) | collective-permute-done | bytes 114720 | tf_op jit(solution)/shard_map/ppermute | solution.py:398
  69.4 1.4 %collective-permute-done.22.other_ref = bf16[10,64,128]{2,1,0:T(8,128)(2,1)S(1)} collective-permute-done((bf16[10,64,128]{2,1,0:T(8,128)(2,1)S(1)}, bf16[10,64,128]{2,1,0:T(8,128)(2,1)S(1)}, u32[]{:S(2)}, u32[]{:S(2)}) %collective-permute-start.22) | collective-permute-done | bytes 163872 | tf_op jit(solution)/shard_map/ppermute | solution.py:398
  70.8 12.0 %top_kernel.1 = (bf16[128,512]{1,0:T(8,128)(2,1)S(1)}, f32[256,256]{1,0:T(8,128)S(1)}, bf16[256,128]{1,0:T(8,128)(2,1)S(1)}) custom-call(s32[1]{0:T(128)} %bitcast.pos_ref, bf16[10,64,128]{2,1,0:T(8,128)(2,1)S(1)} %slice_dynamic-update-slice_fusion.mine_ref, bf16[10,64,128]{2,1,0:T(8,128)(2,1)S(1)} %collective-permute-done.22.other_ref, ...), custom_call_target="tpu_custom_call" | custom-call | tf_op jit(solution)/shard_map/top_kernel/pallas_call | solution.py:356
  82.7 2.5 %collective-permute-start.25 = (bf16[128,512]{1,0:T(8,128)(2,1)S(1)}, bf16[128,512]{1,0:T(8,128)(2,1)S(1)}, u32[]{:S(2)}, u32[]{:S(2)}) collective-permute-start(bf16[128,512]{1,0:T(8,128)(2,1)S(1)} %get-tuple-element.66.refs_0_), channel_id=1, source_target_pairs={{0,24},{1,25},{2,26},{3,27},{4,28},{5,29},{6,30},{7,31},{8,16},{9,... | collective-permute-start | bytes 393224 | tf_op jit(solution)/shard_map/ppermute | solution.py:398
  85.3 1.9 %collective-permute-start.23 = (bf16[128,512]{1,0:T(8,128)(2,1)S(1)}, bf16[128,512]{1,0:T(8,128)(2,1)S(1)}, u32[]{:S(2)}, u32[]{:S(2)}) collective-permute-start(bf16[128,512]{1,0:T(8,128)(2,1)S(1)} %get-tuple-element.66.refs_0_), channel_id=1, source_target_pairs={{0,8},{1,9},{2,10},{3,11},{4,12},{5,13},{6,14},{7,15},{8,0},{9,1},... | collective-permute-start | bytes 393224 | tf_op jit(solution)/shard_map/ppermute | solution.py:398
  87.2 3.4 %factor_kernel.1.factor_ref = f32[128,128]{1,0:T(8,128)S(1)} custom-call(f32[256,256]{1,0:T(8,128)S(1)} %get-tuple-element.64.gram_ref, bf16[256,128]{1,0:T(8,128)(2,1)S(1)} %get-tuple-element.65.low_ref), custom_call_target="tpu_custom_call" | custom-call | tf_op jit(solution)/shard_map/factor_kernel/pallas_call | solution.py:356
  90.6 0.5 collective-permute-done.25.refs_3_
  91.1 5.9 %collective-permute-done.24.refs_2_ = bf16[128,512]{1,0:T(8,128)(2,1)S(1)} collective-permute-done((bf16[128,512]{1,0:T(8,128)(2,1)S(1)}, bf16[128,512]{1,0:T(8,128)(2,1)S(1)}, u32[]{:S(2)}, u32[]{:S(2)}) %collective-permute-start.24) | collective-permute-done | bytes 131104 | tf_op jit(solution)/shard_map/ppermute | solution.py:398
  96.9 0.8 coeffs_kernel.1
  97.9 1.2 collective-permute-done.26
  99.1 1.6 %collective-permute-start.29 = (bf16[1,128,128]{2,1,0:T(8,128)(2,1)S(1)}, bf16[1,128,128]{2,1,0:T(8,128)(2,1)S(1)}, u32[]{:S(2)}, u32[]{:S(2)}) collective-permute-start(bf16[1,128,128]{2,1,0:T(8,128)(2,1)S(1)} %add_convert_fusion.6), channel_id=1, source_target_pairs={{0,6},{1,7},{2,4},{3,5},{4,2},{5,3},{6,0},{7,1},{8,14},{9,15},{10,... | collective-permute-start | bytes 98312 | tf_op jit(solution)/shard_map/ppermute | solution.py:398
  100.7 0.3 collective-permute-start.28
  101.0 1.6 %collective-permute-start.27 = (bf16[1,128,128]{2,1,0:T(8,128)(2,1)S(1)}, bf16[1,128,128]{2,1,0:T(8,128)(2,1)S(1)}, u32[]{:S(2)}, u32[]{:S(2)}) collective-permute-start(bf16[1,128,128]{2,1,0:T(8,128)(2,1)S(1)} %add_convert_fusion.6), channel_id=1, source_target_pairs={{0,2},{1,3},{2,0},{3,1},{4,6},{5,7},{6,4},{7,5},{8,10},{9,11},{10,... | collective-permute-start | bytes 98312 | tf_op jit(solution)/shard_map/ppermute | solution.py:398
  102.7 1.3 %collective-permute-done.29 = bf16[1,128,128]{2,1,0:T(8,128)(2,1)S(1)} collective-permute-done((bf16[1,128,128]{2,1,0:T(8,128)(2,1)S(1)}, bf16[1,128,128]{2,1,0:T(8,128)(2,1)S(1)}, u32[]{:S(2)}, u32[]{:S(2)}) %collective-permute-start.29) | collective-permute-done | bytes 32800 | tf_op jit(solution)/shard_map/ppermute | solution.py:398
  104.0 0.6 collective-permute-done.28
  104.6 0.3 collective-permute-done.27
  105.1 1.2 collective-permute-done.30.other_ref
  106.3 0.8 project_kernel.1
  107.0 1.2 collective-permute-start.35
  108.2 1.3 %collective-permute-start.36 = (bf16[32,2048]{1,0:T(8,128)(2,1)S(1)}, bf16[32,2048]{1,0:T(8,128)(2,1)S(1)}, u32[]{:S(2)}, u32[]{:S(2)}) collective-permute-start(bf16[32,2048]{1,0:T(8,128)(2,1)S(1)} %get-tuple-element.74), channel_id=1, source_target_pairs={{0,7},{1,6},{2,5},{3,4},{4,3},{5,2},{6,1},{7,0},{8,15},{9,14},{10,... | collective-permute-start | bytes 393224 | tf_op jit(solution)/shard_map/ppermute | solution.py:398
  109.5 1.7 %collective-permute-start.31 = (bf16[32,2048]{1,0:T(8,128)(2,1)S(1)}, bf16[32,2048]{1,0:T(8,128)(2,1)S(1)}, u32[]{:S(2)}, u32[]{:S(2)}) collective-permute-start(bf16[32,2048]{1,0:T(8,128)(2,1)S(1)} %get-tuple-element.69), channel_id=1, source_target_pairs={{0,4},{1,5},{2,6},{3,7},{4,0},{5,1},{6,2},{7,3},{8,12},{9,13},{10,... | collective-permute-start | bytes 393224 | tf_op jit(solution)/shard_map/ppermute | solution.py:398
  111.4 1.8 %collective-permute-start.37 = (bf16[32,2048]{1,0:T(8,128)(2,1)S(1)}, bf16[32,2048]{1,0:T(8,128)(2,1)S(1)}, u32[]{:S(2)}, u32[]{:S(2)}) collective-permute-start(bf16[32,2048]{1,0:T(8,128)(2,1)S(1)} %get-tuple-element.75), channel_id=1, source_target_pairs={{0,2},{1,3},{2,0},{3,1},{4,6},{5,7},{6,4},{7,5},{8,10},{9,11},{10,... | collective-permute-start | bytes 393224 | tf_op jit(solution)/shard_map/ppermute | solution.py:398
  113.2 1.3 %collective-permute-done.35.refs_0_ = bf16[32,2048]{1,0:T(8,128)(2,1)S(1)} collective-permute-done((bf16[32,2048]{1,0:T(8,128)(2,1)S(1)}, bf16[32,2048]{1,0:T(8,128)(2,1)S(1)}, u32[]{:S(2)}, u32[]{:S(2)}) %collective-permute-start.35) | collective-permute-done | bytes 131104 | tf_op jit(solution)/shard_map/ppermute | solution.py:398
  114.4 1.3 %collective-permute-done.36.refs_1_ = bf16[32,2048]{1,0:T(8,128)(2,1)S(1)} collective-permute-done((bf16[32,2048]{1,0:T(8,128)(2,1)S(1)}, bf16[32,2048]{1,0:T(8,128)(2,1)S(1)}, u32[]{:S(2)}, u32[]{:S(2)}) %collective-permute-start.36) | collective-permute-done | bytes 131104 | tf_op jit(solution)/shard_map/ppermute | solution.py:398
  115.7 1.3 %collective-permute-start.34 = (bf16[32,2048]{1,0:T(8,128)(2,1)S(1)}, bf16[32,2048]{1,0:T(8,128)(2,1)S(1)}, u32[]{:S(2)}, u32[]{:S(2)}) collective-permute-start(bf16[32,2048]{1,0:T(8,128)(2,1)S(1)} %get-tuple-element.72), channel_id=1, source_target_pairs={{0,1},{1,0},{2,3},{3,2},{4,5},{5,4},{6,7},{7,6},{8,9},{9,8},{10,11... | collective-permute-start | bytes 393224 | tf_op jit(solution)/shard_map/ppermute | solution.py:398
  117.0 5.2 %collective-permute-done.37.refs_2_ = bf16[32,2048]{1,0:T(8,128)(2,1)S(1)} collective-permute-done((bf16[32,2048]{1,0:T(8,128)(2,1)S(1)}, bf16[32,2048]{1,0:T(8,128)(2,1)S(1)}, u32[]{:S(2)}, u32[]{:S(2)}) %collective-permute-start.37) | collective-permute-done | bytes 131104 | tf_op jit(solution)/shard_map/ppermute | solution.py:398
  122.3 0.8 whole_kernel.2.refs_4_
  123.1 0.8 whole_kernel.3
  (36 shorter events, 1.1 us)
Async XLA Ops:
  1.1 8.4 %collective-permute-start = (bf16[32,2048]{1,0:T(8,128)(2,1)S(1)}, bf16[32,2048]{1,0:T(8,128)(2,1)S(1)}, u32[]{:S(2)}, u32[]{:S(2)}) collective-permute-start(bf16[32,2048]{1,0:T(8,128)(2,1)S(1)} %get-tuple-element.45), channel_id=1, source_target_pairs={{0,6},{1,7},{2,4},{3,5},{4,2},{5,3},{6,0},{7,1},{8,14},{9,15},{10,... | collective-permute-start | bytes 393224 | tf_op jit(solution)/shard_map/ppermute | solution.py:398
  5.1 6.8 %collective-permute-start.1 = (bf16[32,2048]{1,0:T(8,128)(2,1)S(1)}, bf16[32,2048]{1,0:T(8,128)(2,1)S(1)}, u32[]{:S(2)}, u32[]{:S(2)}) collective-permute-start(bf16[32,2048]{1,0:T(8,128)(2,1)S(1)} %get-tuple-element.46), channel_id=1, source_target_pairs={{0,7},{1,6},{2,5},{3,4},{4,3},{5,2},{6,1},{7,0},{8,15},{9,14},{10,... | collective-permute-start | bytes 393224 | tf_op jit(solution)/shard_map/ppermute | solution.py:398
  5.1 10.2 %collective-permute-start.2 = (bf16[32,2048]{1,0:T(8,128)(2,1)S(1)}, bf16[32,2048]{1,0:T(8,128)(2,1)S(1)}, u32[]{:S(2)}, u32[]{:S(2)}) collective-permute-start(bf16[32,2048]{1,0:T(8,128)(2,1)S(1)} %get-tuple-element.47), channel_id=1, source_target_pairs={{0,2},{1,3},{2,0},{3,1},{4,6},{5,7},{6,4},{7,5},{8,10},{9,11},{10,... | collective-permute-start | bytes 393224 | tf_op jit(solution)/shard_map/ppermute | solution.py:398
  6.2 9.1 %collective-permute-start.3 = (bf16[32,2048]{1,0:T(8,128)(2,1)S(1)}, bf16[32,2048]{1,0:T(8,128)(2,1)S(1)}, u32[]{:S(2)}, u32[]{:S(2)}) collective-permute-start(bf16[32,2048]{1,0:T(8,128)(2,1)S(1)} %get-tuple-element.48), channel_id=1, source_target_pairs={{0,4},{1,5},{2,6},{3,7},{4,0},{5,1},{6,2},{7,3},{8,12},{9,13},{10,... | collective-permute-start | bytes 393224 | tf_op jit(solution)/shard_map/ppermute | solution.py:398
  8.9 7.5 %collective-permute-start.4 = (bf16[32,2048]{1,0:T(8,128)(2,1)S(1)}, bf16[32,2048]{1,0:T(8,128)(2,1)S(1)}, u32[]{:S(2)}, u32[]{:S(2)}) collective-permute-start(bf16[32,2048]{1,0:T(8,128)(2,1)S(1)} %get-tuple-element.50), channel_id=1, source_target_pairs={{0,3},{1,2},{2,1},{3,0},{4,7},{5,6},{6,5},{7,4},{8,11},{9,10},{10,... | collective-permute-start | bytes 393224 | tf_op jit(solution)/shard_map/ppermute | solution.py:398
  9.5 7.6 %collective-permute-start.5 = (bf16[32,2048]{1,0:T(8,128)(2,1)S(1)}, bf16[32,2048]{1,0:T(8,128)(2,1)S(1)}, u32[]{:S(2)}, u32[]{:S(2)}) collective-permute-start(bf16[32,2048]{1,0:T(8,128)(2,1)S(1)} %get-tuple-element.51), channel_id=1, source_target_pairs={{0,5},{1,4},{2,7},{3,6},{4,1},{5,0},{6,3},{7,2},{8,13},{9,12},{10,... | collective-permute-start | bytes 393224 | tf_op jit(solution)/shard_map/ppermute | solution.py:398
  11.9 5.3 %collective-permute-start.6 = (bf16[32,2048]{1,0:T(8,128)(2,1)S(1)}, bf16[32,2048]{1,0:T(8,128)(2,1)S(1)}, u32[]{:S(2)}, u32[]{:S(2)}) collective-permute-start(bf16[32,2048]{1,0:T(8,128)(2,1)S(1)} %get-tuple-element.52), channel_id=1, source_target_pairs={{0,1},{1,0},{2,3},{3,2},{4,5},{5,4},{6,7},{7,6},{8,9},{9,8},{10,11... | collective-permute-start | bytes 393224 | tf_op jit(solution)/shard_map/ppermute | solution.py:398
  17.7 1.4 %collective-permute-start.7 = (f32[3,64,128]{2,1,0:T(8,128)S(1)}, f32[3,64,128]{2,1,0:T(8,128)S(1)}, u32[]{:S(2)}, u32[]{:S(2)}) collective-permute-start(f32[3,64,128]{2,1,0:T(8,128)S(1)} %get-tuple-element.56), channel_id=1, source_target_pairs={{0,1},{1,0},{2,3},{3,2},{4,5},{5,4},{6,7},{7,6},{8,9},{9,8},{10,11... | collective-permute-start | bytes 294920 | tf_op jit(solution)/shard_map/ppermute | solution.py:398
  19.1 5.1 %collective-permute-start.10 = (bf16[3,64,128]{2,1,0:T(8,128)(2,1)S(1)}, bf16[3,64,128]{2,1,0:T(8,128)(2,1)S(1)}, u32[]{:S(2)}, u32[]{:S(2)}) collective-permute-start(bf16[3,64,128]{2,1,0:T(8,128)(2,1)S(1)} %add_convert_fusion.4), channel_id=1, source_target_pairs={{0,6},{1,7},{2,4},{3,5},{4,2},{5,3},{6,0},{7,1},{8,14},{9,15},{10,... | collective-permute-start | bytes 147464 | tf_op jit(solution)/shard_map/ppermute | solution.py:398
  21.6 4.1 %collective-permute-start.9 = (bf16[3,64,128]{2,1,0:T(8,128)(2,1)S(1)}, bf16[3,64,128]{2,1,0:T(8,128)(2,1)S(1)}, u32[]{:S(2)}, u32[]{:S(2)}) collective-permute-start(bf16[3,64,128]{2,1,0:T(8,128)(2,1)S(1)} %add_convert_fusion.4), channel_id=1, source_target_pairs={{0,4},{1,5},{2,6},{3,7},{4,0},{5,1},{6,2},{7,3},{8,12},{9,13},{10,... | collective-permute-start | bytes 147464 | tf_op jit(solution)/shard_map/ppermute | solution.py:398
  22.1 4.1 %collective-permute-start.8 = (bf16[3,64,128]{2,1,0:T(8,128)(2,1)S(1)}, bf16[3,64,128]{2,1,0:T(8,128)(2,1)S(1)}, u32[]{:S(2)}, u32[]{:S(2)}) collective-permute-start(bf16[3,64,128]{2,1,0:T(8,128)(2,1)S(1)} %add_convert_fusion.4), channel_id=1, source_target_pairs={{0,2},{1,3},{2,0},{3,1},{4,6},{5,7},{6,4},{7,5},{8,10},{9,11},{10,... | collective-permute-start | bytes 147464 | tf_op jit(solution)/shard_map/ppermute | solution.py:398
  26.2 1.3 %collective-permute-start.11 = (bf16[3,64,128]{2,1,0:T(8,128)(2,1)S(1)}, bf16[3,64,128]{2,1,0:T(8,128)(2,1)S(1)}, u32[]{:S(2)}, u32[]{:S(2)}) collective-permute-start(bf16[3,64,128]{2,1,0:T(8,128)(2,1)S(1)} %add_convert_fusion.3.mine_ref), channel_id=1, source_target_pairs={{0,1},{1,0},{2,3},{3,2},{4,5},{5,4},{6,7},{7,6},{8,9},{9,8},{10,11... | collective-permute-start | bytes 147464 | tf_op jit(solution)/shard_map/ppermute | solution.py:398
  32.3 8.3 %collective-permute-start.12 = (bf16[128,512]{1,0:T(8,128)(2,1)S(1)}, bf16[128,512]{1,0:T(8,128)(2,1)S(1)}, u32[]{:S(2)}, u32[]{:S(2)}) collective-permute-start(bf16[128,512]{1,0:T(8,128)(2,1)S(1)} %get-tuple-element.58), channel_id=1, source_target_pairs={{0,24},{1,25},{2,26},{3,27},{4,28},{5,29},{6,30},{7,31},{8,16},{9,... | collective-permute-start | bytes 393224 | tf_op jit(solution)/shard_map/ppermute | solution.py:398
  36.0 11.4 %collective-permute-start.13 = (bf16[128,512]{1,0:T(8,128)(2,1)S(1)}, bf16[128,512]{1,0:T(8,128)(2,1)S(1)}, u32[]{:S(2)}, u32[]{:S(2)}) collective-permute-start(bf16[128,512]{1,0:T(8,128)(2,1)S(1)} %get-tuple-element.59), channel_id=1, source_target_pairs={{0,16},{1,17},{2,18},{3,19},{4,20},{5,21},{6,22},{7,23},{8,24},{9,... | collective-permute-start | bytes 393224 | tf_op jit(solution)/shard_map/ppermute | solution.py:398
  36.0 11.4 %collective-permute-start.14 = (bf16[128,512]{1,0:T(8,128)(2,1)S(1)}, bf16[128,512]{1,0:T(8,128)(2,1)S(1)}, u32[]{:S(2)}, u32[]{:S(2)}) collective-permute-start(bf16[128,512]{1,0:T(8,128)(2,1)S(1)} %get-tuple-element.60), channel_id=1, source_target_pairs={{0,8},{1,9},{2,10},{3,11},{4,12},{5,13},{6,14},{7,15},{8,0},{9,1},... | collective-permute-start | bytes 393224 | tf_op jit(solution)/shard_map/ppermute | solution.py:398
  47.8 1.5 %collective-permute-start.15 = (f32[6,64,128]{2,1,0:T(8,128)S(1)}, f32[6,64,128]{2,1,0:T(8,128)S(1)}, u32[]{:S(2)}, u32[]{:S(2)}) collective-permute-start(f32[6,64,128]{2,1,0:T(8,128)S(1)} %get-tuple-element.62), channel_id=1, source_target_pairs={{0,1},{1,0},{2,3},{3,2},{4,5},{5,4},{6,7},{7,6},{8,9},{9,8},{10,11... | collective-permute-start | bytes 589832 | tf_op jit(solution)/shard_map/ppermute | solution.py:398
  49.3 6.4 %collective-permute-start.18 = (bf16[6,64,128]{2,1,0:T(8,128)(2,1)S(1)}, bf16[6,64,128]{2,1,0:T(8,128)(2,1)S(1)}, u32[]{:S(2)}, u32[]{:S(2)}) collective-permute-start(bf16[6,64,128]{2,1,0:T(8,128)(2,1)S(1)} %add_convert_fusion.2), channel_id=1, source_target_pairs={{0,6},{1,7},{2,4},{3,5},{4,2},{5,3},{6,0},{7,1},{8,14},{9,15},{10,... | collective-permute-start | bytes 294920 | tf_op jit(solution)/shard_map/ppermute | solution.py:398
  50.9 6.3 %collective-permute-start.17 = (bf16[6,64,128]{2,1,0:T(8,128)(2,1)S(1)}, bf16[6,64,128]{2,1,0:T(8,128)(2,1)S(1)}, u32[]{:S(2)}, u32[]{:S(2)}) collective-permute-start(bf16[6,64,128]{2,1,0:T(8,128)(2,1)S(1)} %add_convert_fusion.2), channel_id=1, source_target_pairs={{0,4},{1,5},{2,6},{3,7},{4,0},{5,1},{6,2},{7,3},{8,12},{9,13},{10,... | collective-permute-start | bytes 294920 | tf_op jit(solution)/shard_map/ppermute | solution.py:398
  51.4 6.0 %collective-permute-start.16 = (bf16[6,64,128]{2,1,0:T(8,128)(2,1)S(1)}, bf16[6,64,128]{2,1,0:T(8,128)(2,1)S(1)}, u32[]{:S(2)}, u32[]{:S(2)}) collective-permute-start(bf16[6,64,128]{2,1,0:T(8,128)(2,1)S(1)} %add_convert_fusion.2), channel_id=1, source_target_pairs={{0,2},{1,3},{2,0},{3,1},{4,6},{5,7},{6,4},{7,5},{8,10},{9,11},{10,... | collective-permute-start | bytes 294920 | tf_op jit(solution)/shard_map/ppermute | solution.py:398
  57.5 8.0 %collective-permute-start.21 = (bf16[7,64,128]{2,1,0:T(8,128)(2,1)S(1)}, bf16[7,64,128]{2,1,0:T(8,128)(2,1)S(1)}, u32[]{:S(2)}, u32[]{:S(2)}) collective-permute-start(bf16[7,64,128]{2,1,0:T(8,128)(2,1)S(1)} %pad_maximum_fusion), channel_id=1, source_target_pairs={{0,24},{1,25},{2,26},{3,27},{4,28},{5,29},{6,30},{7,31},{8,16},{9,... | collective-permute-start | bytes 344072 | tf_op jit(solution)/shard_map/ppermute | solution.py:398
  60.0 9.2 %collective-permute-start.20 = (bf16[7,64,128]{2,1,0:T(8,128)(2,1)S(1)}, bf16[7,64,128]{2,1,0:T(8,128)(2,1)S(1)}, u32[]{:S(2)}, u32[]{:S(2)}) collective-permute-start(bf16[7,64,128]{2,1,0:T(8,128)(2,1)S(1)} %pad_maximum_fusion), channel_id=1, source_target_pairs={{0,16},{1,17},{2,18},{3,19},{4,20},{5,21},{6,22},{7,23},{8,24},{9,... | collective-permute-start | bytes 344072 | tf_op jit(solution)/shard_map/ppermute | solution.py:398
  60.0 9.2 %collective-permute-start.19 = (bf16[7,64,128]{2,1,0:T(8,128)(2,1)S(1)}, bf16[7,64,128]{2,1,0:T(8,128)(2,1)S(1)}, u32[]{:S(2)}, u32[]{:S(2)}) collective-permute-start(bf16[7,64,128]{2,1,0:T(8,128)(2,1)S(1)} %pad_maximum_fusion), channel_id=1, source_target_pairs={{0,8},{1,9},{2,10},{3,11},{4,12},{5,13},{6,14},{7,15},{8,0},{9,1},... | collective-permute-start | bytes 344072 | tf_op jit(solution)/shard_map/ppermute | solution.py:398
  69.3 1.5 %collective-permute-start.22 = (bf16[10,64,128]{2,1,0:T(8,128)(2,1)S(1)}, bf16[10,64,128]{2,1,0:T(8,128)(2,1)S(1)}, u32[]{:S(2)}, u32[]{:S(2)}) collective-permute-start(bf16[10,64,128]{2,1,0:T(8,128)(2,1)S(1)} %slice_dynamic-update-slice_fusion.mine_ref), channel_id=1, source_target_pairs={{0,1},{1,0},{2,3},{3,2},{4,5},{5,4},{6,7},{7,6},{8,9},{9,8},{10,11... | collective-permute-start | bytes 491528 | tf_op jit(solution)/shard_map/ppermute | solution.py:398
  82.7 8.3 %collective-permute-start.25 = (bf16[128,512]{1,0:T(8,128)(2,1)S(1)}, bf16[128,512]{1,0:T(8,128)(2,1)S(1)}, u32[]{:S(2)}, u32[]{:S(2)}) collective-permute-start(bf16[128,512]{1,0:T(8,128)(2,1)S(1)} %get-tuple-element.66.refs_0_), channel_id=1, source_target_pairs={{0,24},{1,25},{2,26},{3,27},{4,28},{5,29},{6,30},{7,31},{8,16},{9,... | collective-permute-start | bytes 393224 | tf_op jit(solution)/shard_map/ppermute | solution.py:398
  85.3 11.7 %collective-permute-start.24 = (bf16[128,512]{1,0:T(8,128)(2,1)S(1)}, bf16[128,512]{1,0:T(8,128)(2,1)S(1)}, u32[]{:S(2)}, u32[]{:S(2)}) collective-permute-start(bf16[128,512]{1,0:T(8,128)(2,1)S(1)} %get-tuple-element.66.refs_0_), channel_id=1, source_target_pairs={{0,16},{1,17},{2,18},{3,19},{4,20},{5,21},{6,22},{7,23},{8,24},{9,... | collective-permute-start | bytes 393224 | tf_op jit(solution)/shard_map/ppermute | solution.py:398
  85.3 11.7 %collective-permute-start.23 = (bf16[128,512]{1,0:T(8,128)(2,1)S(1)}, bf16[128,512]{1,0:T(8,128)(2,1)S(1)}, u32[]{:S(2)}, u32[]{:S(2)}) collective-permute-start(bf16[128,512]{1,0:T(8,128)(2,1)S(1)} %get-tuple-element.66.refs_0_), channel_id=1, source_target_pairs={{0,8},{1,9},{2,10},{3,11},{4,12},{5,13},{6,14},{7,15},{8,0},{9,1},... | collective-permute-start | bytes 393224 | tf_op jit(solution)/shard_map/ppermute | solution.py:398
  97.8 1.3 %collective-permute-start.26 = (f32[1,128,128]{2,1,0:T(8,128)S(1)}, f32[1,128,128]{2,1,0:T(8,128)S(1)}, u32[]{:S(2)}, u32[]{:S(2)}) collective-permute-start(f32[1,128,128]{2,1,0:T(8,128)S(1)} %get-tuple-element.68), channel_id=1, source_target_pairs={{0,1},{1,0},{2,3},{3,2},{4,5},{5,4},{6,7},{7,6},{8,9},{9,8},{10,11... | collective-permute-start | bytes 196616 | tf_op jit(solution)/shard_map/ppermute | solution.py:398
  99.1 4.9 %collective-permute-start.29 = (bf16[1,128,128]{2,1,0:T(8,128)(2,1)S(1)}, bf16[1,128,128]{2,1,0:T(8,128)(2,1)S(1)}, u32[]{:S(2)}, u32[]{:S(2)}) collective-permute-start(bf16[1,128,128]{2,1,0:T(8,128)(2,1)S(1)} %add_convert_fusion.6), channel_id=1, source_target_pairs={{0,6},{1,7},{2,4},{3,5},{4,2},{5,3},{6,0},{7,1},{8,14},{9,15},{10,... | collective-permute-start | bytes 98312 | tf_op jit(solution)/shard_map/ppermute | solution.py:398
  100.7 3.9 %collective-permute-start.28 = (bf16[1,128,128]{2,1,0:T(8,128)(2,1)S(1)}, bf16[1,128,128]{2,1,0:T(8,128)(2,1)S(1)}, u32[]{:S(2)}, u32[]{:S(2)}) collective-permute-start(bf16[1,128,128]{2,1,0:T(8,128)(2,1)S(1)} %add_convert_fusion.6), channel_id=1, source_target_pairs={{0,4},{1,5},{2,6},{3,7},{4,0},{5,1},{6,2},{7,3},{8,12},{9,13},{10,... | collective-permute-start | bytes 98312 | tf_op jit(solution)/shard_map/ppermute | solution.py:398
  101.0 3.9 %collective-permute-start.27 = (bf16[1,128,128]{2,1,0:T(8,128)(2,1)S(1)}, bf16[1,128,128]{2,1,0:T(8,128)(2,1)S(1)}, u32[]{:S(2)}, u32[]{:S(2)}) collective-permute-start(bf16[1,128,128]{2,1,0:T(8,128)(2,1)S(1)} %add_convert_fusion.6), channel_id=1, source_target_pairs={{0,2},{1,3},{2,0},{3,1},{4,6},{5,7},{6,4},{7,5},{8,10},{9,11},{10,... | collective-permute-start | bytes 98312 | tf_op jit(solution)/shard_map/ppermute | solution.py:398
  105.0 1.3 %collective-permute-start.30 = (bf16[1,128,128]{2,1,0:T(8,128)(2,1)S(1)}, bf16[1,128,128]{2,1,0:T(8,128)(2,1)S(1)}, u32[]{:S(2)}, u32[]{:S(2)}) collective-permute-start(bf16[1,128,128]{2,1,0:T(8,128)(2,1)S(1)} %add_convert_fusion.5.mine_ref), channel_id=1, source_target_pairs={{0,1},{1,0},{2,3},{3,2},{4,5},{5,4},{6,7},{7,6},{8,9},{9,8},{10,11... | collective-permute-start | bytes 98312 | tf_op jit(solution)/shard_map/ppermute | solution.py:398
  107.0 7.4 %collective-permute-start.35 = (bf16[32,2048]{1,0:T(8,128)(2,1)S(1)}, bf16[32,2048]{1,0:T(8,128)(2,1)S(1)}, u32[]{:S(2)}, u32[]{:S(2)}) collective-permute-start(bf16[32,2048]{1,0:T(8,128)(2,1)S(1)} %get-tuple-element.73), channel_id=1, source_target_pairs={{0,6},{1,7},{2,4},{3,5},{4,2},{5,3},{6,0},{7,1},{8,14},{9,15},{10,... | collective-permute-start | bytes 393224 | tf_op jit(solution)/shard_map/ppermute | solution.py:398
  108.2 7.5 %collective-permute-start.36 = (bf16[32,2048]{1,0:T(8,128)(2,1)S(1)}, bf16[32,2048]{1,0:T(8,128)(2,1)S(1)}, u32[]{:S(2)}, u32[]{:S(2)}) collective-permute-start(bf16[32,2048]{1,0:T(8,128)(2,1)S(1)} %get-tuple-element.74), channel_id=1, source_target_pairs={{0,7},{1,6},{2,5},{3,4},{4,3},{5,2},{6,1},{7,0},{8,15},{9,14},{10,... | collective-permute-start | bytes 393224 | tf_op jit(solution)/shard_map/ppermute | solution.py:398
  109.5 13.6 %collective-permute-start.31 = (bf16[32,2048]{1,0:T(8,128)(2,1)S(1)}, bf16[32,2048]{1,0:T(8,128)(2,1)S(1)}, u32[]{:S(2)}, u32[]{:S(2)}) collective-permute-start(bf16[32,2048]{1,0:T(8,128)(2,1)S(1)} %get-tuple-element.69), channel_id=1, source_target_pairs={{0,4},{1,5},{2,6},{3,7},{4,0},{5,1},{6,2},{7,3},{8,12},{9,13},{10,... | collective-permute-start | bytes 393224 | tf_op jit(solution)/shard_map/ppermute | solution.py:398
  111.2 11.9 %collective-permute-start.32 = (bf16[32,2048]{1,0:T(8,128)(2,1)S(1)}, bf16[32,2048]{1,0:T(8,128)(2,1)S(1)}, u32[]{:S(2)}, u32[]{:S(2)}) collective-permute-start(bf16[32,2048]{1,0:T(8,128)(2,1)S(1)} %get-tuple-element.70), channel_id=1, source_target_pairs={{0,3},{1,2},{2,1},{3,0},{4,7},{5,6},{6,5},{7,4},{8,11},{9,10},{10,... | collective-permute-start | bytes 393224 | tf_op jit(solution)/shard_map/ppermute | solution.py:398
  111.4 10.9 %collective-permute-start.37 = (bf16[32,2048]{1,0:T(8,128)(2,1)S(1)}, bf16[32,2048]{1,0:T(8,128)(2,1)S(1)}, u32[]{:S(2)}, u32[]{:S(2)}) collective-permute-start(bf16[32,2048]{1,0:T(8,128)(2,1)S(1)} %get-tuple-element.75), channel_id=1, source_target_pairs={{0,2},{1,3},{2,0},{3,1},{4,6},{5,7},{6,4},{7,5},{8,10},{9,11},{10,... | collective-permute-start | bytes 393224 | tf_op jit(solution)/shard_map/ppermute | solution.py:398
  114.4 8.7 %collective-permute-start.33 = (bf16[32,2048]{1,0:T(8,128)(2,1)S(1)}, bf16[32,2048]{1,0:T(8,128)(2,1)S(1)}, u32[]{:S(2)}, u32[]{:S(2)}) collective-permute-start(bf16[32,2048]{1,0:T(8,128)(2,1)S(1)} %get-tuple-element.71), channel_id=1, source_target_pairs={{0,5},{1,4},{2,7},{3,6},{4,1},{5,0},{6,3},{7,2},{8,13},{9,12},{10,... | collective-permute-start | bytes 393224 | tf_op jit(solution)/shard_map/ppermute | solution.py:398
  115.7 7.4 %collective-permute-start.34 = (bf16[32,2048]{1,0:T(8,128)(2,1)S(1)}, bf16[32,2048]{1,0:T(8,128)(2,1)S(1)}, u32[]{:S(2)}, u32[]{:S(2)}) collective-permute-start(bf16[32,2048]{1,0:T(8,128)(2,1)S(1)} %get-tuple-element.72), channel_id=1, source_target_pairs={{0,1},{1,0},{2,3},{3,2},{4,5},{5,4},{6,7},{7,6},{8,9},{9,8},{10,11... | collective-permute-start | bytes 393224 | tf_op jit(solution)/shard_map/ppermute | solution.py:398

commit v6 on v3

--- a/solution.py
+++ b/solution.py
@@ -13,7 +13,8 @@
 TILE = 8
 PANEL = 64
 PLANE_ORDER = (0, 6, 7, 2, 4, 3, 5, 1)
-TREE_ORDER = (0, 3, 2, 1)
+TREE_ORDER = (0, 2, 3, 1)
+SUM_ORDER = (0, 1, 3, 2)
 PIVOT_SHARE = 2e-4
 
 precise = lax.Precision.HIGHEST
@@ -275,7 +276,7 @@
     core, z = place(pos_ref)
     for ref, m in zip(nodes, TREE_ORDER):
         all_ref[z ^ m] = ref[...]
-        diag_ref[z ^ m] = joined(mine_ref, other_ref, core, len(PAIRS) + m)
+        diag_ref[z ^ m] = joined(mine_ref, other_ref, core, len(PAIRS) + SUM_ORDER.index(m))
 
     def attempt(careful):
         cross = {pair: joined(mine_ref, other_ref, core, b) for b, pair in enumerate(PAIRS)}
@@ -313,7 +314,7 @@
     core, z = place(pos_ref)
     width = tops[0].shape[1]
     total = None
-    for m, ref in enumerate(tops):
+    for m, ref in zip(SUM_ORDER, tops):
         part = dot_low(rows_ref[:, chunk(z, m, width)], ref[...], 1, 1)
         total = part if total is None else total + part
     split([dot(total, factor_ref[...], 1, 1)], core, mine_ref, theirs_ref)
@@ -326,7 +327,7 @@
     solved_ref[...] = dot(joined(mine_ref, other_ref, core, 0), factor_ref[...], 1, 0)
     solved = [solved_ref[chunk(member(pos_ref), m, height), :] for m in PLANE_ORDER]
     solved = jnp.concatenate(solved, 0).astype(bf16)
-    for m, ref in enumerate(tops):
+    for m, ref in zip(SUM_ORDER, tops):
         made = dot_low(solved, ref[...], 1, 0).astype(bf16)
         for k in range(PLANE):
             outs[k][:, chunk(z, m, width)] = made[k * height : (k + 1) * height, :]
@@ -403,7 +404,7 @@
         scratch=[pltpu.VMEM((PLANES, RANK, part), bf16)],
     )
     mine = plane_sum(mine, theirs)
-    both = swap_all([jnp.concatenate([mine.astype(bf16), diag], 0)] * PLANES, range(PLANES), PLANE)
+    both = swap_all([jnp.concatenate([mine.astype(bf16), diag], 0)] * PLANES, SUM_ORDER, PLANE)
     mine = jnp.concatenate([sum4([x[: len(PAIRS)] for x in both])] + [x[len(PAIRS) :].astype(f32) for x in both], 0)
     top, gram, low = kernel(
         top_kernel,
@@ -413,7 +414,7 @@
         + sound_shape
         + work_shapes * 2,
     )
-    tops = swap_all([top] * PLANES, range(PLANES), PLANE)
+    tops = swap_all([top] * PLANES, SUM_ORDER, PLANE)
     (factor,) = kernel(factor_kernel, [((RANK, RANK), f32)], gram, low, scalar=False)
 
     mine, theirs = kernel(coeffs_kernel, [((1, height // 2, RANK), f32)] * 2, pos, rows, factor, *tops)

time: 124 us -> 123 us (level)
  no operation moved by 1% of the time
where the time goes in v6:
time: 123 us
  waiting for transfers between devices  58.4 us (47%)
  starting transfers between devices  38.7 us (31%)
  Pallas kernels  24.3 us (20%)
    ppermute x38, waiting for transfers between devices, swap(): return lax.ppermute(x, 'cols', [(i, i ^ apart) for i in range(count)])  58.4 us
    ppermute x38, starting transfers between devices, swap(): return lax.ppermute(x, 'cols', [(i, i ^ apart) for i in range(count)])  38.7 us
    pallas_call x10, Pallas kernels, kernel(): pl.pallas_call(fn, out_shape=[jax.ShapeDtypeStruct(s, d) for s, d in shap...  24.3 us
  transfers between devices with their start and end apart: 38, of which 31 were waited for; matrix products, arithmetic and copies ran while one was open for 0% of the time, Pallas kernels for 3%

profile of v6, /device:TPU:0, one launch (start us, length us, event | category | flops | bytes accessed | tf_op | source)
XLA Modules:
  0.0 123.1 jit_solution(16245179674791559148)
XLA Ops:
  0.0 1.2 copy-done
  1.3 4.0 %collective-permute-start = (bf16[32,2048]{1,0:T(8,128)(2,1)S(1)}, bf16[32,2048]{1,0:T(8,128)(2,1)S(1)}, u32[]{:S(2)}, u32[]{:S(2)}) collective-permute-start(bf16[32,2048]{1,0:T(8,128)(2,1)S(1)} %get-tuple-element.37), channel_id=1, source_target_pairs={{0,6},{1,7},{2,4},{3,5},{4,2},{5,3},{6,0},{7,1},{8,14},{9,15},{10,... | collective-permute-start | bytes 393224 | tf_op jit(solution)/shard_map/ppermute | solution.py:367
  5.3 1.1 collective-permute-start.2
  6.4 1.5 %collective-permute-start.3 = (bf16[32,2048]{1,0:T(8,128)(2,1)S(1)}, bf16[32,2048]{1,0:T(8,128)(2,1)S(1)}, u32[]{:S(2)}, u32[]{:S(2)}) collective-permute-start(bf16[32,2048]{1,0:T(8,128)(2,1)S(1)} %get-tuple-element.40), channel_id=1, source_target_pairs={{0,4},{1,5},{2,6},{3,7},{4,0},{5,1},{6,2},{7,3},{8,12},{9,13},{10,... | collective-permute-start | bytes 393224 | tf_op jit(solution)/shard_map/ppermute | solution.py:367
  7.9 0.6 collective-permute-start.4
  8.5 0.7 collective-permute-done.refs_1_
  9.2 2.8 %collective-permute-done.1.refs_2_ = bf16[32,2048]{1,0:T(8,128)(2,1)S(1)} collective-permute-done((bf16[32,2048]{1,0:T(8,128)(2,1)S(1)}, bf16[32,2048]{1,0:T(8,128)(2,1)S(1)}, u32[]{:S(2)}, u32[]{:S(2)}) %collective-permute-start.1) | collective-permute-done | bytes 131104 | tf_op jit(solution)/shard_map/ppermute | solution.py:367
  12.0 3.4 %collective-permute-done.2.refs_3_ = bf16[32,2048]{1,0:T(8,128)(2,1)S(1)} collective-permute-done((bf16[32,2048]{1,0:T(8,128)(2,1)S(1)}, bf16[32,2048]{1,0:T(8,128)(2,1)S(1)}, u32[]{:S(2)}, u32[]{:S(2)}) %collective-permute-start.2) | collective-permute-done | bytes 131104 | tf_op jit(solution)/shard_map/ppermute | solution.py:367
  15.5 1.1 collective-permute-done.4.refs_5_
  16.6 0.7 collective-permute-done.5.refs_6_
  17.3 0.5 gram_kernel.1
  18.0 1.2 collective-permute-done.7
  19.2 2.6 %collective-permute-start.10 = (bf16[3,64,128]{2,1,0:T(8,128)(2,1)S(1)}, bf16[3,64,128]{2,1,0:T(8,128)(2,1)S(1)}, u32[]{:S(2)}, u32[]{:S(2)}) collective-permute-start(bf16[3,64,128]{2,1,0:T(8,128)(2,1)S(1)} %add_convert_fusion.2), channel_id=1, source_target_pairs={{0,6},{1,7},{2,4},{3,5},{4,2},{5,3},{6,0},{7,1},{8,14},{9,15},{10,... | collective-permute-start | bytes 147464 | tf_op jit(solution)/shard_map/ppermute | solution.py:367
  21.8 0.5 collective-permute-start.9
  22.2 0.5 collective-permute-start.8
  22.8 1.5 %collective-permute-done.10 = bf16[3,64,128]{2,1,0:T(8,128)(2,1)S(1)} collective-permute-done((bf16[3,64,128]{2,1,0:T(8,128)(2,1)S(1)}, bf16[3,64,128]{2,1,0:T(8,128)(2,1)S(1)}, u32[]{:S(2)}, u32[]{:S(2)}) %collective-permute-start.10) | collective-permute-done | bytes 49184 | tf_op jit(solution)/shard_map/ppermute | solution.py:367
  24.3 1.6 %collective-permute-done.9 = bf16[3,64,128]{2,1,0:T(8,128)(2,1)S(1)} collective-permute-done((bf16[3,64,128]{2,1,0:T(8,128)(2,1)S(1)}, bf16[3,64,128]{2,1,0:T(8,128)(2,1)S(1)}, u32[]{:S(2)}, u32[]{:S(2)}) %collective-permute-start.9) | collective-permute-done | bytes 49184 | tf_op jit(solution)/shard_map/ppermute | solution.py:367
  25.9 0.5 collective-permute-done.8
  26.4 1.3 %collective-permute-done.11.other_ref = f32[3,64,128]{2,1,0:T(8,128)S(1)} collective-permute-done((f32[3,64,128]{2,1,0:T(8,128)S(1)}, f32[3,64,128]{2,1,0:T(8,128)S(1)}, u32[]{:S(2)}, u32[]{:S(2)}) %collective-permute-start.11) | collective-permute-done | bytes 98336 | tf_op jit(solution)/shard_map/ppermute | solution.py:367
  27.7 4.8 %node_kernel.1 = (bf16[128,512]{1,0:T(8,128)(2,1)S(1)}, bf16[128,512]{1,0:T(8,128)(2,1)S(1)}, bf16[128,512]{1,0:T(8,128)(2,1)S(1)}, bf16[128,512]{1,0:T(8,128)(2,1)S(1)}, bf16[256,128]{1,0:T(8,128)(2,1)S(1)}) custom-call(s32[1]{0:T(128)} %bitcast.pos_ref, f32[3,64,128]{2,1,0:T(8,128)S(1)} %add_add_fusion.mine_ref, ...), custom_call_target="tpu_custom_call" | custom-call | tf_op jit(solution)/shard_map/node_kernel/pallas_call | solution.py:350
  32.5 2.7 %collective-permute-start.12 = (bf16[128,512]{1,0:T(8,128)(2,1)S(1)}, bf16[128,512]{1,0:T(8,128)(2,1)S(1)}, u32[]{:S(2)}, u32[]{:S(2)}) collective-permute-start(bf16[128,512]{1,0:T(8,128)(2,1)S(1)} %get-tuple-element.48), channel_id=1, source_target_pairs={{0,16},{1,17},{2,18},{3,19},{4,20},{5,21},{6,22},{7,23},{8,24},{9,... | collective-permute-start | bytes 393224 | tf_op jit(solution)/shard_map/ppermute | solution.py:367
  35.2 1.3 %collective-permute-start.13 = (bf16[128,512]{1,0:T(8,128)(2,1)S(1)}, bf16[128,512]{1,0:T(8,128)(2,1)S(1)}, u32[]{:S(2)}, u32[]{:S(2)}) collective-permute-start(bf16[128,512]{1,0:T(8,128)(2,1)S(1)} %get-tuple-element.49), channel_id=1, source_target_pairs={{0,24},{1,25},{2,26},{3,27},{4,28},{5,29},{6,30},{7,31},{8,16},{9,... | collective-permute-start | bytes 393224 | tf_op jit(solution)/shard_map/ppermute | solution.py:367
  36.8 8.7 %collective-permute-done.12.refs_1_ = bf16[128,512]{1,0:T(8,128)(2,1)S(1)} collective-permute-done((bf16[128,512]{1,0:T(8,128)(2,1)S(1)}, bf16[128,512]{1,0:T(8,128)(2,1)S(1)}, u32[]{:S(2)}, u32[]{:S(2)}) %collective-permute-start.12) | collective-permute-done | bytes 131104 | tf_op jit(solution)/shard_map/ppermute | solution.py:367
  45.5 0.5 collective-permute-done.14.refs_3_
  46.0 0.4 cross_kernel.1
  46.5 1.4 %collective-permute-done.15 = f32[6,64,128]{2,1,0:T(8,128)S(1)} collective-permute-done((f32[6,64,128]{2,1,0:T(8,128)S(1)}, f32[6,64,128]{2,1,0:T(8,128)S(1)}, u32[]{:S(2)}, u32[]{:S(2)}) %collective-permute-start.15) | collective-permute-done | bytes 196640 | tf_op jit(solution)/shard_map/ppermute | solution.py:367
  48.0 1.6 %collective-permute-start.18 = (bf16[6,64,128]{2,1,0:T(8,128)(2,1)S(1)}, bf16[6,64,128]{2,1,0:T(8,128)(2,1)S(1)}, u32[]{:S(2)}, u32[]{:S(2)}) collective-permute-start(bf16[6,64,128]{2,1,0:T(8,128)(2,1)S(1)} %add_convert_fusion.1), channel_id=1, source_target_pairs={{0,6},{1,7},{2,4},{3,5},{4,2},{5,3},{6,0},{7,1},{8,14},{9,15},{10,... | collective-permute-start | bytes 294920 | tf_op jit(solution)/shard_map/ppermute | solution.py:367
  49.6 0.5 collective-permute-start.17
  50.1 1.5 %collective-permute-start.16 = (bf16[6,64,128]{2,1,0:T(8,128)(2,1)S(1)}, bf16[6,64,128]{2,1,0:T(8,128)(2,1)S(1)}, u32[]{:S(2)}, u32[]{:S(2)}) collective-permute-start(bf16[6,64,128]{2,1,0:T(8,128)(2,1)S(1)} %add_convert_fusion.1), channel_id=1, source_target_pairs={{0,2},{1,3},{2,0},{3,1},{4,6},{5,7},{6,4},{7,5},{8,10},{9,11},{10,... | collective-permute-start | bytes 294920 | tf_op jit(solution)/shard_map/ppermute | solution.py:367
  51.5 0.4 diag_kernel.1
  52.0 2.4 %collective-permute-done.18 = bf16[6,64,128]{2,1,0:T(8,128)(2,1)S(1)} collective-permute-done((bf16[6,64,128]{2,1,0:T(8,128)(2,1)S(1)}, bf16[6,64,128]{2,1,0:T(8,128)(2,1)S(1)}, u32[]{:S(2)}, u32[]{:S(2)}) %collective-permute-start.18) | collective-permute-done | bytes 98336 | tf_op jit(solution)/shard_map/ppermute | solution.py:367
  54.4 1.5 %collective-permute-done.17 = bf16[6,64,128]{2,1,0:T(8,128)(2,1)S(1)} collective-permute-done((bf16[6,64,128]{2,1,0:T(8,128)(2,1)S(1)}, bf16[6,64,128]{2,1,0:T(8,128)(2,1)S(1)}, u32[]{:S(2)}, u32[]{:S(2)}) %collective-permute-start.17) | collective-permute-done | bytes 98336 | tf_op jit(solution)/shard_map/ppermute | solution.py:367
  56.1 4.1 %collective-permute-start.21 = (bf16[7,64,128]{2,1,0:T(8,128)(2,1)S(1)}, bf16[7,64,128]{2,1,0:T(8,128)(2,1)S(1)}, u32[]{:S(2)}, u32[]{:S(2)}) collective-permute-start(bf16[7,64,128]{2,1,0:T(8,128)(2,1)S(1)} %pad_maximum_fusion), channel_id=1, source_target_pairs={{0,16},{1,17},{2,18},{3,19},{4,20},{5,21},{6,22},{7,23},{8,24},{9,... | collective-permute-start | bytes 344072 | tf_op jit(solution)/shard_map/ppermute | solution.py:367
  60.3 0.5 collective-permute-start.20
  60.9 7.8 %collective-permute-done.21 = bf16[7,64,128]{2,1,0:T(8,128)(2,1)S(1)} collective-permute-done((bf16[7,64,128]{2,1,0:T(8,128)(2,1)S(1)}, bf16[7,64,128]{2,1,0:T(8,128)(2,1)S(1)}, u32[]{:S(2)}, u32[]{:S(2)}) %collective-permute-start.21) | collective-permute-done | bytes 114720 | tf_op jit(solution)/shard_map/ppermute | solution.py:367
  68.7 1.0 collective-permute-done.19
  69.9 1.6 %collective-permute-done.22.other_ref = f32[10,64,128]{2,1,0:T(8,128)S(1)} collective-permute-done((f32[10,64,128]{2,1,0:T(8,128)S(1)}, f32[10,64,128]{2,1,0:T(8,128)S(1)}, u32[]{:S(2)}, u32[]{:S(2)}) %collective-permute-start.22) | collective-permute-done | bytes 327712 | tf_op jit(solution)/shard_map/ppermute | solution.py:367
  71.6 12.0 %top_kernel.1 = (bf16[128,512]{1,0:T(8,128)(2,1)S(1)}, f32[256,256]{1,0:T(8,128)S(1)}, bf16[256,128]{1,0:T(8,128)(2,1)S(1)}) custom-call(s32[1]{0:T(128)} %bitcast.pos_ref, f32[10,64,128]{2,1,0:T(8,128)S(1)} %convert_dynamic-update-slice_fusion.mine_ref, f32[10,64,128]{2,1,0:T(8,128)S(1)} %collective-permute-done.22.other_ref, ...), custom_call_target="tpu_custom_call" | custom-call | tf_op jit(solution)/shard_map/top_kernel/pallas_call | solution.py:350
  83.5 2.3 %collective-permute-start.25 = (bf16[128,512]{1,0:T(8,128)(2,1)S(1)}, bf16[128,512]{1,0:T(8,128)(2,1)S(1)}, u32[]{:S(2)}, u32[]{:S(2)}) collective-permute-start(bf16[128,512]{1,0:T(8,128)(2,1)S(1)} %get-tuple-element.56.refs_0_), channel_id=1, source_target_pairs={{0,16},{1,17},{2,18},{3,19},{4,20},{5,21},{6,22},{7,23},{8,24},{9,... | collective-permute-start | bytes 393224 | tf_op jit(solution)/shard_map/ppermute | solution.py:367
  85.8 1.8 %collective-permute-start.24 = (bf16[128,512]{1,0:T(8,128)(2,1)S(1)}, bf16[128,512]{1,0:T(8,128)(2,1)S(1)}, u32[]{:S(2)}, u32[]{:S(2)}) collective-permute-start(bf16[128,512]{1,0:T(8,128)(2,1)S(1)} %get-tuple-element.56.refs_0_), channel_id=1, source_target_pairs={{0,24},{1,25},{2,26},{3,27},{4,28},{5,29},{6,30},{7,31},{8,16},{9,... | collective-permute-start | bytes 393224 | tf_op jit(solution)/shard_map/ppermute | solution.py:367
  87.7 3.4 %factor_kernel.1.factor_ref = f32[128,128]{1,0:T(8,128)S(1)} custom-call(f32[256,256]{1,0:T(8,128)S(1)} %get-tuple-element.54.gram_ref, bf16[256,128]{1,0:T(8,128)(2,1)S(1)} %get-tuple-element.55.low_ref), custom_call_target="tpu_custom_call" | custom-call | tf_op jit(solution)/shard_map/factor_kernel/pallas_call | solution.py:350
  91.1 5.4 %collective-permute-done.25.refs_3_ = bf16[128,512]{1,0:T(8,128)(2,1)S(1)} collective-permute-done((bf16[128,512]{1,0:T(8,128)(2,1)S(1)}, bf16[128,512]{1,0:T(8,128)(2,1)S(1)}, u32[]{:S(2)}, u32[]{:S(2)}) %collective-permute-start.25) | collective-permute-done | bytes 131104 | tf_op jit(solution)/shard_map/ppermute | solution.py:367
  96.5 0.5 collective-permute-done.23.refs_1_
  97.0 0.8 coeffs_kernel.1
  97.9 1.2 %collective-permute-done.26 = f32[1,128,128]{2,1,0:T(8,128)S(1)} collective-permute-done((f32[1,128,128]{2,1,0:T(8,128)S(1)}, f32[1,128,128]{2,1,0:T(8,128)S(1)}, u32[]{:S(2)}, u32[]{:S(2)}) %collective-permute-start.26) | collective-permute-done | bytes 65568 | tf_op jit(solution)/shard_map/ppermute | solution.py:367
  99.2 1.6 %collective-permute-start.29 = (bf16[1,128,128]{2,1,0:T(8,128)(2,1)S(1)}, bf16[1,128,128]{2,1,0:T(8,128)(2,1)S(1)}, u32[]{:S(2)}, u32[]{:S(2)}) collective-permute-start(bf16[1,128,128]{2,1,0:T(8,128)(2,1)S(1)} %add_convert_fusion.3), channel_id=1, source_target_pairs={{0,6},{1,7},{2,4},{3,5},{4,2},{5,3},{6,0},{7,1},{8,14},{9,15},{10,... | collective-permute-start | bytes 98312 | tf_op jit(solution)/shard_map/ppermute | solution.py:367
  100.8 0.3 collective-permute-start.28
  101.1 1.7 %collective-permute-start.27 = (bf16[1,128,128]{2,1,0:T(8,128)(2,1)S(1)}, bf16[1,128,128]{2,1,0:T(8,128)(2,1)S(1)}, u32[]{:S(2)}, u32[]{:S(2)}) collective-permute-start(bf16[1,128,128]{2,1,0:T(8,128)(2,1)S(1)} %add_convert_fusion.3), channel_id=1, source_target_pairs={{0,2},{1,3},{2,0},{3,1},{4,6},{5,7},{6,4},{7,5},{8,10},{9,11},{10,... | collective-permute-start | bytes 98312 | tf_op jit(solution)/shard_map/ppermute | solution.py:367
  102.8 1.3 %collective-permute-done.29 = bf16[1,128,128]{2,1,0:T(8,128)(2,1)S(1)} collective-permute-done((bf16[1,128,128]{2,1,0:T(8,128)(2,1)S(1)}, bf16[1,128,128]{2,1,0:T(8,128)(2,1)S(1)}, u32[]{:S(2)}, u32[]{:S(2)}) %collective-permute-start.29) | collective-permute-done | bytes 32800 | tf_op jit(solution)/shard_map/ppermute | solution.py:367
  104.1 0.6 collective-permute-done.28
  104.7 0.3 collective-permute-done.27
  105.1 1.2 %collective-permute-done.30.other_ref = f32[1,128,128]{2,1,0:T(8,128)S(1)} collective-permute-done((f32[1,128,128]{2,1,0:T(8,128)S(1)}, f32[1,128,128]{2,1,0:T(8,128)S(1)}, u32[]{:S(2)}, u32[]{:S(2)}) %collective-permute-start.30) | collective-permute-done | bytes 65568 | tf_op jit(solution)/shard_map/ppermute | solution.py:367
  106.3 0.8 project_kernel.1
  107.1 1.2 collective-permute-start.31
  108.4 1.2 %collective-permute-start.32 = (bf16[32,2048]{1,0:T(8,128)(2,1)S(1)}, bf16[32,2048]{1,0:T(8,128)(2,1)S(1)}, u32[]{:S(2)}, u32[]{:S(2)}) collective-permute-start(bf16[32,2048]{1,0:T(8,128)(2,1)S(1)} %get-tuple-element.61), channel_id=1, source_target_pairs={{0,7},{1,6},{2,5},{3,4},{4,3},{5,2},{6,1},{7,0},{8,15},{9,14},{10,... | collective-permute-start | bytes 393224 | tf_op jit(solution)/shard_map/ppermute | solution.py:367
  109.6 1.7 %collective-permute-start.33 = (bf16[32,2048]{1,0:T(8,128)(2,1)S(1)}, bf16[32,2048]{1,0:T(8,128)(2,1)S(1)}, u32[]{:S(2)}, u32[]{:S(2)}) collective-permute-start(bf16[32,2048]{1,0:T(8,128)(2,1)S(1)} %get-tuple-element.62), channel_id=1, source_target_pairs={{0,2},{1,3},{2,0},{3,1},{4,6},{5,7},{6,4},{7,5},{8,10},{9,11},{10,... | collective-permute-start | bytes 393224 | tf_op jit(solution)/shard_map/ppermute | solution.py:367
  111.3 1.7 %collective-permute-start.35 = (bf16[32,2048]{1,0:T(8,128)(2,1)S(1)}, bf16[32,2048]{1,0:T(8,128)(2,1)S(1)}, u32[]{:S(2)}, u32[]{:S(2)}) collective-permute-start(bf16[32,2048]{1,0:T(8,128)(2,1)S(1)} %get-tuple-element.64), channel_id=1, source_target_pairs={{0,3},{1,2},{2,1},{3,0},{4,7},{5,6},{6,5},{7,4},{8,11},{9,10},{10,... | collective-permute-start | bytes 393224 | tf_op jit(solution)/shard_map/ppermute | solution.py:367
  113.0 1.4 %collective-permute-done.31.refs_1_ = bf16[32,2048]{1,0:T(8,128)(2,1)S(1)} collective-permute-done((bf16[32,2048]{1,0:T(8,128)(2,1)S(1)}, bf16[32,2048]{1,0:T(8,128)(2,1)S(1)}, u32[]{:S(2)}, u32[]{:S(2)}) %collective-permute-start.31) | collective-permute-done | bytes 131104 | tf_op jit(solution)/shard_map/ppermute | solution.py:367
  114.5 1.3 %collective-permute-done.32.refs_2_ = bf16[32,2048]{1,0:T(8,128)(2,1)S(1)} collective-permute-done((bf16[32,2048]{1,0:T(8,128)(2,1)S(1)}, bf16[32,2048]{1,0:T(8,128)(2,1)S(1)}, u32[]{:S(2)}, u32[]{:S(2)}) %collective-permute-start.32) | collective-permute-done | bytes 131104 | tf_op jit(solution)/shard_map/ppermute | solution.py:367
  115.8 1.3 %collective-permute-start.37 = (bf16[32,2048]{1,0:T(8,128)(2,1)S(1)}, bf16[32,2048]{1,0:T(8,128)(2,1)S(1)}, u32[]{:S(2)}, u32[]{:S(2)}) collective-permute-start(bf16[32,2048]{1,0:T(8,128)(2,1)S(1)} %get-tuple-element.66), channel_id=1, source_target_pairs={{0,1},{1,0},{2,3},{3,2},{4,5},{5,4},{6,7},{7,6},{8,9},{9,8},{10,11... | collective-permute-start | bytes 393224 | tf_op jit(solution)/shard_map/ppermute | solution.py:367
  117.1 3.3 %collective-permute-done.33.refs_3_ = bf16[32,2048]{1,0:T(8,128)(2,1)S(1)} collective-permute-done((bf16[32,2048]{1,0:T(8,128)(2,1)S(1)}, bf16[32,2048]{1,0:T(8,128)(2,1)S(1)}, u32[]{:S(2)}, u32[]{:S(2)}) %collective-permute-start.33) | collective-permute-done | bytes 131104 | tf_op jit(solution)/shard_map/ppermute | solution.py:367
  120.4 1.2 %collective-permute-done.35.refs_5_ = bf16[32,2048]{1,0:T(8,128)(2,1)S(1)} collective-permute-done((bf16[32,2048]{1,0:T(8,128)(2,1)S(1)}, bf16[32,2048]{1,0:T(8,128)(2,1)S(1)}, u32[]{:S(2)}, u32[]{:S(2)}) %collective-permute-start.35) | collective-permute-done | bytes 131104 | tf_op jit(solution)/shard_map/ppermute | solution.py:367
  121.6 0.4 collective-permute-done.36.refs_6_
  122.0 1.0 whole_kernel.1
  (36 shorter events, 1.5 us)
Async XLA Ops:
  0.0 1.2 copy-start
  1.3 7.9 %collective-permute-start = (bf16[32,2048]{1,0:T(8,128)(2,1)S(1)}, bf16[32,2048]{1,0:T(8,128)(2,1)S(1)}, u32[]{:S(2)}, u32[]{:S(2)}) collective-permute-start(bf16[32,2048]{1,0:T(8,128)(2,1)S(1)} %get-tuple-element.37), channel_id=1, source_target_pairs={{0,6},{1,7},{2,4},{3,5},{4,2},{5,3},{6,0},{7,1},{8,14},{9,15},{10,... | collective-permute-start | bytes 393224 | tf_op jit(solution)/shard_map/ppermute | solution.py:367
  5.3 6.8 %collective-permute-start.1 = (bf16[32,2048]{1,0:T(8,128)(2,1)S(1)}, bf16[32,2048]{1,0:T(8,128)(2,1)S(1)}, u32[]{:S(2)}, u32[]{:S(2)}) collective-permute-start(bf16[32,2048]{1,0:T(8,128)(2,1)S(1)} %get-tuple-element.38), channel_id=1, source_target_pairs={{0,7},{1,6},{2,5},{3,4},{4,3},{5,2},{6,1},{7,0},{8,15},{9,14},{10,... | collective-permute-start | bytes 393224 | tf_op jit(solution)/shard_map/ppermute | solution.py:367
  5.3 10.2 %collective-permute-start.2 = (bf16[32,2048]{1,0:T(8,128)(2,1)S(1)}, bf16[32,2048]{1,0:T(8,128)(2,1)S(1)}, u32[]{:S(2)}, u32[]{:S(2)}) collective-permute-start(bf16[32,2048]{1,0:T(8,128)(2,1)S(1)} %get-tuple-element.39), channel_id=1, source_target_pairs={{0,2},{1,3},{2,0},{3,1},{4,6},{5,7},{6,4},{7,5},{8,10},{9,11},{10,... | collective-permute-start | bytes 393224 | tf_op jit(solution)/shard_map/ppermute | solution.py:367
  6.4 9.1 %collective-permute-start.3 = (bf16[32,2048]{1,0:T(8,128)(2,1)S(1)}, bf16[32,2048]{1,0:T(8,128)(2,1)S(1)}, u32[]{:S(2)}, u32[]{:S(2)}) collective-permute-start(bf16[32,2048]{1,0:T(8,128)(2,1)S(1)} %get-tuple-element.40), channel_id=1, source_target_pairs={{0,4},{1,5},{2,6},{3,7},{4,0},{5,1},{6,2},{7,3},{8,12},{9,13},{10,... | collective-permute-start | bytes 393224 | tf_op jit(solution)/shard_map/ppermute | solution.py:367
  7.9 8.7 %collective-permute-start.4 = (bf16[32,2048]{1,0:T(8,128)(2,1)S(1)}, bf16[32,2048]{1,0:T(8,128)(2,1)S(1)}, u32[]{:S(2)}, u32[]{:S(2)}) collective-permute-start(bf16[32,2048]{1,0:T(8,128)(2,1)S(1)} %get-tuple-element.41), channel_id=1, source_target_pairs={{0,3},{1,2},{2,1},{3,0},{4,7},{5,6},{6,5},{7,4},{8,11},{9,10},{10,... | collective-permute-start | bytes 393224 | tf_op jit(solution)/shard_map/ppermute | solution.py:367
  9.2 8.1 %collective-permute-start.5 = (bf16[32,2048]{1,0:T(8,128)(2,1)S(1)}, bf16[32,2048]{1,0:T(8,128)(2,1)S(1)}, u32[]{:S(2)}, u32[]{:S(2)}) collective-permute-start(bf16[32,2048]{1,0:T(8,128)(2,1)S(1)} %get-tuple-element.42), channel_id=1, source_target_pairs={{0,5},{1,4},{2,7},{3,6},{4,1},{5,0},{6,3},{7,2},{8,13},{9,12},{10,... | collective-permute-start | bytes 393224 | tf_op jit(solution)/shard_map/ppermute | solution.py:367
  12.0 5.3 %collective-permute-start.6 = (bf16[32,2048]{1,0:T(8,128)(2,1)S(1)}, bf16[32,2048]{1,0:T(8,128)(2,1)S(1)}, u32[]{:S(2)}, u32[]{:S(2)}) collective-permute-start(bf16[32,2048]{1,0:T(8,128)(2,1)S(1)} %get-tuple-element.43), channel_id=1, source_target_pairs={{0,1},{1,0},{2,3},{3,2},{4,5},{5,4},{6,7},{7,6},{8,9},{9,8},{10,11... | collective-permute-start | bytes 393224 | tf_op jit(solution)/shard_map/ppermute | solution.py:367
  17.8 1.4 %collective-permute-start.7 = (f32[3,64,128]{2,1,0:T(8,128)S(1)}, f32[3,64,128]{2,1,0:T(8,128)S(1)}, u32[]{:S(2)}, u32[]{:S(2)}) collective-permute-start(f32[3,64,128]{2,1,0:T(8,128)S(1)} %get-tuple-element.46), channel_id=1, source_target_pairs={{0,1},{1,0},{2,3},{3,2},{4,5},{5,4},{6,7},{7,6},{8,9},{9,8},{10,11... | collective-permute-start | bytes 294920 | tf_op jit(solution)/shard_map/ppermute | solution.py:367
  19.2 5.1 %collective-permute-start.10 = (bf16[3,64,128]{2,1,0:T(8,128)(2,1)S(1)}, bf16[3,64,128]{2,1,0:T(8,128)(2,1)S(1)}, u32[]{:S(2)}, u32[]{:S(2)}) collective-permute-start(bf16[3,64,128]{2,1,0:T(8,128)(2,1)S(1)} %add_convert_fusion.2), channel_id=1, source_target_pairs={{0,6},{1,7},{2,4},{3,5},{4,2},{5,3},{6,0},{7,1},{8,14},{9,15},{10,... | collective-permute-start | bytes 147464 | tf_op jit(solution)/shard_map/ppermute | solution.py:367
  21.8 4.1 %collective-permute-start.9 = (bf16[3,64,128]{2,1,0:T(8,128)(2,1)S(1)}, bf16[3,64,128]{2,1,0:T(8,128)(2,1)S(1)}, u32[]{:S(2)}, u32[]{:S(2)}) collective-permute-start(bf16[3,64,128]{2,1,0:T(8,128)(2,1)S(1)} %add_convert_fusion.2), channel_id=1, source_target_pairs={{0,4},{1,5},{2,6},{3,7},{4,0},{5,1},{6,2},{7,3},{8,12},{9,13},{10,... | collective-permute-start | bytes 147464 | tf_op jit(solution)/shard_map/ppermute | solution.py:367
  22.2 4.1 %collective-permute-start.8 = (bf16[3,64,128]{2,1,0:T(8,128)(2,1)S(1)}, bf16[3,64,128]{2,1,0:T(8,128)(2,1)S(1)}, u32[]{:S(2)}, u32[]{:S(2)}) collective-permute-start(bf16[3,64,128]{2,1,0:T(8,128)(2,1)S(1)} %add_convert_fusion.2), channel_id=1, source_target_pairs={{0,2},{1,3},{2,0},{3,1},{4,6},{5,7},{6,4},{7,5},{8,10},{9,11},{10,... | collective-permute-start | bytes 147464 | tf_op jit(solution)/shard_map/ppermute | solution.py:367
  26.4 1.4 %collective-permute-start.11 = (f32[3,64,128]{2,1,0:T(8,128)S(1)}, f32[3,64,128]{2,1,0:T(8,128)S(1)}, u32[]{:S(2)}, u32[]{:S(2)}) collective-permute-start(f32[3,64,128]{2,1,0:T(8,128)S(1)} %add_add_fusion.mine_ref), channel_id=1, source_target_pairs={{0,1},{1,0},{2,3},{3,2},{4,5},{5,4},{6,7},{7,6},{8,9},{9,8},{10,11... | collective-permute-start | bytes 294920 | tf_op jit(solution)/shard_map/ppermute | solution.py:367
  32.5 13.0 %collective-permute-start.12 = (bf16[128,512]{1,0:T(8,128)(2,1)S(1)}, bf16[128,512]{1,0:T(8,128)(2,1)S(1)}, u32[]{:S(2)}, u32[]{:S(2)}) collective-permute-start(bf16[128,512]{1,0:T(8,128)(2,1)S(1)} %get-tuple-element.48), channel_id=1, source_target_pairs={{0,16},{1,17},{2,18},{3,19},{4,20},{5,21},{6,22},{7,23},{8,24},{9,... | collective-permute-start | bytes 393224 | tf_op jit(solution)/shard_map/ppermute | solution.py:367
  35.2 10.3 %collective-permute-start.13 = (bf16[128,512]{1,0:T(8,128)(2,1)S(1)}, bf16[128,512]{1,0:T(8,128)(2,1)S(1)}, u32[]{:S(2)}, u32[]{:S(2)}) collective-permute-start(bf16[128,512]{1,0:T(8,128)(2,1)S(1)} %get-tuple-element.49), channel_id=1, source_target_pairs={{0,24},{1,25},{2,26},{3,27},{4,28},{5,29},{6,30},{7,31},{8,16},{9,... | collective-permute-start | bytes 393224 | tf_op jit(solution)/shard_map/ppermute | solution.py:367
  36.5 9.5 %collective-permute-start.14 = (bf16[128,512]{1,0:T(8,128)(2,1)S(1)}, bf16[128,512]{1,0:T(8,128)(2,1)S(1)}, u32[]{:S(2)}, u32[]{:S(2)}) collective-permute-start(bf16[128,512]{1,0:T(8,128)(2,1)S(1)} %get-tuple-element.50), channel_id=1, source_target_pairs={{0,8},{1,9},{2,10},{3,11},{4,12},{5,13},{6,14},{7,15},{8,0},{9,1},... | collective-permute-start | bytes 393224 | tf_op jit(solution)/shard_map/ppermute | solution.py:367
  46.5 1.5 %collective-permute-start.15 = (f32[6,64,128]{2,1,0:T(8,128)S(1)}, f32[6,64,128]{2,1,0:T(8,128)S(1)}, u32[]{:S(2)}, u32[]{:S(2)}) collective-permute-start(f32[6,64,128]{2,1,0:T(8,128)S(1)} %get-tuple-element.52), channel_id=1, source_target_pairs={{0,1},{1,0},{2,3},{3,2},{4,5},{5,4},{6,7},{7,6},{8,9},{9,8},{10,11... | collective-permute-start | bytes 589832 | tf_op jit(solution)/shard_map/ppermute | solution.py:367
  48.0 6.4 %collective-permute-start.18 = (bf16[6,64,128]{2,1,0:T(8,128)(2,1)S(1)}, bf16[6,64,128]{2,1,0:T(8,128)(2,1)S(1)}, u32[]{:S(2)}, u32[]{:S(2)}) collective-permute-start(bf16[6,64,128]{2,1,0:T(8,128)(2,1)S(1)} %add_convert_fusion.1), channel_id=1, source_target_pairs={{0,6},{1,7},{2,4},{3,5},{4,2},{5,3},{6,0},{7,1},{8,14},{9,15},{10,... | collective-permute-start | bytes 294920 | tf_op jit(solution)/shard_map/ppermute | solution.py:367
  49.6 6.3 %collective-permute-start.17 = (bf16[6,64,128]{2,1,0:T(8,128)(2,1)S(1)}, bf16[6,64,128]{2,1,0:T(8,128)(2,1)S(1)}, u32[]{:S(2)}, u32[]{:S(2)}) collective-permute-start(bf16[6,64,128]{2,1,0:T(8,128)(2,1)S(1)} %add_convert_fusion.1), channel_id=1, source_target_pairs={{0,4},{1,5},{2,6},{3,7},{4,0},{5,1},{6,2},{7,3},{8,12},{9,13},{10,... | collective-permute-start | bytes 294920 | tf_op jit(solution)/shard_map/ppermute | solution.py:367
  50.1 6.0 %collective-permute-start.16 = (bf16[6,64,128]{2,1,0:T(8,128)(2,1)S(1)}, bf16[6,64,128]{2,1,0:T(8,128)(2,1)S(1)}, u32[]{:S(2)}, u32[]{:S(2)}) collective-permute-start(bf16[6,64,128]{2,1,0:T(8,128)(2,1)S(1)} %add_convert_fusion.1), channel_id=1, source_target_pairs={{0,2},{1,3},{2,0},{3,1},{4,6},{5,7},{6,4},{7,5},{8,10},{9,11},{10,... | collective-permute-start | bytes 294920 | tf_op jit(solution)/shard_map/ppermute | solution.py:367
  56.1 12.6 %collective-permute-start.21 = (bf16[7,64,128]{2,1,0:T(8,128)(2,1)S(1)}, bf16[7,64,128]{2,1,0:T(8,128)(2,1)S(1)}, u32[]{:S(2)}, u32[]{:S(2)}) collective-permute-start(bf16[7,64,128]{2,1,0:T(8,128)(2,1)S(1)} %pad_maximum_fusion), channel_id=1, source_target_pairs={{0,16},{1,17},{2,18},{3,19},{4,20},{5,21},{6,22},{7,23},{8,24},{9,... | collective-permute-start | bytes 344072 | tf_op jit(solution)/shard_map/ppermute | solution.py:367
  60.3 8.4 %collective-permute-start.20 = (bf16[7,64,128]{2,1,0:T(8,128)(2,1)S(1)}, bf16[7,64,128]{2,1,0:T(8,128)(2,1)S(1)}, u32[]{:S(2)}, u32[]{:S(2)}) collective-permute-start(bf16[7,64,128]{2,1,0:T(8,128)(2,1)S(1)} %pad_maximum_fusion), channel_id=1, source_target_pairs={{0,24},{1,25},{2,26},{3,27},{4,28},{5,29},{6,30},{7,31},{8,16},{9,... | collective-permute-start | bytes 344072 | tf_op jit(solution)/shard_map/ppermute | solution.py:367
  60.7 9.0 %collective-permute-start.19 = (bf16[7,64,128]{2,1,0:T(8,128)(2,1)S(1)}, bf16[7,64,128]{2,1,0:T(8,128)(2,1)S(1)}, u32[]{:S(2)}, u32[]{:S(2)}) collective-permute-start(bf16[7,64,128]{2,1,0:T(8,128)(2,1)S(1)} %pad_maximum_fusion), channel_id=1, source_target_pairs={{0,8},{1,9},{2,10},{3,11},{4,12},{5,13},{6,14},{7,15},{8,0},{9,1},... | collective-permute-start | bytes 344072 | tf_op jit(solution)/shard_map/ppermute | solution.py:367
  69.9 1.7 %collective-permute-start.22 = (f32[10,64,128]{2,1,0:T(8,128)S(1)}, f32[10,64,128]{2,1,0:T(8,128)S(1)}, u32[]{:S(2)}, u32[]{:S(2)}) collective-permute-start(f32[10,64,128]{2,1,0:T(8,128)S(1)} %convert_dynamic-update-slice_fusion.mine_ref), channel_id=1, source_target_pairs={{0,1},{1,0},{2,3},{3,2},{4,5},{5,4},{6,7},{7,6},{8,9},{9,8},{10,11... | collective-permute-start | bytes 983048 | tf_op jit(solution)/shard_map/ppermute | solution.py:367
  83.5 13.0 %collective-permute-start.25 = (bf16[128,512]{1,0:T(8,128)(2,1)S(1)}, bf16[128,512]{1,0:T(8,128)(2,1)S(1)}, u32[]{:S(2)}, u32[]{:S(2)}) collective-permute-start(bf16[128,512]{1,0:T(8,128)(2,1)S(1)} %get-tuple-element.56.refs_0_), channel_id=1, source_target_pairs={{0,16},{1,17},{2,18},{3,19},{4,20},{5,21},{6,22},{7,23},{8,24},{9,... | collective-permute-start | bytes 393224 | tf_op jit(solution)/shard_map/ppermute | solution.py:367
  85.8 10.7 %collective-permute-start.24 = (bf16[128,512]{1,0:T(8,128)(2,1)S(1)}, bf16[128,512]{1,0:T(8,128)(2,1)S(1)}, u32[]{:S(2)}, u32[]{:S(2)}) collective-permute-start(bf16[128,512]{1,0:T(8,128)(2,1)S(1)} %get-tuple-element.56.refs_0_), channel_id=1, source_target_pairs={{0,24},{1,25},{2,26},{3,27},{4,28},{5,29},{6,30},{7,31},{8,16},{9,... | collective-permute-start | bytes 393224 | tf_op jit(solution)/shard_map/ppermute | solution.py:367
  87.7 9.4 %collective-permute-start.23 = (bf16[128,512]{1,0:T(8,128)(2,1)S(1)}, bf16[128,512]{1,0:T(8,128)(2,1)S(1)}, u32[]{:S(2)}, u32[]{:S(2)}) collective-permute-start(bf16[128,512]{1,0:T(8,128)(2,1)S(1)} %get-tuple-element.56.refs_0_), channel_id=1, source_target_pairs={{0,8},{1,9},{2,10},{3,11},{4,12},{5,13},{6,14},{7,15},{8,0},{9,1},... | collective-permute-start | bytes 393224 | tf_op jit(solution)/shard_map/ppermute | solution.py:367
  97.9 1.3 %collective-permute-start.26 = (f32[1,128,128]{2,1,0:T(8,128)S(1)}, f32[1,128,128]{2,1,0:T(8,128)S(1)}, u32[]{:S(2)}, u32[]{:S(2)}) collective-permute-start(f32[1,128,128]{2,1,0:T(8,128)S(1)} %get-tuple-element.58), channel_id=1, source_target_pairs={{0,1},{1,0},{2,3},{3,2},{4,5},{5,4},{6,7},{7,6},{8,9},{9,8},{10,11... | collective-permute-start | bytes 196616 | tf_op jit(solution)/shard_map/ppermute | solution.py:367
  99.2 4.9 %collective-permute-start.29 = (bf16[1,128,128]{2,1,0:T(8,128)(2,1)S(1)}, bf16[1,128,128]{2,1,0:T(8,128)(2,1)S(1)}, u32[]{:S(2)}, u32[]{:S(2)}) collective-permute-start(bf16[1,128,128]{2,1,0:T(8,128)(2,1)S(1)} %add_convert_fusion.3), channel_id=1, source_target_pairs={{0,6},{1,7},{2,4},{3,5},{4,2},{5,3},{6,0},{7,1},{8,14},{9,15},{10,... | collective-permute-start | bytes 98312 | tf_op jit(solution)/shard_map/ppermute | solution.py:367
  100.8 3.9 %collective-permute-start.28 = (bf16[1,128,128]{2,1,0:T(8,128)(2,1)S(1)}, bf16[1,128,128]{2,1,0:T(8,128)(2,1)S(1)}, u32[]{:S(2)}, u32[]{:S(2)}) collective-permute-start(bf16[1,128,128]{2,1,0:T(8,128)(2,1)S(1)} %add_convert_fusion.3), channel_id=1, source_target_pairs={{0,4},{1,5},{2,6},{3,7},{4,0},{5,1},{6,2},{7,3},{8,12},{9,13},{10,... | collective-permute-start | bytes 98312 | tf_op jit(solution)/shard_map/ppermute | solution.py:367
  101.1 3.9 %collective-permute-start.27 = (bf16[1,128,128]{2,1,0:T(8,128)(2,1)S(1)}, bf16[1,128,128]{2,1,0:T(8,128)(2,1)S(1)}, u32[]{:S(2)}, u32[]{:S(2)}) collective-permute-start(bf16[1,128,128]{2,1,0:T(8,128)(2,1)S(1)} %add_convert_fusion.3), channel_id=1, source_target_pairs={{0,2},{1,3},{2,0},{3,1},{4,6},{5,7},{6,4},{7,5},{8,10},{9,11},{10,... | collective-permute-start | bytes 98312 | tf_op jit(solution)/shard_map/ppermute | solution.py:367
  105.0 1.3 %collective-permute-start.30 = (f32[1,128,128]{2,1,0:T(8,128)S(1)}, f32[1,128,128]{2,1,0:T(8,128)S(1)}, u32[]{:S(2)}, u32[]{:S(2)}) collective-permute-start(f32[1,128,128]{2,1,0:T(8,128)S(1)} %add_add_fusion.1.mine_ref), channel_id=1, source_target_pairs={{0,1},{1,0},{2,3},{3,2},{4,5},{5,4},{6,7},{7,6},{8,9},{9,8},{10,11... | collective-permute-start | bytes 196616 | tf_op jit(solution)/shard_map/ppermute | solution.py:367
  107.1 7.3 %collective-permute-start.31 = (bf16[32,2048]{1,0:T(8,128)(2,1)S(1)}, bf16[32,2048]{1,0:T(8,128)(2,1)S(1)}, u32[]{:S(2)}, u32[]{:S(2)}) collective-permute-start(bf16[32,2048]{1,0:T(8,128)(2,1)S(1)} %get-tuple-element.60), channel_id=1, source_target_pairs={{0,6},{1,7},{2,4},{3,5},{4,2},{5,3},{6,0},{7,1},{8,14},{9,15},{10,... | collective-permute-start | bytes 393224 | tf_op jit(solution)/shard_map/ppermute | solution.py:367
  108.4 7.4 %collective-permute-start.32 = (bf16[32,2048]{1,0:T(8,128)(2,1)S(1)}, bf16[32,2048]{1,0:T(8,128)(2,1)S(1)}, u32[]{:S(2)}, u32[]{:S(2)}) collective-permute-start(bf16[32,2048]{1,0:T(8,128)(2,1)S(1)} %get-tuple-element.61), channel_id=1, source_target_pairs={{0,7},{1,6},{2,5},{3,4},{4,3},{5,2},{6,1},{7,0},{8,15},{9,14},{10,... | collective-permute-start | bytes 393224 | tf_op jit(solution)/shard_map/ppermute | solution.py:367
  109.6 10.7 %collective-permute-start.33 = (bf16[32,2048]{1,0:T(8,128)(2,1)S(1)}, bf16[32,2048]{1,0:T(8,128)(2,1)S(1)}, u32[]{:S(2)}, u32[]{:S(2)}) collective-permute-start(bf16[32,2048]{1,0:T(8,128)(2,1)S(1)} %get-tuple-element.62), channel_id=1, source_target_pairs={{0,2},{1,3},{2,0},{3,1},{4,6},{5,7},{6,4},{7,5},{8,10},{9,11},{10,... | collective-permute-start | bytes 393224 | tf_op jit(solution)/shard_map/ppermute | solution.py:367
  111.3 9.1 %collective-permute-start.34 = (bf16[32,2048]{1,0:T(8,128)(2,1)S(1)}, bf16[32,2048]{1,0:T(8,128)(2,1)S(1)}, u32[]{:S(2)}, u32[]{:S(2)}) collective-permute-start(bf16[32,2048]{1,0:T(8,128)(2,1)S(1)} %get-tuple-element.63), channel_id=1, source_target_pairs={{0,4},{1,5},{2,6},{3,7},{4,0},{5,1},{6,2},{7,3},{8,12},{9,13},{10,... | collective-permute-start | bytes 393224 | tf_op jit(solution)/shard_map/ppermute | solution.py:367
  111.3 10.3 %collective-permute-start.35 = (bf16[32,2048]{1,0:T(8,128)(2,1)S(1)}, bf16[32,2048]{1,0:T(8,128)(2,1)S(1)}, u32[]{:S(2)}, u32[]{:S(2)}) collective-permute-start(bf16[32,2048]{1,0:T(8,128)(2,1)S(1)} %get-tuple-element.64), channel_id=1, source_target_pairs={{0,3},{1,2},{2,1},{3,0},{4,7},{5,6},{6,5},{7,4},{8,11},{9,10},{10,... | collective-permute-start | bytes 393224 | tf_op jit(solution)/shard_map/ppermute | solution.py:367
  114.5 7.6 %collective-permute-start.36 = (bf16[32,2048]{1,0:T(8,128)(2,1)S(1)}, bf16[32,2048]{1,0:T(8,128)(2,1)S(1)}, u32[]{:S(2)}, u32[]{:S(2)}) collective-permute-start(bf16[32,2048]{1,0:T(8,128)(2,1)S(1)} %get-tuple-element.65), channel_id=1, source_target_pairs={{0,5},{1,4},{2,7},{3,6},{4,1},{5,0},{6,3},{7,2},{8,13},{9,12},{10,... | collective-permute-start | bytes 393224 | tf_op jit(solution)/shard_map/ppermute | solution.py:367
  115.8 6.3 %collective-permute-start.37 = (bf16[32,2048]{1,0:T(8,128)(2,1)S(1)}, bf16[32,2048]{1,0:T(8,128)(2,1)S(1)}, u32[]{:S(2)}, u32[]{:S(2)}) collective-permute-start(bf16[32,2048]{1,0:T(8,128)(2,1)S(1)} %get-tuple-element.66), channel_id=1, source_target_pairs={{0,1},{1,0},{2,3},{3,2},{4,5},{5,4},{6,7},{7,6},{8,9},{9,8},{10,11... | collective-permute-start | bytes 393224 | tf_op jit(solution)/shard_map/ppermute | solution.py:367

commit v7 on v3

--- a/solution.py
+++ b/solution.py
@@ -13,7 +13,8 @@
 TILE = 8
 PANEL = 64
 PLANE_ORDER = (0, 6, 7, 2, 4, 3, 5, 1)
-TREE_ORDER = (0, 3, 2, 1)
+TREE_ORDER = (0, 2, 3, 1)
+TOP_ORDER = (0, 1, 3, 2)
 PIVOT_SHARE = 2e-4
 
 precise = lax.Precision.HIGHEST
@@ -313,7 +314,7 @@
     core, z = place(pos_ref)
     width = tops[0].shape[1]
     total = None
-    for m, ref in enumerate(tops):
+    for m, ref in zip(TOP_ORDER, tops):
         part = dot_low(rows_ref[:, chunk(z, m, width)], ref[...], 1, 1)
         total = part if total is None else total + part
     split([dot(total, factor_ref[...], 1, 1)], core, mine_ref, theirs_ref)
@@ -326,7 +327,7 @@
     solved_ref[...] = dot(joined(mine_ref, other_ref, core, 0), factor_ref[...], 1, 0)
     solved = [solved_ref[chunk(member(pos_ref), m, height), :] for m in PLANE_ORDER]
     solved = jnp.concatenate(solved, 0).astype(bf16)
-    for m, ref in enumerate(tops):
+    for m, ref in zip(TOP_ORDER, tops):
         made = dot_low(solved, ref[...], 1, 0).astype(bf16)
         for k in range(PLANE):
             outs[k][:, chunk(z, m, width)] = made[k * height : (k + 1) * height, :]
@@ -413,7 +414,7 @@
         + sound_shape
         + work_shapes * 2,
     )
-    tops = swap_all([top] * PLANES, range(PLANES), PLANE)
+    tops = swap_all([top] * PLANES, TOP_ORDER, PLANE)
     (factor,) = kernel(factor_kernel, [((RANK, RANK), f32)], gram, low, scalar=False)
 
     mine, theirs = kernel(coeffs_kernel, [((1, height // 2, RANK), f32)] * 2, pos, rows, factor, *tops)

time: 124 us -> 124 us (level)
  no operation moved by 1% of the time
where the time goes in v7:
time: 124 us
  waiting for transfers between devices  59.3 us (48%)
  starting transfers between devices  38.4 us (31%)
  Pallas kernels  24.3 us (20%)
    ppermute x38, waiting for transfers between devices, swap(): return lax.ppermute(x, 'cols', [(i, i ^ apart) for i in range(count)])  59.3 us
    ppermute x38, starting transfers between devices, swap(): return lax.ppermute(x, 'cols', [(i, i ^ apart) for i in range(count)])  38.4 us
    pallas_call x10, Pallas kernels, kernel(): pl.pallas_call(fn, out_shape=[jax.ShapeDtypeStruct(s, d) for s, d in shap...  24.3 us
  transfers between devices with their start and end apart: 38, of which 31 were waited for; matrix products, arithmetic and copies ran while one was open for 0% of the time, Pallas kernels for 3%

profile of v7, /device:TPU:0, one launch (start us, length us, event | category | flops | bytes accessed | tf_op | source)
XLA Modules:
  0.0 123.6 jit_solution(539804661493938836)
XLA Ops:
  0.0 1.2 copy-done
  1.3 4.0 %collective-permute-start = (bf16[32,2048]{1,0:T(8,128)(2,1)S(1)}, bf16[32,2048]{1,0:T(8,128)(2,1)S(1)}, u32[]{:S(2)}, u32[]{:S(2)}) collective-permute-start(bf16[32,2048]{1,0:T(8,128)(2,1)S(1)} %get-tuple-element.37), channel_id=1, source_target_pairs={{0,6},{1,7},{2,4},{3,5},{4,2},{5,3},{6,0},{7,1},{8,14},{9,15},{10,... | collective-permute-start | bytes 393224 | tf_op jit(solution)/shard_map/ppermute | solution.py:367
  5.3 1.1 collective-permute-start.2
  6.4 1.5 %collective-permute-start.3 = (bf16[32,2048]{1,0:T(8,128)(2,1)S(1)}, bf16[32,2048]{1,0:T(8,128)(2,1)S(1)}, u32[]{:S(2)}, u32[]{:S(2)}) collective-permute-start(bf16[32,2048]{1,0:T(8,128)(2,1)S(1)} %get-tuple-element.40), channel_id=1, source_target_pairs={{0,4},{1,5},{2,6},{3,7},{4,0},{5,1},{6,2},{7,3},{8,12},{9,13},{10,... | collective-permute-start | bytes 393224 | tf_op jit(solution)/shard_map/ppermute | solution.py:367
  7.9 0.6 collective-permute-start.4
  8.5 0.7 collective-permute-done.refs_1_
  9.2 2.8 %collective-permute-done.1.refs_2_ = bf16[32,2048]{1,0:T(8,128)(2,1)S(1)} collective-permute-done((bf16[32,2048]{1,0:T(8,128)(2,1)S(1)}, bf16[32,2048]{1,0:T(8,128)(2,1)S(1)}, u32[]{:S(2)}, u32[]{:S(2)}) %collective-permute-start.1) | collective-permute-done | bytes 131104 | tf_op jit(solution)/shard_map/ppermute | solution.py:367
  12.0 3.4 %collective-permute-done.2.refs_3_ = bf16[32,2048]{1,0:T(8,128)(2,1)S(1)} collective-permute-done((bf16[32,2048]{1,0:T(8,128)(2,1)S(1)}, bf16[32,2048]{1,0:T(8,128)(2,1)S(1)}, u32[]{:S(2)}, u32[]{:S(2)}) %collective-permute-start.2) | collective-permute-done | bytes 131104 | tf_op jit(solution)/shard_map/ppermute | solution.py:367
  15.5 1.1 collective-permute-done.4.refs_5_
  16.6 0.7 collective-permute-done.5.refs_6_
  17.3 0.5 gram_kernel.1
  18.0 1.2 collective-permute-done.7
  19.2 2.6 %collective-permute-start.10 = (bf16[3,64,128]{2,1,0:T(8,128)(2,1)S(1)}, bf16[3,64,128]{2,1,0:T(8,128)(2,1)S(1)}, u32[]{:S(2)}, u32[]{:S(2)}) collective-permute-start(bf16[3,64,128]{2,1,0:T(8,128)(2,1)S(1)} %add_convert_fusion.2), channel_id=1, source_target_pairs={{0,6},{1,7},{2,4},{3,5},{4,2},{5,3},{6,0},{7,1},{8,14},{9,15},{10,... | collective-permute-start | bytes 147464 | tf_op jit(solution)/shard_map/ppermute | solution.py:367
  21.8 0.5 collective-permute-start.9
  22.2 0.5 collective-permute-start.8
  22.8 1.5 %collective-permute-done.10 = bf16[3,64,128]{2,1,0:T(8,128)(2,1)S(1)} collective-permute-done((bf16[3,64,128]{2,1,0:T(8,128)(2,1)S(1)}, bf16[3,64,128]{2,1,0:T(8,128)(2,1)S(1)}, u32[]{:S(2)}, u32[]{:S(2)}) %collective-permute-start.10) | collective-permute-done | bytes 49184 | tf_op jit(solution)/shard_map/ppermute | solution.py:367
  24.3 1.6 %collective-permute-done.9 = bf16[3,64,128]{2,1,0:T(8,128)(2,1)S(1)} collective-permute-done((bf16[3,64,128]{2,1,0:T(8,128)(2,1)S(1)}, bf16[3,64,128]{2,1,0:T(8,128)(2,1)S(1)}, u32[]{:S(2)}, u32[]{:S(2)}) %collective-permute-start.9) | collective-permute-done | bytes 49184 | tf_op jit(solution)/shard_map/ppermute | solution.py:367
  25.9 0.5 collective-permute-done.8
  26.4 1.3 %collective-permute-done.11.other_ref = f32[3,64,128]{2,1,0:T(8,128)S(1)} collective-permute-done((f32[3,64,128]{2,1,0:T(8,128)S(1)}, f32[3,64,128]{2,1,0:T(8,128)S(1)}, u32[]{:S(2)}, u32[]{:S(2)}) %collective-permute-start.11) | collective-permute-done | bytes 98336 | tf_op jit(solution)/shard_map/ppermute | solution.py:367
  27.7 4.8 %node_kernel.1 = (bf16[128,512]{1,0:T(8,128)(2,1)S(1)}, bf16[128,512]{1,0:T(8,128)(2,1)S(1)}, bf16[128,512]{1,0:T(8,128)(2,1)S(1)}, bf16[128,512]{1,0:T(8,128)(2,1)S(1)}, bf16[256,128]{1,0:T(8,128)(2,1)S(1)}) custom-call(s32[1]{0:T(128)} %bitcast.pos_ref, f32[3,64,128]{2,1,0:T(8,128)S(1)} %add_add_fusion.mine_ref, ...), custom_call_target="tpu_custom_call" | custom-call | tf_op jit(solution)/shard_map/node_kernel/pallas_call | solution.py:350
  32.5 2.7 %collective-permute-start.12 = (bf16[128,512]{1,0:T(8,128)(2,1)S(1)}, bf16[128,512]{1,0:T(8,128)(2,1)S(1)}, u32[]{:S(2)}, u32[]{:S(2)}) collective-permute-start(bf16[128,512]{1,0:T(8,128)(2,1)S(1)} %get-tuple-element.48), channel_id=1, source_target_pairs={{0,16},{1,17},{2,18},{3,19},{4,20},{5,21},{6,22},{7,23},{8,24},{9,... | collective-permute-start | bytes 393224 | tf_op jit(solution)/shard_map/ppermute | solution.py:367
  35.2 1.3 %collective-permute-start.13 = (bf16[128,512]{1,0:T(8,128)(2,1)S(1)}, bf16[128,512]{1,0:T(8,128)(2,1)S(1)}, u32[]{:S(2)}, u32[]{:S(2)}) collective-permute-start(bf16[128,512]{1,0:T(8,128)(2,1)S(1)} %get-tuple-element.49), channel_id=1, source_target_pairs={{0,24},{1,25},{2,26},{3,27},{4,28},{5,29},{6,30},{7,31},{8,16},{9,... | collective-permute-start | bytes 393224 | tf_op jit(solution)/shard_map/ppermute | solution.py:367
  36.8 8.7 %collective-permute-done.12.refs_1_ = bf16[128,512]{1,0:T(8,128)(2,1)S(1)} collective-permute-done((bf16[128,512]{1,0:T(8,128)(2,1)S(1)}, bf16[128,512]{1,0:T(8,128)(2,1)S(1)}, u32[]{:S(2)}, u32[]{:S(2)}) %collective-permute-start.12) | collective-permute-done | bytes 131104 | tf_op jit(solution)/shard_map/ppermute | solution.py:367
  45.5 0.5 collective-permute-done.14.refs_3_
  46.0 0.4 cross_kernel.1
  46.5 1.4 %collective-permute-done.15 = f32[6,64,128]{2,1,0:T(8,128)S(1)} collective-permute-done((f32[6,64,128]{2,1,0:T(8,128)S(1)}, f32[6,64,128]{2,1,0:T(8,128)S(1)}, u32[]{:S(2)}, u32[]{:S(2)}) %collective-permute-start.15) | collective-permute-done | bytes 196640 | tf_op jit(solution)/shard_map/ppermute | solution.py:367
  48.0 1.6 %collective-permute-start.18 = (bf16[6,64,128]{2,1,0:T(8,128)(2,1)S(1)}, bf16[6,64,128]{2,1,0:T(8,128)(2,1)S(1)}, u32[]{:S(2)}, u32[]{:S(2)}) collective-permute-start(bf16[6,64,128]{2,1,0:T(8,128)(2,1)S(1)} %add_convert_fusion.1), channel_id=1, source_target_pairs={{0,6},{1,7},{2,4},{3,5},{4,2},{5,3},{6,0},{7,1},{8,14},{9,15},{10,... | collective-permute-start | bytes 294920 | tf_op jit(solution)/shard_map/ppermute | solution.py:367
  49.6 0.5 collective-permute-start.17
  50.1 1.5 %collective-permute-start.16 = (bf16[6,64,128]{2,1,0:T(8,128)(2,1)S(1)}, bf16[6,64,128]{2,1,0:T(8,128)(2,1)S(1)}, u32[]{:S(2)}, u32[]{:S(2)}) collective-permute-start(bf16[6,64,128]{2,1,0:T(8,128)(2,1)S(1)} %add_convert_fusion.1), channel_id=1, source_target_pairs={{0,2},{1,3},{2,0},{3,1},{4,6},{5,7},{6,4},{7,5},{8,10},{9,11},{10,... | collective-permute-start | bytes 294920 | tf_op jit(solution)/shard_map/ppermute | solution.py:367
  51.5 0.4 diag_kernel.1
  52.0 2.4 %collective-permute-done.18 = bf16[6,64,128]{2,1,0:T(8,128)(2,1)S(1)} collective-permute-done((bf16[6,64,128]{2,1,0:T(8,128)(2,1)S(1)}, bf16[6,64,128]{2,1,0:T(8,128)(2,1)S(1)}, u32[]{:S(2)}, u32[]{:S(2)}) %collective-permute-start.18) | collective-permute-done | bytes 98336 | tf_op jit(solution)/shard_map/ppermute | solution.py:367
  54.4 1.5 %collective-permute-done.17 = bf16[6,64,128]{2,1,0:T(8,128)(2,1)S(1)} collective-permute-done((bf16[6,64,128]{2,1,0:T(8,128)(2,1)S(1)}, bf16[6,64,128]{2,1,0:T(8,128)(2,1)S(1)}, u32[]{:S(2)}, u32[]{:S(2)}) %collective-permute-start.17) | collective-permute-done | bytes 98336 | tf_op jit(solution)/shard_map/ppermute | solution.py:367
  56.1 3.5 %collective-permute-start.21 = (bf16[7,64,128]{2,1,0:T(8,128)(2,1)S(1)}, bf16[7,64,128]{2,1,0:T(8,128)(2,1)S(1)}, u32[]{:S(2)}, u32[]{:S(2)}) collective-permute-start(bf16[7,64,128]{2,1,0:T(8,128)(2,1)S(1)} %pad_maximum_fusion), channel_id=1, source_target_pairs={{0,24},{1,25},{2,26},{3,27},{4,28},{5,29},{6,30},{7,31},{8,16},{9,... | collective-permute-start | bytes 344072 | tf_op jit(solution)/shard_map/ppermute | solution.py:367
  59.7 0.7 collective-permute-start.20
  60.4 0.5 collective-permute-start.19
  60.8 2.4 %collective-permute-done.21 = bf16[7,64,128]{2,1,0:T(8,128)(2,1)S(1)} collective-permute-done((bf16[7,64,128]{2,1,0:T(8,128)(2,1)S(1)}, bf16[7,64,128]{2,1,0:T(8,128)(2,1)S(1)}, u32[]{:S(2)}, u32[]{:S(2)}) %collective-permute-start.21) | collective-permute-done | bytes 114720 | tf_op jit(solution)/shard_map/ppermute | solution.py:367
  63.2 7.1 %collective-permute-done.20 = bf16[7,64,128]{2,1,0:T(8,128)(2,1)S(1)} collective-permute-done((bf16[7,64,128]{2,1,0:T(8,128)(2,1)S(1)}, bf16[7,64,128]{2,1,0:T(8,128)(2,1)S(1)}, u32[]{:S(2)}, u32[]{:S(2)}) %collective-permute-start.20) | collective-permute-done | bytes 114720 | tf_op jit(solution)/shard_map/ppermute | solution.py:367
  70.5 1.6 %collective-permute-done.22.other_ref = f32[10,64,128]{2,1,0:T(8,128)S(1)} collective-permute-done((f32[10,64,128]{2,1,0:T(8,128)S(1)}, f32[10,64,128]{2,1,0:T(8,128)S(1)}, u32[]{:S(2)}, u32[]{:S(2)}) %collective-permute-start.22) | collective-permute-done | bytes 327712 | tf_op jit(solution)/shard_map/ppermute | solution.py:367
  72.1 12.0 %top_kernel.1 = (bf16[128,512]{1,0:T(8,128)(2,1)S(1)}, f32[256,256]{1,0:T(8,128)S(1)}, bf16[256,128]{1,0:T(8,128)(2,1)S(1)}) custom-call(s32[1]{0:T(128)} %bitcast.pos_ref, f32[10,64,128]{2,1,0:T(8,128)S(1)} %convert_dynamic-update-slice_fusion.mine_ref, f32[10,64,128]{2,1,0:T(8,128)S(1)} %collective-permute-done.22.other_ref, ...), custom_call_target="tpu_custom_call" | custom-call | tf_op jit(solution)/shard_map/top_kernel/pallas_call | solution.py:350
  84.1 0.3 collective-permute-start.25
  84.4 3.0 %collective-permute-start.24 = (bf16[128,512]{1,0:T(8,128)(2,1)S(1)}, bf16[128,512]{1,0:T(8,128)(2,1)S(1)}, u32[]{:S(2)}, u32[]{:S(2)}) collective-permute-start(bf16[128,512]{1,0:T(8,128)(2,1)S(1)} %get-tuple-element.56.refs_0_), channel_id=1, source_target_pairs={{0,24},{1,25},{2,26},{3,27},{4,28},{5,29},{6,30},{7,31},{8,16},{9,... | collective-permute-start | bytes 393224 | tf_op jit(solution)/shard_map/ppermute | solution.py:367
  87.4 0.5 collective-permute-start.23
  87.9 3.4 %factor_kernel.1.factor_ref = f32[128,128]{1,0:T(8,128)S(1)} custom-call(f32[256,256]{1,0:T(8,128)S(1)} %get-tuple-element.54.gram_ref, bf16[256,128]{1,0:T(8,128)(2,1)S(1)} %get-tuple-element.55.low_ref), custom_call_target="tpu_custom_call" | custom-call | tf_op jit(solution)/shard_map/factor_kernel/pallas_call | solution.py:350
  91.3 5.6 %collective-permute-done.25.refs_3_ = bf16[128,512]{1,0:T(8,128)(2,1)S(1)} collective-permute-done((bf16[128,512]{1,0:T(8,128)(2,1)S(1)}, bf16[128,512]{1,0:T(8,128)(2,1)S(1)}, u32[]{:S(2)}, u32[]{:S(2)}) %collective-permute-start.25) | collective-permute-done | bytes 131104 | tf_op jit(solution)/shard_map/ppermute | solution.py:367
  96.9 0.8 collective-permute-done.23.refs_1_
  97.6 0.8 coeffs_kernel.1
  98.5 1.2 %collective-permute-done.26 = f32[1,128,128]{2,1,0:T(8,128)S(1)} collective-permute-done((f32[1,128,128]{2,1,0:T(8,128)S(1)}, f32[1,128,128]{2,1,0:T(8,128)S(1)}, u32[]{:S(2)}, u32[]{:S(2)}) %collective-permute-start.26) | collective-permute-done | bytes 65568 | tf_op jit(solution)/shard_map/ppermute | solution.py:367
  99.8 1.6 %collective-permute-start.29 = (bf16[1,128,128]{2,1,0:T(8,128)(2,1)S(1)}, bf16[1,128,128]{2,1,0:T(8,128)(2,1)S(1)}, u32[]{:S(2)}, u32[]{:S(2)}) collective-permute-start(bf16[1,128,128]{2,1,0:T(8,128)(2,1)S(1)} %add_convert_fusion.3), channel_id=1, source_target_pairs={{0,6},{1,7},{2,4},{3,5},{4,2},{5,3},{6,0},{7,1},{8,14},{9,15},{10,... | collective-permute-start | bytes 98312 | tf_op jit(solution)/shard_map/ppermute | solution.py:367
  101.7 1.7 %collective-permute-start.27 = (bf16[1,128,128]{2,1,0:T(8,128)(2,1)S(1)}, bf16[1,128,128]{2,1,0:T(8,128)(2,1)S(1)}, u32[]{:S(2)}, u32[]{:S(2)}) collective-permute-start(bf16[1,128,128]{2,1,0:T(8,128)(2,1)S(1)} %add_convert_fusion.3), channel_id=1, source_target_pairs={{0,2},{1,3},{2,0},{3,1},{4,6},{5,7},{6,4},{7,5},{8,10},{9,11},{10,... | collective-permute-start | bytes 98312 | tf_op jit(solution)/shard_map/ppermute | solution.py:367
  103.4 1.3 %collective-permute-done.29 = bf16[1,128,128]{2,1,0:T(8,128)(2,1)S(1)} collective-permute-done((bf16[1,128,128]{2,1,0:T(8,128)(2,1)S(1)}, bf16[1,128,128]{2,1,0:T(8,128)(2,1)S(1)}, u32[]{:S(2)}, u32[]{:S(2)}) %collective-permute-start.29) | collective-permute-done | bytes 32800 | tf_op jit(solution)/shard_map/ppermute | solution.py:367
  104.7 0.6 collective-permute-done.28
  105.7 1.2 %collective-permute-done.30.other_ref = f32[1,128,128]{2,1,0:T(8,128)S(1)} collective-permute-done((f32[1,128,128]{2,1,0:T(8,128)S(1)}, f32[1,128,128]{2,1,0:T(8,128)S(1)}, u32[]{:S(2)}, u32[]{:S(2)}) %collective-permute-start.30) | collective-permute-done | bytes 65568 | tf_op jit(solution)/shard_map/ppermute | solution.py:367
  106.9 0.8 project_kernel.1
  107.7 1.3 %collective-permute-start.31 = (bf16[32,2048]{1,0:T(8,128)(2,1)S(1)}, bf16[32,2048]{1,0:T(8,128)(2,1)S(1)}, u32[]{:S(2)}, u32[]{:S(2)}) collective-permute-start(bf16[32,2048]{1,0:T(8,128)(2,1)S(1)} %get-tuple-element.60), channel_id=1, source_target_pairs={{0,6},{1,7},{2,4},{3,5},{4,2},{5,3},{6,0},{7,1},{8,14},{9,15},{10,... | collective-permute-start | bytes 393224 | tf_op jit(solution)/shard_map/ppermute | solution.py:367
  109.0 1.2 collective-permute-start.32
  110.2 1.7 %collective-permute-start.33 = (bf16[32,2048]{1,0:T(8,128)(2,1)S(1)}, bf16[32,2048]{1,0:T(8,128)(2,1)S(1)}, u32[]{:S(2)}, u32[]{:S(2)}) collective-permute-start(bf16[32,2048]{1,0:T(8,128)(2,1)S(1)} %get-tuple-element.62), channel_id=1, source_target_pairs={{0,2},{1,3},{2,0},{3,1},{4,6},{5,7},{6,4},{7,5},{8,10},{9,11},{10,... | collective-permute-start | bytes 393224 | tf_op jit(solution)/shard_map/ppermute | solution.py:367
  112.0 1.7 %collective-permute-start.35 = (bf16[32,2048]{1,0:T(8,128)(2,1)S(1)}, bf16[32,2048]{1,0:T(8,128)(2,1)S(1)}, u32[]{:S(2)}, u32[]{:S(2)}) collective-permute-start(bf16[32,2048]{1,0:T(8,128)(2,1)S(1)} %get-tuple-element.64), channel_id=1, source_target_pairs={{0,3},{1,2},{2,1},{3,0},{4,7},{5,6},{6,5},{7,4},{8,11},{9,10},{10,... | collective-permute-start | bytes 393224 | tf_op jit(solution)/shard_map/ppermute | solution.py:367
  113.7 1.4 %collective-permute-done.31.refs_1_ = bf16[32,2048]{1,0:T(8,128)(2,1)S(1)} collective-permute-done((bf16[32,2048]{1,0:T(8,128)(2,1)S(1)}, bf16[32,2048]{1,0:T(8,128)(2,1)S(1)}, u32[]{:S(2)}, u32[]{:S(2)}) %collective-permute-start.31) | collective-permute-done | bytes 131104 | tf_op jit(solution)/shard_map/ppermute | solution.py:367
  115.0 1.3 %collective-permute-done.32.refs_2_ = bf16[32,2048]{1,0:T(8,128)(2,1)S(1)} collective-permute-done((bf16[32,2048]{1,0:T(8,128)(2,1)S(1)}, bf16[32,2048]{1,0:T(8,128)(2,1)S(1)}, u32[]{:S(2)}, u32[]{:S(2)}) %collective-permute-start.32) | collective-permute-done | bytes 131104 | tf_op jit(solution)/shard_map/ppermute | solution.py:367
  116.3 1.3 %collective-permute-start.37 = (bf16[32,2048]{1,0:T(8,128)(2,1)S(1)}, bf16[32,2048]{1,0:T(8,128)(2,1)S(1)}, u32[]{:S(2)}, u32[]{:S(2)}) collective-permute-start(bf16[32,2048]{1,0:T(8,128)(2,1)S(1)} %get-tuple-element.66), channel_id=1, source_target_pairs={{0,1},{1,0},{2,3},{3,2},{4,5},{5,4},{6,7},{7,6},{8,9},{9,8},{10,11... | collective-permute-start | bytes 393224 | tf_op jit(solution)/shard_map/ppermute | solution.py:367
  117.6 3.3 %collective-permute-done.33.refs_3_ = bf16[32,2048]{1,0:T(8,128)(2,1)S(1)} collective-permute-done((bf16[32,2048]{1,0:T(8,128)(2,1)S(1)}, bf16[32,2048]{1,0:T(8,128)(2,1)S(1)}, u32[]{:S(2)}, u32[]{:S(2)}) %collective-permute-start.33) | collective-permute-done | bytes 131104 | tf_op jit(solution)/shard_map/ppermute | solution.py:367
  121.0 1.2 collective-permute-done.35.refs_5_
  122.2 0.4 collective-permute-done.36.refs_6_
  122.6 1.0 whole_kernel.1
  (36 shorter events, 1.9 us)
Async XLA Ops:
  0.0 1.2 copy-start
  1.3 7.9 %collective-permute-start = (bf16[32,2048]{1,0:T(8,128)(2,1)S(1)}, bf16[32,2048]{1,0:T(8,128)(2,1)S(1)}, u32[]{:S(2)}, u32[]{:S(2)}) collective-permute-start(bf16[32,2048]{1,0:T(8,128)(2,1)S(1)} %get-tuple-element.37), channel_id=1, source_target_pairs={{0,6},{1,7},{2,4},{3,5},{4,2},{5,3},{6,0},{7,1},{8,14},{9,15},{10,... | collective-permute-start | bytes 393224 | tf_op jit(solution)/shard_map/ppermute | solution.py:367
  5.3 6.8 %collective-permute-start.1 = (bf16[32,2048]{1,0:T(8,128)(2,1)S(1)}, bf16[32,2048]{1,0:T(8,128)(2,1)S(1)}, u32[]{:S(2)}, u32[]{:S(2)}) collective-permute-start(bf16[32,2048]{1,0:T(8,128)(2,1)S(1)} %get-tuple-element.38), channel_id=1, source_target_pairs={{0,7},{1,6},{2,5},{3,4},{4,3},{5,2},{6,1},{7,0},{8,15},{9,14},{10,... | collective-permute-start | bytes 393224 | tf_op jit(solution)/shard_map/ppermute | solution.py:367
  5.3 10.2 %collective-permute-start.2 = (bf16[32,2048]{1,0:T(8,128)(2,1)S(1)}, bf16[32,2048]{1,0:T(8,128)(2,1)S(1)}, u32[]{:S(2)}, u32[]{:S(2)}) collective-permute-start(bf16[32,2048]{1,0:T(8,128)(2,1)S(1)} %get-tuple-element.39), channel_id=1, source_target_pairs={{0,2},{1,3},{2,0},{3,1},{4,6},{5,7},{6,4},{7,5},{8,10},{9,11},{10,... | collective-permute-start | bytes 393224 | tf_op jit(solution)/shard_map/ppermute | solution.py:367
  6.4 9.1 %collective-permute-start.3 = (bf16[32,2048]{1,0:T(8,128)(2,1)S(1)}, bf16[32,2048]{1,0:T(8,128)(2,1)S(1)}, u32[]{:S(2)}, u32[]{:S(2)}) collective-permute-start(bf16[32,2048]{1,0:T(8,128)(2,1)S(1)} %get-tuple-element.40), channel_id=1, source_target_pairs={{0,4},{1,5},{2,6},{3,7},{4,0},{5,1},{6,2},{7,3},{8,12},{9,13},{10,... | collective-permute-start | bytes 393224 | tf_op jit(solution)/shard_map/ppermute | solution.py:367
  7.9 8.7 %collective-permute-start.4 = (bf16[32,2048]{1,0:T(8,128)(2,1)S(1)}, bf16[32,2048]{1,0:T(8,128)(2,1)S(1)}, u32[]{:S(2)}, u32[]{:S(2)}) collective-permute-start(bf16[32,2048]{1,0:T(8,128)(2,1)S(1)} %get-tuple-element.41), channel_id=1, source_target_pairs={{0,3},{1,2},{2,1},{3,0},{4,7},{5,6},{6,5},{7,4},{8,11},{9,10},{10,... | collective-permute-start | bytes 393224 | tf_op jit(solution)/shard_map/ppermute | solution.py:367
  9.2 8.1 %collective-permute-start.5 = (bf16[32,2048]{1,0:T(8,128)(2,1)S(1)}, bf16[32,2048]{1,0:T(8,128)(2,1)S(1)}, u32[]{:S(2)}, u32[]{:S(2)}) collective-permute-start(bf16[32,2048]{1,0:T(8,128)(2,1)S(1)} %get-tuple-element.42), channel_id=1, source_target_pairs={{0,5},{1,4},{2,7},{3,6},{4,1},{5,0},{6,3},{7,2},{8,13},{9,12},{10,... | collective-permute-start | bytes 393224 | tf_op jit(solution)/shard_map/ppermute | solution.py:367
  12.0 5.3 %collective-permute-start.6 = (bf16[32,2048]{1,0:T(8,128)(2,1)S(1)}, bf16[32,2048]{1,0:T(8,128)(2,1)S(1)}, u32[]{:S(2)}, u32[]{:S(2)}) collective-permute-start(bf16[32,2048]{1,0:T(8,128)(2,1)S(1)} %get-tuple-element.43), channel_id=1, source_target_pairs={{0,1},{1,0},{2,3},{3,2},{4,5},{5,4},{6,7},{7,6},{8,9},{9,8},{10,11... | collective-permute-start | bytes 393224 | tf_op jit(solution)/shard_map/ppermute | solution.py:367
  17.8 1.4 %collective-permute-start.7 = (f32[3,64,128]{2,1,0:T(8,128)S(1)}, f32[3,64,128]{2,1,0:T(8,128)S(1)}, u32[]{:S(2)}, u32[]{:S(2)}) collective-permute-start(f32[3,64,128]{2,1,0:T(8,128)S(1)} %get-tuple-element.46), channel_id=1, source_target_pairs={{0,1},{1,0},{2,3},{3,2},{4,5},{5,4},{6,7},{7,6},{8,9},{9,8},{10,11... | collective-permute-start | bytes 294920 | tf_op jit(solution)/shard_map/ppermute | solution.py:367
  19.2 5.1 %collective-permute-start.10 = (bf16[3,64,128]{2,1,0:T(8,128)(2,1)S(1)}, bf16[3,64,128]{2,1,0:T(8,128)(2,1)S(1)}, u32[]{:S(2)}, u32[]{:S(2)}) collective-permute-start(bf16[3,64,128]{2,1,0:T(8,128)(2,1)S(1)} %add_convert_fusion.2), channel_id=1, source_target_pairs={{0,6},{1,7},{2,4},{3,5},{4,2},{5,3},{6,0},{7,1},{8,14},{9,15},{10,... | collective-permute-start | bytes 147464 | tf_op jit(solution)/shard_map/ppermute | solution.py:367
  21.8 4.1 %collective-permute-start.9 = (bf16[3,64,128]{2,1,0:T(8,128)(2,1)S(1)}, bf16[3,64,128]{2,1,0:T(8,128)(2,1)S(1)}, u32[]{:S(2)}, u32[]{:S(2)}) collective-permute-start(bf16[3,64,128]{2,1,0:T(8,128)(2,1)S(1)} %add_convert_fusion.2), channel_id=1, source_target_pairs={{0,4},{1,5},{2,6},{3,7},{4,0},{5,1},{6,2},{7,3},{8,12},{9,13},{10,... | collective-permute-start | bytes 147464 | tf_op jit(solution)/shard_map/ppermute | solution.py:367
  22.2 4.1 %collective-permute-start.8 = (bf16[3,64,128]{2,1,0:T(8,128)(2,1)S(1)}, bf16[3,64,128]{2,1,0:T(8,128)(2,1)S(1)}, u32[]{:S(2)}, u32[]{:S(2)}) collective-permute-start(bf16[3,64,128]{2,1,0:T(8,128)(2,1)S(1)} %add_convert_fusion.2), channel_id=1, source_target_pairs={{0,2},{1,3},{2,0},{3,1},{4,6},{5,7},{6,4},{7,5},{8,10},{9,11},{10,... | collective-permute-start | bytes 147464 | tf_op jit(solution)/shard_map/ppermute | solution.py:367
  26.4 1.4 %collective-permute-start.11 = (f32[3,64,128]{2,1,0:T(8,128)S(1)}, f32[3,64,128]{2,1,0:T(8,128)S(1)}, u32[]{:S(2)}, u32[]{:S(2)}) collective-permute-start(f32[3,64,128]{2,1,0:T(8,128)S(1)} %add_add_fusion.mine_ref), channel_id=1, source_target_pairs={{0,1},{1,0},{2,3},{3,2},{4,5},{5,4},{6,7},{7,6},{8,9},{9,8},{10,11... | collective-permute-start | bytes 294920 | tf_op jit(solution)/shard_map/ppermute | solution.py:367
  32.5 13.0 %collective-permute-start.12 = (bf16[128,512]{1,0:T(8,128)(2,1)S(1)}, bf16[128,512]{1,0:T(8,128)(2,1)S(1)}, u32[]{:S(2)}, u32[]{:S(2)}) collective-permute-start(bf16[128,512]{1,0:T(8,128)(2,1)S(1)} %get-tuple-element.48), channel_id=1, source_target_pairs={{0,16},{1,17},{2,18},{3,19},{4,20},{5,21},{6,22},{7,23},{8,24},{9,... | collective-permute-start | bytes 393224 | tf_op jit(solution)/shard_map/ppermute | solution.py:367
  35.2 10.3 %collective-permute-start.13 = (bf16[128,512]{1,0:T(8,128)(2,1)S(1)}, bf16[128,512]{1,0:T(8,128)(2,1)S(1)}, u32[]{:S(2)}, u32[]{:S(2)}) collective-permute-start(bf16[128,512]{1,0:T(8,128)(2,1)S(1)} %get-tuple-element.49), channel_id=1, source_target_pairs={{0,24},{1,25},{2,26},{3,27},{4,28},{5,29},{6,30},{7,31},{8,16},{9,... | collective-permute-start | bytes 393224 | tf_op jit(solution)/shard_map/ppermute | solution.py:367
  36.5 9.5 %collective-permute-start.14 = (bf16[128,512]{1,0:T(8,128)(2,1)S(1)}, bf16[128,512]{1,0:T(8,128)(2,1)S(1)}, u32[]{:S(2)}, u32[]{:S(2)}) collective-permute-start(bf16[128,512]{1,0:T(8,128)(2,1)S(1)} %get-tuple-element.50), channel_id=1, source_target_pairs={{0,8},{1,9},{2,10},{3,11},{4,12},{5,13},{6,14},{7,15},{8,0},{9,1},... | collective-permute-start | bytes 393224 | tf_op jit(solution)/shard_map/ppermute | solution.py:367
  46.5 1.5 %collective-permute-start.15 = (f32[6,64,128]{2,1,0:T(8,128)S(1)}, f32[6,64,128]{2,1,0:T(8,128)S(1)}, u32[]{:S(2)}, u32[]{:S(2)}) collective-permute-start(f32[6,64,128]{2,1,0:T(8,128)S(1)} %get-tuple-element.52), channel_id=1, source_target_pairs={{0,1},{1,0},{2,3},{3,2},{4,5},{5,4},{6,7},{7,6},{8,9},{9,8},{10,11... | collective-permute-start | bytes 589832 | tf_op jit(solution)/shard_map/ppermute | solution.py:367
  48.0 6.4 %collective-permute-start.18 = (bf16[6,64,128]{2,1,0:T(8,128)(2,1)S(1)}, bf16[6,64,128]{2,1,0:T(8,128)(2,1)S(1)}, u32[]{:S(2)}, u32[]{:S(2)}) collective-permute-start(bf16[6,64,128]{2,1,0:T(8,128)(2,1)S(1)} %add_convert_fusion.1), channel_id=1, source_target_pairs={{0,6},{1,7},{2,4},{3,5},{4,2},{5,3},{6,0},{7,1},{8,14},{9,15},{10,... | collective-permute-start | bytes 294920 | tf_op jit(solution)/shard_map/ppermute | solution.py:367
  49.6 6.3 %collective-permute-start.17 = (bf16[6,64,128]{2,1,0:T(8,128)(2,1)S(1)}, bf16[6,64,128]{2,1,0:T(8,128)(2,1)S(1)}, u32[]{:S(2)}, u32[]{:S(2)}) collective-permute-start(bf16[6,64,128]{2,1,0:T(8,128)(2,1)S(1)} %add_convert_fusion.1), channel_id=1, source_target_pairs={{0,4},{1,5},{2,6},{3,7},{4,0},{5,1},{6,2},{7,3},{8,12},{9,13},{10,... | collective-permute-start | bytes 294920 | tf_op jit(solution)/shard_map/ppermute | solution.py:367
  50.1 6.0 %collective-permute-start.16 = (bf16[6,64,128]{2,1,0:T(8,128)(2,1)S(1)}, bf16[6,64,128]{2,1,0:T(8,128)(2,1)S(1)}, u32[]{:S(2)}, u32[]{:S(2)}) collective-permute-start(bf16[6,64,128]{2,1,0:T(8,128)(2,1)S(1)} %add_convert_fusion.1), channel_id=1, source_target_pairs={{0,2},{1,3},{2,0},{3,1},{4,6},{5,7},{6,4},{7,5},{8,10},{9,11},{10,... | collective-permute-start | bytes 294920 | tf_op jit(solution)/shard_map/ppermute | solution.py:367
  56.1 7.1 %collective-permute-start.21 = (bf16[7,64,128]{2,1,0:T(8,128)(2,1)S(1)}, bf16[7,64,128]{2,1,0:T(8,128)(2,1)S(1)}, u32[]{:S(2)}, u32[]{:S(2)}) collective-permute-start(bf16[7,64,128]{2,1,0:T(8,128)(2,1)S(1)} %pad_maximum_fusion), channel_id=1, source_target_pairs={{0,24},{1,25},{2,26},{3,27},{4,28},{5,29},{6,30},{7,31},{8,16},{9,... | collective-permute-start | bytes 344072 | tf_op jit(solution)/shard_map/ppermute | solution.py:367
  59.7 10.6 %collective-permute-start.20 = (bf16[7,64,128]{2,1,0:T(8,128)(2,1)S(1)}, bf16[7,64,128]{2,1,0:T(8,128)(2,1)S(1)}, u32[]{:S(2)}, u32[]{:S(2)}) collective-permute-start(bf16[7,64,128]{2,1,0:T(8,128)(2,1)S(1)} %pad_maximum_fusion), channel_id=1, source_target_pairs={{0,16},{1,17},{2,18},{3,19},{4,20},{5,21},{6,22},{7,23},{8,24},{9,... | collective-permute-start | bytes 344072 | tf_op jit(solution)/shard_map/ppermute | solution.py:367
  60.4 9.9 %collective-permute-start.19 = (bf16[7,64,128]{2,1,0:T(8,128)(2,1)S(1)}, bf16[7,64,128]{2,1,0:T(8,128)(2,1)S(1)}, u32[]{:S(2)}, u32[]{:S(2)}) collective-permute-start(bf16[7,64,128]{2,1,0:T(8,128)(2,1)S(1)} %pad_maximum_fusion), channel_id=1, source_target_pairs={{0,8},{1,9},{2,10},{3,11},{4,12},{5,13},{6,14},{7,15},{8,0},{9,1},... | collective-permute-start | bytes 344072 | tf_op jit(solution)/shard_map/ppermute | solution.py:367
  70.4 1.7 %collective-permute-start.22 = (f32[10,64,128]{2,1,0:T(8,128)S(1)}, f32[10,64,128]{2,1,0:T(8,128)S(1)}, u32[]{:S(2)}, u32[]{:S(2)}) collective-permute-start(f32[10,64,128]{2,1,0:T(8,128)S(1)} %convert_dynamic-update-slice_fusion.mine_ref), channel_id=1, source_target_pairs={{0,1},{1,0},{2,3},{3,2},{4,5},{5,4},{6,7},{7,6},{8,9},{9,8},{10,11... | collective-permute-start | bytes 983048 | tf_op jit(solution)/shard_map/ppermute | solution.py:367
  84.1 12.8 %collective-permute-start.25 = (bf16[128,512]{1,0:T(8,128)(2,1)S(1)}, bf16[128,512]{1,0:T(8,128)(2,1)S(1)}, u32[]{:S(2)}, u32[]{:S(2)}) collective-permute-start(bf16[128,512]{1,0:T(8,128)(2,1)S(1)} %get-tuple-element.56.refs_0_), channel_id=1, source_target_pairs={{0,16},{1,17},{2,18},{3,19},{4,20},{5,21},{6,22},{7,23},{8,24},{9,... | collective-permute-start | bytes 393224 | tf_op jit(solution)/shard_map/ppermute | solution.py:367
  84.4 12.5 %collective-permute-start.24 = (bf16[128,512]{1,0:T(8,128)(2,1)S(1)}, bf16[128,512]{1,0:T(8,128)(2,1)S(1)}, u32[]{:S(2)}, u32[]{:S(2)}) collective-permute-start(bf16[128,512]{1,0:T(8,128)(2,1)S(1)} %get-tuple-element.56.refs_0_), channel_id=1, source_target_pairs={{0,24},{1,25},{2,26},{3,27},{4,28},{5,29},{6,30},{7,31},{8,16},{9,... | collective-permute-start | bytes 393224 | tf_op jit(solution)/shard_map/ppermute | solution.py:367
  87.4 10.2 %collective-permute-start.23 = (bf16[128,512]{1,0:T(8,128)(2,1)S(1)}, bf16[128,512]{1,0:T(8,128)(2,1)S(1)}, u32[]{:S(2)}, u32[]{:S(2)}) collective-permute-start(bf16[128,512]{1,0:T(8,128)(2,1)S(1)} %get-tuple-element.56.refs_0_), channel_id=1, source_target_pairs={{0,8},{1,9},{2,10},{3,11},{4,12},{5,13},{6,14},{7,15},{8,0},{9,1},... | collective-permute-start | bytes 393224 | tf_op jit(solution)/shard_map/ppermute | solution.py:367
  98.5 1.3 %collective-permute-start.26 = (f32[1,128,128]{2,1,0:T(8,128)S(1)}, f32[1,128,128]{2,1,0:T(8,128)S(1)}, u32[]{:S(2)}, u32[]{:S(2)}) collective-permute-start(f32[1,128,128]{2,1,0:T(8,128)S(1)} %get-tuple-element.58), channel_id=1, source_target_pairs={{0,1},{1,0},{2,3},{3,2},{4,5},{5,4},{6,7},{7,6},{8,9},{9,8},{10,11... | collective-permute-start | bytes 196616 | tf_op jit(solution)/shard_map/ppermute | solution.py:367
  99.8 4.9 %collective-permute-start.29 = (bf16[1,128,128]{2,1,0:T(8,128)(2,1)S(1)}, bf16[1,128,128]{2,1,0:T(8,128)(2,1)S(1)}, u32[]{:S(2)}, u32[]{:S(2)}) collective-permute-start(bf16[1,128,128]{2,1,0:T(8,128)(2,1)S(1)} %add_convert_fusion.3), channel_id=1, source_target_pairs={{0,6},{1,7},{2,4},{3,5},{4,2},{5,3},{6,0},{7,1},{8,14},{9,15},{10,... | collective-permute-start | bytes 98312 | tf_op jit(solution)/shard_map/ppermute | solution.py:367
  101.4 3.9 %collective-permute-start.28 = (bf16[1,128,128]{2,1,0:T(8,128)(2,1)S(1)}, bf16[1,128,128]{2,1,0:T(8,128)(2,1)S(1)}, u32[]{:S(2)}, u32[]{:S(2)}) collective-permute-start(bf16[1,128,128]{2,1,0:T(8,128)(2,1)S(1)} %add_convert_fusion.3), channel_id=1, source_target_pairs={{0,4},{1,5},{2,6},{3,7},{4,0},{5,1},{6,2},{7,3},{8,12},{9,13},{10,... | collective-permute-start | bytes 98312 | tf_op jit(solution)/shard_map/ppermute | solution.py:367
  101.7 3.9 %collective-permute-start.27 = (bf16[1,128,128]{2,1,0:T(8,128)(2,1)S(1)}, bf16[1,128,128]{2,1,0:T(8,128)(2,1)S(1)}, u32[]{:S(2)}, u32[]{:S(2)}) collective-permute-start(bf16[1,128,128]{2,1,0:T(8,128)(2,1)S(1)} %add_convert_fusion.3), channel_id=1, source_target_pairs={{0,2},{1,3},{2,0},{3,1},{4,6},{5,7},{6,4},{7,5},{8,10},{9,11},{10,... | collective-permute-start | bytes 98312 | tf_op jit(solution)/shard_map/ppermute | solution.py:367
  105.6 1.3 %collective-permute-start.30 = (f32[1,128,128]{2,1,0:T(8,128)S(1)}, f32[1,128,128]{2,1,0:T(8,128)S(1)}, u32[]{:S(2)}, u32[]{:S(2)}) collective-permute-start(f32[1,128,128]{2,1,0:T(8,128)S(1)} %add_add_fusion.1.mine_ref), channel_id=1, source_target_pairs={{0,1},{1,0},{2,3},{3,2},{4,5},{5,4},{6,7},{7,6},{8,9},{9,8},{10,11... | collective-permute-start | bytes 196616 | tf_op jit(solution)/shard_map/ppermute | solution.py:367
  107.7 7.3 %collective-permute-start.31 = (bf16[32,2048]{1,0:T(8,128)(2,1)S(1)}, bf16[32,2048]{1,0:T(8,128)(2,1)S(1)}, u32[]{:S(2)}, u32[]{:S(2)}) collective-permute-start(bf16[32,2048]{1,0:T(8,128)(2,1)S(1)} %get-tuple-element.60), channel_id=1, source_target_pairs={{0,6},{1,7},{2,4},{3,5},{4,2},{5,3},{6,0},{7,1},{8,14},{9,15},{10,... | collective-permute-start | bytes 393224 | tf_op jit(solution)/shard_map/ppermute | solution.py:367
  109.0 7.4 %collective-permute-start.32 = (bf16[32,2048]{1,0:T(8,128)(2,1)S(1)}, bf16[32,2048]{1,0:T(8,128)(2,1)S(1)}, u32[]{:S(2)}, u32[]{:S(2)}) collective-permute-start(bf16[32,2048]{1,0:T(8,128)(2,1)S(1)} %get-tuple-element.61), channel_id=1, source_target_pairs={{0,7},{1,6},{2,5},{3,4},{4,3},{5,2},{6,1},{7,0},{8,15},{9,14},{10,... | collective-permute-start | bytes 393224 | tf_op jit(solution)/shard_map/ppermute | solution.py:367
  110.2 10.8 %collective-permute-start.33 = (bf16[32,2048]{1,0:T(8,128)(2,1)S(1)}, bf16[32,2048]{1,0:T(8,128)(2,1)S(1)}, u32[]{:S(2)}, u32[]{:S(2)}) collective-permute-start(bf16[32,2048]{1,0:T(8,128)(2,1)S(1)} %get-tuple-element.62), channel_id=1, source_target_pairs={{0,2},{1,3},{2,0},{3,1},{4,6},{5,7},{6,4},{7,5},{8,10},{9,11},{10,... | collective-permute-start | bytes 393224 | tf_op jit(solution)/shard_map/ppermute | solution.py:367
  111.9 9.1 %collective-permute-start.34 = (bf16[32,2048]{1,0:T(8,128)(2,1)S(1)}, bf16[32,2048]{1,0:T(8,128)(2,1)S(1)}, u32[]{:S(2)}, u32[]{:S(2)}) collective-permute-start(bf16[32,2048]{1,0:T(8,128)(2,1)S(1)} %get-tuple-element.63), channel_id=1, source_target_pairs={{0,4},{1,5},{2,6},{3,7},{4,0},{5,1},{6,2},{7,3},{8,12},{9,13},{10,... | collective-permute-start | bytes 393224 | tf_op jit(solution)/shard_map/ppermute | solution.py:367
  112.0 10.3 %collective-permute-start.35 = (bf16[32,2048]{1,0:T(8,128)(2,1)S(1)}, bf16[32,2048]{1,0:T(8,128)(2,1)S(1)}, u32[]{:S(2)}, u32[]{:S(2)}) collective-permute-start(bf16[32,2048]{1,0:T(8,128)(2,1)S(1)} %get-tuple-element.64), channel_id=1, source_target_pairs={{0,3},{1,2},{2,1},{3,0},{4,7},{5,6},{6,5},{7,4},{8,11},{9,10},{10,... | collective-permute-start | bytes 393224 | tf_op jit(solution)/shard_map/ppermute | solution.py:367
  115.0 7.6 %collective-permute-start.36 = (bf16[32,2048]{1,0:T(8,128)(2,1)S(1)}, bf16[32,2048]{1,0:T(8,128)(2,1)S(1)}, u32[]{:S(2)}, u32[]{:S(2)}) collective-permute-start(bf16[32,2048]{1,0:T(8,128)(2,1)S(1)} %get-tuple-element.65), channel_id=1, source_target_pairs={{0,5},{1,4},{2,7},{3,6},{4,1},{5,0},{6,3},{7,2},{8,13},{9,12},{10,... | collective-permute-start | bytes 393224 | tf_op jit(solution)/shard_map/ppermute | solution.py:367
  116.3 6.3 %collective-permute-start.37 = (bf16[32,2048]{1,0:T(8,128)(2,1)S(1)}, bf16[32,2048]{1,0:T(8,128)(2,1)S(1)}, u32[]{:S(2)}, u32[]{:S(2)}) collective-permute-start(bf16[32,2048]{1,0:T(8,128)(2,1)S(1)} %get-tuple-element.66), channel_id=1, source_target_pairs={{0,1},{1,0},{2,3},{3,2},{4,5},{5,4},{6,7},{7,6},{8,9},{9,8},{10,11... | collective-permute-start | bytes 393224 | tf_op jit(solution)/shard_map/ppermute | solution.py:367

commit v8 on v6

--- a/solution.py
+++ b/solution.py
@@ -12,7 +12,7 @@
 PLANES = 2**LEVELS // PLANE
 TILE = 8
 PANEL = 64
-PLANE_ORDER = (0, 6, 7, 2, 4, 3, 5, 1)
+PLANE_ORDER = (0, 2, 4, 6, 7, 3, 5, 1)
 TREE_ORDER = (0, 2, 3, 1)
 SUM_ORDER = (0, 1, 3, 2)
 PIVOT_SHARE = 2e-4

time: 123 us -> 124 us (level)
  transfers between devices with their start and end apart: 38 -> 38, of which waited for: 31 -> 27; matrix products, arithmetic and copies ran while one was open for 0% -> 0% of each run, Pallas kernels for 3% -> 3%
where the time goes in v8:
time: 124 us
  waiting for transfers between devices  59.5 us (48%)
  starting transfers between devices  38.1 us (31%)
  Pallas kernels  24.3 us (20%)
    ppermute x38, waiting for transfers between devices, swap(): return lax.ppermute(x, 'cols', [(i, i ^ apart) for i in range(count)])  59.5 us
    ppermute x38, starting transfers between devices, swap(): return lax.ppermute(x, 'cols', [(i, i ^ apart) for i in range(count)])  38.1 us
    pallas_call x10, Pallas kernels, kernel(): pl.pallas_call(fn, out_shape=[jax.ShapeDtypeStruct(s, d) for s, d in shap...  24.3 us
  transfers between devices with their start and end apart: 38, of which 27 were waited for; matrix products, arithmetic and copies ran while one was open for 0% of the time, Pallas kernels for 3%

profile of v8, /device:TPU:0, one launch (start us, length us, event | category | flops | bytes accessed | tf_op | source)
XLA Modules:
  0.0 123.6 jit_solution(8484290902554278647)
XLA Ops:
  0.0 1.2 copy-done
  1.3 3.0 %collective-permute-start = (bf16[32,2048]{1,0:T(8,128)(2,1)S(1)}, bf16[32,2048]{1,0:T(8,128)(2,1)S(1)}, u32[]{:S(2)}, u32[]{:S(2)}) collective-permute-start(bf16[32,2048]{1,0:T(8,128)(2,1)S(1)} %get-tuple-element.37), channel_id=1, source_target_pairs={{0,2},{1,3},{2,0},{3,1},{4,6},{5,7},{6,4},{7,5},{8,10},{9,11},{10,... | collective-permute-start | bytes 393224 | tf_op jit(solution)/shard_map/ppermute | solution.py:367
  4.3 1.5 %collective-permute-start.1 = (bf16[32,2048]{1,0:T(8,128)(2,1)S(1)}, bf16[32,2048]{1,0:T(8,128)(2,1)S(1)}, u32[]{:S(2)}, u32[]{:S(2)}) collective-permute-start(bf16[32,2048]{1,0:T(8,128)(2,1)S(1)} %get-tuple-element.38), channel_id=1, source_target_pairs={{0,4},{1,5},{2,6},{3,7},{4,0},{5,1},{6,2},{7,3},{8,12},{9,13},{10,... | collective-permute-start | bytes 393224 | tf_op jit(solution)/shard_map/ppermute | solution.py:367
  5.8 1.5 %collective-permute-start.3 = (bf16[32,2048]{1,0:T(8,128)(2,1)S(1)}, bf16[32,2048]{1,0:T(8,128)(2,1)S(1)}, u32[]{:S(2)}, u32[]{:S(2)}) collective-permute-start(bf16[32,2048]{1,0:T(8,128)(2,1)S(1)} %get-tuple-element.40), channel_id=1, source_target_pairs={{0,7},{1,6},{2,5},{3,4},{4,3},{5,2},{6,1},{7,0},{8,15},{9,14},{10,... | collective-permute-start | bytes 393224 | tf_op jit(solution)/shard_map/ppermute | solution.py:367
  7.3 1.7 %collective-permute-start.4 = (bf16[32,2048]{1,0:T(8,128)(2,1)S(1)}, bf16[32,2048]{1,0:T(8,128)(2,1)S(1)}, u32[]{:S(2)}, u32[]{:S(2)}) collective-permute-start(bf16[32,2048]{1,0:T(8,128)(2,1)S(1)} %get-tuple-element.41), channel_id=1, source_target_pairs={{0,3},{1,2},{2,1},{3,0},{4,7},{5,6},{6,5},{7,4},{8,11},{9,10},{10,... | collective-permute-start | bytes 393224 | tf_op jit(solution)/shard_map/ppermute | solution.py:367
  9.0 6.2 %collective-permute-done.1.refs_2_ = bf16[32,2048]{1,0:T(8,128)(2,1)S(1)} collective-permute-done((bf16[32,2048]{1,0:T(8,128)(2,1)S(1)}, bf16[32,2048]{1,0:T(8,128)(2,1)S(1)}, u32[]{:S(2)}, u32[]{:S(2)}) %collective-permute-start.1) | collective-permute-done | bytes 131104 | tf_op jit(solution)/shard_map/ppermute | solution.py:367
  15.3 0.6 collective-permute-done.4.refs_5_
  15.8 1.7 %collective-permute-done.5.refs_6_ = bf16[32,2048]{1,0:T(8,128)(2,1)S(1)} collective-permute-done((bf16[32,2048]{1,0:T(8,128)(2,1)S(1)}, bf16[32,2048]{1,0:T(8,128)(2,1)S(1)}, u32[]{:S(2)}, u32[]{:S(2)}) %collective-permute-start.5) | collective-permute-done | bytes 131104 | tf_op jit(solution)/shard_map/ppermute | solution.py:367
  17.6 0.5 gram_kernel.1
  18.1 0.2 collective-permute-start.7
  18.3 1.2 collective-permute-done.7
  19.5 1.5 %collective-permute-start.10 = (bf16[3,64,128]{2,1,0:T(8,128)(2,1)S(1)}, bf16[3,64,128]{2,1,0:T(8,128)(2,1)S(1)}, u32[]{:S(2)}, u32[]{:S(2)}) collective-permute-start(bf16[3,64,128]{2,1,0:T(8,128)(2,1)S(1)} %add_convert_fusion.2), channel_id=1, source_target_pairs={{0,6},{1,7},{2,4},{3,5},{4,2},{5,3},{6,0},{7,1},{8,14},{9,15},{10,... | collective-permute-start | bytes 147464 | tf_op jit(solution)/shard_map/ppermute | solution.py:367
  21.0 1.4 %collective-permute-start.9 = (bf16[3,64,128]{2,1,0:T(8,128)(2,1)S(1)}, bf16[3,64,128]{2,1,0:T(8,128)(2,1)S(1)}, u32[]{:S(2)}, u32[]{:S(2)}) collective-permute-start(bf16[3,64,128]{2,1,0:T(8,128)(2,1)S(1)} %add_convert_fusion.2), channel_id=1, source_target_pairs={{0,4},{1,5},{2,6},{3,7},{4,0},{5,1},{6,2},{7,3},{8,12},{9,13},{10,... | collective-permute-start | bytes 147464 | tf_op jit(solution)/shard_map/ppermute | solution.py:367
  22.4 0.7 collective-permute-start.8
  23.1 1.6 %collective-permute-done.10 = bf16[3,64,128]{2,1,0:T(8,128)(2,1)S(1)} collective-permute-done((bf16[3,64,128]{2,1,0:T(8,128)(2,1)S(1)}, bf16[3,64,128]{2,1,0:T(8,128)(2,1)S(1)}, u32[]{:S(2)}, u32[]{:S(2)}) %collective-permute-start.10) | collective-permute-done | bytes 49184 | tf_op jit(solution)/shard_map/ppermute | solution.py:367
  24.6 0.7 collective-permute-done.9
  25.4 1.1 collective-permute-done.8
  26.6 1.3 %collective-permute-done.11.other_ref = f32[3,64,128]{2,1,0:T(8,128)S(1)} collective-permute-done((f32[3,64,128]{2,1,0:T(8,128)S(1)}, f32[3,64,128]{2,1,0:T(8,128)S(1)}, u32[]{:S(2)}, u32[]{:S(2)}) %collective-permute-start.11) | collective-permute-done | bytes 98336 | tf_op jit(solution)/shard_map/ppermute | solution.py:367
  27.9 4.8 %node_kernel.1 = (bf16[128,512]{1,0:T(8,128)(2,1)S(1)}, bf16[128,512]{1,0:T(8,128)(2,1)S(1)}, bf16[128,512]{1,0:T(8,128)(2,1)S(1)}, bf16[128,512]{1,0:T(8,128)(2,1)S(1)}, bf16[256,128]{1,0:T(8,128)(2,1)S(1)}) custom-call(s32[1]{0:T(128)} %bitcast.pos_ref, f32[3,64,128]{2,1,0:T(8,128)S(1)} %add_add_fusion.mine_ref, ...), custom_call_target="tpu_custom_call" | custom-call | tf_op jit(solution)/shard_map/node_kernel/pallas_call | solution.py:350
  32.6 2.7 %collective-permute-start.12 = (bf16[128,512]{1,0:T(8,128)(2,1)S(1)}, bf16[128,512]{1,0:T(8,128)(2,1)S(1)}, u32[]{:S(2)}, u32[]{:S(2)}) collective-permute-start(bf16[128,512]{1,0:T(8,128)(2,1)S(1)} %get-tuple-element.48), channel_id=1, source_target_pairs={{0,16},{1,17},{2,18},{3,19},{4,20},{5,21},{6,22},{7,23},{8,24},{9,... | collective-permute-start | bytes 393224 | tf_op jit(solution)/shard_map/ppermute | solution.py:367
  35.3 1.4 %collective-permute-start.13 = (bf16[128,512]{1,0:T(8,128)(2,1)S(1)}, bf16[128,512]{1,0:T(8,128)(2,1)S(1)}, u32[]{:S(2)}, u32[]{:S(2)}) collective-permute-start(bf16[128,512]{1,0:T(8,128)(2,1)S(1)} %get-tuple-element.49), channel_id=1, source_target_pairs={{0,24},{1,25},{2,26},{3,27},{4,28},{5,29},{6,30},{7,31},{8,16},{9,... | collective-permute-start | bytes 393224 | tf_op jit(solution)/shard_map/ppermute | solution.py:367
  36.7 0.2 collective-permute-start.14
  36.9 8.7 %collective-permute-done.12.refs_1_ = bf16[128,512]{1,0:T(8,128)(2,1)S(1)} collective-permute-done((bf16[128,512]{1,0:T(8,128)(2,1)S(1)}, bf16[128,512]{1,0:T(8,128)(2,1)S(1)}, u32[]{:S(2)}, u32[]{:S(2)}) %collective-permute-start.12) | collective-permute-done | bytes 131104 | tf_op jit(solution)/shard_map/ppermute | solution.py:367
  45.6 0.5 collective-permute-done.14.refs_3_
  46.2 0.4 cross_kernel.1
  46.7 1.4 %collective-permute-done.15 = f32[6,64,128]{2,1,0:T(8,128)S(1)} collective-permute-done((f32[6,64,128]{2,1,0:T(8,128)S(1)}, f32[6,64,128]{2,1,0:T(8,128)S(1)}, u32[]{:S(2)}, u32[]{:S(2)}) %collective-permute-start.15) | collective-permute-done | bytes 196640 | tf_op jit(solution)/shard_map/ppermute | solution.py:367
  48.1 1.7 %collective-permute-start.18 = (bf16[6,64,128]{2,1,0:T(8,128)(2,1)S(1)}, bf16[6,64,128]{2,1,0:T(8,128)(2,1)S(1)}, u32[]{:S(2)}, u32[]{:S(2)}) collective-permute-start(bf16[6,64,128]{2,1,0:T(8,128)(2,1)S(1)} %add_convert_fusion.1), channel_id=1, source_target_pairs={{0,6},{1,7},{2,4},{3,5},{4,2},{5,3},{6,0},{7,1},{8,14},{9,15},{10,... | collective-permute-start | bytes 294920 | tf_op jit(solution)/shard_map/ppermute | solution.py:367
  49.8 0.5 collective-permute-start.17
  50.4 1.3 %collective-permute-start.16 = (bf16[6,64,128]{2,1,0:T(8,128)(2,1)S(1)}, bf16[6,64,128]{2,1,0:T(8,128)(2,1)S(1)}, u32[]{:S(2)}, u32[]{:S(2)}) collective-permute-start(bf16[6,64,128]{2,1,0:T(8,128)(2,1)S(1)} %add_convert_fusion.1), channel_id=1, source_target_pairs={{0,2},{1,3},{2,0},{3,1},{4,6},{5,7},{6,4},{7,5},{8,10},{9,11},{10,... | collective-permute-start | bytes 294920 | tf_op jit(solution)/shard_map/ppermute | solution.py:367
  51.7 0.4 diag_kernel.1
  52.1 2.3 %collective-permute-done.18 = bf16[6,64,128]{2,1,0:T(8,128)(2,1)S(1)} collective-permute-done((bf16[6,64,128]{2,1,0:T(8,128)(2,1)S(1)}, bf16[6,64,128]{2,1,0:T(8,128)(2,1)S(1)}, u32[]{:S(2)}, u32[]{:S(2)}) %collective-permute-start.18) | collective-permute-done | bytes 98336 | tf_op jit(solution)/shard_map/ppermute | solution.py:367
  54.5 1.6 %collective-permute-done.17 = bf16[6,64,128]{2,1,0:T(8,128)(2,1)S(1)} collective-permute-done((bf16[6,64,128]{2,1,0:T(8,128)(2,1)S(1)}, bf16[6,64,128]{2,1,0:T(8,128)(2,1)S(1)}, u32[]{:S(2)}, u32[]{:S(2)}) %collective-permute-start.17) | collective-permute-done | bytes 98336 | tf_op jit(solution)/shard_map/ppermute | solution.py:367
  56.1 4.1 %collective-permute-start.21 = (bf16[7,64,128]{2,1,0:T(8,128)(2,1)S(1)}, bf16[7,64,128]{2,1,0:T(8,128)(2,1)S(1)}, u32[]{:S(2)}, u32[]{:S(2)}) collective-permute-start(bf16[7,64,128]{2,1,0:T(8,128)(2,1)S(1)} %pad_maximum_fusion), channel_id=1, source_target_pairs={{0,16},{1,17},{2,18},{3,19},{4,20},{5,21},{6,22},{7,23},{8,24},{9,... | collective-permute-start | bytes 344072 | tf_op jit(solution)/shard_map/ppermute | solution.py:367
  60.2 0.5 collective-permute-start.20
  60.7 0.2 collective-permute-start.19
  60.9 7.9 %collective-permute-done.21 = bf16[7,64,128]{2,1,0:T(8,128)(2,1)S(1)} collective-permute-done((bf16[7,64,128]{2,1,0:T(8,128)(2,1)S(1)}, bf16[7,64,128]{2,1,0:T(8,128)(2,1)S(1)}, u32[]{:S(2)}, u32[]{:S(2)}) %collective-permute-start.21) | collective-permute-done | bytes 114720 | tf_op jit(solution)/shard_map/ppermute | solution.py:367
  68.8 1.0 collective-permute-done.19
  70.0 1.6 %collective-permute-done.22.other_ref = f32[10,64,128]{2,1,0:T(8,128)S(1)} collective-permute-done((f32[10,64,128]{2,1,0:T(8,128)S(1)}, f32[10,64,128]{2,1,0:T(8,128)S(1)}, u32[]{:S(2)}, u32[]{:S(2)}) %collective-permute-start.22) | collective-permute-done | bytes 327712 | tf_op jit(solution)/shard_map/ppermute | solution.py:367
  71.7 12.0 %top_kernel.1 = (bf16[128,512]{1,0:T(8,128)(2,1)S(1)}, f32[256,256]{1,0:T(8,128)S(1)}, bf16[256,128]{1,0:T(8,128)(2,1)S(1)}) custom-call(s32[1]{0:T(128)} %bitcast.pos_ref, f32[10,64,128]{2,1,0:T(8,128)S(1)} %convert_dynamic-update-slice_fusion.mine_ref, f32[10,64,128]{2,1,0:T(8,128)S(1)} %collective-permute-done.22.other_ref, ...), custom_call_target="tpu_custom_call" | custom-call | tf_op jit(solution)/shard_map/top_kernel/pallas_call | solution.py:350
  83.6 2.3 %collective-permute-start.25 = (bf16[128,512]{1,0:T(8,128)(2,1)S(1)}, bf16[128,512]{1,0:T(8,128)(2,1)S(1)}, u32[]{:S(2)}, u32[]{:S(2)}) collective-permute-start(bf16[128,512]{1,0:T(8,128)(2,1)S(1)} %get-tuple-element.56.refs_0_), channel_id=1, source_target_pairs={{0,16},{1,17},{2,18},{3,19},{4,20},{5,21},{6,22},{7,23},{8,24},{9,... | collective-permute-start | bytes 393224 | tf_op jit(solution)/shard_map/ppermute | solution.py:367
  85.9 1.8 %collective-permute-start.24 = (bf16[128,512]{1,0:T(8,128)(2,1)S(1)}, bf16[128,512]{1,0:T(8,128)(2,1)S(1)}, u32[]{:S(2)}, u32[]{:S(2)}) collective-permute-start(bf16[128,512]{1,0:T(8,128)(2,1)S(1)} %get-tuple-element.56.refs_0_), channel_id=1, source_target_pairs={{0,24},{1,25},{2,26},{3,27},{4,28},{5,29},{6,30},{7,31},{8,16},{9,... | collective-permute-start | bytes 393224 | tf_op jit(solution)/shard_map/ppermute | solution.py:367
  87.8 3.4 %factor_kernel.1.factor_ref = f32[128,128]{1,0:T(8,128)S(1)} custom-call(f32[256,256]{1,0:T(8,128)S(1)} %get-tuple-element.54.gram_ref, bf16[256,128]{1,0:T(8,128)(2,1)S(1)} %get-tuple-element.55.low_ref), custom_call_target="tpu_custom_call" | custom-call | tf_op jit(solution)/shard_map/factor_kernel/pallas_call | solution.py:350
  91.2 5.4 %collective-permute-done.25.refs_3_ = bf16[128,512]{1,0:T(8,128)(2,1)S(1)} collective-permute-done((bf16[128,512]{1,0:T(8,128)(2,1)S(1)}, bf16[128,512]{1,0:T(8,128)(2,1)S(1)}, u32[]{:S(2)}, u32[]{:S(2)}) %collective-permute-start.25) | collective-permute-done | bytes 131104 | tf_op jit(solution)/shard_map/ppermute | solution.py:367
  96.6 0.5 collective-permute-done.23.refs_1_
  97.1 0.8 coeffs_kernel.1
  98.0 1.2 %collective-permute-done.26 = f32[1,128,128]{2,1,0:T(8,128)S(1)} collective-permute-done((f32[1,128,128]{2,1,0:T(8,128)S(1)}, f32[1,128,128]{2,1,0:T(8,128)S(1)}, u32[]{:S(2)}, u32[]{:S(2)}) %collective-permute-start.26) | collective-permute-done | bytes 65568 | tf_op jit(solution)/shard_map/ppermute | solution.py:367
  99.3 1.5 %collective-permute-start.29 = (bf16[1,128,128]{2,1,0:T(8,128)(2,1)S(1)}, bf16[1,128,128]{2,1,0:T(8,128)(2,1)S(1)}, u32[]{:S(2)}, u32[]{:S(2)}) collective-permute-start(bf16[1,128,128]{2,1,0:T(8,128)(2,1)S(1)} %add_convert_fusion.3), channel_id=1, source_target_pairs={{0,6},{1,7},{2,4},{3,5},{4,2},{5,3},{6,0},{7,1},{8,14},{9,15},{10,... | collective-permute-start | bytes 98312 | tf_op jit(solution)/shard_map/ppermute | solution.py:367
  100.8 0.7 collective-permute-start.28
  101.5 1.3 %collective-permute-start.27 = (bf16[1,128,128]{2,1,0:T(8,128)(2,1)S(1)}, bf16[1,128,128]{2,1,0:T(8,128)(2,1)S(1)}, u32[]{:S(2)}, u32[]{:S(2)}) collective-permute-start(bf16[1,128,128]{2,1,0:T(8,128)(2,1)S(1)} %add_convert_fusion.3), channel_id=1, source_target_pairs={{0,2},{1,3},{2,0},{3,1},{4,6},{5,7},{6,4},{7,5},{8,10},{9,11},{10,... | collective-permute-start | bytes 98312 | tf_op jit(solution)/shard_map/ppermute | solution.py:367
  102.8 1.3 %collective-permute-done.29 = bf16[1,128,128]{2,1,0:T(8,128)(2,1)S(1)} collective-permute-done((bf16[1,128,128]{2,1,0:T(8,128)(2,1)S(1)}, bf16[1,128,128]{2,1,0:T(8,128)(2,1)S(1)}, u32[]{:S(2)}, u32[]{:S(2)}) %collective-permute-start.29) | collective-permute-done | bytes 32800 | tf_op jit(solution)/shard_map/ppermute | solution.py:367
  104.2 0.6 collective-permute-done.28
  104.7 0.7 collective-permute-done.27
  105.5 1.2 %collective-permute-done.30.other_ref = f32[1,128,128]{2,1,0:T(8,128)S(1)} collective-permute-done((f32[1,128,128]{2,1,0:T(8,128)S(1)}, f32[1,128,128]{2,1,0:T(8,128)S(1)}, u32[]{:S(2)}, u32[]{:S(2)}) %collective-permute-start.30) | collective-permute-done | bytes 65568 | tf_op jit(solution)/shard_map/ppermute | solution.py:367
  106.8 0.8 project_kernel.1
  107.6 1.4 %collective-permute-start.31 = (bf16[32,2048]{1,0:T(8,128)(2,1)S(1)}, bf16[32,2048]{1,0:T(8,128)(2,1)S(1)}, u32[]{:S(2)}, u32[]{:S(2)}) collective-permute-start(bf16[32,2048]{1,0:T(8,128)(2,1)S(1)} %get-tuple-element.60), channel_id=1, source_target_pairs={{0,2},{1,3},{2,0},{3,1},{4,6},{5,7},{6,4},{7,5},{8,10},{9,11},{10,... | collective-permute-start | bytes 393224 | tf_op jit(solution)/shard_map/ppermute | solution.py:367
  108.9 0.7 collective-permute-start.32
  109.6 1.5 %collective-permute-start.33 = (bf16[32,2048]{1,0:T(8,128)(2,1)S(1)}, bf16[32,2048]{1,0:T(8,128)(2,1)S(1)}, u32[]{:S(2)}, u32[]{:S(2)}) collective-permute-start(bf16[32,2048]{1,0:T(8,128)(2,1)S(1)} %get-tuple-element.62), channel_id=1, source_target_pairs={{0,6},{1,7},{2,4},{3,5},{4,2},{5,3},{6,0},{7,1},{8,14},{9,15},{10,... | collective-permute-start | bytes 393224 | tf_op jit(solution)/shard_map/ppermute | solution.py:367
  111.1 0.3 collective-permute-start.34
  111.5 2.1 %collective-permute-start.35 = (bf16[32,2048]{1,0:T(8,128)(2,1)S(1)}, bf16[32,2048]{1,0:T(8,128)(2,1)S(1)}, u32[]{:S(2)}, u32[]{:S(2)}) collective-permute-start(bf16[32,2048]{1,0:T(8,128)(2,1)S(1)} %get-tuple-element.64), channel_id=1, source_target_pairs={{0,3},{1,2},{2,1},{3,0},{4,7},{5,6},{6,5},{7,4},{8,11},{9,10},{10,... | collective-permute-start | bytes 393224 | tf_op jit(solution)/shard_map/ppermute | solution.py:367
  113.6 0.1 collective-permute-done.31.refs_1_
  113.7 5.8 %collective-permute-done.32.refs_2_ = bf16[32,2048]{1,0:T(8,128)(2,1)S(1)} collective-permute-done((bf16[32,2048]{1,0:T(8,128)(2,1)S(1)}, bf16[32,2048]{1,0:T(8,128)(2,1)S(1)}, u32[]{:S(2)}, u32[]{:S(2)}) %collective-permute-start.32) | collective-permute-done | bytes 131104 | tf_op jit(solution)/shard_map/ppermute | solution.py:367
  119.5 1.3 %collective-permute-done.35.refs_5_ = bf16[32,2048]{1,0:T(8,128)(2,1)S(1)} collective-permute-done((bf16[32,2048]{1,0:T(8,128)(2,1)S(1)}, bf16[32,2048]{1,0:T(8,128)(2,1)S(1)}, u32[]{:S(2)}, u32[]{:S(2)}) %collective-permute-start.35) | collective-permute-done | bytes 131104 | tf_op jit(solution)/shard_map/ppermute | solution.py:367
  120.8 1.7 %collective-permute-done.36.refs_6_ = bf16[32,2048]{1,0:T(8,128)(2,1)S(1)} collective-permute-done((bf16[32,2048]{1,0:T(8,128)(2,1)S(1)}, bf16[32,2048]{1,0:T(8,128)(2,1)S(1)}, u32[]{:S(2)}, u32[]{:S(2)}) %collective-permute-start.36) | collective-permute-done | bytes 131104 | tf_op jit(solution)/shard_map/ppermute | solution.py:367
  122.5 1.0 whole_kernel.1
  (36 shorter events, 0.8 us)
Async XLA Ops:
  0.0 1.2 copy-start
  1.3 7.7 %collective-permute-start = (bf16[32,2048]{1,0:T(8,128)(2,1)S(1)}, bf16[32,2048]{1,0:T(8,128)(2,1)S(1)}, u32[]{:S(2)}, u32[]{:S(2)}) collective-permute-start(bf16[32,2048]{1,0:T(8,128)(2,1)S(1)} %get-tuple-element.37), channel_id=1, source_target_pairs={{0,2},{1,3},{2,0},{3,1},{4,6},{5,7},{6,4},{7,5},{8,10},{9,11},{10,... | collective-permute-start | bytes 393224 | tf_op jit(solution)/shard_map/ppermute | solution.py:367
  4.3 11.0 %collective-permute-start.1 = (bf16[32,2048]{1,0:T(8,128)(2,1)S(1)}, bf16[32,2048]{1,0:T(8,128)(2,1)S(1)}, u32[]{:S(2)}, u32[]{:S(2)}) collective-permute-start(bf16[32,2048]{1,0:T(8,128)(2,1)S(1)} %get-tuple-element.38), channel_id=1, source_target_pairs={{0,4},{1,5},{2,6},{3,7},{4,0},{5,1},{6,2},{7,3},{8,12},{9,13},{10,... | collective-permute-start | bytes 393224 | tf_op jit(solution)/shard_map/ppermute | solution.py:367
  5.8 9.4 %collective-permute-start.2 = (bf16[32,2048]{1,0:T(8,128)(2,1)S(1)}, bf16[32,2048]{1,0:T(8,128)(2,1)S(1)}, u32[]{:S(2)}, u32[]{:S(2)}) collective-permute-start(bf16[32,2048]{1,0:T(8,128)(2,1)S(1)} %get-tuple-element.39), channel_id=1, source_target_pairs={{0,6},{1,7},{2,4},{3,5},{4,2},{5,3},{6,0},{7,1},{8,14},{9,15},{10,... | collective-permute-start | bytes 393224 | tf_op jit(solution)/shard_map/ppermute | solution.py:367
  5.8 9.4 %collective-permute-start.3 = (bf16[32,2048]{1,0:T(8,128)(2,1)S(1)}, bf16[32,2048]{1,0:T(8,128)(2,1)S(1)}, u32[]{:S(2)}, u32[]{:S(2)}) collective-permute-start(bf16[32,2048]{1,0:T(8,128)(2,1)S(1)} %get-tuple-element.40), channel_id=1, source_target_pairs={{0,7},{1,6},{2,5},{3,4},{4,3},{5,2},{6,1},{7,0},{8,15},{9,14},{10,... | collective-permute-start | bytes 393224 | tf_op jit(solution)/shard_map/ppermute | solution.py:367
  7.3 8.5 %collective-permute-start.4 = (bf16[32,2048]{1,0:T(8,128)(2,1)S(1)}, bf16[32,2048]{1,0:T(8,128)(2,1)S(1)}, u32[]{:S(2)}, u32[]{:S(2)}) collective-permute-start(bf16[32,2048]{1,0:T(8,128)(2,1)S(1)} %get-tuple-element.41), channel_id=1, source_target_pairs={{0,3},{1,2},{2,1},{3,0},{4,7},{5,6},{6,5},{7,4},{8,11},{9,10},{10,... | collective-permute-start | bytes 393224 | tf_op jit(solution)/shard_map/ppermute | solution.py:367
  9.0 8.6 %collective-permute-start.5 = (bf16[32,2048]{1,0:T(8,128)(2,1)S(1)}, bf16[32,2048]{1,0:T(8,128)(2,1)S(1)}, u32[]{:S(2)}, u32[]{:S(2)}) collective-permute-start(bf16[32,2048]{1,0:T(8,128)(2,1)S(1)} %get-tuple-element.42), channel_id=1, source_target_pairs={{0,5},{1,4},{2,7},{3,6},{4,1},{5,0},{6,3},{7,2},{8,13},{9,12},{10,... | collective-permute-start | bytes 393224 | tf_op jit(solution)/shard_map/ppermute | solution.py:367
  15.3 2.3 %collective-permute-start.6 = (bf16[32,2048]{1,0:T(8,128)(2,1)S(1)}, bf16[32,2048]{1,0:T(8,128)(2,1)S(1)}, u32[]{:S(2)}, u32[]{:S(2)}) collective-permute-start(bf16[32,2048]{1,0:T(8,128)(2,1)S(1)} %get-tuple-element.43), channel_id=1, source_target_pairs={{0,1},{1,0},{2,3},{3,2},{4,5},{5,4},{6,7},{7,6},{8,9},{9,8},{10,11... | collective-permute-start | bytes 393224 | tf_op jit(solution)/shard_map/ppermute | solution.py:367
  18.1 1.4 %collective-permute-start.7 = (f32[3,64,128]{2,1,0:T(8,128)S(1)}, f32[3,64,128]{2,1,0:T(8,128)S(1)}, u32[]{:S(2)}, u32[]{:S(2)}) collective-permute-start(f32[3,64,128]{2,1,0:T(8,128)S(1)} %get-tuple-element.46), channel_id=1, source_target_pairs={{0,1},{1,0},{2,3},{3,2},{4,5},{5,4},{6,7},{7,6},{8,9},{9,8},{10,11... | collective-permute-start | bytes 294920 | tf_op jit(solution)/shard_map/ppermute | solution.py:367
  19.5 5.1 %collective-permute-start.10 = (bf16[3,64,128]{2,1,0:T(8,128)(2,1)S(1)}, bf16[3,64,128]{2,1,0:T(8,128)(2,1)S(1)}, u32[]{:S(2)}, u32[]{:S(2)}) collective-permute-start(bf16[3,64,128]{2,1,0:T(8,128)(2,1)S(1)} %add_convert_fusion.2), channel_id=1, source_target_pairs={{0,6},{1,7},{2,4},{3,5},{4,2},{5,3},{6,0},{7,1},{8,14},{9,15},{10,... | collective-permute-start | bytes 147464 | tf_op jit(solution)/shard_map/ppermute | solution.py:367
  21.0 4.3 %collective-permute-start.9 = (bf16[3,64,128]{2,1,0:T(8,128)(2,1)S(1)}, bf16[3,64,128]{2,1,0:T(8,128)(2,1)S(1)}, u32[]{:S(2)}, u32[]{:S(2)}) collective-permute-start(bf16[3,64,128]{2,1,0:T(8,128)(2,1)S(1)} %add_convert_fusion.2), channel_id=1, source_target_pairs={{0,4},{1,5},{2,6},{3,7},{4,0},{5,1},{6,2},{7,3},{8,12},{9,13},{10,... | collective-permute-start | bytes 147464 | tf_op jit(solution)/shard_map/ppermute | solution.py:367
  22.4 4.1 %collective-permute-start.8 = (bf16[3,64,128]{2,1,0:T(8,128)(2,1)S(1)}, bf16[3,64,128]{2,1,0:T(8,128)(2,1)S(1)}, u32[]{:S(2)}, u32[]{:S(2)}) collective-permute-start(bf16[3,64,128]{2,1,0:T(8,128)(2,1)S(1)} %add_convert_fusion.2), channel_id=1, source_target_pairs={{0,2},{1,3},{2,0},{3,1},{4,6},{5,7},{6,4},{7,5},{8,10},{9,11},{10,... | collective-permute-start | bytes 147464 | tf_op jit(solution)/shard_map/ppermute | solution.py:367
  26.5 1.4 %collective-permute-start.11 = (f32[3,64,128]{2,1,0:T(8,128)S(1)}, f32[3,64,128]{2,1,0:T(8,128)S(1)}, u32[]{:S(2)}, u32[]{:S(2)}) collective-permute-start(f32[3,64,128]{2,1,0:T(8,128)S(1)} %add_add_fusion.mine_ref), channel_id=1, source_target_pairs={{0,1},{1,0},{2,3},{3,2},{4,5},{5,4},{6,7},{7,6},{8,9},{9,8},{10,11... | collective-permute-start | bytes 294920 | tf_op jit(solution)/shard_map/ppermute | solution.py:367
  32.6 13.0 %collective-permute-start.12 = (bf16[128,512]{1,0:T(8,128)(2,1)S(1)}, bf16[128,512]{1,0:T(8,128)(2,1)S(1)}, u32[]{:S(2)}, u32[]{:S(2)}) collective-permute-start(bf16[128,512]{1,0:T(8,128)(2,1)S(1)} %get-tuple-element.48), channel_id=1, source_target_pairs={{0,16},{1,17},{2,18},{3,19},{4,20},{5,21},{6,22},{7,23},{8,24},{9,... | collective-permute-start | bytes 393224 | tf_op jit(solution)/shard_map/ppermute | solution.py:367
  35.3 10.3 %collective-permute-start.13 = (bf16[128,512]{1,0:T(8,128)(2,1)S(1)}, bf16[128,512]{1,0:T(8,128)(2,1)S(1)}, u32[]{:S(2)}, u32[]{:S(2)}) collective-permute-start(bf16[128,512]{1,0:T(8,128)(2,1)S(1)} %get-tuple-element.49), channel_id=1, source_target_pairs={{0,24},{1,25},{2,26},{3,27},{4,28},{5,29},{6,30},{7,31},{8,16},{9,... | collective-permute-start | bytes 393224 | tf_op jit(solution)/shard_map/ppermute | solution.py:367
  36.7 9.5 %collective-permute-start.14 = (bf16[128,512]{1,0:T(8,128)(2,1)S(1)}, bf16[128,512]{1,0:T(8,128)(2,1)S(1)}, u32[]{:S(2)}, u32[]{:S(2)}) collective-permute-start(bf16[128,512]{1,0:T(8,128)(2,1)S(1)} %get-tuple-element.50), channel_id=1, source_target_pairs={{0,8},{1,9},{2,10},{3,11},{4,12},{5,13},{6,14},{7,15},{8,0},{9,1},... | collective-permute-start | bytes 393224 | tf_op jit(solution)/shard_map/ppermute | solution.py:367
  46.6 1.5 %collective-permute-start.15 = (f32[6,64,128]{2,1,0:T(8,128)S(1)}, f32[6,64,128]{2,1,0:T(8,128)S(1)}, u32[]{:S(2)}, u32[]{:S(2)}) collective-permute-start(f32[6,64,128]{2,1,0:T(8,128)S(1)} %get-tuple-element.52), channel_id=1, source_target_pairs={{0,1},{1,0},{2,3},{3,2},{4,5},{5,4},{6,7},{7,6},{8,9},{9,8},{10,11... | collective-permute-start | bytes 589832 | tf_op jit(solution)/shard_map/ppermute | solution.py:367
  48.1 6.3 %collective-permute-start.18 = (bf16[6,64,128]{2,1,0:T(8,128)(2,1)S(1)}, bf16[6,64,128]{2,1,0:T(8,128)(2,1)S(1)}, u32[]{:S(2)}, u32[]{:S(2)}) collective-permute-start(bf16[6,64,128]{2,1,0:T(8,128)(2,1)S(1)} %add_convert_fusion.1), channel_id=1, source_target_pairs={{0,6},{1,7},{2,4},{3,5},{4,2},{5,3},{6,0},{7,1},{8,14},{9,15},{10,... | collective-permute-start | bytes 294920 | tf_op jit(solution)/shard_map/ppermute | solution.py:367
  49.8 6.2 %collective-permute-start.17 = (bf16[6,64,128]{2,1,0:T(8,128)(2,1)S(1)}, bf16[6,64,128]{2,1,0:T(8,128)(2,1)S(1)}, u32[]{:S(2)}, u32[]{:S(2)}) collective-permute-start(bf16[6,64,128]{2,1,0:T(8,128)(2,1)S(1)} %add_convert_fusion.1), channel_id=1, source_target_pairs={{0,4},{1,5},{2,6},{3,7},{4,0},{5,1},{6,2},{7,3},{8,12},{9,13},{10,... | collective-permute-start | bytes 294920 | tf_op jit(solution)/shard_map/ppermute | solution.py:367
  50.4 5.7 %collective-permute-start.16 = (bf16[6,64,128]{2,1,0:T(8,128)(2,1)S(1)}, bf16[6,64,128]{2,1,0:T(8,128)(2,1)S(1)}, u32[]{:S(2)}, u32[]{:S(2)}) collective-permute-start(bf16[6,64,128]{2,1,0:T(8,128)(2,1)S(1)} %add_convert_fusion.1), channel_id=1, source_target_pairs={{0,2},{1,3},{2,0},{3,1},{4,6},{5,7},{6,4},{7,5},{8,10},{9,11},{10,... | collective-permute-start | bytes 294920 | tf_op jit(solution)/shard_map/ppermute | solution.py:367
  56.1 12.7 %collective-permute-start.21 = (bf16[7,64,128]{2,1,0:T(8,128)(2,1)S(1)}, bf16[7,64,128]{2,1,0:T(8,128)(2,1)S(1)}, u32[]{:S(2)}, u32[]{:S(2)}) collective-permute-start(bf16[7,64,128]{2,1,0:T(8,128)(2,1)S(1)} %pad_maximum_fusion), channel_id=1, source_target_pairs={{0,16},{1,17},{2,18},{3,19},{4,20},{5,21},{6,22},{7,23},{8,24},{9,... | collective-permute-start | bytes 344072 | tf_op jit(solution)/shard_map/ppermute | solution.py:367
  60.2 8.6 %collective-permute-start.20 = (bf16[7,64,128]{2,1,0:T(8,128)(2,1)S(1)}, bf16[7,64,128]{2,1,0:T(8,128)(2,1)S(1)}, u32[]{:S(2)}, u32[]{:S(2)}) collective-permute-start(bf16[7,64,128]{2,1,0:T(8,128)(2,1)S(1)} %pad_maximum_fusion), channel_id=1, source_target_pairs={{0,24},{1,25},{2,26},{3,27},{4,28},{5,29},{6,30},{7,31},{8,16},{9,... | collective-permute-start | bytes 344072 | tf_op jit(solution)/shard_map/ppermute | solution.py:367
  60.7 9.1 %collective-permute-start.19 = (bf16[7,64,128]{2,1,0:T(8,128)(2,1)S(1)}, bf16[7,64,128]{2,1,0:T(8,128)(2,1)S(1)}, u32[]{:S(2)}, u32[]{:S(2)}) collective-permute-start(bf16[7,64,128]{2,1,0:T(8,128)(2,1)S(1)} %pad_maximum_fusion), channel_id=1, source_target_pairs={{0,8},{1,9},{2,10},{3,11},{4,12},{5,13},{6,14},{7,15},{8,0},{9,1},... | collective-permute-start | bytes 344072 | tf_op jit(solution)/shard_map/ppermute | solution.py:367
  70.0 1.7 %collective-permute-start.22 = (f32[10,64,128]{2,1,0:T(8,128)S(1)}, f32[10,64,128]{2,1,0:T(8,128)S(1)}, u32[]{:S(2)}, u32[]{:S(2)}) collective-permute-start(f32[10,64,128]{2,1,0:T(8,128)S(1)} %convert_dynamic-update-slice_fusion.mine_ref), channel_id=1, source_target_pairs={{0,1},{1,0},{2,3},{3,2},{4,5},{5,4},{6,7},{7,6},{8,9},{9,8},{10,11... | collective-permute-start | bytes 983048 | tf_op jit(solution)/shard_map/ppermute | solution.py:367
  83.6 13.0 %collective-permute-start.25 = (bf16[128,512]{1,0:T(8,128)(2,1)S(1)}, bf16[128,512]{1,0:T(8,128)(2,1)S(1)}, u32[]{:S(2)}, u32[]{:S(2)}) collective-permute-start(bf16[128,512]{1,0:T(8,128)(2,1)S(1)} %get-tuple-element.56.refs_0_), channel_id=1, source_target_pairs={{0,16},{1,17},{2,18},{3,19},{4,20},{5,21},{6,22},{7,23},{8,24},{9,... | collective-permute-start | bytes 393224 | tf_op jit(solution)/shard_map/ppermute | solution.py:367
  85.9 10.7 %collective-permute-start.24 = (bf16[128,512]{1,0:T(8,128)(2,1)S(1)}, bf16[128,512]{1,0:T(8,128)(2,1)S(1)}, u32[]{:S(2)}, u32[]{:S(2)}) collective-permute-start(bf16[128,512]{1,0:T(8,128)(2,1)S(1)} %get-tuple-element.56.refs_0_), channel_id=1, source_target_pairs={{0,24},{1,25},{2,26},{3,27},{4,28},{5,29},{6,30},{7,31},{8,16},{9,... | collective-permute-start | bytes 393224 | tf_op jit(solution)/shard_map/ppermute | solution.py:367
  87.8 9.3 %collective-permute-start.23 = (bf16[128,512]{1,0:T(8,128)(2,1)S(1)}, bf16[128,512]{1,0:T(8,128)(2,1)S(1)}, u32[]{:S(2)}, u32[]{:S(2)}) collective-permute-start(bf16[128,512]{1,0:T(8,128)(2,1)S(1)} %get-tuple-element.56.refs_0_), channel_id=1, source_target_pairs={{0,8},{1,9},{2,10},{3,11},{4,12},{5,13},{6,14},{7,15},{8,0},{9,1},... | collective-permute-start | bytes 393224 | tf_op jit(solution)/shard_map/ppermute | solution.py:367
  97.9 1.3 %collective-permute-start.26 = (f32[1,128,128]{2,1,0:T(8,128)S(1)}, f32[1,128,128]{2,1,0:T(8,128)S(1)}, u32[]{:S(2)}, u32[]{:S(2)}) collective-permute-start(f32[1,128,128]{2,1,0:T(8,128)S(1)} %get-tuple-element.58), channel_id=1, source_target_pairs={{0,1},{1,0},{2,3},{3,2},{4,5},{5,4},{6,7},{7,6},{8,9},{9,8},{10,11... | collective-permute-start | bytes 196616 | tf_op jit(solution)/shard_map/ppermute | solution.py:367
  99.3 4.9 %collective-permute-start.29 = (bf16[1,128,128]{2,1,0:T(8,128)(2,1)S(1)}, bf16[1,128,128]{2,1,0:T(8,128)(2,1)S(1)}, u32[]{:S(2)}, u32[]{:S(2)}) collective-permute-start(bf16[1,128,128]{2,1,0:T(8,128)(2,1)S(1)} %add_convert_fusion.3), channel_id=1, source_target_pairs={{0,6},{1,7},{2,4},{3,5},{4,2},{5,3},{6,0},{7,1},{8,14},{9,15},{10,... | collective-permute-start | bytes 98312 | tf_op jit(solution)/shard_map/ppermute | solution.py:367
  100.8 3.9 %collective-permute-start.28 = (bf16[1,128,128]{2,1,0:T(8,128)(2,1)S(1)}, bf16[1,128,128]{2,1,0:T(8,128)(2,1)S(1)}, u32[]{:S(2)}, u32[]{:S(2)}) collective-permute-start(bf16[1,128,128]{2,1,0:T(8,128)(2,1)S(1)} %add_convert_fusion.3), channel_id=1, source_target_pairs={{0,4},{1,5},{2,6},{3,7},{4,0},{5,1},{6,2},{7,3},{8,12},{9,13},{10,... | collective-permute-start | bytes 98312 | tf_op jit(solution)/shard_map/ppermute | solution.py:367
  101.5 3.9 %collective-permute-start.27 = (bf16[1,128,128]{2,1,0:T(8,128)(2,1)S(1)}, bf16[1,128,128]{2,1,0:T(8,128)(2,1)S(1)}, u32[]{:S(2)}, u32[]{:S(2)}) collective-permute-start(bf16[1,128,128]{2,1,0:T(8,128)(2,1)S(1)} %add_convert_fusion.3), channel_id=1, source_target_pairs={{0,2},{1,3},{2,0},{3,1},{4,6},{5,7},{6,4},{7,5},{8,10},{9,11},{10,... | collective-permute-start | bytes 98312 | tf_op jit(solution)/shard_map/ppermute | solution.py:367
  105.5 1.3 %collective-permute-start.30 = (f32[1,128,128]{2,1,0:T(8,128)S(1)}, f32[1,128,128]{2,1,0:T(8,128)S(1)}, u32[]{:S(2)}, u32[]{:S(2)}) collective-permute-start(f32[1,128,128]{2,1,0:T(8,128)S(1)} %add_add_fusion.1.mine_ref), channel_id=1, source_target_pairs={{0,1},{1,0},{2,3},{3,2},{4,5},{5,4},{6,7},{7,6},{8,9},{9,8},{10,11... | collective-permute-start | bytes 196616 | tf_op jit(solution)/shard_map/ppermute | solution.py:367
  107.6 6.2 %collective-permute-start.31 = (bf16[32,2048]{1,0:T(8,128)(2,1)S(1)}, bf16[32,2048]{1,0:T(8,128)(2,1)S(1)}, u32[]{:S(2)}, u32[]{:S(2)}) collective-permute-start(bf16[32,2048]{1,0:T(8,128)(2,1)S(1)} %get-tuple-element.60), channel_id=1, source_target_pairs={{0,2},{1,3},{2,0},{3,1},{4,6},{5,7},{6,4},{7,5},{8,10},{9,11},{10,... | collective-permute-start | bytes 393224 | tf_op jit(solution)/shard_map/ppermute | solution.py:367
  108.9 10.6 %collective-permute-start.32 = (bf16[32,2048]{1,0:T(8,128)(2,1)S(1)}, bf16[32,2048]{1,0:T(8,128)(2,1)S(1)}, u32[]{:S(2)}, u32[]{:S(2)}) collective-permute-start(bf16[32,2048]{1,0:T(8,128)(2,1)S(1)} %get-tuple-element.61), channel_id=1, source_target_pairs={{0,4},{1,5},{2,6},{3,7},{4,0},{5,1},{6,2},{7,3},{8,12},{9,13},{10,... | collective-permute-start | bytes 393224 | tf_op jit(solution)/shard_map/ppermute | solution.py:367
  109.6 9.9 %collective-permute-start.33 = (bf16[32,2048]{1,0:T(8,128)(2,1)S(1)}, bf16[32,2048]{1,0:T(8,128)(2,1)S(1)}, u32[]{:S(2)}, u32[]{:S(2)}) collective-permute-start(bf16[32,2048]{1,0:T(8,128)(2,1)S(1)} %get-tuple-element.62), channel_id=1, source_target_pairs={{0,6},{1,7},{2,4},{3,5},{4,2},{5,3},{6,0},{7,1},{8,14},{9,15},{10,... | collective-permute-start | bytes 393224 | tf_op jit(solution)/shard_map/ppermute | solution.py:367
  111.1 8.4 %collective-permute-start.34 = (bf16[32,2048]{1,0:T(8,128)(2,1)S(1)}, bf16[32,2048]{1,0:T(8,128)(2,1)S(1)}, u32[]{:S(2)}, u32[]{:S(2)}) collective-permute-start(bf16[32,2048]{1,0:T(8,128)(2,1)S(1)} %get-tuple-element.63), channel_id=1, source_target_pairs={{0,7},{1,6},{2,5},{3,4},{4,3},{5,2},{6,1},{7,0},{8,15},{9,14},{10,... | collective-permute-start | bytes 393224 | tf_op jit(solution)/shard_map/ppermute | solution.py:367
  111.5 9.4 %collective-permute-start.35 = (bf16[32,2048]{1,0:T(8,128)(2,1)S(1)}, bf16[32,2048]{1,0:T(8,128)(2,1)S(1)}, u32[]{:S(2)}, u32[]{:S(2)}) collective-permute-start(bf16[32,2048]{1,0:T(8,128)(2,1)S(1)} %get-tuple-element.64), channel_id=1, source_target_pairs={{0,3},{1,2},{2,1},{3,0},{4,7},{5,6},{6,5},{7,4},{8,11},{9,10},{10,... | collective-permute-start | bytes 393224 | tf_op jit(solution)/shard_map/ppermute | solution.py:367
  113.7 8.8 %collective-permute-start.36 = (bf16[32,2048]{1,0:T(8,128)(2,1)S(1)}, bf16[32,2048]{1,0:T(8,128)(2,1)S(1)}, u32[]{:S(2)}, u32[]{:S(2)}) collective-permute-start(bf16[32,2048]{1,0:T(8,128)(2,1)S(1)} %get-tuple-element.65), channel_id=1, source_target_pairs={{0,5},{1,4},{2,7},{3,6},{4,1},{5,0},{6,3},{7,2},{8,13},{9,12},{10,... | collective-permute-start | bytes 393224 | tf_op jit(solution)/shard_map/ppermute | solution.py:367
  119.5 3.0 %collective-permute-start.37 = (bf16[32,2048]{1,0:T(8,128)(2,1)S(1)}, bf16[32,2048]{1,0:T(8,128)(2,1)S(1)}, u32[]{:S(2)}, u32[]{:S(2)}) collective-permute-start(bf16[32,2048]{1,0:T(8,128)(2,1)S(1)} %get-tuple-element.66), channel_id=1, source_target_pairs={{0,1},{1,0},{2,3},{3,2},{4,5},{5,4},{6,7},{7,6},{8,9},{9,8},{10,11... | collective-permute-start | bytes 393224 | tf_op jit(solution)/shard_map/ppermute | solution.py:367

commit v9 on v6

--- a/solution.py
+++ b/solution.py
@@ -374,7 +374,7 @@
         return (parts[0] + parts[1]) + (parts[2] + parts[3])
 
     def plane_sum(mine, theirs):
-        return sum4(swap_all([(mine + swap(theirs, 1)).astype(bf16)] * 4, range(4), 2))
+        return sum4(swap_all([(mine + swap(theirs, 1)).astype(bf16)] * 4, (0, 3, 2, 1), 2))
 
     block, total = mortality.shape
     height, width = block * PLANE, total // PLANE

time: 123 us -> 123 us (level)
  no operation moved by 1% of the time
where the time goes in v9:
time: 123 us
  waiting for transfers between devices  59.2 us (48%)
  starting transfers between devices  38 us (31%)
  Pallas kernels  24.3 us (20%)
    ppermute x38, waiting for transfers between devices, swap(): return lax.ppermute(x, 'cols', [(i, i ^ apart) for i in range(count)])  59.2 us
    ppermute x38, starting transfers between devices, swap(): return lax.ppermute(x, 'cols', [(i, i ^ apart) for i in range(count)])  38 us
    pallas_call x10, Pallas kernels, kernel(): pl.pallas_call(fn, out_shape=[jax.ShapeDtypeStruct(s, d) for s, d in shap...  24.3 us
  transfers between devices with their start and end apart: 38, of which 31 were waited for; matrix products, arithmetic and copies ran while one was open for 0% of the time, Pallas kernels for 3%

profile of v9, /device:TPU:0, one launch (start us, length us, event | category | flops | bytes accessed | tf_op | source)
XLA Modules:
  0.0 123.2 jit_solution(11300019730726967809)
XLA Ops:
  0.0 1.2 copy-done
  1.3 4.0 %collective-permute-start = (bf16[32,2048]{1,0:T(8,128)(2,1)S(1)}, bf16[32,2048]{1,0:T(8,128)(2,1)S(1)}, u32[]{:S(2)}, u32[]{:S(2)}) collective-permute-start(bf16[32,2048]{1,0:T(8,128)(2,1)S(1)} %get-tuple-element.37), channel_id=1, source_target_pairs={{0,6},{1,7},{2,4},{3,5},{4,2},{5,3},{6,0},{7,1},{8,14},{9,15},{10,... | collective-permute-start | bytes 393224 | tf_op jit(solution)/shard_map/ppermute | solution.py:367
  5.3 1.1 collective-permute-start.2
  6.4 1.5 %collective-permute-start.3 = (bf16[32,2048]{1,0:T(8,128)(2,1)S(1)}, bf16[32,2048]{1,0:T(8,128)(2,1)S(1)}, u32[]{:S(2)}, u32[]{:S(2)}) collective-permute-start(bf16[32,2048]{1,0:T(8,128)(2,1)S(1)} %get-tuple-element.40), channel_id=1, source_target_pairs={{0,4},{1,5},{2,6},{3,7},{4,0},{5,1},{6,2},{7,3},{8,12},{9,13},{10,... | collective-permute-start | bytes 393224 | tf_op jit(solution)/shard_map/ppermute | solution.py:367
  7.9 0.6 collective-permute-start.4
  8.5 0.7 collective-permute-done.refs_1_
  9.2 2.8 %collective-permute-done.1.refs_2_ = bf16[32,2048]{1,0:T(8,128)(2,1)S(1)} collective-permute-done((bf16[32,2048]{1,0:T(8,128)(2,1)S(1)}, bf16[32,2048]{1,0:T(8,128)(2,1)S(1)}, u32[]{:S(2)}, u32[]{:S(2)}) %collective-permute-start.1) | collective-permute-done | bytes 131104 | tf_op jit(solution)/shard_map/ppermute | solution.py:367
  12.0 3.4 %collective-permute-done.2.refs_3_ = bf16[32,2048]{1,0:T(8,128)(2,1)S(1)} collective-permute-done((bf16[32,2048]{1,0:T(8,128)(2,1)S(1)}, bf16[32,2048]{1,0:T(8,128)(2,1)S(1)}, u32[]{:S(2)}, u32[]{:S(2)}) %collective-permute-start.2) | collective-permute-done | bytes 131104 | tf_op jit(solution)/shard_map/ppermute | solution.py:367
  15.5 1.1 collective-permute-done.4.refs_5_
  16.6 0.7 collective-permute-done.5.refs_6_
  17.3 0.5 gram_kernel.1
  18.0 1.2 collective-permute-done.7
  19.2 1.6 %collective-permute-start.10 = (bf16[3,64,128]{2,1,0:T(8,128)(2,1)S(1)}, bf16[3,64,128]{2,1,0:T(8,128)(2,1)S(1)}, u32[]{:S(2)}, u32[]{:S(2)}) collective-permute-start(bf16[3,64,128]{2,1,0:T(8,128)(2,1)S(1)} %add_convert_fusion.2), channel_id=1, source_target_pairs={{0,2},{1,3},{2,0},{3,1},{4,6},{5,7},{6,4},{7,5},{8,10},{9,11},{10,... | collective-permute-start | bytes 147464 | tf_op jit(solution)/shard_map/ppermute | solution.py:367
  20.8 1.6 %collective-permute-start.9 = (bf16[3,64,128]{2,1,0:T(8,128)(2,1)S(1)}, bf16[3,64,128]{2,1,0:T(8,128)(2,1)S(1)}, u32[]{:S(2)}, u32[]{:S(2)}) collective-permute-start(bf16[3,64,128]{2,1,0:T(8,128)(2,1)S(1)} %add_convert_fusion.2), channel_id=1, source_target_pairs={{0,4},{1,5},{2,6},{3,7},{4,0},{5,1},{6,2},{7,3},{8,12},{9,13},{10,... | collective-permute-start | bytes 147464 | tf_op jit(solution)/shard_map/ppermute | solution.py:367
  22.4 0.4 collective-permute-start.8
  22.8 0.6 collective-permute-done.10
  23.4 1.5 %collective-permute-done.9 = bf16[3,64,128]{2,1,0:T(8,128)(2,1)S(1)} collective-permute-done((bf16[3,64,128]{2,1,0:T(8,128)(2,1)S(1)}, bf16[3,64,128]{2,1,0:T(8,128)(2,1)S(1)}, u32[]{:S(2)}, u32[]{:S(2)}) %collective-permute-start.9) | collective-permute-done | bytes 49184 | tf_op jit(solution)/shard_map/ppermute | solution.py:367
  24.9 2.5 %collective-permute-done.8 = bf16[3,64,128]{2,1,0:T(8,128)(2,1)S(1)} collective-permute-done((bf16[3,64,128]{2,1,0:T(8,128)(2,1)S(1)}, bf16[3,64,128]{2,1,0:T(8,128)(2,1)S(1)}, u32[]{:S(2)}, u32[]{:S(2)}) %collective-permute-start.8) | collective-permute-done | bytes 49184 | tf_op jit(solution)/shard_map/ppermute | solution.py:367
  27.5 1.3 %collective-permute-done.11.other_ref = f32[3,64,128]{2,1,0:T(8,128)S(1)} collective-permute-done((f32[3,64,128]{2,1,0:T(8,128)S(1)}, f32[3,64,128]{2,1,0:T(8,128)S(1)}, u32[]{:S(2)}, u32[]{:S(2)}) %collective-permute-start.11) | collective-permute-done | bytes 98336 | tf_op jit(solution)/shard_map/ppermute | solution.py:367
  28.7 4.8 %node_kernel.1 = (bf16[128,512]{1,0:T(8,128)(2,1)S(1)}, bf16[128,512]{1,0:T(8,128)(2,1)S(1)}, bf16[128,512]{1,0:T(8,128)(2,1)S(1)}, bf16[128,512]{1,0:T(8,128)(2,1)S(1)}, bf16[256,128]{1,0:T(8,128)(2,1)S(1)}) custom-call(s32[1]{0:T(128)} %bitcast.pos_ref, f32[3,64,128]{2,1,0:T(8,128)S(1)} %add_add_fusion.mine_ref, ...), custom_call_target="tpu_custom_call" | custom-call | tf_op jit(solution)/shard_map/node_kernel/pallas_call | solution.py:350
  33.5 2.7 %collective-permute-start.12 = (bf16[128,512]{1,0:T(8,128)(2,1)S(1)}, bf16[128,512]{1,0:T(8,128)(2,1)S(1)}, u32[]{:S(2)}, u32[]{:S(2)}) collective-permute-start(bf16[128,512]{1,0:T(8,128)(2,1)S(1)} %get-tuple-element.48), channel_id=1, source_target_pairs={{0,16},{1,17},{2,18},{3,19},{4,20},{5,21},{6,22},{7,23},{8,24},{9,... | collective-permute-start | bytes 393224 | tf_op jit(solution)/shard_map/ppermute | solution.py:367
  36.2 1.3 %collective-permute-start.13 = (bf16[128,512]{1,0:T(8,128)(2,1)S(1)}, bf16[128,512]{1,0:T(8,128)(2,1)S(1)}, u32[]{:S(2)}, u32[]{:S(2)}) collective-permute-start(bf16[128,512]{1,0:T(8,128)(2,1)S(1)} %get-tuple-element.49), channel_id=1, source_target_pairs={{0,24},{1,25},{2,26},{3,27},{4,28},{5,29},{6,30},{7,31},{8,16},{9,... | collective-permute-start | bytes 393224 | tf_op jit(solution)/shard_map/ppermute | solution.py:367
  37.8 8.7 %collective-permute-done.12.refs_1_ = bf16[128,512]{1,0:T(8,128)(2,1)S(1)} collective-permute-done((bf16[128,512]{1,0:T(8,128)(2,1)S(1)}, bf16[128,512]{1,0:T(8,128)(2,1)S(1)}, u32[]{:S(2)}, u32[]{:S(2)}) %collective-permute-start.12) | collective-permute-done | bytes 131104 | tf_op jit(solution)/shard_map/ppermute | solution.py:367
  46.5 0.6 collective-permute-done.14.refs_3_
  47.1 0.4 cross_kernel.1
  47.5 1.4 %collective-permute-done.15 = f32[6,64,128]{2,1,0:T(8,128)S(1)} collective-permute-done((f32[6,64,128]{2,1,0:T(8,128)S(1)}, f32[6,64,128]{2,1,0:T(8,128)S(1)}, u32[]{:S(2)}, u32[]{:S(2)}) %collective-permute-start.15) | collective-permute-done | bytes 196640 | tf_op jit(solution)/shard_map/ppermute | solution.py:367
  49.0 0.6 collective-permute-start.18
  49.6 0.5 collective-permute-start.17
  50.1 2.5 %collective-permute-start.16 = (bf16[6,64,128]{2,1,0:T(8,128)(2,1)S(1)}, bf16[6,64,128]{2,1,0:T(8,128)(2,1)S(1)}, u32[]{:S(2)}, u32[]{:S(2)}) collective-permute-start(bf16[6,64,128]{2,1,0:T(8,128)(2,1)S(1)} %add_convert_fusion.1), channel_id=1, source_target_pairs={{0,6},{1,7},{2,4},{3,5},{4,2},{5,3},{6,0},{7,1},{8,14},{9,15},{10,... | collective-permute-start | bytes 294920 | tf_op jit(solution)/shard_map/ppermute | solution.py:367
  52.6 0.4 diag_kernel.1
  53.0 1.6 %collective-permute-done.18 = bf16[6,64,128]{2,1,0:T(8,128)(2,1)S(1)} collective-permute-done((bf16[6,64,128]{2,1,0:T(8,128)(2,1)S(1)}, bf16[6,64,128]{2,1,0:T(8,128)(2,1)S(1)}, u32[]{:S(2)}, u32[]{:S(2)}) %collective-permute-start.18) | collective-permute-done | bytes 98336 | tf_op jit(solution)/shard_map/ppermute | solution.py:367
  54.6 1.7 %collective-permute-done.17 = bf16[6,64,128]{2,1,0:T(8,128)(2,1)S(1)} collective-permute-done((bf16[6,64,128]{2,1,0:T(8,128)(2,1)S(1)}, bf16[6,64,128]{2,1,0:T(8,128)(2,1)S(1)}, u32[]{:S(2)}, u32[]{:S(2)}) %collective-permute-start.17) | collective-permute-done | bytes 98336 | tf_op jit(solution)/shard_map/ppermute | solution.py:367
  56.4 4.2 %collective-permute-start.21 = (bf16[7,64,128]{2,1,0:T(8,128)(2,1)S(1)}, bf16[7,64,128]{2,1,0:T(8,128)(2,1)S(1)}, u32[]{:S(2)}, u32[]{:S(2)}) collective-permute-start(bf16[7,64,128]{2,1,0:T(8,128)(2,1)S(1)} %pad_maximum_fusion), channel_id=1, source_target_pairs={{0,16},{1,17},{2,18},{3,19},{4,20},{5,21},{6,22},{7,23},{8,24},{9,... | collective-permute-start | bytes 344072 | tf_op jit(solution)/shard_map/ppermute | solution.py:367
  60.5 0.5 collective-permute-start.20
  61.2 7.1 %collective-permute-done.21 = bf16[7,64,128]{2,1,0:T(8,128)(2,1)S(1)} collective-permute-done((bf16[7,64,128]{2,1,0:T(8,128)(2,1)S(1)}, bf16[7,64,128]{2,1,0:T(8,128)(2,1)S(1)}, u32[]{:S(2)}, u32[]{:S(2)}) %collective-permute-start.21) | collective-permute-done | bytes 114720 | tf_op jit(solution)/shard_map/ppermute | solution.py:367
  68.3 0.6 collective-permute-done.19
  69.1 1.6 %collective-permute-done.22.other_ref = f32[10,64,128]{2,1,0:T(8,128)S(1)} collective-permute-done((f32[10,64,128]{2,1,0:T(8,128)S(1)}, f32[10,64,128]{2,1,0:T(8,128)S(1)}, u32[]{:S(2)}, u32[]{:S(2)}) %collective-permute-start.22) | collective-permute-done | bytes 327712 | tf_op jit(solution)/shard_map/ppermute | solution.py:367
  70.7 12.0 %top_kernel.1 = (bf16[128,512]{1,0:T(8,128)(2,1)S(1)}, f32[256,256]{1,0:T(8,128)S(1)}, bf16[256,128]{1,0:T(8,128)(2,1)S(1)}) custom-call(s32[1]{0:T(128)} %bitcast.pos_ref, f32[10,64,128]{2,1,0:T(8,128)S(1)} %convert_dynamic-update-slice_fusion.mine_ref, f32[10,64,128]{2,1,0:T(8,128)S(1)} %collective-permute-done.22.other_ref, ...), custom_call_target="tpu_custom_call" | custom-call | tf_op jit(solution)/shard_map/top_kernel/pallas_call | solution.py:350
  82.7 2.5 %collective-permute-start.25 = (bf16[128,512]{1,0:T(8,128)(2,1)S(1)}, bf16[128,512]{1,0:T(8,128)(2,1)S(1)}, u32[]{:S(2)}, u32[]{:S(2)}) collective-permute-start(bf16[128,512]{1,0:T(8,128)(2,1)S(1)} %get-tuple-element.56.refs_0_), channel_id=1, source_target_pairs={{0,16},{1,17},{2,18},{3,19},{4,20},{5,21},{6,22},{7,23},{8,24},{9,... | collective-permute-start | bytes 393224 | tf_op jit(solution)/shard_map/ppermute | solution.py:367
  85.1 1.8 %collective-permute-start.24 = (bf16[128,512]{1,0:T(8,128)(2,1)S(1)}, bf16[128,512]{1,0:T(8,128)(2,1)S(1)}, u32[]{:S(2)}, u32[]{:S(2)}) collective-permute-start(bf16[128,512]{1,0:T(8,128)(2,1)S(1)} %get-tuple-element.56.refs_0_), channel_id=1, source_target_pairs={{0,24},{1,25},{2,26},{3,27},{4,28},{5,29},{6,30},{7,31},{8,16},{9,... | collective-permute-start | bytes 393224 | tf_op jit(solution)/shard_map/ppermute | solution.py:367
  86.9 3.4 %factor_kernel.1.factor_ref = f32[128,128]{1,0:T(8,128)S(1)} custom-call(f32[256,256]{1,0:T(8,128)S(1)} %get-tuple-element.54.gram_ref, bf16[256,128]{1,0:T(8,128)(2,1)S(1)} %get-tuple-element.55.low_ref), custom_call_target="tpu_custom_call" | custom-call | tf_op jit(solution)/shard_map/factor_kernel/pallas_call | solution.py:350
  90.3 5.3 %collective-permute-done.25.refs_3_ = bf16[128,512]{1,0:T(8,128)(2,1)S(1)} collective-permute-done((bf16[128,512]{1,0:T(8,128)(2,1)S(1)}, bf16[128,512]{1,0:T(8,128)(2,1)S(1)}, u32[]{:S(2)}, u32[]{:S(2)}) %collective-permute-start.25) | collective-permute-done | bytes 131104 | tf_op jit(solution)/shard_map/ppermute | solution.py:367
  95.7 0.5 collective-permute-done.23.refs_1_
  96.2 0.8 coeffs_kernel.1
  97.1 1.2 %collective-permute-done.26 = f32[1,128,128]{2,1,0:T(8,128)S(1)} collective-permute-done((f32[1,128,128]{2,1,0:T(8,128)S(1)}, f32[1,128,128]{2,1,0:T(8,128)S(1)}, u32[]{:S(2)}, u32[]{:S(2)}) %collective-permute-start.26) | collective-permute-done | bytes 65568 | tf_op jit(solution)/shard_map/ppermute | solution.py:367
  98.3 0.9 collective-permute-start.29
  99.2 1.1 collective-permute-start.28
  100.3 1.6 %collective-permute-start.27 = (bf16[1,128,128]{2,1,0:T(8,128)(2,1)S(1)}, bf16[1,128,128]{2,1,0:T(8,128)(2,1)S(1)}, u32[]{:S(2)}, u32[]{:S(2)}) collective-permute-start(bf16[1,128,128]{2,1,0:T(8,128)(2,1)S(1)} %add_convert_fusion.3), channel_id=1, source_target_pairs={{0,6},{1,7},{2,4},{3,5},{4,2},{5,3},{6,0},{7,1},{8,14},{9,15},{10,... | collective-permute-start | bytes 98312 | tf_op jit(solution)/shard_map/ppermute | solution.py:367
  101.9 0.4 collective-permute-done.29
  102.3 0.8 collective-permute-done.28
  103.1 2.0 %collective-permute-done.27 = bf16[1,128,128]{2,1,0:T(8,128)(2,1)S(1)} collective-permute-done((bf16[1,128,128]{2,1,0:T(8,128)(2,1)S(1)}, bf16[1,128,128]{2,1,0:T(8,128)(2,1)S(1)}, u32[]{:S(2)}, u32[]{:S(2)}) %collective-permute-start.27) | collective-permute-done | bytes 32800 | tf_op jit(solution)/shard_map/ppermute | solution.py:367
  105.2 1.2 %collective-permute-done.30.other_ref = f32[1,128,128]{2,1,0:T(8,128)S(1)} collective-permute-done((f32[1,128,128]{2,1,0:T(8,128)S(1)}, f32[1,128,128]{2,1,0:T(8,128)S(1)}, u32[]{:S(2)}, u32[]{:S(2)}) %collective-permute-start.30) | collective-permute-done | bytes 65568 | tf_op jit(solution)/shard_map/ppermute | solution.py:367
  106.5 0.8 project_kernel.1
  107.3 1.6 %collective-permute-start.31 = (bf16[32,2048]{1,0:T(8,128)(2,1)S(1)}, bf16[32,2048]{1,0:T(8,128)(2,1)S(1)}, u32[]{:S(2)}, u32[]{:S(2)}) collective-permute-start(bf16[32,2048]{1,0:T(8,128)(2,1)S(1)} %get-tuple-element.60), channel_id=1, source_target_pairs={{0,6},{1,7},{2,4},{3,5},{4,2},{5,3},{6,0},{7,1},{8,14},{9,15},{10,... | collective-permute-start | bytes 393224 | tf_op jit(solution)/shard_map/ppermute | solution.py:367
  108.9 0.9 collective-permute-start.32
  109.7 1.7 %collective-permute-start.33 = (bf16[32,2048]{1,0:T(8,128)(2,1)S(1)}, bf16[32,2048]{1,0:T(8,128)(2,1)S(1)}, u32[]{:S(2)}, u32[]{:S(2)}) collective-permute-start(bf16[32,2048]{1,0:T(8,128)(2,1)S(1)} %get-tuple-element.62), channel_id=1, source_target_pairs={{0,2},{1,3},{2,0},{3,1},{4,6},{5,7},{6,4},{7,5},{8,10},{9,11},{10,... | collective-permute-start | bytes 393224 | tf_op jit(solution)/shard_map/ppermute | solution.py:367
  111.9 0.5 collective-permute-start.35
  112.4 2.2 %collective-permute-done.31.refs_1_ = bf16[32,2048]{1,0:T(8,128)(2,1)S(1)} collective-permute-done((bf16[32,2048]{1,0:T(8,128)(2,1)S(1)}, bf16[32,2048]{1,0:T(8,128)(2,1)S(1)}, u32[]{:S(2)}, u32[]{:S(2)}) %collective-permute-start.31) | collective-permute-done | bytes 131104 | tf_op jit(solution)/shard_map/ppermute | solution.py:367
  114.6 1.3 %collective-permute-done.32.refs_2_ = bf16[32,2048]{1,0:T(8,128)(2,1)S(1)} collective-permute-done((bf16[32,2048]{1,0:T(8,128)(2,1)S(1)}, bf16[32,2048]{1,0:T(8,128)(2,1)S(1)}, u32[]{:S(2)}, u32[]{:S(2)}) %collective-permute-start.32) | collective-permute-done | bytes 131104 | tf_op jit(solution)/shard_map/ppermute | solution.py:367
  115.9 1.3 %collective-permute-start.37 = (bf16[32,2048]{1,0:T(8,128)(2,1)S(1)}, bf16[32,2048]{1,0:T(8,128)(2,1)S(1)}, u32[]{:S(2)}, u32[]{:S(2)}) collective-permute-start(bf16[32,2048]{1,0:T(8,128)(2,1)S(1)} %get-tuple-element.66), channel_id=1, source_target_pairs={{0,1},{1,0},{2,3},{3,2},{4,5},{5,4},{6,7},{7,6},{8,9},{9,8},{10,11... | collective-permute-start | bytes 393224 | tf_op jit(solution)/shard_map/ppermute | solution.py:367
  117.2 2.0 %collective-permute-done.33.refs_3_ = bf16[32,2048]{1,0:T(8,128)(2,1)S(1)} collective-permute-done((bf16[32,2048]{1,0:T(8,128)(2,1)S(1)}, bf16[32,2048]{1,0:T(8,128)(2,1)S(1)}, u32[]{:S(2)}, u32[]{:S(2)}) %collective-permute-start.33) | collective-permute-done | bytes 131104 | tf_op jit(solution)/shard_map/ppermute | solution.py:367
  119.5 2.0 %collective-permute-done.35.refs_5_ = bf16[32,2048]{1,0:T(8,128)(2,1)S(1)} collective-permute-done((bf16[32,2048]{1,0:T(8,128)(2,1)S(1)}, bf16[32,2048]{1,0:T(8,128)(2,1)S(1)}, u32[]{:S(2)}, u32[]{:S(2)}) %collective-permute-start.35) | collective-permute-done | bytes 131104 | tf_op jit(solution)/shard_map/ppermute | solution.py:367
  121.5 0.7 collective-permute-done.36.refs_6_
  122.2 1.0 whole_kernel.1
  (36 shorter events, 2.0 us)
Async XLA Ops:
  0.0 1.2 copy-start
  1.3 7.9 %collective-permute-start = (bf16[32,2048]{1,0:T(8,128)(2,1)S(1)}, bf16[32,2048]{1,0:T(8,128)(2,1)S(1)}, u32[]{:S(2)}, u32[]{:S(2)}) collective-permute-start(bf16[32,2048]{1,0:T(8,128)(2,1)S(1)} %get-tuple-element.37), channel_id=1, source_target_pairs={{0,6},{1,7},{2,4},{3,5},{4,2},{5,3},{6,0},{7,1},{8,14},{9,15},{10,... | collective-permute-start | bytes 393224 | tf_op jit(solution)/shard_map/ppermute | solution.py:367
  5.3 6.8 %collective-permute-start.1 = (bf16[32,2048]{1,0:T(8,128)(2,1)S(1)}, bf16[32,2048]{1,0:T(8,128)(2,1)S(1)}, u32[]{:S(2)}, u32[]{:S(2)}) collective-permute-start(bf16[32,2048]{1,0:T(8,128)(2,1)S(1)} %get-tuple-element.38), channel_id=1, source_target_pairs={{0,7},{1,6},{2,5},{3,4},{4,3},{5,2},{6,1},{7,0},{8,15},{9,14},{10,... | collective-permute-start | bytes 393224 | tf_op jit(solution)/shard_map/ppermute | solution.py:367
  5.3 10.2 %collective-permute-start.2 = (bf16[32,2048]{1,0:T(8,128)(2,1)S(1)}, bf16[32,2048]{1,0:T(8,128)(2,1)S(1)}, u32[]{:S(2)}, u32[]{:S(2)}) collective-permute-start(bf16[32,2048]{1,0:T(8,128)(2,1)S(1)} %get-tuple-element.39), channel_id=1, source_target_pairs={{0,2},{1,3},{2,0},{3,1},{4,6},{5,7},{6,4},{7,5},{8,10},{9,11},{10,... | collective-permute-start | bytes 393224 | tf_op jit(solution)/shard_map/ppermute | solution.py:367
  6.4 9.1 %collective-permute-start.3 = (bf16[32,2048]{1,0:T(8,128)(2,1)S(1)}, bf16[32,2048]{1,0:T(8,128)(2,1)S(1)}, u32[]{:S(2)}, u32[]{:S(2)}) collective-permute-start(bf16[32,2048]{1,0:T(8,128)(2,1)S(1)} %get-tuple-element.40), channel_id=1, source_target_pairs={{0,4},{1,5},{2,6},{3,7},{4,0},{5,1},{6,2},{7,3},{8,12},{9,13},{10,... | collective-permute-start | bytes 393224 | tf_op jit(solution)/shard_map/ppermute | solution.py:367
  7.9 8.7 %collective-permute-start.4 = (bf16[32,2048]{1,0:T(8,128)(2,1)S(1)}, bf16[32,2048]{1,0:T(8,128)(2,1)S(1)}, u32[]{:S(2)}, u32[]{:S(2)}) collective-permute-start(bf16[32,2048]{1,0:T(8,128)(2,1)S(1)} %get-tuple-element.41), channel_id=1, source_target_pairs={{0,3},{1,2},{2,1},{3,0},{4,7},{5,6},{6,5},{7,4},{8,11},{9,10},{10,... | collective-permute-start | bytes 393224 | tf_op jit(solution)/shard_map/ppermute | solution.py:367
  9.2 8.1 %collective-permute-start.5 = (bf16[32,2048]{1,0:T(8,128)(2,1)S(1)}, bf16[32,2048]{1,0:T(8,128)(2,1)S(1)}, u32[]{:S(2)}, u32[]{:S(2)}) collective-permute-start(bf16[32,2048]{1,0:T(8,128)(2,1)S(1)} %get-tuple-element.42), channel_id=1, source_target_pairs={{0,5},{1,4},{2,7},{3,6},{4,1},{5,0},{6,3},{7,2},{8,13},{9,12},{10,... | collective-permute-start | bytes 393224 | tf_op jit(solution)/shard_map/ppermute | solution.py:367
  12.0 5.3 %collective-permute-start.6 = (bf16[32,2048]{1,0:T(8,128)(2,1)S(1)}, bf16[32,2048]{1,0:T(8,128)(2,1)S(1)}, u32[]{:S(2)}, u32[]{:S(2)}) collective-permute-start(bf16[32,2048]{1,0:T(8,128)(2,1)S(1)} %get-tuple-element.43), channel_id=1, source_target_pairs={{0,1},{1,0},{2,3},{3,2},{4,5},{5,4},{6,7},{7,6},{8,9},{9,8},{10,11... | collective-permute-start | bytes 393224 | tf_op jit(solution)/shard_map/ppermute | solution.py:367
  17.8 1.4 %collective-permute-start.7 = (f32[3,64,128]{2,1,0:T(8,128)S(1)}, f32[3,64,128]{2,1,0:T(8,128)S(1)}, u32[]{:S(2)}, u32[]{:S(2)}) collective-permute-start(f32[3,64,128]{2,1,0:T(8,128)S(1)} %get-tuple-element.46), channel_id=1, source_target_pairs={{0,1},{1,0},{2,3},{3,2},{4,5},{5,4},{6,7},{7,6},{8,9},{9,8},{10,11... | collective-permute-start | bytes 294920 | tf_op jit(solution)/shard_map/ppermute | solution.py:367
  19.2 4.2 %collective-permute-start.10 = (bf16[3,64,128]{2,1,0:T(8,128)(2,1)S(1)}, bf16[3,64,128]{2,1,0:T(8,128)(2,1)S(1)}, u32[]{:S(2)}, u32[]{:S(2)}) collective-permute-start(bf16[3,64,128]{2,1,0:T(8,128)(2,1)S(1)} %add_convert_fusion.2), channel_id=1, source_target_pairs={{0,2},{1,3},{2,0},{3,1},{4,6},{5,7},{6,4},{7,5},{8,10},{9,11},{10,... | collective-permute-start | bytes 147464 | tf_op jit(solution)/shard_map/ppermute | solution.py:367
  20.8 4.1 %collective-permute-start.9 = (bf16[3,64,128]{2,1,0:T(8,128)(2,1)S(1)}, bf16[3,64,128]{2,1,0:T(8,128)(2,1)S(1)}, u32[]{:S(2)}, u32[]{:S(2)}) collective-permute-start(bf16[3,64,128]{2,1,0:T(8,128)(2,1)S(1)} %add_convert_fusion.2), channel_id=1, source_target_pairs={{0,4},{1,5},{2,6},{3,7},{4,0},{5,1},{6,2},{7,3},{8,12},{9,13},{10,... | collective-permute-start | bytes 147464 | tf_op jit(solution)/shard_map/ppermute | solution.py:367
  22.4 5.0 %collective-permute-start.8 = (bf16[3,64,128]{2,1,0:T(8,128)(2,1)S(1)}, bf16[3,64,128]{2,1,0:T(8,128)(2,1)S(1)}, u32[]{:S(2)}, u32[]{:S(2)}) collective-permute-start(bf16[3,64,128]{2,1,0:T(8,128)(2,1)S(1)} %add_convert_fusion.2), channel_id=1, source_target_pairs={{0,6},{1,7},{2,4},{3,5},{4,2},{5,3},{6,0},{7,1},{8,14},{9,15},{10,... | collective-permute-start | bytes 147464 | tf_op jit(solution)/shard_map/ppermute | solution.py:367
  27.4 1.4 %collective-permute-start.11 = (f32[3,64,128]{2,1,0:T(8,128)S(1)}, f32[3,64,128]{2,1,0:T(8,128)S(1)}, u32[]{:S(2)}, u32[]{:S(2)}) collective-permute-start(f32[3,64,128]{2,1,0:T(8,128)S(1)} %add_add_fusion.mine_ref), channel_id=1, source_target_pairs={{0,1},{1,0},{2,3},{3,2},{4,5},{5,4},{6,7},{7,6},{8,9},{9,8},{10,11... | collective-permute-start | bytes 294920 | tf_op jit(solution)/shard_map/ppermute | solution.py:367
  33.5 13.0 %collective-permute-start.12 = (bf16[128,512]{1,0:T(8,128)(2,1)S(1)}, bf16[128,512]{1,0:T(8,128)(2,1)S(1)}, u32[]{:S(2)}, u32[]{:S(2)}) collective-permute-start(bf16[128,512]{1,0:T(8,128)(2,1)S(1)} %get-tuple-element.48), channel_id=1, source_target_pairs={{0,16},{1,17},{2,18},{3,19},{4,20},{5,21},{6,22},{7,23},{8,24},{9,... | collective-permute-start | bytes 393224 | tf_op jit(solution)/shard_map/ppermute | solution.py:367
  36.2 10.3 %collective-permute-start.13 = (bf16[128,512]{1,0:T(8,128)(2,1)S(1)}, bf16[128,512]{1,0:T(8,128)(2,1)S(1)}, u32[]{:S(2)}, u32[]{:S(2)}) collective-permute-start(bf16[128,512]{1,0:T(8,128)(2,1)S(1)} %get-tuple-element.49), channel_id=1, source_target_pairs={{0,24},{1,25},{2,26},{3,27},{4,28},{5,29},{6,30},{7,31},{8,16},{9,... | collective-permute-start | bytes 393224 | tf_op jit(solution)/shard_map/ppermute | solution.py:367
  37.5 9.5 %collective-permute-start.14 = (bf16[128,512]{1,0:T(8,128)(2,1)S(1)}, bf16[128,512]{1,0:T(8,128)(2,1)S(1)}, u32[]{:S(2)}, u32[]{:S(2)}) collective-permute-start(bf16[128,512]{1,0:T(8,128)(2,1)S(1)} %get-tuple-element.50), channel_id=1, source_target_pairs={{0,8},{1,9},{2,10},{3,11},{4,12},{5,13},{6,14},{7,15},{8,0},{9,1},... | collective-permute-start | bytes 393224 | tf_op jit(solution)/shard_map/ppermute | solution.py:367
  47.5 1.5 %collective-permute-start.15 = (f32[6,64,128]{2,1,0:T(8,128)S(1)}, f32[6,64,128]{2,1,0:T(8,128)S(1)}, u32[]{:S(2)}, u32[]{:S(2)}) collective-permute-start(f32[6,64,128]{2,1,0:T(8,128)S(1)} %get-tuple-element.52), channel_id=1, source_target_pairs={{0,1},{1,0},{2,3},{3,2},{4,5},{5,4},{6,7},{7,6},{8,9},{9,8},{10,11... | collective-permute-start | bytes 589832 | tf_op jit(solution)/shard_map/ppermute | solution.py:367
  49.0 5.6 %collective-permute-start.18 = (bf16[6,64,128]{2,1,0:T(8,128)(2,1)S(1)}, bf16[6,64,128]{2,1,0:T(8,128)(2,1)S(1)}, u32[]{:S(2)}, u32[]{:S(2)}) collective-permute-start(bf16[6,64,128]{2,1,0:T(8,128)(2,1)S(1)} %add_convert_fusion.1), channel_id=1, source_target_pairs={{0,2},{1,3},{2,0},{3,1},{4,6},{5,7},{6,4},{7,5},{8,10},{9,11},{10,... | collective-permute-start | bytes 294920 | tf_op jit(solution)/shard_map/ppermute | solution.py:367
  49.6 6.7 %collective-permute-start.17 = (bf16[6,64,128]{2,1,0:T(8,128)(2,1)S(1)}, bf16[6,64,128]{2,1,0:T(8,128)(2,1)S(1)}, u32[]{:S(2)}, u32[]{:S(2)}) collective-permute-start(bf16[6,64,128]{2,1,0:T(8,128)(2,1)S(1)} %add_convert_fusion.1), channel_id=1, source_target_pairs={{0,4},{1,5},{2,6},{3,7},{4,0},{5,1},{6,2},{7,3},{8,12},{9,13},{10,... | collective-permute-start | bytes 294920 | tf_op jit(solution)/shard_map/ppermute | solution.py:367
  50.1 6.2 %collective-permute-start.16 = (bf16[6,64,128]{2,1,0:T(8,128)(2,1)S(1)}, bf16[6,64,128]{2,1,0:T(8,128)(2,1)S(1)}, u32[]{:S(2)}, u32[]{:S(2)}) collective-permute-start(bf16[6,64,128]{2,1,0:T(8,128)(2,1)S(1)} %add_convert_fusion.1), channel_id=1, source_target_pairs={{0,6},{1,7},{2,4},{3,5},{4,2},{5,3},{6,0},{7,1},{8,14},{9,15},{10,... | collective-permute-start | bytes 294920 | tf_op jit(solution)/shard_map/ppermute | solution.py:367
  56.4 11.9 %collective-permute-start.21 = (bf16[7,64,128]{2,1,0:T(8,128)(2,1)S(1)}, bf16[7,64,128]{2,1,0:T(8,128)(2,1)S(1)}, u32[]{:S(2)}, u32[]{:S(2)}) collective-permute-start(bf16[7,64,128]{2,1,0:T(8,128)(2,1)S(1)} %pad_maximum_fusion), channel_id=1, source_target_pairs={{0,16},{1,17},{2,18},{3,19},{4,20},{5,21},{6,22},{7,23},{8,24},{9,... | collective-permute-start | bytes 344072 | tf_op jit(solution)/shard_map/ppermute | solution.py:367
  60.5 7.8 %collective-permute-start.20 = (bf16[7,64,128]{2,1,0:T(8,128)(2,1)S(1)}, bf16[7,64,128]{2,1,0:T(8,128)(2,1)S(1)}, u32[]{:S(2)}, u32[]{:S(2)}) collective-permute-start(bf16[7,64,128]{2,1,0:T(8,128)(2,1)S(1)} %pad_maximum_fusion), channel_id=1, source_target_pairs={{0,24},{1,25},{2,26},{3,27},{4,28},{5,29},{6,30},{7,31},{8,16},{9,... | collective-permute-start | bytes 344072 | tf_op jit(solution)/shard_map/ppermute | solution.py:367
  61.0 7.9 %collective-permute-start.19 = (bf16[7,64,128]{2,1,0:T(8,128)(2,1)S(1)}, bf16[7,64,128]{2,1,0:T(8,128)(2,1)S(1)}, u32[]{:S(2)}, u32[]{:S(2)}) collective-permute-start(bf16[7,64,128]{2,1,0:T(8,128)(2,1)S(1)} %pad_maximum_fusion), channel_id=1, source_target_pairs={{0,8},{1,9},{2,10},{3,11},{4,12},{5,13},{6,14},{7,15},{8,0},{9,1},... | collective-permute-start | bytes 344072 | tf_op jit(solution)/shard_map/ppermute | solution.py:367
  69.0 1.7 %collective-permute-start.22 = (f32[10,64,128]{2,1,0:T(8,128)S(1)}, f32[10,64,128]{2,1,0:T(8,128)S(1)}, u32[]{:S(2)}, u32[]{:S(2)}) collective-permute-start(f32[10,64,128]{2,1,0:T(8,128)S(1)} %convert_dynamic-update-slice_fusion.mine_ref), channel_id=1, source_target_pairs={{0,1},{1,0},{2,3},{3,2},{4,5},{5,4},{6,7},{7,6},{8,9},{9,8},{10,11... | collective-permute-start | bytes 983048 | tf_op jit(solution)/shard_map/ppermute | solution.py:367
  82.7 13.0 %collective-permute-start.25 = (bf16[128,512]{1,0:T(8,128)(2,1)S(1)}, bf16[128,512]{1,0:T(8,128)(2,1)S(1)}, u32[]{:S(2)}, u32[]{:S(2)}) collective-permute-start(bf16[128,512]{1,0:T(8,128)(2,1)S(1)} %get-tuple-element.56.refs_0_), channel_id=1, source_target_pairs={{0,16},{1,17},{2,18},{3,19},{4,20},{5,21},{6,22},{7,23},{8,24},{9,... | collective-permute-start | bytes 393224 | tf_op jit(solution)/shard_map/ppermute | solution.py:367
  85.1 10.5 %collective-permute-start.24 = (bf16[128,512]{1,0:T(8,128)(2,1)S(1)}, bf16[128,512]{1,0:T(8,128)(2,1)S(1)}, u32[]{:S(2)}, u32[]{:S(2)}) collective-permute-start(bf16[128,512]{1,0:T(8,128)(2,1)S(1)} %get-tuple-element.56.refs_0_), channel_id=1, source_target_pairs={{0,24},{1,25},{2,26},{3,27},{4,28},{5,29},{6,30},{7,31},{8,16},{9,... | collective-permute-start | bytes 393224 | tf_op jit(solution)/shard_map/ppermute | solution.py:367
  86.9 9.3 %collective-permute-start.23 = (bf16[128,512]{1,0:T(8,128)(2,1)S(1)}, bf16[128,512]{1,0:T(8,128)(2,1)S(1)}, u32[]{:S(2)}, u32[]{:S(2)}) collective-permute-start(bf16[128,512]{1,0:T(8,128)(2,1)S(1)} %get-tuple-element.56.refs_0_), channel_id=1, source_target_pairs={{0,8},{1,9},{2,10},{3,11},{4,12},{5,13},{6,14},{7,15},{8,0},{9,1},... | collective-permute-start | bytes 393224 | tf_op jit(solution)/shard_map/ppermute | solution.py:367
  97.0 1.3 %collective-permute-start.26 = (f32[1,128,128]{2,1,0:T(8,128)S(1)}, f32[1,128,128]{2,1,0:T(8,128)S(1)}, u32[]{:S(2)}, u32[]{:S(2)}) collective-permute-start(f32[1,128,128]{2,1,0:T(8,128)S(1)} %get-tuple-element.58), channel_id=1, source_target_pairs={{0,1},{1,0},{2,3},{3,2},{4,5},{5,4},{6,7},{7,6},{8,9},{9,8},{10,11... | collective-permute-start | bytes 196616 | tf_op jit(solution)/shard_map/ppermute | solution.py:367
  98.3 4.0 %collective-permute-start.29 = (bf16[1,128,128]{2,1,0:T(8,128)(2,1)S(1)}, bf16[1,128,128]{2,1,0:T(8,128)(2,1)S(1)}, u32[]{:S(2)}, u32[]{:S(2)}) collective-permute-start(bf16[1,128,128]{2,1,0:T(8,128)(2,1)S(1)} %add_convert_fusion.3), channel_id=1, source_target_pairs={{0,2},{1,3},{2,0},{3,1},{4,6},{5,7},{6,4},{7,5},{8,10},{9,11},{10,... | collective-permute-start | bytes 98312 | tf_op jit(solution)/shard_map/ppermute | solution.py:367
  99.2 3.9 %collective-permute-start.28 = (bf16[1,128,128]{2,1,0:T(8,128)(2,1)S(1)}, bf16[1,128,128]{2,1,0:T(8,128)(2,1)S(1)}, u32[]{:S(2)}, u32[]{:S(2)}) collective-permute-start(bf16[1,128,128]{2,1,0:T(8,128)(2,1)S(1)} %add_convert_fusion.3), channel_id=1, source_target_pairs={{0,4},{1,5},{2,6},{3,7},{4,0},{5,1},{6,2},{7,3},{8,12},{9,13},{10,... | collective-permute-start | bytes 98312 | tf_op jit(solution)/shard_map/ppermute | solution.py:367
  100.3 4.8 %collective-permute-start.27 = (bf16[1,128,128]{2,1,0:T(8,128)(2,1)S(1)}, bf16[1,128,128]{2,1,0:T(8,128)(2,1)S(1)}, u32[]{:S(2)}, u32[]{:S(2)}) collective-permute-start(bf16[1,128,128]{2,1,0:T(8,128)(2,1)S(1)} %add_convert_fusion.3), channel_id=1, source_target_pairs={{0,6},{1,7},{2,4},{3,5},{4,2},{5,3},{6,0},{7,1},{8,14},{9,15},{10,... | collective-permute-start | bytes 98312 | tf_op jit(solution)/shard_map/ppermute | solution.py:367
  105.2 1.3 %collective-permute-start.30 = (f32[1,128,128]{2,1,0:T(8,128)S(1)}, f32[1,128,128]{2,1,0:T(8,128)S(1)}, u32[]{:S(2)}, u32[]{:S(2)}) collective-permute-start(f32[1,128,128]{2,1,0:T(8,128)S(1)} %add_add_fusion.1.mine_ref), channel_id=1, source_target_pairs={{0,1},{1,0},{2,3},{3,2},{4,5},{5,4},{6,7},{7,6},{8,9},{9,8},{10,11... | collective-permute-start | bytes 196616 | tf_op jit(solution)/shard_map/ppermute | solution.py:367
  107.3 7.3 %collective-permute-start.31 = (bf16[32,2048]{1,0:T(8,128)(2,1)S(1)}, bf16[32,2048]{1,0:T(8,128)(2,1)S(1)}, u32[]{:S(2)}, u32[]{:S(2)}) collective-permute-start(bf16[32,2048]{1,0:T(8,128)(2,1)S(1)} %get-tuple-element.60), channel_id=1, source_target_pairs={{0,6},{1,7},{2,4},{3,5},{4,2},{5,3},{6,0},{7,1},{8,14},{9,15},{10,... | collective-permute-start | bytes 393224 | tf_op jit(solution)/shard_map/ppermute | solution.py:367
  108.9 7.0 %collective-permute-start.32 = (bf16[32,2048]{1,0:T(8,128)(2,1)S(1)}, bf16[32,2048]{1,0:T(8,128)(2,1)S(1)}, u32[]{:S(2)}, u32[]{:S(2)}) collective-permute-start(bf16[32,2048]{1,0:T(8,128)(2,1)S(1)} %get-tuple-element.61), channel_id=1, source_target_pairs={{0,7},{1,6},{2,5},{3,4},{4,3},{5,2},{6,1},{7,0},{8,15},{9,14},{10,... | collective-permute-start | bytes 393224 | tf_op jit(solution)/shard_map/ppermute | solution.py:367
  109.7 9.4 %collective-permute-start.33 = (bf16[32,2048]{1,0:T(8,128)(2,1)S(1)}, bf16[32,2048]{1,0:T(8,128)(2,1)S(1)}, u32[]{:S(2)}, u32[]{:S(2)}) collective-permute-start(bf16[32,2048]{1,0:T(8,128)(2,1)S(1)} %get-tuple-element.62), channel_id=1, source_target_pairs={{0,2},{1,3},{2,0},{3,1},{4,6},{5,7},{6,4},{7,5},{8,10},{9,11},{10,... | collective-permute-start | bytes 393224 | tf_op jit(solution)/shard_map/ppermute | solution.py:367
  111.5 8.0 %collective-permute-start.34 = (bf16[32,2048]{1,0:T(8,128)(2,1)S(1)}, bf16[32,2048]{1,0:T(8,128)(2,1)S(1)}, u32[]{:S(2)}, u32[]{:S(2)}) collective-permute-start(bf16[32,2048]{1,0:T(8,128)(2,1)S(1)} %get-tuple-element.63), channel_id=1, source_target_pairs={{0,4},{1,5},{2,6},{3,7},{4,0},{5,1},{6,2},{7,3},{8,12},{9,13},{10,... | collective-permute-start | bytes 393224 | tf_op jit(solution)/shard_map/ppermute | solution.py:367
  111.9 9.6 %collective-permute-start.35 = (bf16[32,2048]{1,0:T(8,128)(2,1)S(1)}, bf16[32,2048]{1,0:T(8,128)(2,1)S(1)}, u32[]{:S(2)}, u32[]{:S(2)}) collective-permute-start(bf16[32,2048]{1,0:T(8,128)(2,1)S(1)} %get-tuple-element.64), channel_id=1, source_target_pairs={{0,3},{1,2},{2,1},{3,0},{4,7},{5,6},{6,5},{7,4},{8,11},{9,10},{10,... | collective-permute-start | bytes 393224 | tf_op jit(solution)/shard_map/ppermute | solution.py:367
  114.6 7.6 %collective-permute-start.36 = (bf16[32,2048]{1,0:T(8,128)(2,1)S(1)}, bf16[32,2048]{1,0:T(8,128)(2,1)S(1)}, u32[]{:S(2)}, u32[]{:S(2)}) collective-permute-start(bf16[32,2048]{1,0:T(8,128)(2,1)S(1)} %get-tuple-element.65), channel_id=1, source_target_pairs={{0,5},{1,4},{2,7},{3,6},{4,1},{5,0},{6,3},{7,2},{8,13},{9,12},{10,... | collective-permute-start | bytes 393224 | tf_op jit(solution)/shard_map/ppermute | solution.py:367
  115.9 6.3 %collective-permute-start.37 = (bf16[32,2048]{1,0:T(8,128)(2,1)S(1)}, bf16[32,2048]{1,0:T(8,128)(2,1)S(1)}, u32[]{:S(2)}, u32[]{:S(2)}) collective-permute-start(bf16[32,2048]{1,0:T(8,128)(2,1)S(1)} %get-tuple-element.66), channel_id=1, source_target_pairs={{0,1},{1,0},{2,3},{3,2},{4,5},{5,4},{6,7},{7,6},{8,9},{9,8},{10,11... | collective-permute-start | bytes 393224 | tf_op jit(solution)/shard_map/ppermute | solution.py:367
